TPU v7x, 32 devices: a whole 2x2x4 slice. The times are simulated.
32 devices in a mesh: groups: 2 (over x), frame: 16 (over z, y, core).
Axes of the slice: x: 2, y: 2, z: 4, core: 2. Of those that a mesh axis runs over, the one named last changes fastest.
Arguments:
- latent: bfloat16 [2048, 1536], P(('groups', 'frame')), parts along dimension 0, may hold values from -6 to 6
- norm_gain: float32 [1536], replicated, may hold values from 0.25 to 1.75
- w_query: bfloat16 [1536, 1536], P('frame'), may hold values from -0.3125 to 0.3125
- w_key: bfloat16 [1536, 1536], P('frame'), may hold values from -0.15625 to 0.15625
- w_value: bfloat16 [1536, 1536], P('frame'), may hold values from -0.625 to 0.625
- mem_cache: bfloat16 [256, 16, 2, 1536], P('groups', 'frame'), parts along dimension 0, may hold values from -60 to 60
- intersection: int32 [8, 8], P('groups'), parts along dimension 0, may hold values from 0 to 127, as said below
- counts: int32 [8], P('groups'), parts along dimension 0, may hold values from 1 to 8, as said below
- slot_of: int32 [256], P('groups'), parts along dimension 0, may hold values from 0 to 127, each once
- step_scale: float32 [2], replicated, may hold values from 0.5 to 1.5
Outputs:
- denoised: bfloat16 [2048, 1536], P(('groups', 'frame')), parts along dimension 0
There are 2 independent parts, one for each index of `groups`. A program takes and returns all parts, laid end to end along the dimension named above; an argument that names none is the same for every part. Nothing has to cross between parts.
Inputs may be any that keep to these rules, and one draw needn't show every extreme that they name: `intersection`: each row names 8 different memory frames. `counts`: some frame has all 8 entries live.
All inputs are finite; a program needn't handle non-finite values.
Results may differ from a plain program's by a relative error of at most 0.025.
The roundings to bfloat16 on the way count: a program that leaves them out, or rounds other values in their place, can miss the bound.
Values may be sent and summed in bfloat16 or wider, within the bound.
No kernel may reach another device: no remote copies, remote signals or barrier semaphores. Data moves between devices by JAX's collectives and lax.ppermute only.
A program may use at most 128 MiB of HBM per device.

v0:
```python
import math

import jax
import jax.numpy as jnp
from jax import lax
from jax.sharding import PartitionSpec as P

HEADS = 12
HS = 128
SPATIAL = 4
STEPS = 2


def from_partner(array, axis, bit):
    return lax.ppermute(array, axis, [(i, i ^ 1 << bit) for i in range(lax.axis_size(axis))])


def in_order(mine, theirs, upper, axis_dim):
    low_first = jnp.concatenate([mine, theirs], axis=axis_dim)
    high_first = jnp.concatenate([theirs, mine], axis=axis_dim)
    return jnp.where(upper, high_first, low_first)


def attend(queries, frame_pair, mem_keys, mem_values, live_keys, head_count):
    tok_rows, feature_width = queries.shape
    head_size = feature_width // head_count
    scale_dot = 1.0 / math.sqrt(head_size)
    q_heads = queries.reshape(tok_rows, head_count, head_size)
    k_heads = frame_pair[0].reshape(-1, head_count, head_size)
    v_heads = frame_pair[1].reshape(-1, head_count, head_size)
    frame_scores = (
        jnp.einsum("thd,khd->htk", q_heads, k_heads, preferred_element_type=jnp.float32) * scale_dot
    )
    remote_scores = (
        jnp.einsum("thd,khd->htk", q_heads, mem_keys, preferred_element_type=jnp.float32)
        * scale_dot
    )
    remote_scores = jnp.where(live_keys[None, None, :], remote_scores, -1e30)
    largest = jnp.maximum(
        jnp.max(frame_scores, axis=-1, keepdims=True),
        jnp.max(remote_scores, axis=-1, keepdims=True),
    )
    frame_weights = jnp.exp(frame_scores - largest)
    remote_weights = jnp.exp(remote_scores - largest)
    denominator = jnp.sum(frame_weights, axis=-1) + jnp.sum(remote_weights, axis=-1)
    blended = jnp.einsum(
        "htk,khd->thd",
        frame_weights.astype(jnp.bfloat16),
        v_heads,
        preferred_element_type=jnp.float32,
    )
    blended = blended + jnp.einsum(
        "htk,khd->thd",
        remote_weights.astype(jnp.bfloat16),
        mem_values,
        preferred_element_type=jnp.float32,
    )
    blended = blended / jnp.transpose(denominator)[:, :, None]
    return blended.reshape(tok_rows, feature_width).astype(jnp.bfloat16)


def rms_normed(current, norm_gain):
    widened = current.astype(jnp.float32)
    inverse = lax.rsqrt(jnp.mean(widened * widened, axis=-1, keepdims=True) + 1e-06)
    return (widened, (widened * inverse * norm_gain).astype(jnp.bfloat16))


def per_device(
    latent, norm_gain, w_query, w_key, w_value, mem_cache, intersection, counts, slot_of, step_scale
):
    devices = lax.axis_size("frame")
    position = lax.axis_index("frame")
    frame_index = position // SPATIAL
    doublings = SPATIAL.bit_length() - 1
    target_frame = jnp.arange(devices, dtype=jnp.int32) // SPATIAL
    current = latent
    feature_width = latent.shape[1]
    share_width = feature_width // SPATIAL
    head_share = HEADS // SPATIAL

    def column_pieces(weight):
        row_count = weight.shape[0]
        split_cols = jnp.transpose(weight.reshape(row_count, SPATIAL, share_width), (1, 0, 2))
        return jnp.tile(split_cols, (devices // SPATIAL, 1, 1))

    own_query, own_key, own_value = (
        lax.all_to_all(column_pieces(w_query), "frame", split_axis=0, concat_axis=1, tiled=True),
        lax.all_to_all(column_pieces(w_key), "frame", split_axis=0, concat_axis=1, tiled=True),
        lax.all_to_all(column_pieces(w_value), "frame", split_axis=0, concat_axis=1, tiled=True),
    )
    own_query, own_key, own_value = (own_query[0], own_key[0], own_value[0])
    listed = mem_cache[slot_of[intersection[target_frame]]]
    list_len = listed.shape[1]
    local_mem = listed.shape[2]
    grouped = listed.reshape(
        devices // SPATIAL, SPATIAL, list_len, local_mem, 2, SPATIAL, share_width
    )
    diagonal_part = jnp.diagonal(grouped, axis1=1, axis2=5)
    outgoing = jnp.moveaxis(diagonal_part, -1, 1).reshape(
        devices, list_len, local_mem, 2, share_width
    )
    fetched = lax.all_to_all(outgoing, "frame", split_axis=0, concat_axis=2, tiled=True)[0]
    mem_len = fetched.shape[1]
    mem_keys = fetched[:, :, 0, :].reshape(list_len * mem_len, head_share, HS)
    mem_values = fetched[:, :, 1, :].reshape(list_len * mem_len, head_share, HS)
    live_keys = jnp.arange(list_len * mem_len, dtype=jnp.int32) // mem_len < counts[frame_index]
    tok_rows = latent.shape[0]
    for step_index in range(STEPS):
        widened, normed = rms_normed(current, norm_gain)
        gathered = normed
        for bit_index in range(doublings):
            partner = from_partner(gathered, "frame", bit_index)
            gathered = in_order(gathered, partner, position >> bit_index & 1 == 1, 0)
        queries = jnp.dot(gathered, own_query, preferred_element_type=jnp.float32).astype(
            jnp.bfloat16
        )
        keys_frame = jnp.dot(gathered, own_key, preferred_element_type=jnp.float32).astype(
            jnp.bfloat16
        )
        values_frame = jnp.dot(gathered, own_value, preferred_element_type=jnp.float32).astype(
            jnp.bfloat16
        )
        frame_pair = jnp.stack([keys_frame, values_frame])
        attended = attend(queries, frame_pair, mem_keys, mem_values, live_keys, head_share)
        blocks = attended.reshape(SPATIAL, tok_rows, share_width)[:, None]
        for bit_index in range(doublings):
            upper = position >> bit_index & 1 == 1
            dest_count = blocks.shape[0]
            paired = blocks.reshape((dest_count // 2, 2) + blocks.shape[1:])
            kept = jnp.where(upper, paired[:, 1], paired[:, 0])
            sent = jnp.where(upper, paired[:, 0], paired[:, 1])
            arrived = from_partner(sent, "frame", bit_index)
            blocks = in_order(kept, arrived, upper, 1)
        joined = jnp.transpose(blocks[0], (1, 0, 2)).reshape(tok_rows, feature_width)
        current = (widened + step_scale[step_index] * joined.astype(jnp.float32)).astype(
            jnp.bfloat16
        )
    return current


def solution(mesh):
    placed = (
        P(("groups", "frame"), None),
        P(),
        P("frame", None),
        P("frame", None),
        P("frame", None),
        P("groups", "frame", None, None),
        P("groups", None),
        P("groups"),
        P("groups"),
        P(),
    )
    return jax.shard_map(
        per_device,
        mesh=mesh,
        in_specs=placed,
        out_specs=P(("groups", "frame"), None),
        check_vma=False,
    )
```

profile of v0, /device:TPU:1, one launch (start us, length us, event | category | flops | bytes accessed | tf_op | source)
XLA Modules:
  0.0 162.8 jit_solution(6667244412967508299)
XLA Ops:
  0.0 1.3 gather_fusion
  1.6 1.2 gather_fusion.1
  3.2 2.2 %gather_fusion.2 = bf16[128,2,1536]{2,1,0:T(2,128)(2,1)S(1)} fusion(bf16[128,2,1536]{2,1,0:T(2,128)(2,1)S(1)} %bitcast.131, s32[1024]{0:T(1024)S(1)} %pad_clamp_fusion), kind=kCustom, calls=%fused_computation.2 | custom fusion | bytes 1573376 | tf_op jit(solution)/shard_map/gather | solution.py:92
  5.4 0.5 reshape.556
  6.1 0.6 gather_fusion.3
  6.7 0.7 copy.106
  7.4 7.3 %all-to-all-start.3 = ((bf16[16,8,1,2,384]{4,1,3,2,0:T(8,128)(2,1)}), bf16[16,8,1,2,384]{4,1,3,2,0:T(8,128)(2,1)S(1)}, u32[]{:S(2)}, u32[]{:S(2)}) async-start(bf16[16,8,1,2,384]{4,1,3,2,0:T(8,128)(2,1)} %bitcast.25), calls=%async_computation.3 | async-start | bytes 393216 | tf_op jit(solution)/shard_map/all_to_all | solution.py:102
  14.8 8.2 %all-to-all-done.3 = bf16[16,8,1,2,384]{4,1,3,2,0:T(8,128)(2,1)S(1)} async-done(((bf16[16,8,1,2,384]{4,1,3,2,0:T(8,128)(2,1)}), bf16[16,8,1,2,384]{4,1,3,2,0:T(8,128)(2,1)S(1)}, u32[]{:S(2)}, u32[]{:S(2)}) %all-to-all-start.3) | async-done | bytes 196640 | tf_op jit(solution)/shard_map/all_to_all | solution.py:102
  23.0 1.1 tile.12
  24.1 4.4 %all-to-all-start = ((bf16[16,96,384]{2,1,0:T(8,128)(2,1)}), bf16[16,96,384]{2,1,0:T(8,128)(2,1)S(1)}, u32[]{:S(2)}, u32[]{:S(2)}) async-start(bf16[16,96,384]{2,1,0:T(8,128)(2,1)} %bitcast.4), calls=%async_computation | async-start | bytes 2359296 | tf_op jit(solution)/shard_map/all_to_all | solution.py:89
  28.7 25.5 %all-to-all-done = bf16[16,96,384]{2,1,0:T(8,128)(2,1)S(1)} async-done(((bf16[16,96,384]{2,1,0:T(8,128)(2,1)}), bf16[16,96,384]{2,1,0:T(8,128)(2,1)S(1)}, u32[]{:S(2)}, u32[]{:S(2)}) %all-to-all-start) | async-done | bytes 1179680 | tf_op jit(solution)/shard_map/all_to_all | solution.py:89
  54.1 1.2 tile.31
  55.3 7.0 %all-to-all-start.2 = ((bf16[16,96,384]{2,1,0:T(8,128)(2,1)}), bf16[16,96,384]{2,1,0:T(8,128)(2,1)}, u32[]{:S(2)}, u32[]{:S(2)}) async-start(bf16[16,96,384]{2,1,0:T(8,128)(2,1)} %bitcast.12), calls=%async_computation.2 | async-start | bytes 2359296 | tf_op jit(solution)/shard_map/all_to_all | solution.py:88
  62.5 25.5 %all-to-all-done.2 = bf16[16,96,384]{2,1,0:T(8,128)(2,1)} async-done(((bf16[16,96,384]{2,1,0:T(8,128)(2,1)}), bf16[16,96,384]{2,1,0:T(8,128)(2,1)}, u32[]{:S(2)}, u32[]{:S(2)}) %all-to-all-start.2) | async-done | bytes 1179680 | tf_op jit(solution)/shard_map/all_to_all | solution.py:88
  88.0 1.2 tile.14
  89.2 7.1 %all-to-all-start.1 = ((bf16[16,96,384]{2,1,0:T(8,128)(2,1)}), bf16[16,96,384]{2,1,0:T(8,128)(2,1)}, u32[]{:S(2)}, u32[]{:S(2)}) async-start(bf16[16,96,384]{2,1,0:T(8,128)(2,1)} %bitcast.8), calls=%async_computation.1 | async-start | bytes 2359296 | tf_op jit(solution)/shard_map/all_to_all | solution.py:87
  96.8 1.3 collective-permute-done
  98.1 1.4 collective-permute-start.1
  99.6 0.6 dynamic_slice.3
  100.1 0.7 fusion.40
  100.9 0.8 copy.112
  101.7 14.8 %collective-permute-done.1 = bf16[128,1536]{1,0:T(8,128)(2,1)} collective-permute-done((bf16[128,1536]{1,0:T(8,128)(2,1)S(1)}, bf16[128,1536]{1,0:T(8,128)(2,1)}, u32[]{:S(2)}, u32[]{:S(2)}) %collective-permute-start.1) | collective-permute-done | bytes 393248 | tf_op jit(solution)/shard_map/ppermute | solution.py:15
  116.5 1.7 %convolution_convert_fusion.5 = bf16[256,384]{1,0:T(8,128)(2,1)S(1)} fusion(bf16[1536,384]{1,0:T(8,128)(2,1)S(1)} %bitcast.140, bf16[128,1536]{1,0:T(8,128)(2,1)S(1)} %maximum_select_fusion.2, bf16[128,1536]{1,0:T(8,128)(2,1)} %collective-permute-done.1, pred[]{:T(512)S(6)} %eq.4), kind=kOutput, calls=%fused_computation.21 | convolution fusion | flops 305627136 | bytes 2162689 | tf_op jit(solution)/shard_map/dot_general | solution.py:120
  118.3 2.1 %convolution_convert_fusion.3 = bf16[256,384]{1,0:T(8,128)(2,1)S(1)} fusion(bf16[1536,384]{1,0:T(8,128)(2,1)} %bitcast.13, bf16[128,1536]{1,0:T(8,128)(2,1)S(1)} %maximum_select_fusion.2, bf16[128,1536]{1,0:T(8,128)(2,1)} %collective-permute-done.1, pred[]{:T(512)S(6)} %eq.4), kind=kOutput, calls=%fused_computation.19 | convolution fusion | flops 305627136 | bytes 2162689 | tf_op jit(solution)/shard_map/dot_general | solution.py:117
  120.6 1.3 all-to-all-done.1
  121.9 2.1 %convolution_convert_fusion.4 = bf16[256,384]{1,0:T(8,128)(2,1)S(1)} fusion(bf16[1536,384]{1,0:T(8,128)(2,1)} %bitcast.9, bf16[128,1536]{1,0:T(8,128)(2,1)S(1)} %maximum_select_fusion.2, bf16[128,1536]{1,0:T(8,128)(2,1)} %collective-permute-done.1, pred[]{:T(512)S(6)} %eq.4), kind=kOutput, calls=%fused_computation.20 | convolution fusion | flops 305627136 | bytes 2162689 | tf_op jit(solution)/shard_map/dot_general | solution.py:114
  126.4 1.3 collective-permute-done.2
  127.8 1.9 %collective-permute-start.3 = (bf16[1,2,64,384]{3,2,1,0:T(8,128)(2,1)S(1)}, bf16[1,2,64,384]{3,2,1,0:T(8,128)(2,1)S(1)}, u32[]{:S(2)}, u32[]{:S(2)}) collective-permute-start(bf16[1,2,64,384]{3,2,1,0:T(8,128)(2,1)S(1)} %get-tuple-element.13), channel_id=1, source_target_pairs={{0,2},{1,3},{2,0},{3,1},{4,6},{5,7},{6,4},{7,5},{8,10},{9,11},{10,... | collective-permute-start | bytes 294920 | tf_op jit(solution)/shard_map/ppermute | solution.py:15
  129.7 0.6 fusion.45
  130.3 2.4 %collective-permute-done.3 = bf16[1,2,64,384]{3,2,1,0:T(8,128)(2,1)S(1)} collective-permute-done((bf16[1,2,64,384]{3,2,1,0:T(8,128)(2,1)S(1)}, bf16[1,2,64,384]{3,2,1,0:T(8,128)(2,1)S(1)}, u32[]{:S(2)}, u32[]{:S(2)}) %collective-permute-start.3) | collective-permute-done | bytes 98336 | tf_op jit(solution)/shard_map/ppermute | solution.py:15
  132.7 0.7 multiply_bitcast_fusion.1
  133.7 0.8 collective-permute-start.4
  134.5 1.1 collective-permute-done.4
  135.7 1.5 collective-permute-start.5
  137.2 8.8 %collective-permute-done.5 = bf16[128,1536]{1,0:T(8,128)(2,1)S(1)} collective-permute-done((bf16[128,1536]{1,0:T(8,128)(2,1)S(1)}, bf16[128,1536]{1,0:T(8,128)(2,1)S(1)}, u32[]{:S(2)}, u32[]{:S(2)}) %collective-permute-start.5) | collective-permute-done | bytes 393248 | tf_op jit(solution)/shard_map/ppermute | solution.py:15
  146.1 0.7 copy-done.9
  146.8 0.6 convolution_convert_fusion.2
  147.5 2.1 %convolution_convert_fusion = bf16[256,384]{1,0:T(8,128)(2,1)S(1)} fusion(bf16[1536,384]{1,0:T(8,128)(2,1)} %bitcast.13, bf16[128,1536]{1,0:T(8,128)(2,1)S(1)} %maximum_select_fusion.3, bf16[128,1536]{1,0:T(8,128)(2,1)} %copy-done.9, pred[]{:T(512)S(6)} %eq.4), kind=kOutput, calls=%fused_computation.16 | convolution fusion | flops 305627136 | bytes 2162689 | tf_op jit(solution)/shard_map/dot_general | solution.py:117
  149.8 1.9 %convolution_convert_fusion.1 = bf16[256,384]{1,0:T(8,128)(2,1)S(1)} fusion(bf16[1536,384]{1,0:T(8,128)(2,1)} %bitcast.9, bf16[128,1536]{1,0:T(8,128)(2,1)S(1)} %maximum_select_fusion.3, bf16[128,1536]{1,0:T(8,128)(2,1)S(1)} %copy-done.10, pred[]{:T(512)S(6)} %eq.4), kind=kOutput, calls=%fused_computation.17 | convolution fusion | flops 305627136 | bytes 2162689 | tf_op jit(solution)/shard_map/dot_general | solution.py:114
  153.3 0.5 fusion.43
  153.9 0.5 copy.149
  154.4 0.5 copy.150
  155.0 1.3 collective-permute-start.6
  156.3 0.9 collective-permute-done.6
  157.3 1.5 collective-permute-start.7
  158.8 2.5 %collective-permute-done.7 = bf16[1,2,64,384]{3,2,1,0:T(8,128)(2,1)S(1)} collective-permute-done((bf16[1,2,64,384]{3,2,1,0:T(8,128)(2,1)S(1)}, bf16[1,2,64,384]{3,2,1,0:T(8,128)(2,1)S(1)}, u32[]{:S(2)}, u32[]{:S(2)}) %collective-permute-start.7) | collective-permute-done | bytes 98336 | tf_op jit(solution)/shard_map/ppermute | solution.py:15
  161.4 0.7 multiply_bitcast_fusion
  162.1 0.7 fusion.19
  (92 shorter events, 6.8 us)
Async XLA Ops:
  0.0 3.2 %copy-start = (bf16[128,1,2,1536]{3,2,1,0:T(2,128)(2,1)S(1)}, bf16[128,1,2,1536]{3,2,1,0:T(2,128)(2,1)}, u32[]{:S(2)}) copy-start(bf16[128,1,2,1536]{3,2,1,0:T(2,128)(2,1)} %param.15) | copy-start | bytes 2359300
  0.0 1.6 copy-start.1
  6.1 8.7 %copy-start.3 = (bf16[96,1536]{1,0:T(8,128)(2,1)S(1)}, bf16[96,1536]{1,0:T(8,128)(2,1)}, u32[]{:S(2)}) copy-start(bf16[96,1536]{1,0:T(8,128)(2,1)} %param.14) | copy-start | bytes 884740
  7.4 15.6 %all-to-all-start.3 = ((bf16[16,8,1,2,384]{4,1,3,2,0:T(8,128)(2,1)}), bf16[16,8,1,2,384]{4,1,3,2,0:T(8,128)(2,1)S(1)}, u32[]{:S(2)}, u32[]{:S(2)}) async-start(bf16[16,8,1,2,384]{4,1,3,2,0:T(8,128)(2,1)} %bitcast.25), calls=%async_computation.3 | async-start | bytes 393216 | tf_op jit(solution)/shard_map/all_to_all | solution.py:102
  24.1 4.4 %copy-start.4 = (bf16[96,1536]{1,0:T(8,128)(2,1)S(1)}, bf16[96,1536]{1,0:T(8,128)(2,1)}, u32[]{:S(2)}) copy-start(bf16[96,1536]{1,0:T(8,128)(2,1)} %param.13) | copy-start | bytes 884740
  24.1 30.0 %all-to-all-start = ((bf16[16,96,384]{2,1,0:T(8,128)(2,1)}), bf16[16,96,384]{2,1,0:T(8,128)(2,1)S(1)}, u32[]{:S(2)}, u32[]{:S(2)}) async-start(bf16[16,96,384]{2,1,0:T(8,128)(2,1)} %bitcast.4), calls=%async_computation | async-start | bytes 2359296 | tf_op jit(solution)/shard_map/all_to_all | solution.py:89
  55.3 7.1 %copy-start.5 = (bf16[96,1536]{1,0:T(8,128)(2,1)S(1)}, bf16[96,1536]{1,0:T(8,128)(2,1)}, u32[]{:S(2)}) copy-start(bf16[96,1536]{1,0:T(8,128)(2,1)} %param.12) | copy-start | bytes 884740
  55.3 32.7 %all-to-all-start.2 = ((bf16[16,96,384]{2,1,0:T(8,128)(2,1)}), bf16[16,96,384]{2,1,0:T(8,128)(2,1)}, u32[]{:S(2)}, u32[]{:S(2)}) async-start(bf16[16,96,384]{2,1,0:T(8,128)(2,1)} %bitcast.12), calls=%async_computation.2 | async-start | bytes 2359296 | tf_op jit(solution)/shard_map/all_to_all | solution.py:88
  89.2 7.1 %copy-start.2 = (bf16[64,1536]{1,0:T(8,128)(2,1)S(1)}, bf16[64,1536]{1,0:T(8,128)(2,1)}, u32[]{:S(2)}) copy-start(bf16[64,1536]{1,0:T(8,128)(2,1)} %param.10) | copy-start | bytes 589828
  89.2 7.2 %copy-start.7 = (f32[1536]{0:T(1024)S(1)}, f32[1536]{0:T(1024)}, u32[]{:S(2)}) copy-start(f32[1536]{0:T(1024)} %param.11) | copy-start | bytes 18436
  89.2 32.7 %all-to-all-start.1 = ((bf16[16,96,384]{2,1,0:T(8,128)(2,1)}), bf16[16,96,384]{2,1,0:T(8,128)(2,1)}, u32[]{:S(2)}, u32[]{:S(2)}) async-start(bf16[16,96,384]{2,1,0:T(8,128)(2,1)} %bitcast.8), calls=%async_computation.1 | async-start | bytes 2359296 | tf_op jit(solution)/shard_map/all_to_all | solution.py:87
  96.2 3.3 %copy-start.11 = (s32[4]{0:T(128)S(1)}, s32[4]{0:T(128)}, u32[]{:S(2)}) copy-start(s32[4]{0:T(128)} %param.17) | copy-start | bytes 52
  96.5 1.5 collective-permute-start
  98.1 18.4 %collective-permute-start.1 = (bf16[128,1536]{1,0:T(8,128)(2,1)S(1)}, bf16[128,1536]{1,0:T(8,128)(2,1)}, u32[]{:S(2)}, u32[]{:S(2)}) collective-permute-start(bf16[128,1536]{1,0:T(8,128)(2,1)S(1)} %maximum_select_fusion.2), channel_id=1, source_target_pairs={{0,2},{1,3},{2,0},{3,1},{4,6},{5,7},{6,4},{7,5},{8,10},{9,11},{10,... | collective-permute-start | bytes 1179656 | tf_op jit(solution)/shard_map/ppermute | solution.py:15
  124.8 0.9 copy-start.6
  125.9 3.8 %copy-start.8 = (f32[2]{0:T(128)S(1)}, f32[2]{0:T(128)}, u32[]{:S(2)}) copy-start(f32[2]{0:T(128)} %param.19) | copy-start | bytes 28
  126.3 1.4 collective-permute-start.2
  127.8 5.0 %collective-permute-start.3 = (bf16[1,2,64,384]{3,2,1,0:T(8,128)(2,1)S(1)}, bf16[1,2,64,384]{3,2,1,0:T(8,128)(2,1)S(1)}, u32[]{:S(2)}, u32[]{:S(2)}) collective-permute-start(bf16[1,2,64,384]{3,2,1,0:T(8,128)(2,1)S(1)} %get-tuple-element.13), channel_id=1, source_target_pairs={{0,2},{1,3},{2,0},{3,1},{4,6},{5,7},{6,4},{7,5},{8,10},{9,11},{10,... | collective-permute-start | bytes 294920 | tf_op jit(solution)/shard_map/ppermute | solution.py:15
  133.7 1.9 %collective-permute-start.4 = (bf16[64,1536]{1,0:T(8,128)(2,1)S(1)}, bf16[64,1536]{1,0:T(8,128)(2,1)S(1)}, u32[]{:S(2)}, u32[]{:S(2)}) collective-permute-start(bf16[64,1536]{1,0:T(8,128)(2,1)S(1)} %fusion.18), channel_id=1, source_target_pairs={{0,1},{1,0},{2,3},{3,2},{4,5},{5,4},{6,7},{7,6},{8,9},{9,8},{10,11... | collective-permute-start | bytes 589832 | tf_op jit(solution)/shard_map/ppermute | solution.py:15
  135.7 10.4 %collective-permute-start.5 = (bf16[128,1536]{1,0:T(8,128)(2,1)S(1)}, bf16[128,1536]{1,0:T(8,128)(2,1)S(1)}, u32[]{:S(2)}, u32[]{:S(2)}) collective-permute-start(bf16[128,1536]{1,0:T(8,128)(2,1)S(1)} %maximum_select_fusion.3), channel_id=1, source_target_pairs={{0,2},{1,3},{2,0},{3,1},{4,6},{5,7},{6,4},{7,5},{8,10},{9,11},{10,... | collective-permute-start | bytes 1179656 | tf_op jit(solution)/shard_map/ppermute | solution.py:15
  146.0 0.7 copy-start.9
  147.5 2.3 %copy-start.10 = (bf16[128,1536]{1,0:T(8,128)(2,1)S(1)}, bf16[128,1536]{1,0:T(8,128)(2,1)}, u32[]{:S(2)}) copy-start(bf16[128,1536]{1,0:T(8,128)(2,1)} %copy-done.9) | copy-start | bytes 1179652
  155.0 2.2 %collective-permute-start.6 = (bf16[2,1,64,384]{3,2,0,1:T(8,128)(2,1)S(1)}, bf16[2,1,64,384]{3,2,0,1:T(8,128)(2,1)S(1)}, u32[]{:S(2)}, u32[]{:S(2)}) collective-permute-start(bf16[2,1,64,384]{3,2,0,1:T(8,128)(2,1)S(1)} %get-tuple-element.11), channel_id=1, source_target_pairs={{0,1},{1,0},{2,3},{3,2},{4,5},{5,4},{6,7},{7,6},{8,9},{9,8},{10,11... | collective-permute-start | bytes 294920 | tf_op jit(solution)/shard_map/ppermute | solution.py:15
  157.3 4.1 %collective-permute-start.7 = (bf16[1,2,64,384]{3,2,1,0:T(8,128)(2,1)S(1)}, bf16[1,2,64,384]{3,2,1,0:T(8,128)(2,1)S(1)}, u32[]{:S(2)}, u32[]{:S(2)}) collective-permute-start(bf16[1,2,64,384]{3,2,1,0:T(8,128)(2,1)S(1)} %get-tuple-element.9), channel_id=1, source_target_pairs={{0,2},{1,3},{2,0},{3,1},{4,6},{5,7},{6,4},{7,5},{8,10},{9,11},{10,... | collective-permute-start | bytes 294920 | tf_op jit(solution)/shard_map/ppermute | solution.py:15
where the time goes:
time: 165 us; the launch traced here: 163 us
  waiting for transfers between devices  93.7 us (57%)
  starting transfers between devices  34.7 us (21%)
  local copies, waits for them, and re-layouts  17.4 us (11%)
  matrix products  12.5 us (8%)
  other arithmetic  4.09 us (2%)
    ppermute x8, waiting for transfers between devices, from_partner(): lax.ppermute(array, axis, [(i, i ^ 1 << bit) for i in range(lax.axis_size...  33.2 us
    all_to_all x1, waiting for transfers between devices, per_device(): lax.all_to_all(column_pieces(w_key), 'frame', split_axis=0, concat_axis=1...  25.5 us
    all_to_all x1, waiting for transfers between devices, per_device(): lax.all_to_all(column_pieces(w_value), 'frame', split_axis=0, concat_axis...  25.5 us
    ppermute x8, starting transfers between devices, from_partner(): lax.ppermute(array, axis, [(i, i ^ 1 << bit) for i in range(lax.axis_size...  8.81 us
    all_to_all x1, waiting for transfers between devices, per_device(): lax.all_to_all(outgoing, 'frame', split_axis=0, concat_axis=2, tiled=True)  8.16 us
    all_to_all x1, starting transfers between devices, per_device(): lax.all_to_all(outgoing, 'frame', split_axis=0, concat_axis=2, tiled=True)  7.34 us
    all_to_all x1, starting transfers between devices, per_device(): lax.all_to_all(column_pieces(w_query), 'frame', split_axis=0, concat_axis...  7.07 us
    all_to_all x1, starting transfers between devices, per_device(): lax.all_to_all(column_pieces(w_key), 'frame', split_axis=0, concat_axis=1...  7.05 us
  transfers between devices with their start and end apart: 12, of which 12 were waited for; matrix products, arithmetic and copies ran while one was open for 5% of the time, Pallas kernels for 0%

commit v1 on v0

--- a/solution.py
+++ b/solution.py
@@ -1,14 +1,430 @@
+import functools
 import math
 
 import jax
 import jax.numpy as jnp
 from jax import lax
+from jax.experimental import pallas as pl
+from jax.experimental.pallas import tpu as pltpu
 from jax.sharding import PartitionSpec as P
 
 HEADS = 12
 HS = 128
 SPATIAL = 4
 STEPS = 2
+AXES = ("groups", "frame")
+VMEM_LIMIT = 48 * 1024 * 1024
+
+
+def coords(index):
+    return index // 4, (index // 2) % 2, index % 2
+
+
+def quarter_of(plane, y):
+    return (plane % 2) * 2 + y
+
+
+def moved(array, target):
+    devices = lax.axis_size("frame")
+    pairs = []
+    for x in range(lax.axis_size("groups")):
+        for index in range(devices):
+            place = target(x, *coords(index))
+            if place is not None:
+                to_x, to_plane, to_y, to_c = place
+                pairs.append((x * devices + index, to_x * devices + to_plane * 4 + to_y * 2 + to_c))
+    return lax.ppermute(array, AXES, pairs)
+
+
+def here():
+    x = lax.axis_index("groups")
+    index = lax.axis_index("frame")
+    plane = index // 4
+    rest = index - plane * 4
+    y = rest // 2
+    return x, index, plane, y, rest - y * 2
+
+
+def flipped(value, bits):
+    out = value
+    bit = 1
+    while bit <= bits:
+        if bits & bit:
+            out = out + bit - 2 * bit * ((value // bit) % 2)
+        bit *= 2
+    return out
+
+
+def columns(quarter, width):
+    return pl.ds(pl.multiple_of(quarter * width, 128), width)
+
+
+def pack_kernel(
+    list_ref, slot_ref, w_query, w_key, w_value, mem_ref,
+    own_ref, beside_ref, even_ref, odd_ref, kept_ref, sent_ref,
+    rows, stored, row_sem, mem_sem, out_sem, give_sem,
+):
+    x, index, plane, y, c = here()
+    devices = lax.axis_size("frame")
+    frames, entries = list_ref.shape
+    width = own_ref.shape[2]
+    reads = []
+    for number, weight in enumerate((w_query, w_key, w_value)):
+        reads.append(pltpu.make_async_copy(weight, rows.at[number], row_sem.at[number]))
+        reads[-1].start()
+    picks = []
+    for frame in range(frames):
+        for entry in range(entries):
+            number = frame * entries + entry
+            row = slot_ref[list_ref[frame, entry]]
+            picks.append(pltpu.make_async_copy(mem_ref.at[row, 0], stored.at[number], mem_sem.at[number]))
+            picks[-1].start()
+    across = y + x - 2 * x * y
+    low = plane % 2
+    quarters = (quarter_of(plane, y), low * 2 + 1 - y, low * 2 + across, (1 - low) * 2 + across)
+    for read in reads:
+        read.wait()
+    gives = []
+    for number, (quarter, out) in enumerate(zip(quarters, (own_ref, beside_ref, even_ref, odd_ref))):
+        gives.append(pltpu.make_async_copy(rows.at[:, :, columns(quarter, width)], out, out_sem.at[number]))
+        gives[-1].start()
+    for pick in picks:
+        pick.wait()
+    bits = devices.bit_length() - 1
+    for away in range(devices):
+        target = flipped(index, away)
+        to_plane = target // 4
+        to_y = (target - to_plane * 4) // 2
+        to_frame = (to_plane // 2) * 2 + target % 2
+        place = 0
+        for bit in range(1, bits):
+            place = place * 2 + (away >> bit & 1)
+        out = sent_ref if away & 1 else kept_ref
+        gives.append(
+            pltpu.make_async_copy(
+                stored.at[pl.ds(to_frame * entries, entries), :, columns(quarter_of(to_plane, to_y), width)],
+                out.at[place],
+                give_sem.at[away],
+            )
+        )
+        gives[-1].start()
+    for give in gives:
+        give.wait()
+
+
+def pack(w_query, w_key, w_value, mem_cache, intersection, slot_of):
+    devices = lax.axis_size("frame")
+    shard_rows, features = w_query.shape
+    width = features // SPATIAL
+    frames, entries = intersection.shape
+    piece = jax.ShapeDtypeStruct((3, shard_rows, width), w_query.dtype)
+    half = jax.ShapeDtypeStruct((devices // 2, entries, 2, width), mem_cache.dtype)
+    anywhere = pl.BlockSpec(memory_space=pl.ANY)
+    scalars = pl.BlockSpec(memory_space=pltpu.SMEM)
+    return pl.pallas_call(
+        pack_kernel,
+        out_shape=(piece,) * 4 + (half,) * 2,
+        in_specs=[scalars, scalars] + [anywhere] * 4,
+        out_specs=(anywhere,) * 6,
+        scratch_shapes=[
+            pltpu.VMEM((3, shard_rows, features), w_query.dtype),
+            pltpu.VMEM((frames * entries, 2, features), mem_cache.dtype),
+            pltpu.SemaphoreType.DMA((3,)),
+            pltpu.SemaphoreType.DMA((frames * entries,)),
+            pltpu.SemaphoreType.DMA((4,)),
+            pltpu.SemaphoreType.DMA((devices,)),
+        ],
+        compiler_params=pltpu.CompilerParams(vmem_limit_bytes=VMEM_LIMIT),
+        name="pack",
+    )(intersection, slot_of, w_query, w_key, w_value, mem_cache)
+
+
+def all_pieces(own, beside, even, odd):
+    planes = lax.axis_size("frame") // 4
+    found = []
+    for bits in sorted(range(1, planes), key=lambda value: (-value.bit_length(), value)):
+        direct = moved(even if bits % 2 == 0 else odd, lambda x, p, y, c, bits=bits: (x, p ^ bits, y ^ x, c))
+        found.append((direct, (bits, 0, True)))
+    near = moved(beside, lambda x, p, y, c: (x, p, 1 - y, c))
+    pieces = [(own, (0, 0, False)), (near, (0, 1, False))]
+    for direct, (bits, _, _) in found:
+        pieces.append((direct, (bits, 0, True)))
+        pieces.append((moved(direct, lambda x, p, y, c: (1 - x, p, y, c)), (bits, 1, True)))
+    places = [(array, place + (0,)) for array, place in pieces]
+    places += [(moved(array, lambda x, p, y, c: (x, p, y, 1 - c)), place + (1,)) for array, place in pieces]
+    return places
+
+
+def all_memory(kept, sent):
+    devices = lax.axis_size("frame")
+    held = jnp.stack([kept, hop(sent, 0)])
+    for bit in range(1, devices.bit_length() - 1):
+        half = held.shape[1] // 2
+        held = jnp.concatenate([held[:, :half], hop(held[:, half:], bit)])
+    keys, values = held[:, 0, :, 0, :], held[:, 0, :, 1, :]
+    return keys.reshape(-1, keys.shape[-1]), values.reshape(-1, values.shape[-1])
+
+
+def hop(array, bit):
+    return lax.ppermute(array, "frame", [(i, i ^ 1 << bit) for i in range(lax.axis_size("frame"))])
+
+
+def all_tokens(latent):
+    other = moved(latent, lambda x, p, y, c: (x, p, y, 1 - c) if c != p % 2 else None)
+    block = jnp.concatenate([latent, other])
+    near = moved(block, lambda x, p, y, c: (x, p, 1 - y, c) if c == p % 2 else None)
+    far = moved(block, lambda x, p, y, c: (x, p ^ 1, y, c) if c == p % 2 else None)
+    far_near = moved(far, lambda x, p, y, c: (x, p, 1 - y, c) if c != p % 2 else None)
+    return block, near, far, far_near
+
+
+def step_kernel(places, updates, last, head_count, *refs):
+    refs = list(refs)
+    count_ref, scale_ref, gain_ref, key_ref, value_ref = refs[:5]
+    token_refs = refs[5:9]
+    piece_refs = refs[9 : 9 + len(places)]
+    update_refs = refs[9 + len(places) : 9 + len(places) + len(updates)]
+    outs = refs[9 + len(places) + len(updates) : -8]
+    current, normed, weights, parts, attended, token_sem, piece_sem, update_sem = refs[-8:]
+    x, _, plane, y, c = here()
+    low = plane % 2
+    chip_rows = token_refs[0].shape[0]
+    width = parts.shape[2]
+    at_home = low == c
+
+    def token_copies(first, second):
+        return (
+            pltpu.make_async_copy(first, current.at[pl.ds(y * chip_rows, chip_rows)], token_sem.at[0]),
+            pltpu.make_async_copy(second, current.at[pl.ds((1 - y) * chip_rows, chip_rows)], token_sem.at[1]),
+        )
+
+    @pl.when(at_home)
+    def _():
+        for copy in token_copies(token_refs[0], token_refs[1]):
+            copy.start()
+
+    @pl.when(jnp.logical_not(at_home))
+    def _():
+        for copy in token_copies(token_refs[2], token_refs[3]):
+            copy.start()
+
+    update_copies = []
+    for number, (ref, _) in enumerate(zip(update_refs, updates)):
+        update_copies.append(pltpu.make_async_copy(ref, parts.at[number], update_sem.at[number]))
+        update_copies[-1].start()
+    piece_copies = []
+    shard_rows = piece_refs[0].shape[1]
+    for number, (ref, (plane_bits, y_bits, with_x, c_bits)) in enumerate(zip(piece_refs, places)):
+        from_y = flipped(y, y_bits)
+        if with_x:
+            from_y = from_y + x - 2 * x * from_y
+        shard = flipped(plane, plane_bits) * 4 + from_y * 2 + flipped(c, c_bits)
+        start = pl.multiple_of(shard * shard_rows, 16)
+        piece_copies.append(
+            pltpu.make_async_copy(ref, weights.at[:, pl.ds(start, shard_rows), :], piece_sem.at[number])
+        )
+        piece_copies[-1].start()
+    for copy in token_copies(token_refs[0], token_refs[1]):
+        copy.wait()
+    for copy in update_copies:
+        copy.wait()
+    for number, (plane_bits, y_bits) in enumerate(updates):
+        quarter = quarter_of(flipped(plane, plane_bits), flipped(y, y_bits))
+        spot = columns(quarter, width)
+        current[:, spot] = (
+            current[:, spot].astype(jnp.float32) + scale_ref[0] * parts[number].astype(jnp.float32)
+        ).astype(current.dtype)
+    widened = current[...].astype(jnp.float32)
+    inverse = lax.rsqrt(jnp.mean(widened * widened, axis=-1, keepdims=True) + 1e-06)
+    normed[...] = (widened * inverse * gain_ref[...]).astype(normed.dtype)
+    for copy in piece_copies:
+        copy.wait()
+    queries, keys, values = (
+        jnp.dot(normed[...], weights[number], preferred_element_type=jnp.float32).astype(jnp.bfloat16)
+        for number in range(3)
+    )
+    frame = (plane // 2) * 2 + c
+    entries = key_ref.shape[0] // lax.axis_size("frame")
+    head_size = width // head_count
+    scale_dot = 1.0 / math.sqrt(head_size)
+    entry = lax.broadcasted_iota(jnp.int32, (1, key_ref.shape[0]), 1) % entries
+    live = entry < count_ref[frame]
+    contract_last = (((1,), (1,)), ((), ()))
+    for head in range(head_count):
+        span = slice(head * head_size, (head + 1) * head_size)
+        frame_scores = (
+            lax.dot_general(queries[:, span], keys[:, span], contract_last, preferred_element_type=jnp.float32)
+            * scale_dot
+        )
+        mem_scores = (
+            lax.dot_general(queries[:, span], key_ref[:, span], contract_last, preferred_element_type=jnp.float32)
+            * scale_dot
+        )
+        mem_scores = jnp.where(live, mem_scores, -1e30)
+        largest = jnp.maximum(
+            jnp.max(frame_scores, axis=-1, keepdims=True), jnp.max(mem_scores, axis=-1, keepdims=True)
+        )
+        frame_weights = jnp.exp(frame_scores - largest)
+        mem_weights = jnp.exp(mem_scores - largest)
+        denominator = jnp.sum(frame_weights, axis=-1, keepdims=True) + jnp.sum(mem_weights, axis=-1, keepdims=True)
+        blended = jnp.dot(
+            frame_weights.astype(jnp.bfloat16), values[:, span], preferred_element_type=jnp.float32
+        ) + jnp.dot(mem_weights.astype(jnp.bfloat16), value_ref[:, span], preferred_element_type=jnp.float32)
+        attended[:, span] = (blended / denominator).astype(attended.dtype)
+    if not last:
+        outs[0][...] = attended[...]
+        return
+    spot = columns(quarter_of(plane, y), width)
+    attended[...] = (
+        current[:, spot].astype(jnp.float32) + scale_ref[1] * attended[...].astype(jnp.float32)
+    ).astype(attended.dtype)
+    rows = chip_rows // 2
+    here_rows, there_rows = y * chip_rows, (1 - y) * chip_rows
+
+    def part(start):
+        return attended[pl.ds(pl.multiple_of(start, rows), rows), :]
+
+    keep, first, second, third, fourth = outs
+    keep[...] = part(here_rows)
+    fourth[...] = part(there_rows + rows)
+
+    @pl.when(at_home)
+    def _():
+        first[...] = part(there_rows)
+        second[...] = part(there_rows + rows)
+        third[...] = part(here_rows + rows)
+
+    @pl.when(jnp.logical_not(at_home))
+    def _():
+        first[...] = part(here_rows + rows)
+        second[...] = part(here_rows)
+        third[...] = part(there_rows)
+
+
+def step(pieces, updates, last, counts, scales, norm_gain, keys, values, tokens):
+    shard_rows, width = pieces[0][0].shape[1:]
+    features = norm_gain.shape[0]
+    chip_rows = tokens[0].shape[0]
+    frame_rows = 2 * chip_rows
+    dtype = tokens[0].dtype
+    head_count = HEADS // SPATIAL
+    kernel = functools.partial(
+        step_kernel, tuple(place for _, place in pieces), tuple(bits for _, bits in updates), last, head_count
+    )
+    if last:
+        out_shape = tuple(jax.ShapeDtypeStruct((chip_rows // 2, width), dtype) for _ in range(5))
+    else:
+        out_shape = (jax.ShapeDtypeStruct((frame_rows, width), dtype),)
+    anywhere = pl.BlockSpec(memory_space=pl.ANY)
+    scalars = pl.BlockSpec(memory_space=pltpu.SMEM)
+    vectors = pl.BlockSpec(memory_space=pltpu.VMEM)
+    flops = 2 * frame_rows * width * (3 * features + 2 * (frame_rows + keys.shape[0]))
+    return pl.pallas_call(
+        kernel,
+        out_shape=out_shape,
+        in_specs=[scalars, scalars, vectors, vectors, vectors] + [anywhere] * (4 + len(pieces) + len(updates)),
+        out_specs=tuple(vectors for _ in out_shape),
+        scratch_shapes=[
+            pltpu.VMEM((frame_rows, features), dtype),
+            pltpu.VMEM((frame_rows, features), jnp.bfloat16),
+            pltpu.VMEM((3, features, width), jnp.bfloat16),
+            pltpu.VMEM((max(len(updates), 1), frame_rows, width), dtype),
+            pltpu.VMEM((frame_rows, width), dtype),
+            pltpu.SemaphoreType.DMA((2,)),
+            pltpu.SemaphoreType.DMA((len(pieces),)),
+            pltpu.SemaphoreType.DMA((max(len(updates), 1),)),
+        ],
+        compiler_params=pltpu.CompilerParams(vmem_limit_bytes=VMEM_LIMIT),
+        cost_estimate=pl.CostEstimate(
+            flops=flops, transcendentals=frame_rows * head_count * (frame_rows + keys.shape[0]), bytes_accessed=6 << 20
+        ),
+        name="last_step" if last else "step",
+    )(
+        counts,
+        scales,
+        norm_gain.reshape(1, -1),
+        keys,
+        values,
+        *tokens,
+        *[array for array, _ in pieces],
+        *[array for array, _ in updates],
+    )
+
+
+def join_kernel(keep, first, second, third, fourth, out):
+    _, _, plane, y, c = here()
+    low = plane % 2
+    width = keep.shape[1]
+
+    def put(ref, plane_low, at_y):
+        out[:, columns(plane_low * 2 + at_y, width)] = ref[...]
+
+    @pl.when(low == c)
+    def _():
+        put(keep, low, y)
+        put(first, low, 1 - y)
+        put(second, 1 - low, y)
+        put(third, 1 - low, 1 - y)
+
+    @pl.when(low != c)
+    def _():
+        put(first, 1 - low, y)
+        put(second, low, 1 - y)
+        put(third, low, y)
+        put(fourth, 1 - low, 1 - y)
+
+
+def joined(keep, first, second, third, fourth):
+    at_home = lambda p, c: c == p % 2
+    first = moved(
+        first, lambda x, p, y, c: (x, p, 1 - y, c) if at_home(p, c) else (x, p ^ 1, y, 1 - c)
+    )
+    second = moved(
+        second, lambda x, p, y, c: (x, p, 1 - y, 1 - c) if at_home(p, c) else (x, p ^ 1, y, c)
+    )
+    third = moved(
+        third, lambda x, p, y, c: (x, p, y, 1 - c) if at_home(p, c) else (x, p ^ 1, 1 - y, c)
+    )
+    fourth = moved(
+        fourth, lambda x, p, y, c: None if at_home(p, c) else (x, p ^ 1, 1 - y, 1 - c)
+    )
+    rows, width = keep.shape
+    return pl.pallas_call(
+        join_kernel,
+        out_shape=jax.ShapeDtypeStruct((rows, width * SPATIAL), keep.dtype),
+        name="join",
+    )(keep, first, second, third, fourth)
+
+
+def paired_planes(
+    latent, norm_gain, w_query, w_key, w_value, mem_cache, intersection, counts, slot_of, step_scale
+):
+    own, beside, even, odd, kept, sent = pack(w_query, w_key, w_value, mem_cache, intersection, slot_of)
+    pieces = all_pieces(own, beside, even, odd)
+    tokens = all_tokens(latent)
+    keys, values = all_memory(kept, sent)
+    (attended,) = step(pieces, [], False, counts, step_scale, norm_gain, keys, values, tokens)
+    updates = [
+        (attended, (0, 0)),
+        (moved(attended, lambda x, p, y, c: (x, p ^ 1, 1 - y, c)), (1, 1)),
+        (moved(attended, lambda x, p, y, c: (x, p ^ 1, y, c)), (1, 0)),
+        (moved(attended, lambda x, p, y, c: (x, p, 1 - y, c)), (0, 1)),
+    ]
+    shares = step(pieces, updates, True, counts, step_scale, norm_gain, keys, values, tokens)
+    return joined(*shares)
+
+
+def fits_paired_planes(latent, norm_gain, w_query, w_key, w_value, mem_cache, *_):
+    devices = lax.axis_size("frame")
+    planes = devices // SPATIAL
+    return (
+        lax.axis_size("groups") == 2
+        and devices == planes * SPATIAL
+        and planes >= 2
+        and planes & (planes - 1) == 0
+        and w_query.shape[0] % 16 == 0
+        and mem_cache.shape[1] == 1
+    )
 
 
 def from_partner(array, axis, bit):
@@ -65,7 +481,7 @@
     return (widened, (widened * inverse * norm_gain).astype(jnp.bfloat16))
 
 
-def per_device(
+def separate_frames(
     latent, norm_gain, w_query, w_key, w_value, mem_cache, intersection, counts, slot_of, step_scale
 ):
     devices = lax.axis_size("frame")
@@ -138,6 +554,10 @@
     return current
 
 
+def per_device(*arguments):
+    return (paired_planes if fits_paired_planes(*arguments) else separate_frames)(*arguments)
+
+
 def solution(mesh):
     placed = (
         P(("groups", "frame"), None),

time: 165 us -> 104 us (0.63); the launches traced: 163 us -> 104 us
  waiting for transfers between devices: 93.7 us -> 32.3 us
  Pallas kernels: 0 us -> 16.5 us
  matrix products: 12.5 us -> 0 us
  starting transfers between devices: 34.7 us -> 46.5 us
  local copies, waits for them, and re-layouts: 17.4 us -> 7.37 us
  other arithmetic: 4.09 us -> 1.12 us
    all_to_all x4 -> x0, waiting for transfers between devices: 60.5 us -> none  [the longest x1 25.5 us: per_device(): lax.all_to_all(column_pieces(w_key), 'frame', split_axis=0, concat_axis=1...]
    ppermute x8 -> x30, starting transfers between devices: 8.81 us -> 46.5 us  [the longest x26 45.5 us: moved(): return lax.ppermute(array, AXES, pairs)]
    all_to_all x4 -> x0, starting transfers between devices: 25.8 us -> none  [the longest x1 7.34 us: per_device(): lax.all_to_all(outgoing, 'frame', split_axis=0, concat_axis=2, tiled=True)]
    pallas_call x0 -> x4, Pallas kernels: none -> 16.5 us  [the longest x2 12.7 us: step(): pl.pallas_call(kernel, out_shape=out_shape, in_specs=[scalars, scalars, v...]
    dot_general x14 -> x0, matrix products: 12.5 us -> none  [the longest x2 4.22 us: per_device(): jnp.dot(gathered, own_key, preferred_element_type=jnp.float32)]
    gather x7 -> x0, local copies, waits for them, and re-layouts: 5.56 us -> none  [the longest x6 4.97 us: per_device(): listed = mem_cache[slot_of[intersection[target_frame]]]]
    unnamed x26 -> x34, local copies, waits for them, and re-layouts: 2.34 us -> 7.35 us
    another operation x6 -> x0, local copies, waits for them, and re-layouts: 4.28 us -> none  [the longest x3 3.45 us: column_pieces(): return jnp.tile(split_cols, (devices // SPATIAL, 1, 1))]
  transfers between devices with their start and end apart: 12 -> 30, of which waited for: 12 -> 11; matrix products, arithmetic and copies ran while one was open for 5% -> 1% of each run, Pallas kernels for 0% -> 0%
where the time goes in v1:
time: 104 us
  starting transfers between devices  46.5 us (45%)
  waiting for transfers between devices  32.3 us (31%)
  Pallas kernels  16.5 us (16%)
  local copies, waits for them, and re-layouts  7.37 us (7%)
  other arithmetic  1.12 us (1%)
    ppermute x26, starting transfers between devices, moved(): return lax.ppermute(array, AXES, pairs)  45.5 us
    ppermute x26, waiting for transfers between devices, moved(): return lax.ppermute(array, AXES, pairs)  19.6 us
    ppermute x4, waiting for transfers between devices, hop(): lax.ppermute(array, 'frame', [(i, i ^ 1 << bit) for i in range(lax.axis_s...  12.7 us
    pallas_call x2, Pallas kernels, step(): pl.pallas_call(kernel, out_shape=out_shape, in_specs=[scalars, scalars, v...  12.7 us
    unnamed x34, local copies, waits for them, and re-layouts  7.35 us
    pallas_call x1, Pallas kernels, pack(): pl.pallas_call(pack_kernel, out_shape=(piece,) * 4 + (half,) * 2, in_spec...  2.24 us
  transfers between devices with their start and end apart: 30, of which 11 were waited for; matrix products, arithmetic and copies ran while one was open for 1% of the time, Pallas kernels for 0%

profile of v1, /device:TPU:1, one launch (start us, length us, event | category | flops | bytes accessed | tf_op | source)
XLA Modules:
  0.0 104.0 jit_solution(12460318163625194007)
XLA Ops:
  0.0 1.1 %copy-done.1 = bf16[128,1,2,1536]{3,2,1,0:T(2,128)(2,1)S(1)} copy-done((bf16[128,1,2,1536]{3,2,1,0:T(2,128)(2,1)S(1)}, bf16[128,1,2,1536]{3,2,1,0:T(2,128)(2,1)}, u32[]{:S(2)}) %copy-start.1) | copy-done | bytes 786456
  1.1 1.0 copy-done.2
  2.1 1.0 copy-done.3
  3.1 1.0 copy-done.4
  4.0 0.7 copy-done.6
  4.7 0.7 copy-done.9
  5.4 2.2 %pack.1 = (bf16[3,96,384]{2,1,0:T(8,128)(2,1)S(1)}, bf16[3,96,384]{2,1,0:T(8,128)(2,1)S(1)}, bf16[3,96,384]{2,1,0:T(8,128)(2,1)S(1)}, bf16[3,96,384]{2,1,0:T(8,1...) custom-call(s32[4,8]{1,0:T(4,128)S(1)} %copy-done.6, s32[128]{0:T(128)S(1)} %copy-done.9, ...), custom_call_target="tpu_custom_call" | custom-call | tf_op jit(solution)/shard_map/pack/pallas_call | solution.py:124
  7.7 2.8 %collective-permute-start.13 = (bf16[3,96,384]{2,1,0:T(8,128)(2,1)S(1)}, bf16[3,96,384]{2,1,0:T(8,128)(2,1)S(1)}, u32[]{:S(2)}, u32[]{:S(2)}) collective-permute-start(bf16[3,96,384]{2,1,0:T(8,128)(2,1)S(1)} %get-tuple-element.21), channel_id=1, source_target_pairs={{0,4},{1,5},{2,6},{3,7},{4,0},{5,1},{6,2},{7,3},{8,12},{9,13},{10,... | collective-permute-start | bytes 663560 | tf_op jit(solution)/shard_map/ppermute | solution.py:36
  10.5 2.2 %collective-permute-start.11 = (bf16[3,96,384]{2,1,0:T(8,128)(2,1)S(1)}, bf16[3,96,384]{2,1,0:T(8,128)(2,1)S(1)}, u32[]{:S(2)}, u32[]{:S(2)}) collective-permute-start(bf16[3,96,384]{2,1,0:T(8,128)(2,1)S(1)} %get-tuple-element.21), channel_id=1, source_target_pairs={{0,12},{1,13},{2,14},{3,15},{4,8},{5,9},{6,10},{7,11},{8,4},{9,5},... | collective-permute-start | bytes 663560 | tf_op jit(solution)/shard_map/ppermute | solution.py:36
  12.7 2.5 %collective-permute-start.4 = (bf16[64,1536]{1,0:T(8,128)(2,1)S(1)}, bf16[64,1536]{1,0:T(8,128)(2,1)S(1)}, u32[]{:S(2)}, u32[]{:S(2)}) collective-permute-start(bf16[64,1536]{1,0:T(8,128)(2,1)S(1)} %copy-done.10), channel_id=1, source_target_pairs={{1,0},{3,2},{4,5},{6,7},{9,8},{11,10},{12,13},{14,15},{17,16},{19,... | collective-permute-start | bytes 589832 | tf_op jit(solution)/shard_map/ppermute | solution.py:36
  15.2 1.3 %collective-permute-start.8 = (bf16[3,96,384]{2,1,0:T(8,128)(2,1)S(1)}, bf16[3,96,384]{2,1,0:T(8,128)(2,1)S(1)}, u32[]{:S(2)}, u32[]{:S(2)}) collective-permute-start(bf16[3,96,384]{2,1,0:T(8,128)(2,1)S(1)} %get-tuple-element.19), channel_id=1, source_target_pairs={{0,2},{1,3},{2,0},{3,1},{4,6},{5,7},{6,4},{7,5},{8,10},{9,11},{10,... | collective-permute-start | bytes 663560 | tf_op jit(solution)/shard_map/ppermute | solution.py:36
  16.5 0.3 fusion.2
  16.8 0.3 collective-permute-start.1
  17.1 7.4 %collective-permute-done.1 = bf16[2,4,8,2,384]{4,3,2,1,0:T(2,128)(2,1)S(1)} collective-permute-done((bf16[2,4,8,2,384]{4,3,2,1,0:T(2,128)(2,1)S(1)}, bf16[2,4,8,2,384]{4,3,2,1,0:T(2,128)(2,1)S(1)}, u32[]{:S(2)}, u32[]{:S(2)}) %collective-permute-start.1) | collective-permute-done | bytes 98336 | tf_op jit(solution)/shard_map/ppermute | solution.py:169
  24.8 0.6 collective-permute-start.15
  25.4 0.6 collective-permute-start.2
  26.0 5.3 %collective-permute-done.2 = bf16[4,2,8,2,384]{4,3,2,1,0:T(2,128)(2,1)S(1)} collective-permute-done((bf16[4,2,8,2,384]{4,3,2,1,0:T(2,128)(2,1)S(1)}, bf16[4,2,8,2,384]{4,3,2,1,0:T(2,128)(2,1)S(1)}, u32[]{:S(2)}, u32[]{:S(2)}) %collective-permute-start.2) | collective-permute-done | bytes 98336 | tf_op jit(solution)/shard_map/ppermute | solution.py:169
  31.2 1.3 %collective-permute-start.6 = (bf16[128,1536]{1,0:T(8,128)(2,1)S(1)}, bf16[128,1536]{1,0:T(8,128)(2,1)S(1)}, u32[]{:S(2)}, u32[]{:S(2)}) collective-permute-start(bf16[128,1536]{1,0:T(8,128)(2,1)S(1)} %constant_dynamic-update-slice_fusion.refs_5_), channel_id=1, source_target_pairs={{0,4},{2,6},{5,1},{7,3},{8,12},{10,14},{13,9},{15,11},{16,20},{18,... | collective-permute-start | bytes 1179656 | tf_op jit(solution)/shard_map/ppermute | solution.py:36
  32.8 2.3 %collective-permute-done.9.refs_11_ = bf16[3,96,384]{2,1,0:T(8,128)(2,1)S(1)} collective-permute-done((bf16[3,96,384]{2,1,0:T(8,128)(2,1)S(1)}, bf16[3,96,384]{2,1,0:T(8,128)(2,1)S(1)}, u32[]{:S(2)}, u32[]{:S(2)}) %collective-permute-start.9) | collective-permute-done | bytes 221216 | tf_op jit(solution)/shard_map/ppermute | solution.py:36
  35.1 2.1 %collective-permute-start.16 = (bf16[3,96,384]{2,1,0:T(8,128)(2,1)S(1)}, bf16[3,96,384]{2,1,0:T(8,128)(2,1)S(1)}, u32[]{:S(2)}, u32[]{:S(2)}) collective-permute-start(bf16[3,96,384]{2,1,0:T(8,128)(2,1)S(1)} %collective-permute-done.8.refs_10_), channel_id=1, source_target_pairs={{0,1},{1,0},{2,3},{3,2},{4,5},{5,4},{6,7},{7,6},{8,9},{9,8},{10,11... | collective-permute-start | bytes 663560 | tf_op jit(solution)/shard_map/ppermute | solution.py:36
  37.2 9.1 %collective-permute-start.10 = (bf16[3,96,384]{2,1,0:T(8,128)(2,1)S(1)}, bf16[3,96,384]{2,1,0:T(8,128)(2,1)S(1)}, u32[]{:S(2)}, u32[]{:S(2)}) collective-permute-start(bf16[3,96,384]{2,1,0:T(8,128)(2,1)S(1)} %collective-permute-done.9.refs_11_), channel_id=1, source_target_pairs={{0,16},{1,17},{2,18},{3,19},{4,20},{5,21},{6,22},{7,23},{8,24},{9,... | collective-permute-start | bytes 663560 | tf_op jit(solution)/shard_map/ppermute | solution.py:36
  46.3 0.7 collective-permute-start.21
  47.0 6.3 %collective-permute-start.14 = (bf16[3,96,384]{2,1,0:T(8,128)(2,1)S(1)}, bf16[3,96,384]{2,1,0:T(8,128)(2,1)S(1)}, u32[]{:S(2)}, u32[]{:S(2)}) collective-permute-start(bf16[3,96,384]{2,1,0:T(8,128)(2,1)S(1)} %collective-permute-done.13.refs_15_), channel_id=1, source_target_pairs={{0,16},{1,17},{2,18},{3,19},{4,20},{5,21},{6,22},{7,23},{8,24},{9,... | collective-permute-start | bytes 663560 | tf_op jit(solution)/shard_map/ppermute | solution.py:36
  53.4 0.3 collective-permute-start.19
  53.7 0.7 collective-permute-start.5
  54.4 3.1 %collective-permute-start.7 = (bf16[128,1536]{1,0:T(8,128)(2,1)S(1)}, bf16[128,1536]{1,0:T(8,128)(2,1)S(1)}, u32[]{:S(2)}, u32[]{:S(2)}) collective-permute-start(bf16[128,1536]{1,0:T(8,128)(2,1)S(1)} %collective-permute-done.6.refs_7_), channel_id=1, source_target_pairs={{1,3},{3,1},{4,6},{6,4},{9,11},{11,9},{12,14},{14,12},{17,19},{19,... | collective-permute-start | bytes 1179656 | tf_op jit(solution)/shard_map/ppermute | solution.py:36
  57.5 0.3 pad_maximum_fusion
  57.9 1.3 %collective-permute-done.14.refs_16_ = bf16[3,96,384]{2,1,0:T(8,128)(2,1)S(1)} collective-permute-done((bf16[3,96,384]{2,1,0:T(8,128)(2,1)S(1)}, bf16[3,96,384]{2,1,0:T(8,128)(2,1)S(1)}, u32[]{:S(2)}, u32[]{:S(2)}) %collective-permute-start.14) | collective-permute-done | bytes 221216 | tf_op jit(solution)/shard_map/ppermute | solution.py:36
  59.2 0.8 collective-permute-start.18
  59.9 4.0 %collective-permute-done.12.refs_14_ = bf16[3,96,384]{2,1,0:T(8,128)(2,1)S(1)} collective-permute-done((bf16[3,96,384]{2,1,0:T(8,128)(2,1)S(1)}, bf16[3,96,384]{2,1,0:T(8,128)(2,1)S(1)}, u32[]{:S(2)}, u32[]{:S(2)}) %collective-permute-start.12) | collective-permute-done | bytes 221216 | tf_op jit(solution)/shard_map/ppermute | solution.py:36
  63.9 0.6 collective-permute-start.20
  64.5 1.0 %collective-permute-done.20.refs_22_ = bf16[3,96,384]{2,1,0:T(8,128)(2,1)S(1)} collective-permute-done((bf16[3,96,384]{2,1,0:T(8,128)(2,1)S(1)}, bf16[3,96,384]{2,1,0:T(8,128)(2,1)S(1)}, u32[]{:S(2)}, u32[]{:S(2)}) %collective-permute-start.20) | collective-permute-done | bytes 221216 | tf_op jit(solution)/shard_map/ppermute | solution.py:36
  65.6 1.3 %collective-permute-done.7.refs_8_ = bf16[128,1536]{1,0:T(8,128)(2,1)S(1)} collective-permute-done((bf16[128,1536]{1,0:T(8,128)(2,1)S(1)}, bf16[128,1536]{1,0:T(8,128)(2,1)S(1)}, u32[]{:S(2)}, u32[]{:S(2)}) %collective-permute-start.7) | collective-permute-done | bytes 393248 | tf_op jit(solution)/shard_map/ppermute | solution.py:36
  66.9 0.7 copy-done.7
  67.6 5.7 %step.1.refs_25_ = bf16[256,384]{1,0:T(8,128)(2,1)S(1)} custom-call(s32[4]{0:T(128)S(1)} %copy-done.7, f32[2]{0:T(128)S(1)} %copy-done.8, f32[1,1536]{1,0:T(1,128)S(1)} %reshape.4.refs_2_, bf16[128,384]{1,0:T(8,128)(2,1)S(1)} %get-tuple-element.36.refs_3_, bf16[128,384]{1,0:T(8,128)(2,1)S(1)} %get-tuple-element.35.refs_4_, ...), custom_call_target="tpu_custom_call" | custom-call | flops 1056964608 | bytes 6291456 | tf_op jit(solution)/shard_map/step/pallas_call | solution.py:322
  73.3 1.5 %collective-permute-start.25 = (bf16[256,384]{1,0:T(8,128)(2,1)S(1)}, bf16[256,384]{1,0:T(8,128)(2,1)S(1)}, u32[]{:S(2)}, u32[]{:S(2)}) collective-permute-start(bf16[256,384]{1,0:T(8,128)(2,1)S(1)} %step.1.refs_25_), channel_id=1, source_target_pairs={{0,2},{1,3},{2,0},{3,1},{4,6},{5,7},{6,4},{7,5},{8,10},{9,11},{10,... | collective-permute-start | bytes 589832 | tf_op jit(solution)/shard_map/ppermute | solution.py:36
  74.8 1.3 %collective-permute-start.23 = (bf16[256,384]{1,0:T(8,128)(2,1)S(1)}, bf16[256,384]{1,0:T(8,128)(2,1)S(1)}, u32[]{:S(2)}, u32[]{:S(2)}) collective-permute-start(bf16[256,384]{1,0:T(8,128)(2,1)S(1)} %step.1.refs_25_), channel_id=1, source_target_pairs={{0,6},{1,7},{2,4},{3,5},{4,2},{5,3},{6,0},{7,1},{8,14},{9,15},{10,... | collective-permute-start | bytes 589832 | tf_op jit(solution)/shard_map/ppermute | solution.py:36
  76.0 2.8 %collective-permute-done.25.refs_28_ = bf16[256,384]{1,0:T(8,128)(2,1)S(1)} collective-permute-done((bf16[256,384]{1,0:T(8,128)(2,1)S(1)}, bf16[256,384]{1,0:T(8,128)(2,1)S(1)}, u32[]{:S(2)}, u32[]{:S(2)}) %collective-permute-start.25) | collective-permute-done | bytes 196640 | tf_op jit(solution)/shard_map/ppermute | solution.py:36
  78.8 1.4 %collective-permute-done.24.refs_27_ = bf16[256,384]{1,0:T(8,128)(2,1)S(1)} collective-permute-done((bf16[256,384]{1,0:T(8,128)(2,1)S(1)}, bf16[256,384]{1,0:T(8,128)(2,1)S(1)}, u32[]{:S(2)}, u32[]{:S(2)}) %collective-permute-start.24) | collective-permute-done | bytes 196640 | tf_op jit(solution)/shard_map/ppermute | solution.py:36
  80.2 3.8 %collective-permute-done.23.refs_26_ = bf16[256,384]{1,0:T(8,128)(2,1)S(1)} collective-permute-done((bf16[256,384]{1,0:T(8,128)(2,1)S(1)}, bf16[256,384]{1,0:T(8,128)(2,1)S(1)}, u32[]{:S(2)}, u32[]{:S(2)}) %collective-permute-start.23) | collective-permute-done | bytes 196640 | tf_op jit(solution)/shard_map/ppermute | solution.py:36
  84.1 7.0 %last_step.1 = (bf16[64,384]{1,0:T(8,128)(2,1)S(1)}, bf16[64,384]{1,0:T(8,128)(2,1)S(1)}, bf16[64,384]{1,0:T(8,128)(2,1)S(1)}, bf16[64,384]{1,0:T(8,128)(2,1)S(1)}, bf16[64,384]{1,0:T(8,128)(2,1)S(1)}) custom-call(s32[4]{0:T(128)S(1)} %copy-done.7, f32[2]{0:T(128)S(1)} %copy-done.8, f32[1,1536]{1,0:T(1,128)S(1)} %reshape.4.refs_2_, ...), custom_call_target="tpu_custom_call" | custom-call | flops 1056964608 | bytes 6291456 | tf_op jit(solution)/shard_map/last_step/pallas_call | solution.py:322
  91.1 0.6 copy-done.5
  91.7 2.2 %collective-permute-start.26 = (bf16[64,384]{1,0:T(8,128)(2,1)S(1)}, bf16[64,384]{1,0:T(8,128)(2,1)S(1)}, u32[]{:S(2)}, u32[]{:S(2)}) collective-permute-start(bf16[64,384]{1,0:T(8,128)(2,1)S(1)} %get-tuple-element.23), channel_id=1, source_target_pairs={{0,2},{1,4},{2,0},{3,6},{4,1},{5,7},{6,3},{7,5},{8,10},{9,12},{10,... | collective-permute-start | bytes 147464 | tf_op jit(solution)/shard_map/ppermute | solution.py:36
  93.8 1.2 %collective-permute-start.28 = (bf16[64,384]{1,0:T(8,128)(2,1)S(1)}, bf16[64,384]{1,0:T(8,128)(2,1)S(1)}, u32[]{:S(2)}, u32[]{:S(2)}) collective-permute-start(bf16[64,384]{1,0:T(8,128)(2,1)S(1)} %get-tuple-element.25), channel_id=1, source_target_pairs={{0,1},{1,7},{2,3},{3,5},{4,2},{5,4},{6,0},{7,6},{8,9},{9,15},{10,1... | collective-permute-start | bytes 147464 | tf_op jit(solution)/shard_map/ppermute | solution.py:36
  95.0 5.0 %collective-permute-start.29 = (bf16[64,384]{1,0:T(8,128)(2,1)S(1)}, bf16[64,384]{1,0:T(8,128)(2,1)S(1)}, u32[]{:S(2)}, u32[]{:S(2)}) collective-permute-start(bf16[64,384]{1,0:T(8,128)(2,1)S(1)} %get-tuple-element.26), channel_id=1, source_target_pairs={{1,6},{3,4},{4,3},{6,1},{9,14},{11,12},{12,11},{14,9},{17,22},{19,... | collective-permute-start | bytes 147464 | tf_op jit(solution)/shard_map/ppermute | solution.py:36
  100.1 1.7 %collective-permute-done.29.fourth = bf16[64,384]{1,0:T(8,128)(2,1)S(1)} collective-permute-done((bf16[64,384]{1,0:T(8,128)(2,1)S(1)}, bf16[64,384]{1,0:T(8,128)(2,1)S(1)}, u32[]{:S(2)}, u32[]{:S(2)}) %collective-permute-start.29) | collective-permute-done | bytes 49184 | tf_op jit(solution)/shard_map/ppermute | solution.py:36
  101.8 0.6 copy-done.14
  102.4 1.6 %join.1 = bf16[64,1536]{1,0:T(8,128)(2,1)} custom-call(bf16[64,384]{1,0:T(8,128)(2,1)} %copy-done.5, bf16[64,384]{1,0:T(8,128)(2,1)} %copy-done.11, bf16[64,384]{1,0:T(8,128)(2,1)} %copy-done.12, bf16[64,384]{1,0:T(8,128)(2,1)} %copy-done.13, bf16[64,384]{1,0:T(8,128)(2,1)} %copy-done.14), custom_call_target="tpu_custom_call" | custom-call | tf_op jit(solution)/shard_map/join/pallas_call | solution.py:392
  (56 shorter events, 0.9 us)
Async XLA Ops:
  0.0 1.1 %copy-start.1 = (bf16[128,1,2,1536]{3,2,1,0:T(2,128)(2,1)S(1)}, bf16[128,1,2,1536]{3,2,1,0:T(2,128)(2,1)}, u32[]{:S(2)}) copy-start(bf16[128,1,2,1536]{3,2,1,0:T(2,128)(2,1)} %mem_ref.1) | copy-start | bytes 2359300
  1.1 1.0 copy-start.2
  2.1 1.0 copy-start.3
  3.1 1.0 copy-start.4
  4.0 0.7 copy-start.6
  4.7 0.7 copy-start.9
  5.4 7.3 %copy-start.10 = (bf16[64,1536]{1,0:T(8,128)(2,1)S(1)}, bf16[64,1536]{1,0:T(8,128)(2,1)}, u32[]{:S(2)}) copy-start(bf16[64,1536]{1,0:T(8,128)(2,1)} %param.10) | copy-start | bytes 589828
  7.6 8.9 %collective-permute-start = (bf16[8,8,2,384]{3,2,1,0:T(2,128)(2,1)S(1)}, bf16[8,8,2,384]{3,2,1,0:T(2,128)(2,1)S(1)}, u32[]{:S(2)}, u32[]{:S(2)}) collective-permute-start(bf16[8,8,2,384]{3,2,1,0:T(2,128)(2,1)S(1)} %get-tuple-element.17), channel_id=1, source_target_pairs={{0,1},{1,0},{2,3},{3,2},{4,5},{5,4},{6,7},{7,6},{8,9},{9,8},{10,11... | collective-permute-start | bytes 294920 | tf_op jit(solution)/shard_map/ppermute | solution.py:169
  7.7 27.4 %collective-permute-start.13 = (bf16[3,96,384]{2,1,0:T(8,128)(2,1)S(1)}, bf16[3,96,384]{2,1,0:T(8,128)(2,1)S(1)}, u32[]{:S(2)}, u32[]{:S(2)}) collective-permute-start(bf16[3,96,384]{2,1,0:T(8,128)(2,1)S(1)} %get-tuple-element.21), channel_id=1, source_target_pairs={{0,4},{1,5},{2,6},{3,7},{4,0},{5,1},{6,2},{7,3},{8,12},{9,13},{10,... | collective-permute-start | bytes 663560 | tf_op jit(solution)/shard_map/ppermute | solution.py:36
  10.5 26.7 %collective-permute-start.11 = (bf16[3,96,384]{2,1,0:T(8,128)(2,1)S(1)}, bf16[3,96,384]{2,1,0:T(8,128)(2,1)S(1)}, u32[]{:S(2)}, u32[]{:S(2)}) collective-permute-start(bf16[3,96,384]{2,1,0:T(8,128)(2,1)S(1)} %get-tuple-element.21), channel_id=1, source_target_pairs={{0,12},{1,13},{2,14},{3,15},{4,8},{5,9},{6,10},{7,11},{8,4},{9,5},... | collective-permute-start | bytes 663560 | tf_op jit(solution)/shard_map/ppermute | solution.py:36
  12.7 12.1 %collective-permute-start.4 = (bf16[64,1536]{1,0:T(8,128)(2,1)S(1)}, bf16[64,1536]{1,0:T(8,128)(2,1)S(1)}, u32[]{:S(2)}, u32[]{:S(2)}) collective-permute-start(bf16[64,1536]{1,0:T(8,128)(2,1)S(1)} %copy-done.10), channel_id=1, source_target_pairs={{1,0},{3,2},{4,5},{6,7},{9,8},{11,10},{12,13},{14,15},{17,16},{19,... | collective-permute-start | bytes 589832 | tf_op jit(solution)/shard_map/ppermute | solution.py:36
  15.2 10.1 %collective-permute-start.8 = (bf16[3,96,384]{2,1,0:T(8,128)(2,1)S(1)}, bf16[3,96,384]{2,1,0:T(8,128)(2,1)S(1)}, u32[]{:S(2)}, u32[]{:S(2)}) collective-permute-start(bf16[3,96,384]{2,1,0:T(8,128)(2,1)S(1)} %get-tuple-element.19), channel_id=1, source_target_pairs={{0,2},{1,3},{2,0},{3,1},{4,6},{5,7},{6,4},{7,5},{8,10},{9,11},{10,... | collective-permute-start | bytes 663560 | tf_op jit(solution)/shard_map/ppermute | solution.py:36
  16.8 7.7 %collective-permute-start.1 = (bf16[2,4,8,2,384]{4,3,2,1,0:T(2,128)(2,1)S(1)}, bf16[2,4,8,2,384]{4,3,2,1,0:T(2,128)(2,1)S(1)}, u32[]{:S(2)}, u32[]{:S(2)}) collective-permute-start(bf16[2,4,8,2,384]{4,3,2,1,0:T(2,128)(2,1)S(1)} %get-tuple-element.34), channel_id=1, source_target_pairs={{0,2},{1,3},{2,0},{3,1},{4,6},{5,7},{6,4},{7,5},{8,10},{9,11},{10,... | collective-permute-start | bytes 294920 | tf_op jit(solution)/shard_map/ppermute | solution.py:169
  24.5 10.6 %collective-permute-start.9 = (bf16[3,96,384]{2,1,0:T(8,128)(2,1)S(1)}, bf16[3,96,384]{2,1,0:T(8,128)(2,1)S(1)}, u32[]{:S(2)}, u32[]{:S(2)}) collective-permute-start(bf16[3,96,384]{2,1,0:T(8,128)(2,1)S(1)} %get-tuple-element.20), channel_id=1, source_target_pairs={{0,8},{1,9},{2,10},{3,11},{4,12},{5,13},{6,14},{7,15},{8,0},{9,1},... | collective-permute-start | bytes 663560 | tf_op jit(solution)/shard_map/ppermute | solution.py:36
  24.8 12.5 %collective-permute-start.15 = (bf16[3,96,384]{2,1,0:T(8,128)(2,1)S(1)}, bf16[3,96,384]{2,1,0:T(8,128)(2,1)S(1)}, u32[]{:S(2)}, u32[]{:S(2)}) collective-permute-start(bf16[3,96,384]{2,1,0:T(8,128)(2,1)S(1)} %get-tuple-element.18.refs_9_), channel_id=1, source_target_pairs={{0,1},{1,0},{2,3},{3,2},{4,5},{5,4},{6,7},{7,6},{8,9},{9,8},{10,11... | collective-permute-start | bytes 663560 | tf_op jit(solution)/shard_map/ppermute | solution.py:36
  25.4 5.9 %collective-permute-start.2 = (bf16[4,2,8,2,384]{4,3,2,1,0:T(2,128)(2,1)S(1)}, bf16[4,2,8,2,384]{4,3,2,1,0:T(2,128)(2,1)S(1)}, u32[]{:S(2)}, u32[]{:S(2)}) collective-permute-start(bf16[4,2,8,2,384]{4,3,2,1,0:T(2,128)(2,1)S(1)} %get-tuple-element.32), channel_id=1, source_target_pairs={{0,4},{1,5},{2,6},{3,7},{4,0},{5,1},{6,2},{7,3},{8,12},{9,13},{10,... | collective-permute-start | bytes 294920 | tf_op jit(solution)/shard_map/ppermute | solution.py:169
  31.2 23.1 %collective-permute-start.6 = (bf16[128,1536]{1,0:T(8,128)(2,1)S(1)}, bf16[128,1536]{1,0:T(8,128)(2,1)S(1)}, u32[]{:S(2)}, u32[]{:S(2)}) collective-permute-start(bf16[128,1536]{1,0:T(8,128)(2,1)S(1)} %constant_dynamic-update-slice_fusion.refs_5_), channel_id=1, source_target_pairs={{0,4},{2,6},{5,1},{7,3},{8,12},{10,14},{13,9},{15,11},{16,20},{18,... | collective-permute-start | bytes 1179656 | tf_op jit(solution)/shard_map/ppermute | solution.py:36
  32.5 25.0 %copy-start.15 = (f32[1536]{0:T(1024)S(1)}, f32[1536]{0:T(1024)}, u32[]{:S(2)}) copy-start(f32[1536]{0:T(1024)} %param.11) | copy-start | bytes 18436
  35.1 11.2 %collective-permute-start.3 = (bf16[8,1,8,2,384]{4,3,2,1,0:T(2,128)(2,1)S(1)}, bf16[8,1,8,2,384]{4,3,2,1,0:T(2,128)(2,1)S(1)}, u32[]{:S(2)}, u32[]{:S(2)}) collective-permute-start(bf16[8,1,8,2,384]{4,3,2,1,0:T(2,128)(2,1)S(1)} %get-tuple-element.30), channel_id=1, source_target_pairs={{0,8},{1,9},{2,10},{3,11},{4,12},{5,13},{6,14},{7,15},{8,0},{9,1},... | collective-permute-start | bytes 294920 | tf_op jit(solution)/shard_map/ppermute | solution.py:169
  35.1 11.9 %collective-permute-start.16 = (bf16[3,96,384]{2,1,0:T(8,128)(2,1)S(1)}, bf16[3,96,384]{2,1,0:T(8,128)(2,1)S(1)}, u32[]{:S(2)}, u32[]{:S(2)}) collective-permute-start(bf16[3,96,384]{2,1,0:T(8,128)(2,1)S(1)} %collective-permute-done.8.refs_10_), channel_id=1, source_target_pairs={{0,1},{1,0},{2,3},{3,2},{4,5},{5,4},{6,7},{7,6},{8,9},{9,8},{10,11... | collective-permute-start | bytes 663560 | tf_op jit(solution)/shard_map/ppermute | solution.py:36
  37.2 16.2 %collective-permute-start.17 = (bf16[3,96,384]{2,1,0:T(8,128)(2,1)S(1)}, bf16[3,96,384]{2,1,0:T(8,128)(2,1)S(1)}, u32[]{:S(2)}, u32[]{:S(2)}) collective-permute-start(bf16[3,96,384]{2,1,0:T(8,128)(2,1)S(1)} %collective-permute-done.9.refs_11_), channel_id=1, source_target_pairs={{0,1},{1,0},{2,3},{3,2},{4,5},{5,4},{6,7},{7,6},{8,9},{9,8},{10,11... | collective-permute-start | bytes 663560 | tf_op jit(solution)/shard_map/ppermute | solution.py:36
  37.2 16.4 %collective-permute-start.10 = (bf16[3,96,384]{2,1,0:T(8,128)(2,1)S(1)}, bf16[3,96,384]{2,1,0:T(8,128)(2,1)S(1)}, u32[]{:S(2)}, u32[]{:S(2)}) collective-permute-start(bf16[3,96,384]{2,1,0:T(8,128)(2,1)S(1)} %collective-permute-done.9.refs_11_), channel_id=1, source_target_pairs={{0,16},{1,17},{2,18},{3,19},{4,20},{5,21},{6,22},{7,23},{8,24},{9,... | collective-permute-start | bytes 663560 | tf_op jit(solution)/shard_map/ppermute | solution.py:36
  46.3 7.3 %collective-permute-start.21 = (bf16[3,96,384]{2,1,0:T(8,128)(2,1)S(1)}, bf16[3,96,384]{2,1,0:T(8,128)(2,1)S(1)}, u32[]{:S(2)}, u32[]{:S(2)}) collective-permute-start(bf16[3,96,384]{2,1,0:T(8,128)(2,1)S(1)} %collective-permute-done.13.refs_15_), channel_id=1, source_target_pairs={{0,1},{1,0},{2,3},{3,2},{4,5},{5,4},{6,7},{7,6},{8,9},{9,8},{10,11... | collective-permute-start | bytes 663560 | tf_op jit(solution)/shard_map/ppermute | solution.py:36
  47.0 12.1 %collective-permute-start.14 = (bf16[3,96,384]{2,1,0:T(8,128)(2,1)S(1)}, bf16[3,96,384]{2,1,0:T(8,128)(2,1)S(1)}, u32[]{:S(2)}, u32[]{:S(2)}) collective-permute-start(bf16[3,96,384]{2,1,0:T(8,128)(2,1)S(1)} %collective-permute-done.13.refs_15_), channel_id=1, source_target_pairs={{0,16},{1,17},{2,18},{3,19},{4,20},{5,21},{6,22},{7,23},{8,24},{9,... | collective-permute-start | bytes 663560 | tf_op jit(solution)/shard_map/ppermute | solution.py:36
  53.4 6.6 %collective-permute-start.19 = (bf16[3,96,384]{2,1,0:T(8,128)(2,1)S(1)}, bf16[3,96,384]{2,1,0:T(8,128)(2,1)S(1)}, u32[]{:S(2)}, u32[]{:S(2)}) collective-permute-start(bf16[3,96,384]{2,1,0:T(8,128)(2,1)S(1)} %collective-permute-done.11.refs_13_), channel_id=1, source_target_pairs={{0,1},{1,0},{2,3},{3,2},{4,5},{5,4},{6,7},{7,6},{8,9},{9,8},{10,11... | collective-permute-start | bytes 663560 | tf_op jit(solution)/shard_map/ppermute | solution.py:36
  53.6 10.2 %collective-permute-start.12 = (bf16[3,96,384]{2,1,0:T(8,128)(2,1)S(1)}, bf16[3,96,384]{2,1,0:T(8,128)(2,1)S(1)}, u32[]{:S(2)}, u32[]{:S(2)}) collective-permute-start(bf16[3,96,384]{2,1,0:T(8,128)(2,1)S(1)} %collective-permute-done.11.refs_13_), channel_id=1, source_target_pairs={{0,16},{1,17},{2,18},{3,19},{4,20},{5,21},{6,22},{7,23},{8,24},{9,... | collective-permute-start | bytes 663560 | tf_op jit(solution)/shard_map/ppermute | solution.py:36
  53.7 10.9 %collective-permute-start.5 = (bf16[128,1536]{1,0:T(8,128)(2,1)S(1)}, bf16[128,1536]{1,0:T(8,128)(2,1)S(1)}, u32[]{:S(2)}, u32[]{:S(2)}) collective-permute-start(bf16[128,1536]{1,0:T(8,128)(2,1)S(1)} %constant_dynamic-update-slice_fusion.refs_5_), channel_id=1, source_target_pairs={{0,2},{2,0},{5,7},{7,5},{8,10},{10,8},{13,15},{15,13},{16,18},{18,... | collective-permute-start | bytes 1179656 | tf_op jit(solution)/shard_map/ppermute | solution.py:36
  54.4 12.5 %collective-permute-start.7 = (bf16[128,1536]{1,0:T(8,128)(2,1)S(1)}, bf16[128,1536]{1,0:T(8,128)(2,1)S(1)}, u32[]{:S(2)}, u32[]{:S(2)}) collective-permute-start(bf16[128,1536]{1,0:T(8,128)(2,1)S(1)} %collective-permute-done.6.refs_7_), channel_id=1, source_target_pairs={{1,3},{3,1},{4,6},{6,4},{9,11},{11,9},{12,14},{14,12},{17,19},{19,... | collective-permute-start | bytes 1179656 | tf_op jit(solution)/shard_map/ppermute | solution.py:36
  59.2 5.4 %collective-permute-start.18 = (bf16[3,96,384]{2,1,0:T(8,128)(2,1)S(1)}, bf16[3,96,384]{2,1,0:T(8,128)(2,1)S(1)}, u32[]{:S(2)}, u32[]{:S(2)}) collective-permute-start(bf16[3,96,384]{2,1,0:T(8,128)(2,1)S(1)} %collective-permute-done.10.refs_12_), channel_id=1, source_target_pairs={{0,1},{1,0},{2,3},{3,2},{4,5},{5,4},{6,7},{7,6},{8,9},{9,8},{10,11... | collective-permute-start | bytes 663560 | tf_op jit(solution)/shard_map/ppermute | solution.py:36
  59.9 4.6 %collective-permute-start.22 = (bf16[3,96,384]{2,1,0:T(8,128)(2,1)S(1)}, bf16[3,96,384]{2,1,0:T(8,128)(2,1)S(1)}, u32[]{:S(2)}, u32[]{:S(2)}) collective-permute-start(bf16[3,96,384]{2,1,0:T(8,128)(2,1)S(1)} %collective-permute-done.14.refs_16_), channel_id=1, source_target_pairs={{0,1},{1,0},{2,3},{3,2},{4,5},{5,4},{6,7},{7,6},{8,9},{9,8},{10,11... | collective-permute-start | bytes 663560 | tf_op jit(solution)/shard_map/ppermute | solution.py:36
  63.9 1.7 %collective-permute-start.20 = (bf16[3,96,384]{2,1,0:T(8,128)(2,1)S(1)}, bf16[3,96,384]{2,1,0:T(8,128)(2,1)S(1)}, u32[]{:S(2)}, u32[]{:S(2)}) collective-permute-start(bf16[3,96,384]{2,1,0:T(8,128)(2,1)S(1)} %collective-permute-done.12.refs_14_), channel_id=1, source_target_pairs={{0,1},{1,0},{2,3},{3,2},{4,5},{5,4},{6,7},{7,6},{8,9},{9,8},{10,11... | collective-permute-start | bytes 663560 | tf_op jit(solution)/shard_map/ppermute | solution.py:36
  66.9 6.4 %copy-start = (bf16[128,1536]{1,0:T(8,128)(2,1)}, bf16[128,1536]{1,0:T(8,128)(2,1)S(1)}, u32[]{:S(2)}) copy-start(bf16[128,1536]{1,0:T(8,128)(2,1)S(1)} %collective-permute-done.7.refs_8_) | copy-start | bytes 1179652
  66.9 0.7 copy-start.7
  66.9 0.7 copy-start.8
  73.3 5.5 %collective-permute-start.25 = (bf16[256,384]{1,0:T(8,128)(2,1)S(1)}, bf16[256,384]{1,0:T(8,128)(2,1)S(1)}, u32[]{:S(2)}, u32[]{:S(2)}) collective-permute-start(bf16[256,384]{1,0:T(8,128)(2,1)S(1)} %step.1.refs_25_), channel_id=1, source_target_pairs={{0,2},{1,3},{2,0},{3,1},{4,6},{5,7},{6,4},{7,5},{8,10},{9,11},{10,... | collective-permute-start | bytes 589832 | tf_op jit(solution)/shard_map/ppermute | solution.py:36
  74.8 5.4 %collective-permute-start.24 = (bf16[256,384]{1,0:T(8,128)(2,1)S(1)}, bf16[256,384]{1,0:T(8,128)(2,1)S(1)}, u32[]{:S(2)}, u32[]{:S(2)}) collective-permute-start(bf16[256,384]{1,0:T(8,128)(2,1)S(1)} %step.1.refs_25_), channel_id=1, source_target_pairs={{0,4},{1,5},{2,6},{3,7},{4,0},{5,1},{6,2},{7,3},{8,12},{9,13},{10,... | collective-permute-start | bytes 589832 | tf_op jit(solution)/shard_map/ppermute | solution.py:36
  74.8 9.3 %collective-permute-start.23 = (bf16[256,384]{1,0:T(8,128)(2,1)S(1)}, bf16[256,384]{1,0:T(8,128)(2,1)S(1)}, u32[]{:S(2)}, u32[]{:S(2)}) collective-permute-start(bf16[256,384]{1,0:T(8,128)(2,1)S(1)} %step.1.refs_25_), channel_id=1, source_target_pairs={{0,6},{1,7},{2,4},{3,5},{4,2},{5,3},{6,0},{7,1},{8,14},{9,15},{10,... | collective-permute-start | bytes 589832 | tf_op jit(solution)/shard_map/ppermute | solution.py:36
  91.1 0.6 copy-start.5
  91.7 8.4 %collective-permute-start.26 = (bf16[64,384]{1,0:T(8,128)(2,1)S(1)}, bf16[64,384]{1,0:T(8,128)(2,1)S(1)}, u32[]{:S(2)}, u32[]{:S(2)}) collective-permute-start(bf16[64,384]{1,0:T(8,128)(2,1)S(1)} %get-tuple-element.23), channel_id=1, source_target_pairs={{0,2},{1,4},{2,0},{3,6},{4,1},{5,7},{6,3},{7,5},{8,10},{9,12},{10,... | collective-permute-start | bytes 147464 | tf_op jit(solution)/shard_map/ppermute | solution.py:36
  93.8 6.2 %collective-permute-start.27 = (bf16[64,384]{1,0:T(8,128)(2,1)S(1)}, bf16[64,384]{1,0:T(8,128)(2,1)S(1)}, u32[]{:S(2)}, u32[]{:S(2)}) collective-permute-start(bf16[64,384]{1,0:T(8,128)(2,1)S(1)} %get-tuple-element.24), channel_id=1, source_target_pairs={{0,3},{1,5},{2,1},{3,7},{4,0},{5,6},{6,2},{7,4},{8,11},{9,13},{10,... | collective-permute-start | bytes 147464 | tf_op jit(solution)/shard_map/ppermute | solution.py:36
  93.8 6.2 %collective-permute-start.28 = (bf16[64,384]{1,0:T(8,128)(2,1)S(1)}, bf16[64,384]{1,0:T(8,128)(2,1)S(1)}, u32[]{:S(2)}, u32[]{:S(2)}) collective-permute-start(bf16[64,384]{1,0:T(8,128)(2,1)S(1)} %get-tuple-element.25), channel_id=1, source_target_pairs={{0,1},{1,7},{2,3},{3,5},{4,2},{5,4},{6,0},{7,6},{8,9},{9,15},{10,1... | collective-permute-start | bytes 147464 | tf_op jit(solution)/shard_map/ppermute | solution.py:36
  95.0 6.8 %collective-permute-start.29 = (bf16[64,384]{1,0:T(8,128)(2,1)S(1)}, bf16[64,384]{1,0:T(8,128)(2,1)S(1)}, u32[]{:S(2)}, u32[]{:S(2)}) collective-permute-start(bf16[64,384]{1,0:T(8,128)(2,1)S(1)} %get-tuple-element.26), channel_id=1, source_target_pairs={{1,6},{3,4},{4,3},{6,1},{9,14},{11,12},{12,11},{14,9},{17,22},{19,... | collective-permute-start | bytes 147464 | tf_op jit(solution)/shard_map/ppermute | solution.py:36
  100.0 1.8 %copy-start.11 = (bf16[64,384]{1,0:T(8,128)(2,1)}, bf16[64,384]{1,0:T(8,128)(2,1)S(1)}, u32[]{:S(2)}) copy-start(bf16[64,384]{1,0:T(8,128)(2,1)S(1)} %collective-permute-done.26.first) | copy-start | bytes 147460
  100.0 1.7 %copy-start.12 = (bf16[64,384]{1,0:T(8,128)(2,1)}, bf16[64,384]{1,0:T(8,128)(2,1)S(1)}, u32[]{:S(2)}) copy-start(bf16[64,384]{1,0:T(8,128)(2,1)S(1)} %collective-permute-done.27.second) | copy-start | bytes 147460
  100.1 1.7 %copy-start.13 = (bf16[64,384]{1,0:T(8,128)(2,1)}, bf16[64,384]{1,0:T(8,128)(2,1)S(1)}, u32[]{:S(2)}) copy-start(bf16[64,384]{1,0:T(8,128)(2,1)S(1)} %collective-permute-done.28.third) | copy-start | bytes 147460
  101.8 0.6 copy-start.14

commit v2 on v1

--- a/solution.py
+++ b/solution.py
@@ -7,6 +7,7 @@
 from jax.experimental import pallas as pl
 from jax.experimental.pallas import tpu as pltpu
 from jax.sharding import PartitionSpec as P
+
 
 HEADS = 12
 HS = 128
@@ -55,23 +56,70 @@
     return out
 
 
+def joined_bits(one, other):
+    return one + other - 2 * one * other
+
+
 def columns(quarter, width):
     return pl.ds(pl.multiple_of(quarter * width, 128), width)
 
 
-def pack_kernel(
-    list_ref, slot_ref, w_query, w_key, w_value, mem_ref,
-    own_ref, beside_ref, even_ref, odd_ref, kept_ref, sent_ref,
-    rows, stored, row_sem, mem_sem, out_sem, give_sem,
+def pack_weights_kernel(
+    w_query, w_key, w_value, own_ref, beside_ref, even_ref, odd_ref, rows, row_sem, out_sem
 ):
-    x, index, plane, y, c = here()
-    devices = lax.axis_size("frame")
-    frames, entries = list_ref.shape
+    x, _, plane, y, c = here()
     width = own_ref.shape[2]
     reads = []
     for number, weight in enumerate((w_query, w_key, w_value)):
         reads.append(pltpu.make_async_copy(weight, rows.at[number], row_sem.at[number]))
         reads[-1].start()
+    across = joined_bits(joined_bits(x, y), c)
+    low = plane % 2
+    quarters = (low * 2 + across, (1 - low) * 2 + across, low * 2 + 1 - y, quarter_of(plane, y))
+    for read in reads:
+        read.wait()
+    gives = []
+    for number, (quarter, out) in enumerate(zip(quarters, (even_ref, odd_ref, beside_ref, own_ref))):
+        gives.append(pltpu.make_async_copy(rows.at[:, :, columns(quarter, width)], out, out_sem.at[number]))
+        gives[-1].start()
+    for give in gives:
+        give.wait()
+
+
+def pack_weights(w_query, w_key, w_value):
+    shard_rows, features = w_query.shape
+    piece = jax.ShapeDtypeStruct((3, shard_rows, features // SPATIAL), w_query.dtype)
+    anywhere = pl.BlockSpec(memory_space=pl.ANY)
+    held = pl.BlockSpec(memory_space=pltpu.HBM)
+    return pl.pallas_call(
+        pack_weights_kernel,
+        out_shape=(piece,) * 4,
+        in_specs=[held] * 3,
+        out_specs=(anywhere,) * 4,
+        scratch_shapes=[
+            pltpu.VMEM((3, shard_rows, features), w_query.dtype),
+            pltpu.SemaphoreType.DMA((3,)),
+            pltpu.SemaphoreType.DMA((4,)),
+        ],
+        name="pack_weights",
+    )(w_query, w_key, w_value)
+
+
+def pack_memory_kernel(
+    list_hbm, slot_hbm, mem_ref, kept_ref, sent_ref, list_ref, slot_ref, stored, scalar_sem, mem_sem, give_sem
+):
+    _, index, _, _, _ = here()
+    devices = lax.axis_size("frame")
+    frames, entries = list_ref.shape
+    width = kept_ref.shape[-1]
+    scalars = [
+        pltpu.make_async_copy(list_hbm, list_ref, scalar_sem.at[0]),
+        pltpu.make_async_copy(slot_hbm, slot_ref, scalar_sem.at[1]),
+    ]
+    for copy in scalars:
+        copy.start()
+    for copy in scalars:
+        copy.wait()
     picks = []
     for frame in range(frames):
         for entry in range(entries):
@@ -79,23 +127,14 @@
             row = slot_ref[list_ref[frame, entry]]
             picks.append(pltpu.make_async_copy(mem_ref.at[row, 0], stored.at[number], mem_sem.at[number]))
             picks[-1].start()
-    across = y + x - 2 * x * y
-    low = plane % 2
-    quarters = (quarter_of(plane, y), low * 2 + 1 - y, low * 2 + across, (1 - low) * 2 + across)
-    for read in reads:
-        read.wait()
-    gives = []
-    for number, (quarter, out) in enumerate(zip(quarters, (own_ref, beside_ref, even_ref, odd_ref))):
-        gives.append(pltpu.make_async_copy(rows.at[:, :, columns(quarter, width)], out, out_sem.at[number]))
-        gives[-1].start()
     for pick in picks:
         pick.wait()
+    gives = []
     bits = devices.bit_length() - 1
     for away in range(devices):
         target = flipped(index, away)
-        to_plane = target // 4
-        to_y = (target - to_plane * 4) // 2
-        to_frame = (to_plane // 2) * 2 + target % 2
+        to_plane, to_y, to_c = coords(target)
+        to_frame = (to_plane // 2) * 2 + to_c
         place = 0
         for bit in range(1, bits):
             place = place * 2 + (away >> bit & 1)
@@ -112,46 +151,44 @@
         give.wait()
 
 
-def pack(w_query, w_key, w_value, mem_cache, intersection, slot_of):
+def pack_memory(mem_cache, intersection, slot_of):
     devices = lax.axis_size("frame")
-    shard_rows, features = w_query.shape
-    width = features // SPATIAL
+    features = mem_cache.shape[-1]
     frames, entries = intersection.shape
-    piece = jax.ShapeDtypeStruct((3, shard_rows, width), w_query.dtype)
-    half = jax.ShapeDtypeStruct((devices // 2, entries, 2, width), mem_cache.dtype)
+    half = jax.ShapeDtypeStruct((devices // 2, entries, 2, features // SPATIAL), mem_cache.dtype)
     anywhere = pl.BlockSpec(memory_space=pl.ANY)
-    scalars = pl.BlockSpec(memory_space=pltpu.SMEM)
+    held = pl.BlockSpec(memory_space=pltpu.HBM)
     return pl.pallas_call(
-        pack_kernel,
-        out_shape=(piece,) * 4 + (half,) * 2,
-        in_specs=[scalars, scalars] + [anywhere] * 4,
-        out_specs=(anywhere,) * 6,
+        pack_memory_kernel,
+        out_shape=(half,) * 2,
+        in_specs=[held] * 3,
+        out_specs=(anywhere,) * 2,
         scratch_shapes=[
-            pltpu.VMEM((3, shard_rows, features), w_query.dtype),
+            pltpu.SMEM(intersection.shape, intersection.dtype),
+            pltpu.SMEM(slot_of.shape, slot_of.dtype),
             pltpu.VMEM((frames * entries, 2, features), mem_cache.dtype),
-            pltpu.SemaphoreType.DMA((3,)),
+            pltpu.SemaphoreType.DMA((2,)),
             pltpu.SemaphoreType.DMA((frames * entries,)),
-            pltpu.SemaphoreType.DMA((4,)),
             pltpu.SemaphoreType.DMA((devices,)),
         ],
-        compiler_params=pltpu.CompilerParams(vmem_limit_bytes=VMEM_LIMIT),
-        name="pack",
-    )(intersection, slot_of, w_query, w_key, w_value, mem_cache)
+        name="pack_memory",
+    )(intersection, slot_of, mem_cache)
 
 
 def all_pieces(own, beside, even, odd):
     planes = lax.axis_size("frame") // 4
-    found = []
-    for bits in sorted(range(1, planes), key=lambda value: (-value.bit_length(), value)):
-        direct = moved(even if bits % 2 == 0 else odd, lambda x, p, y, c, bits=bits: (x, p ^ bits, y ^ x, c))
-        found.append((direct, (bits, 0, True)))
-    near = moved(beside, lambda x, p, y, c: (x, p, 1 - y, c))
-    pieces = [(own, (0, 0, False)), (near, (0, 1, False))]
-    for direct, (bits, _, _) in found:
-        pieces.append((direct, (bits, 0, True)))
-        pieces.append((moved(direct, lambda x, p, y, c: (1 - x, p, y, c)), (bits, 1, True)))
-    places = [(array, place + (0,)) for array, place in pieces]
-    places += [(moved(array, lambda x, p, y, c: (x, p, y, 1 - c)), place + (1,)) for array, place in pieces]
+    pieces = [("own", own, (0, 0, False))]
+    pieces.append(("near", moved(beside, lambda x, p, y, c: (x, p, 1 - y, c)), (0, 1, False)))
+    for bits in range(1, planes):
+        name = f"plane{bits}"
+        sent = even if bits % 2 == 0 else odd
+        direct = moved(sent, lambda x, p, y, c, bits=bits: (x, p ^ bits, y ^ x ^ c, c))
+        pieces.append((name, direct, (bits, 0, True)))
+        name = f"cross{bits}"
+        pieces.append((name, moved(direct, lambda x, p, y, c: (1 - x, p, y, c)), (bits, 1, True)))
+    places = [(array, place + (0,)) for _, array, place in pieces]
+    for name, array, place in pieces:
+        places.append((moved(array, lambda x, p, y, c: (x, p, y, 1 - c)), place + (1,)))
     return places
 
 
@@ -180,17 +217,26 @@
 
 def step_kernel(places, updates, last, head_count, *refs):
     refs = list(refs)
-    count_ref, scale_ref, gain_ref, key_ref, value_ref = refs[:5]
+    count_hbm, scale_hbm, gain_ref, key_ref, value_ref = refs[:5]
     token_refs = refs[5:9]
     piece_refs = refs[9 : 9 + len(places)]
     update_refs = refs[9 + len(places) : 9 + len(places) + len(updates)]
-    outs = refs[9 + len(places) + len(updates) : -8]
-    current, normed, weights, parts, attended, token_sem, piece_sem, update_sem = refs[-8:]
+    outs = refs[9 + len(places) + len(updates) : -11]
+    current, normed, weights, parts, attended, count_ref, scale_ref, token_sem, piece_sem, update_sem, scalar_sem = (
+        refs[-11:]
+    )
     x, _, plane, y, c = here()
     low = plane % 2
     chip_rows = token_refs[0].shape[0]
     width = parts.shape[2]
     at_home = low == c
+
+    scalar_copies = (
+        pltpu.make_async_copy(count_hbm, count_ref, scalar_sem.at[0]),
+        pltpu.make_async_copy(scale_hbm, scale_ref, scalar_sem.at[1]),
+    )
+    for copy in scalar_copies:
+        copy.start()
 
     def token_copies(first, second):
         return (
@@ -215,10 +261,10 @@
     piece_copies = []
     shard_rows = piece_refs[0].shape[1]
     for number, (ref, (plane_bits, y_bits, with_x, c_bits)) in enumerate(zip(piece_refs, places)):
-        from_y = flipped(y, y_bits)
+        from_y, from_c = flipped(y, y_bits), flipped(c, c_bits)
         if with_x:
-            from_y = from_y + x - 2 * x * from_y
-        shard = flipped(plane, plane_bits) * 4 + from_y * 2 + flipped(c, c_bits)
+            from_y = joined_bits(joined_bits(from_y, x), from_c)
+        shard = flipped(plane, plane_bits) * 4 + from_y * 2 + from_c
         start = pl.multiple_of(shard * shard_rows, 16)
         piece_copies.append(
             pltpu.make_async_copy(ref, weights.at[:, pl.ds(start, shard_rows), :], piece_sem.at[number])
@@ -227,6 +273,8 @@
     for copy in token_copies(token_refs[0], token_refs[1]):
         copy.wait()
     for copy in update_copies:
+        copy.wait()
+    for copy in scalar_copies:
         copy.wait()
     for number, (plane_bits, y_bits) in enumerate(updates):
         quarter = quarter_of(flipped(plane, plane_bits), flipped(y, y_bits))
@@ -302,7 +350,7 @@
 
 
 def step(pieces, updates, last, counts, scales, norm_gain, keys, values, tokens):
-    shard_rows, width = pieces[0][0].shape[1:]
+    _, width = pieces[0][0].shape[1:]
     features = norm_gain.shape[0]
     chip_rows = tokens[0].shape[0]
     frame_rows = 2 * chip_rows
@@ -316,13 +364,13 @@
     else:
         out_shape = (jax.ShapeDtypeStruct((frame_rows, width), dtype),)
     anywhere = pl.BlockSpec(memory_space=pl.ANY)
-    scalars = pl.BlockSpec(memory_space=pltpu.SMEM)
+    held = pl.BlockSpec(memory_space=pltpu.HBM)
     vectors = pl.BlockSpec(memory_space=pltpu.VMEM)
     flops = 2 * frame_rows * width * (3 * features + 2 * (frame_rows + keys.shape[0]))
     return pl.pallas_call(
         kernel,
         out_shape=out_shape,
-        in_specs=[scalars, scalars, vectors, vectors, vectors] + [anywhere] * (4 + len(pieces) + len(updates)),
+        in_specs=[held, held, vectors, vectors, vectors] + [anywhere] * (4 + len(pieces) + len(updates)),
         out_specs=tuple(vectors for _ in out_shape),
         scratch_shapes=[
             pltpu.VMEM((frame_rows, features), dtype),
@@ -330,9 +378,12 @@
             pltpu.VMEM((3, features, width), jnp.bfloat16),
             pltpu.VMEM((max(len(updates), 1), frame_rows, width), dtype),
             pltpu.VMEM((frame_rows, width), dtype),
+            pltpu.SMEM(counts.shape, counts.dtype),
+            pltpu.SMEM(scales.shape, scales.dtype),
             pltpu.SemaphoreType.DMA((2,)),
             pltpu.SemaphoreType.DMA((len(pieces),)),
             pltpu.SemaphoreType.DMA((max(len(updates), 1),)),
+            pltpu.SemaphoreType.DMA((2,)),
         ],
         compiler_params=pltpu.CompilerParams(vmem_limit_bytes=VMEM_LIMIT),
         cost_estimate=pl.CostEstimate(
@@ -351,47 +402,48 @@
     )
 
 
-def join_kernel(keep, first, second, third, fourth, out):
+def join_kernel(keep, first, second, third, fourth, out, sem):
     _, _, plane, y, c = here()
     low = plane % 2
     width = keep.shape[1]
 
-    def put(ref, plane_low, at_y):
-        out[:, columns(plane_low * 2 + at_y, width)] = ref[...]
+    def put(number, ref, plane_low, at_y):
+        return pltpu.make_async_copy(ref, out.at[:, columns(plane_low * 2 + at_y, width)], sem.at[number])
 
     @pl.when(low == c)
     def _():
-        put(keep, low, y)
-        put(first, low, 1 - y)
-        put(second, 1 - low, y)
-        put(third, 1 - low, 1 - y)
+        put(0, keep, low, y).start()
+        put(1, first, low, 1 - y).start()
+        put(2, second, 1 - low, y).start()
+        put(3, third, 1 - low, 1 - y).start()
 
     @pl.when(low != c)
     def _():
-        put(first, 1 - low, y)
-        put(second, low, 1 - y)
-        put(third, low, y)
-        put(fourth, 1 - low, 1 - y)
+        put(0, first, 1 - low, y).start()
+        put(1, second, low, 1 - y).start()
+        put(2, third, low, y).start()
+        put(3, fourth, 1 - low, 1 - y).start()
+
+    for number in range(4):
+        put(number, first, number // 2, number % 2).wait()
 
 
 def joined(keep, first, second, third, fourth):
-    at_home = lambda p, c: c == p % 2
-    first = moved(
-        first, lambda x, p, y, c: (x, p, 1 - y, c) if at_home(p, c) else (x, p ^ 1, y, 1 - c)
-    )
-    second = moved(
-        second, lambda x, p, y, c: (x, p, 1 - y, 1 - c) if at_home(p, c) else (x, p ^ 1, y, c)
-    )
-    third = moved(
-        third, lambda x, p, y, c: (x, p, y, 1 - c) if at_home(p, c) else (x, p ^ 1, 1 - y, c)
-    )
-    fourth = moved(
-        fourth, lambda x, p, y, c: None if at_home(p, c) else (x, p ^ 1, 1 - y, 1 - c)
-    )
+    def at_home(p, c):
+        return c == p % 2
+
+    first = moved(first, lambda x, p, y, c: (x, p, 1 - y, c) if at_home(p, c) else (x, p ^ 1, y, 1 - c))
+    second = moved(second, lambda x, p, y, c: (x, p, 1 - y, 1 - c) if at_home(p, c) else (x, p ^ 1, y, c))
+    third = moved(third, lambda x, p, y, c: (x, p, y, 1 - c) if at_home(p, c) else (x, p ^ 1, 1 - y, c))
+    fourth = moved(fourth, lambda x, p, y, c: None if at_home(p, c) else (x, p ^ 1, 1 - y, 1 - c))
     rows, width = keep.shape
+    anywhere = pl.BlockSpec(memory_space=pl.ANY)
     return pl.pallas_call(
         join_kernel,
         out_shape=jax.ShapeDtypeStruct((rows, width * SPATIAL), keep.dtype),
+        in_specs=[anywhere] * 5,
+        out_specs=anywhere,
+        scratch_shapes=[pltpu.SemaphoreType.DMA((4,))],
         name="join",
     )(keep, first, second, third, fourth)
 
@@ -399,10 +451,9 @@
 def paired_planes(
     latent, norm_gain, w_query, w_key, w_value, mem_cache, intersection, counts, slot_of, step_scale
 ):
-    own, beside, even, odd, kept, sent = pack(w_query, w_key, w_value, mem_cache, intersection, slot_of)
-    pieces = all_pieces(own, beside, even, odd)
+    pieces = all_pieces(*pack_weights(w_query, w_key, w_value))
     tokens = all_tokens(latent)
-    keys, values = all_memory(kept, sent)
+    keys, values = all_memory(*pack_memory(mem_cache, intersection, slot_of))
     (attended,) = step(pieces, [], False, counts, step_scale, norm_gain, keys, values, tokens)
     updates = [
         (attended, (0, 0)),

time: 104 us -> 105 us (level)
  Pallas kernels: 16.5 us -> 23.9 us
  local copies, waits for them, and re-layouts: 7.37 us -> 2.02 us
  starting transfers between devices: 46.5 us -> 42.6 us
  waiting for transfers between devices: 32.3 us -> 34.4 us
    ppermute x26, starting transfers between devices: 45.5 us -> 39.6 us  [moved(): return lax.ppermute(array, AXES, pairs)]
    ppermute x4, waiting for transfers between devices: 12.7 us -> 18.4 us  [hop(): lax.ppermute(array, 'frame', [(i, i ^ 1 << bit) for i in range(lax.axis_s...]
    pallas_call x1, Pallas kernels: 1.59 us -> 7.09 us  [joined(): pl.pallas_call(join_kernel, out_shape=jax.ShapeDtypeStruct((rows, width *...]
    unnamed x34 -> x28, local copies, waits for them, and re-layouts: 7.35 us -> 2 us
    ppermute x26, waiting for transfers between devices: 19.6 us -> 16 us  [moved(): return lax.ppermute(array, AXES, pairs)]
    ppermute x4, starting transfers between devices: 0.96 us -> 2.93 us  [hop(): lax.ppermute(array, 'frame', [(i, i ^ 1 << bit) for i in range(lax.axis_s...]
    pallas_call x3 -> x4, Pallas kernels: 14.9 us -> 16.8 us  [the longest x2 11.6 us: step(): pl.pallas_call(kernel, out_shape=out_shape, in_specs=[held, held, vectors...]
  transfers between devices with their start and end apart: 30 -> 30, of which waited for: 11 -> 11; matrix products, arithmetic and copies ran while one was open for 1% -> 1% of each run, Pallas kernels for 0% -> 2%
where the time goes in v2:
time: 105 us; the launch traced here: 104 us
  starting transfers between devices  42.6 us (41%)
  waiting for transfers between devices  34.4 us (33%)
  Pallas kernels  23.9 us (23%)
  local copies, waits for them, and re-layouts  2.02 us (2%)
  other arithmetic  1.12 us (1%)
    ppermute x26, starting transfers between devices, moved(): return lax.ppermute(array, AXES, pairs)  39.6 us
    ppermute x4, waiting for transfers between devices, hop(): lax.ppermute(array, 'frame', [(i, i ^ 1 << bit) for i in range(lax.axis_s...  18.4 us
    ppermute x26, waiting for transfers between devices, moved(): return lax.ppermute(array, AXES, pairs)  16 us
    pallas_call x2, Pallas kernels, step(): pl.pallas_call(kernel, out_shape=out_shape, in_specs=[held, held, vectors...  11.6 us
    pallas_call x1, Pallas kernels, joined(): pl.pallas_call(join_kernel, out_shape=jax.ShapeDtypeStruct((rows, width *...  7.09 us
    pallas_call x1, Pallas kernels, pack_memory(): pl.pallas_call(pack_memory_kernel, out_shape=(half,) * 2, in_specs=[held]...  2.98 us
    ppermute x4, starting transfers between devices, hop(): lax.ppermute(array, 'frame', [(i, i ^ 1 << bit) for i in range(lax.axis_s...  2.93 us
    pallas_call x1, Pallas kernels, pack_weights(): pl.pallas_call(pack_weights_kernel, out_shape=(piece,) * 4, in_specs=[hel...  2.17 us
  transfers between devices with their start and end apart: 30, of which 11 were waited for; matrix products, arithmetic and copies ran while one was open for 1% of the time, Pallas kernels for 2%

profile of v2, /device:TPU:1, one launch (start us, length us, event | category | flops | bytes accessed | tf_op | source)
XLA Modules:
  0.0 104.3 jit_solution(15091306573817677812)
XLA Ops:
  0.0 3.0 %pack_memory.1 = (bf16[8,8,2,384]{3,2,1,0:T(2,128)(2,1)}, bf16[8,8,2,384]{3,2,1,0:T(2,128)(2,1)}) custom-call(s32[4,8]{1,0:T(4,128)} %list_hbm.1, s32[128]{0:T(128)} %slot_hbm.1, bf16[128,1,2,1536]{3,2,1,0:T(2,128)(2,1)} %mem_ref.1), custom_call_target="tpu_custom_call" | custom-call | tf_op jit(solution)/shard_map/pack_memory/pallas_call | solution.py:161
  3.0 0.1 collective-permute-start
  3.1 2.2 %pack_weights.1 = (bf16[3,96,384]{2,1,0:T(8,128)(2,1)}, bf16[3,96,384]{2,1,0:T(8,128)(2,1)}, bf16[3,96,384]{2,1,0:T(8,128)(2,1)}, bf16[3,96,384]{2,1,0:T(8,128)(2,1)}) custom-call(bf16[96,1536]{1,0:T(8,128)(2,1)} %w_query.1, bf16[96,1536]{1,0:T(8,128)(2,1)} %w_key.1, bf16[96,1536]{1,0:T(8,128)(2,1)} %w_value.1), custom_call_target="tpu_custom_call" | custom-call | tf_op jit(solution)/shard_map/pack_weights/pallas_call | solution.py:94
  5.3 5.8 %collective-permute-start.13 = (bf16[3,96,384]{2,1,0:T(8,128)(2,1)}, bf16[3,96,384]{2,1,0:T(8,128)(2,1)S(1)}, u32[]{:S(2)}, u32[]{:S(2)}) collective-permute-start(bf16[3,96,384]{2,1,0:T(8,128)(2,1)} %get-tuple-element.20), channel_id=1, source_target_pairs={{0,12},{1,15},{2,14},{3,13},{4,8},{5,11},{6,10},{7,9},{8,4},{9,7},... | collective-permute-start | bytes 663560 | tf_op jit(solution)/shard_map/ppermute | solution.py:37
  11.1 1.3 %collective-permute-start.4 = (bf16[64,1536]{1,0:T(8,128)(2,1)S(1)}, bf16[64,1536]{1,0:T(8,128)(2,1)S(1)}, u32[]{:S(2)}, u32[]{:S(2)}) collective-permute-start(bf16[64,1536]{1,0:T(8,128)(2,1)S(1)} %copy-done.5), channel_id=1, source_target_pairs={{1,0},{3,2},{4,5},{6,7},{9,8},{11,10},{12,13},{14,15},{17,16},{19,... | collective-permute-start | bytes 589832 | tf_op jit(solution)/shard_map/ppermute | solution.py:37
  12.4 1.3 %collective-permute-start.8 = (bf16[3,96,384]{2,1,0:T(8,128)(2,1)}, bf16[3,96,384]{2,1,0:T(8,128)(2,1)S(1)}, u32[]{:S(2)}, u32[]{:S(2)}) collective-permute-start(bf16[3,96,384]{2,1,0:T(8,128)(2,1)} %get-tuple-element.19), channel_id=1, source_target_pairs={{0,2},{1,3},{2,0},{3,1},{4,6},{5,7},{6,4},{7,5},{8,10},{9,11},{10,... | collective-permute-start | bytes 663560 | tf_op jit(solution)/shard_map/ppermute | solution.py:37
  13.7 0.3 fusion.2
  14.0 0.3 collective-permute-start.1
  14.3 10.9 %collective-permute-done.1 = bf16[2,4,8,2,384]{4,3,2,1,0:T(2,128)(2,1)S(1)} collective-permute-done((bf16[2,4,8,2,384]{4,3,2,1,0:T(2,128)(2,1)S(1)}, bf16[2,4,8,2,384]{4,3,2,1,0:T(2,128)(2,1)S(1)}, u32[]{:S(2)}, u32[]{:S(2)}) %collective-permute-start.1) | collective-permute-done | bytes 98336 | tf_op jit(solution)/shard_map/ppermute | solution.py:206
  25.1 2.1 %collective-permute-start.11 = (bf16[3,96,384]{2,1,0:T(8,128)(2,1)S(1)}, bf16[3,96,384]{2,1,0:T(8,128)(2,1)S(1)}, u32[]{:S(2)}, u32[]{:S(2)}) collective-permute-start(bf16[3,96,384]{2,1,0:T(8,128)(2,1)S(1)} %copy-done.12), channel_id=1, source_target_pairs={{0,8},{1,11},{2,10},{3,9},{4,12},{5,15},{6,14},{7,13},{8,0},{9,3},... | collective-permute-start | bytes 663560 | tf_op jit(solution)/shard_map/ppermute | solution.py:37
  27.3 0.3 fusion.1
  27.6 0.6 collective-permute-start.2
  28.3 5.6 %collective-permute-done.2 = bf16[4,2,8,2,384]{4,3,2,1,0:T(2,128)(2,1)S(1)} collective-permute-done((bf16[4,2,8,2,384]{4,3,2,1,0:T(2,128)(2,1)S(1)}, bf16[4,2,8,2,384]{4,3,2,1,0:T(2,128)(2,1)S(1)}, u32[]{:S(2)}, u32[]{:S(2)}) %collective-permute-start.2) | collective-permute-done | bytes 98336 | tf_op jit(solution)/shard_map/ppermute | solution.py:206
  33.9 1.3 %collective-permute-start.6 = (bf16[128,1536]{1,0:T(8,128)(2,1)S(1)}, bf16[128,1536]{1,0:T(8,128)(2,1)S(1)}, u32[]{:S(2)}, u32[]{:S(2)}) collective-permute-start(bf16[128,1536]{1,0:T(8,128)(2,1)S(1)} %constant_dynamic-update-slice_fusion.refs_5_), channel_id=1, source_target_pairs={{0,4},{2,6},{5,1},{7,3},{8,12},{10,14},{13,9},{15,11},{16,20},{18,... | collective-permute-start | bytes 1179656 | tf_op jit(solution)/shard_map/ppermute | solution.py:37
  35.2 0.3 fusion
  35.5 2.5 %collective-permute-done.11.refs_13_ = bf16[3,96,384]{2,1,0:T(8,128)(2,1)S(1)} collective-permute-done((bf16[3,96,384]{2,1,0:T(8,128)(2,1)S(1)}, bf16[3,96,384]{2,1,0:T(8,128)(2,1)S(1)}, u32[]{:S(2)}, u32[]{:S(2)}) %collective-permute-start.11) | collective-permute-done | bytes 221216 | tf_op jit(solution)/shard_map/ppermute | solution.py:37
  38.0 1.9 %collective-permute-start.3 = (bf16[8,1,8,2,384]{4,3,2,1,0:T(2,128)(2,1)S(1)}, bf16[8,1,8,2,384]{4,3,2,1,0:T(2,128)(2,1)S(1)}, u32[]{:S(2)}, u32[]{:S(2)}) collective-permute-start(bf16[8,1,8,2,384]{4,3,2,1,0:T(2,128)(2,1)S(1)} %get-tuple-element.30), channel_id=1, source_target_pairs={{0,8},{1,9},{2,10},{3,11},{4,12},{5,13},{6,14},{7,15},{8,0},{9,1},... | collective-permute-start | bytes 294920 | tf_op jit(solution)/shard_map/ppermute | solution.py:206
  39.9 1.2 %collective-permute-start.16 = (bf16[3,96,384]{2,1,0:T(8,128)(2,1)S(1)}, bf16[3,96,384]{2,1,0:T(8,128)(2,1)S(1)}, u32[]{:S(2)}, u32[]{:S(2)}) collective-permute-start(bf16[3,96,384]{2,1,0:T(8,128)(2,1)S(1)} %collective-permute-done.8.refs_10_), channel_id=1, source_target_pairs={{0,1},{1,0},{2,3},{3,2},{4,5},{5,4},{6,7},{7,6},{8,9},{9,8},{10,11... | collective-permute-start | bytes 663560 | tf_op jit(solution)/shard_map/ppermute | solution.py:37
  41.1 0.8 collective-permute-start.12
  42.0 2.0 %collective-permute-done.3 = bf16[8,1,8,2,384]{4,3,2,1,0:T(2,128)(2,1)S(1)} collective-permute-done((bf16[8,1,8,2,384]{4,3,2,1,0:T(2,128)(2,1)S(1)}, bf16[8,1,8,2,384]{4,3,2,1,0:T(2,128)(2,1)S(1)}, u32[]{:S(2)}, u32[]{:S(2)}) %collective-permute-start.3) | collective-permute-done | bytes 98336 | tf_op jit(solution)/shard_map/ppermute | solution.py:206
  44.0 1.3 %collective-permute-start.21 = (bf16[3,96,384]{2,1,0:T(8,128)(2,1)S(1)}, bf16[3,96,384]{2,1,0:T(8,128)(2,1)S(1)}, u32[]{:S(2)}, u32[]{:S(2)}) collective-permute-start(bf16[3,96,384]{2,1,0:T(8,128)(2,1)S(1)} %collective-permute-done.13.refs_15_), channel_id=1, source_target_pairs={{0,1},{1,0},{2,3},{3,2},{4,5},{5,4},{6,7},{7,6},{8,9},{9,8},{10,11... | collective-permute-start | bytes 663560 | tf_op jit(solution)/shard_map/ppermute | solution.py:37
  45.3 2.8 %collective-permute-start.14 = (bf16[3,96,384]{2,1,0:T(8,128)(2,1)S(1)}, bf16[3,96,384]{2,1,0:T(8,128)(2,1)S(1)}, u32[]{:S(2)}, u32[]{:S(2)}) collective-permute-start(bf16[3,96,384]{2,1,0:T(8,128)(2,1)S(1)} %collective-permute-done.13.refs_15_), channel_id=1, source_target_pairs={{0,16},{1,17},{2,18},{3,19},{4,20},{5,21},{6,22},{7,23},{8,24},{9,... | collective-permute-start | bytes 663560 | tf_op jit(solution)/shard_map/ppermute | solution.py:37
  48.1 0.3 collective-permute-start.17
  48.4 0.1 collective-permute-start.10
  48.5 0.7 collective-permute-start.5
  49.2 5.5 %collective-permute-start.7 = (bf16[128,1536]{1,0:T(8,128)(2,1)S(1)}, bf16[128,1536]{1,0:T(8,128)(2,1)S(1)}, u32[]{:S(2)}, u32[]{:S(2)}) collective-permute-start(bf16[128,1536]{1,0:T(8,128)(2,1)S(1)} %collective-permute-done.6.refs_7_), channel_id=1, source_target_pairs={{1,3},{3,1},{4,6},{6,4},{9,11},{11,9},{12,14},{14,12},{17,19},{19,... | collective-permute-start | bytes 1179656 | tf_op jit(solution)/shard_map/ppermute | solution.py:37
  54.7 0.3 pad_maximum_fusion
  55.1 2.3 %collective-permute-start.20 = (bf16[3,96,384]{2,1,0:T(8,128)(2,1)S(1)}, bf16[3,96,384]{2,1,0:T(8,128)(2,1)S(1)}, u32[]{:S(2)}, u32[]{:S(2)}) collective-permute-start(bf16[3,96,384]{2,1,0:T(8,128)(2,1)S(1)} %collective-permute-done.12.refs_14_), channel_id=1, source_target_pairs={{0,1},{1,0},{2,3},{3,2},{4,5},{5,4},{6,7},{7,6},{8,9},{9,8},{10,11... | collective-permute-start | bytes 663560 | tf_op jit(solution)/shard_map/ppermute | solution.py:37
  57.3 0.1 collective-permute-start.22
  57.4 1.2 %collective-permute-done.10.refs_12_ = bf16[3,96,384]{2,1,0:T(8,128)(2,1)S(1)} collective-permute-done((bf16[3,96,384]{2,1,0:T(8,128)(2,1)S(1)}, bf16[3,96,384]{2,1,0:T(8,128)(2,1)S(1)}, u32[]{:S(2)}, u32[]{:S(2)}) %collective-permute-start.10) | collective-permute-done | bytes 221216 | tf_op jit(solution)/shard_map/ppermute | solution.py:37
  58.6 0.6 collective-permute-start.18
  59.3 1.0 collective-permute-done.18.refs_20_
  60.3 2.7 %collective-permute-done.7.refs_8_ = bf16[128,1536]{1,0:T(8,128)(2,1)S(1)} collective-permute-done((bf16[128,1536]{1,0:T(8,128)(2,1)S(1)}, bf16[128,1536]{1,0:T(8,128)(2,1)S(1)}, u32[]{:S(2)}, u32[]{:S(2)}) %collective-permute-start.7) | collective-permute-done | bytes 393248 | tf_op jit(solution)/shard_map/ppermute | solution.py:37
  63.0 0.7 copy-done.3
  63.7 5.2 %step.1.refs_25_ = bf16[256,384]{1,0:T(8,128)(2,1)S(1)} custom-call(s32[4]{0:T(128)S(1)} %copy-done.3, f32[2]{0:T(128)S(1)} %copy-done.4, f32[1,1536]{1,0:T(1,128)S(1)} %reshape.4.refs_2_, bf16[128,384]{1,0:T(8,128)(2,1)S(1)} %get-tuple-element.36.refs_3_, bf16[128,384]{1,0:T(8,128)(2,1)S(1)} %get-tuple-element.35.refs_4_, ...), custom_call_target="tpu_custom_call" | custom-call | flops 1056964608 | bytes 6291456 | tf_op jit(solution)/shard_map/step/pallas_call | solution.py:370
  68.9 1.2 %collective-permute-start.25 = (bf16[256,384]{1,0:T(8,128)(2,1)S(1)}, bf16[256,384]{1,0:T(8,128)(2,1)S(1)}, u32[]{:S(2)}, u32[]{:S(2)}) collective-permute-start(bf16[256,384]{1,0:T(8,128)(2,1)S(1)} %step.1.refs_25_), channel_id=1, source_target_pairs={{0,2},{1,3},{2,0},{3,1},{4,6},{5,7},{6,4},{7,5},{8,10},{9,11},{10,... | collective-permute-start | bytes 589832 | tf_op jit(solution)/shard_map/ppermute | solution.py:37
  70.1 1.5 %collective-permute-start.23 = (bf16[256,384]{1,0:T(8,128)(2,1)S(1)}, bf16[256,384]{1,0:T(8,128)(2,1)S(1)}, u32[]{:S(2)}, u32[]{:S(2)}) collective-permute-start(bf16[256,384]{1,0:T(8,128)(2,1)S(1)} %step.1.refs_25_), channel_id=1, source_target_pairs={{0,6},{1,7},{2,4},{3,5},{4,2},{5,3},{6,0},{7,1},{8,14},{9,15},{10,... | collective-permute-start | bytes 589832 | tf_op jit(solution)/shard_map/ppermute | solution.py:37
  71.6 1.9 %collective-permute-done.25.refs_28_ = bf16[256,384]{1,0:T(8,128)(2,1)S(1)} collective-permute-done((bf16[256,384]{1,0:T(8,128)(2,1)S(1)}, bf16[256,384]{1,0:T(8,128)(2,1)S(1)}, u32[]{:S(2)}, u32[]{:S(2)}) %collective-permute-start.25) | collective-permute-done | bytes 196640 | tf_op jit(solution)/shard_map/ppermute | solution.py:37
  73.5 1.5 %collective-permute-done.24.refs_27_ = bf16[256,384]{1,0:T(8,128)(2,1)S(1)} collective-permute-done((bf16[256,384]{1,0:T(8,128)(2,1)S(1)}, bf16[256,384]{1,0:T(8,128)(2,1)S(1)}, u32[]{:S(2)}, u32[]{:S(2)}) %collective-permute-start.24) | collective-permute-done | bytes 196640 | tf_op jit(solution)/shard_map/ppermute | solution.py:37
  74.9 3.4 %collective-permute-done.23.refs_26_ = bf16[256,384]{1,0:T(8,128)(2,1)S(1)} collective-permute-done((bf16[256,384]{1,0:T(8,128)(2,1)S(1)}, bf16[256,384]{1,0:T(8,128)(2,1)S(1)}, u32[]{:S(2)}, u32[]{:S(2)}) %collective-permute-start.23) | collective-permute-done | bytes 196640 | tf_op jit(solution)/shard_map/ppermute | solution.py:37
  78.4 6.5 %last_step.1 = (bf16[64,384]{1,0:T(8,128)(2,1)S(1)}, bf16[64,384]{1,0:T(8,128)(2,1)S(1)}, bf16[64,384]{1,0:T(8,128)(2,1)S(1)}, bf16[64,384]{1,0:T(8,128)(2,1)S(1)}, bf16[64,384]{1,0:T(8,128)(2,1)S(1)}) custom-call(s32[4]{0:T(128)S(1)} %copy-done.3, f32[2]{0:T(128)S(1)} %copy-done.4, f32[1,1536]{1,0:T(1,128)S(1)} %reshape.4.refs_2_, ...), custom_call_target="tpu_custom_call" | custom-call | flops 1056964608 | bytes 6291456 | tf_op jit(solution)/shard_map/last_step/pallas_call | solution.py:370
  84.9 0.6 copy-done.2
  85.5 3.4 %collective-permute-start.26 = (bf16[64,384]{1,0:T(8,128)(2,1)S(1)}, bf16[64,384]{1,0:T(8,128)(2,1)S(1)}, u32[]{:S(2)}, u32[]{:S(2)}) collective-permute-start(bf16[64,384]{1,0:T(8,128)(2,1)S(1)} %get-tuple-element.23), channel_id=1, source_target_pairs={{0,2},{1,4},{2,0},{3,6},{4,1},{5,7},{6,3},{7,5},{8,10},{9,12},{10,... | collective-permute-start | bytes 147464 | tf_op jit(solution)/shard_map/ppermute | solution.py:37
  88.8 1.2 %collective-permute-start.28 = (bf16[64,384]{1,0:T(8,128)(2,1)S(1)}, bf16[64,384]{1,0:T(8,128)(2,1)S(1)}, u32[]{:S(2)}, u32[]{:S(2)}) collective-permute-start(bf16[64,384]{1,0:T(8,128)(2,1)S(1)} %get-tuple-element.25), channel_id=1, source_target_pairs={{0,1},{1,7},{2,3},{3,5},{4,2},{5,4},{6,0},{7,6},{8,9},{9,15},{10,1... | collective-permute-start | bytes 147464 | tf_op jit(solution)/shard_map/ppermute | solution.py:37
  90.0 4.8 %collective-permute-start.29 = (bf16[64,384]{1,0:T(8,128)(2,1)S(1)}, bf16[64,384]{1,0:T(8,128)(2,1)S(1)}, u32[]{:S(2)}, u32[]{:S(2)}) collective-permute-start(bf16[64,384]{1,0:T(8,128)(2,1)S(1)} %get-tuple-element.26), channel_id=1, source_target_pairs={{1,6},{3,4},{4,3},{6,1},{9,14},{11,12},{12,11},{14,9},{17,22},{19,... | collective-permute-start | bytes 147464 | tf_op jit(solution)/shard_map/ppermute | solution.py:37
  94.9 1.7 %collective-permute-done.29.fourth = bf16[64,384]{1,0:T(8,128)(2,1)S(1)} collective-permute-done((bf16[64,384]{1,0:T(8,128)(2,1)S(1)}, bf16[64,384]{1,0:T(8,128)(2,1)S(1)}, u32[]{:S(2)}, u32[]{:S(2)}) %collective-permute-start.29) | collective-permute-done | bytes 49184 | tf_op jit(solution)/shard_map/ppermute | solution.py:37
  96.6 0.6 copy-done.10
  97.2 7.1 %join.1 = bf16[64,1536]{1,0:T(8,128)(2,1)} custom-call(bf16[64,384]{1,0:T(8,128)(2,1)} %copy-done.2, bf16[64,384]{1,0:T(8,128)(2,1)} %copy-done.7, bf16[64,384]{1,0:T(8,128)(2,1)} %copy-done.8, bf16[64,384]{1,0:T(8,128)(2,1)} %copy-done.9, bf16[64,384]{1,0:T(8,128)(2,1)} %copy-done.10), custom_call_target="tpu_custom_call" | custom-call | tf_op jit(solution)/shard_map/join/pallas_call | solution.py:441
  (51 shorter events, 0.4 us)
Async XLA Ops:
  3.0 8.1 %copy-start.5 = (bf16[64,1536]{1,0:T(8,128)(2,1)S(1)}, bf16[64,1536]{1,0:T(8,128)(2,1)}, u32[]{:S(2)}) copy-start(bf16[64,1536]{1,0:T(8,128)(2,1)} %param.10) | copy-start | bytes 589828
  3.0 10.7 %copy-start.6 = (bf16[8,8,2,384]{3,2,1,0:T(2,128)(2,1)S(1)}, bf16[8,8,2,384]{3,2,1,0:T(2,128)(2,1)}, u32[]{:S(2)}) copy-start(bf16[8,8,2,384]{3,2,1,0:T(2,128)(2,1)} %get-tuple-element.16) | copy-start | bytes 294916
  3.0 10.6 %collective-permute-start = (bf16[8,8,2,384]{3,2,1,0:T(2,128)(2,1)}, bf16[8,8,2,384]{3,2,1,0:T(2,128)(2,1)S(1)}, u32[]{:S(2)}, u32[]{:S(2)}) collective-permute-start(bf16[8,8,2,384]{3,2,1,0:T(2,128)(2,1)} %get-tuple-element.17), channel_id=1, source_target_pairs={{0,1},{1,0},{2,3},{3,2},{4,5},{5,4},{6,7},{7,6},{8,9},{9,8},{10,11... | collective-permute-start | bytes 294920 | tf_op jit(solution)/shard_map/ppermute | solution.py:206
  5.3 34.6 %collective-permute-start.13 = (bf16[3,96,384]{2,1,0:T(8,128)(2,1)}, bf16[3,96,384]{2,1,0:T(8,128)(2,1)S(1)}, u32[]{:S(2)}, u32[]{:S(2)}) collective-permute-start(bf16[3,96,384]{2,1,0:T(8,128)(2,1)} %get-tuple-element.20), channel_id=1, source_target_pairs={{0,12},{1,15},{2,14},{3,13},{4,8},{5,11},{6,10},{7,9},{8,4},{9,7},... | collective-permute-start | bytes 663560 | tf_op jit(solution)/shard_map/ppermute | solution.py:37
  11.1 30.0 %collective-permute-start.9 = (bf16[3,96,384]{2,1,0:T(8,128)(2,1)}, bf16[3,96,384]{2,1,0:T(8,128)(2,1)S(1)}, u32[]{:S(2)}, u32[]{:S(2)}) collective-permute-start(bf16[3,96,384]{2,1,0:T(8,128)(2,1)} %get-tuple-element.20), channel_id=1, source_target_pairs={{0,4},{1,7},{2,6},{3,5},{4,0},{5,3},{6,2},{7,1},{8,12},{9,15},{10,... | collective-permute-start | bytes 663560 | tf_op jit(solution)/shard_map/ppermute | solution.py:37
  11.1 16.5 %collective-permute-start.4 = (bf16[64,1536]{1,0:T(8,128)(2,1)S(1)}, bf16[64,1536]{1,0:T(8,128)(2,1)S(1)}, u32[]{:S(2)}, u32[]{:S(2)}) collective-permute-start(bf16[64,1536]{1,0:T(8,128)(2,1)S(1)} %copy-done.5), channel_id=1, source_target_pairs={{1,0},{3,2},{4,5},{6,7},{9,8},{11,10},{12,13},{14,15},{17,16},{19,... | collective-permute-start | bytes 589832 | tf_op jit(solution)/shard_map/ppermute | solution.py:37
  12.4 15.3 %collective-permute-start.8 = (bf16[3,96,384]{2,1,0:T(8,128)(2,1)}, bf16[3,96,384]{2,1,0:T(8,128)(2,1)S(1)}, u32[]{:S(2)}, u32[]{:S(2)}) collective-permute-start(bf16[3,96,384]{2,1,0:T(8,128)(2,1)} %get-tuple-element.19), channel_id=1, source_target_pairs={{0,2},{1,3},{2,0},{3,1},{4,6},{5,7},{6,4},{7,5},{8,10},{9,11},{10,... | collective-permute-start | bytes 663560 | tf_op jit(solution)/shard_map/ppermute | solution.py:37
  13.9 11.2 %copy-start.12 = (bf16[3,96,384]{2,1,0:T(8,128)(2,1)S(1)}, bf16[3,96,384]{2,1,0:T(8,128)(2,1)}, u32[]{:S(2)}) copy-start(bf16[3,96,384]{2,1,0:T(8,128)(2,1)} %get-tuple-element.21) | copy-start | bytes 663556
  14.0 11.2 %collective-permute-start.1 = (bf16[2,4,8,2,384]{4,3,2,1,0:T(2,128)(2,1)S(1)}, bf16[2,4,8,2,384]{4,3,2,1,0:T(2,128)(2,1)S(1)}, u32[]{:S(2)}, u32[]{:S(2)}) collective-permute-start(bf16[2,4,8,2,384]{4,3,2,1,0:T(2,128)(2,1)S(1)} %get-tuple-element.34), channel_id=1, source_target_pairs={{0,2},{1,3},{2,0},{3,1},{4,6},{5,7},{6,4},{7,5},{8,10},{9,11},{10,... | collective-permute-start | bytes 294920 | tf_op jit(solution)/shard_map/ppermute | solution.py:206
  14.3 13.3 %copy-start.1 = (bf16[3,96,384]{2,1,0:T(8,128)(2,1)S(1)}, bf16[3,96,384]{2,1,0:T(8,128)(2,1)}, u32[]{:S(2)}) copy-start(bf16[3,96,384]{2,1,0:T(8,128)(2,1)} %get-tuple-element.18.refs_9_) | copy-start | bytes 663556
  25.1 12.8 %collective-permute-start.11 = (bf16[3,96,384]{2,1,0:T(8,128)(2,1)S(1)}, bf16[3,96,384]{2,1,0:T(8,128)(2,1)S(1)}, u32[]{:S(2)}, u32[]{:S(2)}) collective-permute-start(bf16[3,96,384]{2,1,0:T(8,128)(2,1)S(1)} %copy-done.12), channel_id=1, source_target_pairs={{0,8},{1,11},{2,10},{3,9},{4,12},{5,15},{6,14},{7,13},{8,0},{9,3},... | collective-permute-start | bytes 663560 | tf_op jit(solution)/shard_map/ppermute | solution.py:37
  27.6 13.6 %collective-permute-start.15 = (bf16[3,96,384]{2,1,0:T(8,128)(2,1)S(1)}, bf16[3,96,384]{2,1,0:T(8,128)(2,1)S(1)}, u32[]{:S(2)}, u32[]{:S(2)}) collective-permute-start(bf16[3,96,384]{2,1,0:T(8,128)(2,1)S(1)} %copy-done.1), channel_id=1, source_target_pairs={{0,1},{1,0},{2,3},{3,2},{4,5},{5,4},{6,7},{7,6},{8,9},{9,8},{10,11... | collective-permute-start | bytes 663560 | tf_op jit(solution)/shard_map/ppermute | solution.py:37
  27.6 6.3 %collective-permute-start.2 = (bf16[4,2,8,2,384]{4,3,2,1,0:T(2,128)(2,1)S(1)}, bf16[4,2,8,2,384]{4,3,2,1,0:T(2,128)(2,1)S(1)}, u32[]{:S(2)}, u32[]{:S(2)}) collective-permute-start(bf16[4,2,8,2,384]{4,3,2,1,0:T(2,128)(2,1)S(1)} %get-tuple-element.32), channel_id=1, source_target_pairs={{0,4},{1,5},{2,6},{3,7},{4,0},{5,1},{6,2},{7,3},{8,12},{9,13},{10,... | collective-permute-start | bytes 294920 | tf_op jit(solution)/shard_map/ppermute | solution.py:206
  33.9 15.3 %collective-permute-start.6 = (bf16[128,1536]{1,0:T(8,128)(2,1)S(1)}, bf16[128,1536]{1,0:T(8,128)(2,1)S(1)}, u32[]{:S(2)}, u32[]{:S(2)}) collective-permute-start(bf16[128,1536]{1,0:T(8,128)(2,1)S(1)} %constant_dynamic-update-slice_fusion.refs_5_), channel_id=1, source_target_pairs={{0,4},{2,6},{5,1},{7,3},{8,12},{10,14},{13,9},{15,11},{16,20},{18,... | collective-permute-start | bytes 1179656 | tf_op jit(solution)/shard_map/ppermute | solution.py:37
  35.2 19.5 %copy-start.11 = (f32[1536]{0:T(1024)S(1)}, f32[1536]{0:T(1024)}, u32[]{:S(2)}) copy-start(f32[1536]{0:T(1024)} %param.11) | copy-start | bytes 18436
  38.0 6.0 %collective-permute-start.3 = (bf16[8,1,8,2,384]{4,3,2,1,0:T(2,128)(2,1)S(1)}, bf16[8,1,8,2,384]{4,3,2,1,0:T(2,128)(2,1)S(1)}, u32[]{:S(2)}, u32[]{:S(2)}) collective-permute-start(bf16[8,1,8,2,384]{4,3,2,1,0:T(2,128)(2,1)S(1)} %get-tuple-element.30), channel_id=1, source_target_pairs={{0,8},{1,9},{2,10},{3,11},{4,12},{5,13},{6,14},{7,15},{8,0},{9,1},... | collective-permute-start | bytes 294920 | tf_op jit(solution)/shard_map/ppermute | solution.py:206
  39.9 5.4 %collective-permute-start.16 = (bf16[3,96,384]{2,1,0:T(8,128)(2,1)S(1)}, bf16[3,96,384]{2,1,0:T(8,128)(2,1)S(1)}, u32[]{:S(2)}, u32[]{:S(2)}) collective-permute-start(bf16[3,96,384]{2,1,0:T(8,128)(2,1)S(1)} %collective-permute-done.8.refs_10_), channel_id=1, source_target_pairs={{0,1},{1,0},{2,3},{3,2},{4,5},{5,4},{6,7},{7,6},{8,9},{9,8},{10,11... | collective-permute-start | bytes 663560 | tf_op jit(solution)/shard_map/ppermute | solution.py:37
  41.1 7.0 %collective-permute-start.19 = (bf16[3,96,384]{2,1,0:T(8,128)(2,1)S(1)}, bf16[3,96,384]{2,1,0:T(8,128)(2,1)S(1)}, u32[]{:S(2)}, u32[]{:S(2)}) collective-permute-start(bf16[3,96,384]{2,1,0:T(8,128)(2,1)S(1)} %collective-permute-done.11.refs_13_), channel_id=1, source_target_pairs={{0,1},{1,0},{2,3},{3,2},{4,5},{5,4},{6,7},{7,6},{8,9},{9,8},{10,11... | collective-permute-start | bytes 663560 | tf_op jit(solution)/shard_map/ppermute | solution.py:37
  41.1 7.3 %collective-permute-start.12 = (bf16[3,96,384]{2,1,0:T(8,128)(2,1)S(1)}, bf16[3,96,384]{2,1,0:T(8,128)(2,1)S(1)}, u32[]{:S(2)}, u32[]{:S(2)}) collective-permute-start(bf16[3,96,384]{2,1,0:T(8,128)(2,1)S(1)} %collective-permute-done.11.refs_13_), channel_id=1, source_target_pairs={{0,16},{1,17},{2,18},{3,19},{4,20},{5,21},{6,22},{7,23},{8,24},{9,... | collective-permute-start | bytes 663560 | tf_op jit(solution)/shard_map/ppermute | solution.py:37
  44.0 4.6 %collective-permute-start.21 = (bf16[3,96,384]{2,1,0:T(8,128)(2,1)S(1)}, bf16[3,96,384]{2,1,0:T(8,128)(2,1)S(1)}, u32[]{:S(2)}, u32[]{:S(2)}) collective-permute-start(bf16[3,96,384]{2,1,0:T(8,128)(2,1)S(1)} %collective-permute-done.13.refs_15_), channel_id=1, source_target_pairs={{0,1},{1,0},{2,3},{3,2},{4,5},{5,4},{6,7},{7,6},{8,9},{9,8},{10,11... | collective-permute-start | bytes 663560 | tf_op jit(solution)/shard_map/ppermute | solution.py:37
  45.3 9.8 %collective-permute-start.14 = (bf16[3,96,384]{2,1,0:T(8,128)(2,1)S(1)}, bf16[3,96,384]{2,1,0:T(8,128)(2,1)S(1)}, u32[]{:S(2)}, u32[]{:S(2)}) collective-permute-start(bf16[3,96,384]{2,1,0:T(8,128)(2,1)S(1)} %collective-permute-done.13.refs_15_), channel_id=1, source_target_pairs={{0,16},{1,17},{2,18},{3,19},{4,20},{5,21},{6,22},{7,23},{8,24},{9,... | collective-permute-start | bytes 663560 | tf_op jit(solution)/shard_map/ppermute | solution.py:37
  48.1 9.2 %collective-permute-start.17 = (bf16[3,96,384]{2,1,0:T(8,128)(2,1)S(1)}, bf16[3,96,384]{2,1,0:T(8,128)(2,1)S(1)}, u32[]{:S(2)}, u32[]{:S(2)}) collective-permute-start(bf16[3,96,384]{2,1,0:T(8,128)(2,1)S(1)} %collective-permute-done.9.refs_11_), channel_id=1, source_target_pairs={{0,1},{1,0},{2,3},{3,2},{4,5},{5,4},{6,7},{7,6},{8,9},{9,8},{10,11... | collective-permute-start | bytes 663560 | tf_op jit(solution)/shard_map/ppermute | solution.py:37
  48.4 10.2 %collective-permute-start.10 = (bf16[3,96,384]{2,1,0:T(8,128)(2,1)S(1)}, bf16[3,96,384]{2,1,0:T(8,128)(2,1)S(1)}, u32[]{:S(2)}, u32[]{:S(2)}) collective-permute-start(bf16[3,96,384]{2,1,0:T(8,128)(2,1)S(1)} %collective-permute-done.9.refs_11_), channel_id=1, source_target_pairs={{0,16},{1,17},{2,18},{3,19},{4,20},{5,21},{6,22},{7,23},{8,24},{9,... | collective-permute-start | bytes 663560 | tf_op jit(solution)/shard_map/ppermute | solution.py:37
  48.5 10.7 %collective-permute-start.5 = (bf16[128,1536]{1,0:T(8,128)(2,1)S(1)}, bf16[128,1536]{1,0:T(8,128)(2,1)S(1)}, u32[]{:S(2)}, u32[]{:S(2)}) collective-permute-start(bf16[128,1536]{1,0:T(8,128)(2,1)S(1)} %constant_dynamic-update-slice_fusion.refs_5_), channel_id=1, source_target_pairs={{0,2},{2,0},{5,7},{7,5},{8,10},{10,8},{13,15},{15,13},{16,18},{18,... | collective-permute-start | bytes 1179656 | tf_op jit(solution)/shard_map/ppermute | solution.py:37
  49.2 13.8 %collective-permute-start.7 = (bf16[128,1536]{1,0:T(8,128)(2,1)S(1)}, bf16[128,1536]{1,0:T(8,128)(2,1)S(1)}, u32[]{:S(2)}, u32[]{:S(2)}) collective-permute-start(bf16[128,1536]{1,0:T(8,128)(2,1)S(1)} %collective-permute-done.6.refs_7_), channel_id=1, source_target_pairs={{1,3},{3,1},{4,6},{6,4},{9,11},{11,9},{12,14},{14,12},{17,19},{19,... | collective-permute-start | bytes 1179656 | tf_op jit(solution)/shard_map/ppermute | solution.py:37
  55.1 4.2 %collective-permute-start.20 = (bf16[3,96,384]{2,1,0:T(8,128)(2,1)S(1)}, bf16[3,96,384]{2,1,0:T(8,128)(2,1)S(1)}, u32[]{:S(2)}, u32[]{:S(2)}) collective-permute-start(bf16[3,96,384]{2,1,0:T(8,128)(2,1)S(1)} %collective-permute-done.12.refs_14_), channel_id=1, source_target_pairs={{0,1},{1,0},{2,3},{3,2},{4,5},{5,4},{6,7},{7,6},{8,9},{9,8},{10,11... | collective-permute-start | bytes 663560 | tf_op jit(solution)/shard_map/ppermute | solution.py:37
  57.3 1.9 %collective-permute-start.22 = (bf16[3,96,384]{2,1,0:T(8,128)(2,1)S(1)}, bf16[3,96,384]{2,1,0:T(8,128)(2,1)S(1)}, u32[]{:S(2)}, u32[]{:S(2)}) collective-permute-start(bf16[3,96,384]{2,1,0:T(8,128)(2,1)S(1)} %collective-permute-done.14.refs_16_), channel_id=1, source_target_pairs={{0,1},{1,0},{2,3},{3,2},{4,5},{5,4},{6,7},{7,6},{8,9},{9,8},{10,11... | collective-permute-start | bytes 663560 | tf_op jit(solution)/shard_map/ppermute | solution.py:37
  58.6 1.7 %collective-permute-start.18 = (bf16[3,96,384]{2,1,0:T(8,128)(2,1)S(1)}, bf16[3,96,384]{2,1,0:T(8,128)(2,1)S(1)}, u32[]{:S(2)}, u32[]{:S(2)}) collective-permute-start(bf16[3,96,384]{2,1,0:T(8,128)(2,1)S(1)} %collective-permute-done.10.refs_12_), channel_id=1, source_target_pairs={{0,1},{1,0},{2,3},{3,2},{4,5},{5,4},{6,7},{7,6},{8,9},{9,8},{10,11... | collective-permute-start | bytes 663560 | tf_op jit(solution)/shard_map/ppermute | solution.py:37
  63.0 5.9 %copy-start = (bf16[128,1536]{1,0:T(8,128)(2,1)}, bf16[128,1536]{1,0:T(8,128)(2,1)S(1)}, u32[]{:S(2)}) copy-start(bf16[128,1536]{1,0:T(8,128)(2,1)S(1)} %collective-permute-done.7.refs_8_) | copy-start | bytes 1179652
  63.0 0.7 copy-start.3
  63.0 0.7 copy-start.4
  68.9 4.6 %collective-permute-start.25 = (bf16[256,384]{1,0:T(8,128)(2,1)S(1)}, bf16[256,384]{1,0:T(8,128)(2,1)S(1)}, u32[]{:S(2)}, u32[]{:S(2)}) collective-permute-start(bf16[256,384]{1,0:T(8,128)(2,1)S(1)} %step.1.refs_25_), channel_id=1, source_target_pairs={{0,2},{1,3},{2,0},{3,1},{4,6},{5,7},{6,4},{7,5},{8,10},{9,11},{10,... | collective-permute-start | bytes 589832 | tf_op jit(solution)/shard_map/ppermute | solution.py:37
  70.1 4.8 %collective-permute-start.24 = (bf16[256,384]{1,0:T(8,128)(2,1)S(1)}, bf16[256,384]{1,0:T(8,128)(2,1)S(1)}, u32[]{:S(2)}, u32[]{:S(2)}) collective-permute-start(bf16[256,384]{1,0:T(8,128)(2,1)S(1)} %step.1.refs_25_), channel_id=1, source_target_pairs={{0,4},{1,5},{2,6},{3,7},{4,0},{5,1},{6,2},{7,3},{8,12},{9,13},{10,... | collective-permute-start | bytes 589832 | tf_op jit(solution)/shard_map/ppermute | solution.py:37
  70.1 8.3 %collective-permute-start.23 = (bf16[256,384]{1,0:T(8,128)(2,1)S(1)}, bf16[256,384]{1,0:T(8,128)(2,1)S(1)}, u32[]{:S(2)}, u32[]{:S(2)}) collective-permute-start(bf16[256,384]{1,0:T(8,128)(2,1)S(1)} %step.1.refs_25_), channel_id=1, source_target_pairs={{0,6},{1,7},{2,4},{3,5},{4,2},{5,3},{6,0},{7,1},{8,14},{9,15},{10,... | collective-permute-start | bytes 589832 | tf_op jit(solution)/shard_map/ppermute | solution.py:37
  84.9 0.6 copy-start.2
  85.5 9.4 %collective-permute-start.26 = (bf16[64,384]{1,0:T(8,128)(2,1)S(1)}, bf16[64,384]{1,0:T(8,128)(2,1)S(1)}, u32[]{:S(2)}, u32[]{:S(2)}) collective-permute-start(bf16[64,384]{1,0:T(8,128)(2,1)S(1)} %get-tuple-element.23), channel_id=1, source_target_pairs={{0,2},{1,4},{2,0},{3,6},{4,1},{5,7},{6,3},{7,5},{8,10},{9,12},{10,... | collective-permute-start | bytes 147464 | tf_op jit(solution)/shard_map/ppermute | solution.py:37
  88.8 6.0 %collective-permute-start.27 = (bf16[64,384]{1,0:T(8,128)(2,1)S(1)}, bf16[64,384]{1,0:T(8,128)(2,1)S(1)}, u32[]{:S(2)}, u32[]{:S(2)}) collective-permute-start(bf16[64,384]{1,0:T(8,128)(2,1)S(1)} %get-tuple-element.24), channel_id=1, source_target_pairs={{0,3},{1,5},{2,1},{3,7},{4,0},{5,6},{6,2},{7,4},{8,11},{9,13},{10,... | collective-permute-start | bytes 147464 | tf_op jit(solution)/shard_map/ppermute | solution.py:37
  88.8 6.0 %collective-permute-start.28 = (bf16[64,384]{1,0:T(8,128)(2,1)S(1)}, bf16[64,384]{1,0:T(8,128)(2,1)S(1)}, u32[]{:S(2)}, u32[]{:S(2)}) collective-permute-start(bf16[64,384]{1,0:T(8,128)(2,1)S(1)} %get-tuple-element.25), channel_id=1, source_target_pairs={{0,1},{1,7},{2,3},{3,5},{4,2},{5,4},{6,0},{7,6},{8,9},{9,15},{10,1... | collective-permute-start | bytes 147464 | tf_op jit(solution)/shard_map/ppermute | solution.py:37
  90.0 6.6 %collective-permute-start.29 = (bf16[64,384]{1,0:T(8,128)(2,1)S(1)}, bf16[64,384]{1,0:T(8,128)(2,1)S(1)}, u32[]{:S(2)}, u32[]{:S(2)}) collective-permute-start(bf16[64,384]{1,0:T(8,128)(2,1)S(1)} %get-tuple-element.26), channel_id=1, source_target_pairs={{1,6},{3,4},{4,3},{6,1},{9,14},{11,12},{12,11},{14,9},{17,22},{19,... | collective-permute-start | bytes 147464 | tf_op jit(solution)/shard_map/ppermute | solution.py:37
  94.8 1.8 %copy-start.7 = (bf16[64,384]{1,0:T(8,128)(2,1)}, bf16[64,384]{1,0:T(8,128)(2,1)S(1)}, u32[]{:S(2)}) copy-start(bf16[64,384]{1,0:T(8,128)(2,1)S(1)} %collective-permute-done.26.first) | copy-start | bytes 147460
  94.9 1.7 %copy-start.8 = (bf16[64,384]{1,0:T(8,128)(2,1)}, bf16[64,384]{1,0:T(8,128)(2,1)S(1)}, u32[]{:S(2)}) copy-start(bf16[64,384]{1,0:T(8,128)(2,1)S(1)} %collective-permute-done.27.second) | copy-start | bytes 147460
  94.9 1.7 %copy-start.9 = (bf16[64,384]{1,0:T(8,128)(2,1)}, bf16[64,384]{1,0:T(8,128)(2,1)S(1)}, u32[]{:S(2)}) copy-start(bf16[64,384]{1,0:T(8,128)(2,1)S(1)} %collective-permute-done.28.third) | copy-start | bytes 147460
  96.6 0.6 copy-start.10

commit v3 on v2

--- a/solution.py
+++ b/solution.py
@@ -14,7 +14,6 @@
 SPATIAL = 4
 STEPS = 2
 AXES = ("groups", "frame")
-VMEM_LIMIT = 48 * 1024 * 1024
 
 
 def coords(index):
@@ -68,7 +67,7 @@
     w_query, w_key, w_value, own_ref, beside_ref, even_ref, odd_ref, rows, row_sem, out_sem
 ):
     x, _, plane, y, c = here()
-    width = own_ref.shape[2]
+    width = own_ref.shape[1] // 3
     reads = []
     for number, weight in enumerate((w_query, w_key, w_value)):
         reads.append(pltpu.make_async_copy(weight, rows.at[number], row_sem.at[number]))
@@ -76,19 +75,25 @@
     across = joined_bits(joined_bits(x, y), c)
     low = plane % 2
     quarters = (low * 2 + across, (1 - low) * 2 + across, low * 2 + 1 - y, quarter_of(plane, y))
-    for read in reads:
+    gives = []
+    for number, read in enumerate(reads):
         read.wait()
-    gives = []
-    for number, (quarter, out) in enumerate(zip(quarters, (even_ref, odd_ref, beside_ref, own_ref))):
-        gives.append(pltpu.make_async_copy(rows.at[:, :, columns(quarter, width)], out, out_sem.at[number]))
-        gives[-1].start()
+        for place, (quarter, out) in enumerate(zip(quarters, (even_ref, odd_ref, beside_ref, own_ref))):
+            gives.append(
+                pltpu.make_async_copy(
+                    rows.at[number, :, columns(quarter, width)],
+                    out.at[:, pl.ds(number * width, width)],
+                    out_sem.at[number, place],
+                )
+            )
+            gives[-1].start()
     for give in gives:
         give.wait()
 
 
 def pack_weights(w_query, w_key, w_value):
     shard_rows, features = w_query.shape
-    piece = jax.ShapeDtypeStruct((3, shard_rows, features // SPATIAL), w_query.dtype)
+    piece = jax.ShapeDtypeStruct((shard_rows, 3 * (features // SPATIAL)), w_query.dtype)
     anywhere = pl.BlockSpec(memory_space=pl.ANY)
     held = pl.BlockSpec(memory_space=pltpu.HBM)
     return pl.pallas_call(
@@ -99,7 +104,7 @@
         scratch_shapes=[
             pltpu.VMEM((3, shard_rows, features), w_query.dtype),
             pltpu.SemaphoreType.DMA((3,)),
-            pltpu.SemaphoreType.DMA((4,)),
+            pltpu.SemaphoreType.DMA((3, 4)),
         ],
         name="pack_weights",
     )(w_query, w_key, w_value)
@@ -215,28 +220,45 @@
     return block, near, far, far_near
 
 
-def step_kernel(places, updates, last, head_count, *refs):
-    refs = list(refs)
-    count_hbm, scale_hbm, gain_ref, key_ref, value_ref = refs[:5]
-    token_refs = refs[5:9]
-    piece_refs = refs[9 : 9 + len(places)]
-    update_refs = refs[9 + len(places) : 9 + len(places) + len(updates)]
-    outs = refs[9 + len(places) + len(updates) : -11]
-    current, normed, weights, parts, attended, count_ref, scale_ref, token_sem, piece_sem, update_sem, scalar_sem = (
-        refs[-11:]
-    )
-    x, _, plane, y, c = here()
-    low = plane % 2
-    chip_rows = token_refs[0].shape[0]
-    width = parts.shape[2]
-    at_home = low == c
-
-    scalar_copies = (
-        pltpu.make_async_copy(count_hbm, count_ref, scalar_sem.at[0]),
-        pltpu.make_async_copy(scale_hbm, scale_ref, scalar_sem.at[1]),
-    )
-    for copy in scalar_copies:
-        copy.start()
+def late_plane(devices):
+    return devices // 4 - 1
+
+
+def piece_start(place, shard_rows, plane_number):
+    x, _, _, y, c = here()
+    _, y_bits, with_x, c_bits = place
+    from_y, from_c = flipped(y, y_bits), flipped(c, c_bits)
+    if with_x:
+        from_y = joined_bits(joined_bits(from_y, x), from_c)
+    return pl.multiple_of((plane_number * 4 + from_y * 2 + from_c) * shard_rows, 16)
+
+
+def gather_pieces(piece_refs, places, first_plane, weights, sem):
+    copies = []
+    for number, (ref, place) in enumerate(zip(piece_refs, places)):
+        start = piece_start(place, ref.shape[0], place[0] - first_plane)
+        copies.append(pltpu.make_async_copy(ref, weights.at[pl.ds(start, ref.shape[0])], sem.at[number]))
+        copies[-1].start()
+    return copies
+
+
+def store_normed(current, rows, inverse, gain_ref, normed):
+    _, _, plane, _, _ = here()
+    planes = lax.axis_size("frame") // 4
+    span = current.shape[1] // planes
+    for bits in range(planes):
+        spot = columns(flipped(plane, bits), span)
+        widened = current[rows, spot].astype(jnp.float32)
+        normed[rows, bits * span : (bits + 1) * span] = (widened * inverse * gain_ref[0:1, spot]).astype(normed.dtype)
+
+
+BLOCK = 32
+
+
+def prepare_kernel(extra_ref, block, near, far, far_near, current, normed, token_sem):
+    _, _, plane, y, c = here()
+    chip_rows = block.shape[0]
+    at_home = plane % 2 == c
 
     def token_copies(first, second):
         return (
@@ -246,93 +268,125 @@
 
     @pl.when(at_home)
     def _():
-        for copy in token_copies(token_refs[0], token_refs[1]):
+        for copy in token_copies(block, near):
             copy.start()
 
     @pl.when(jnp.logical_not(at_home))
     def _():
-        for copy in token_copies(token_refs[2], token_refs[3]):
+        for copy in token_copies(far, far_near):
             copy.start()
 
-    update_copies = []
-    for number, (ref, _) in enumerate(zip(update_refs, updates)):
-        update_copies.append(pltpu.make_async_copy(ref, parts.at[number], update_sem.at[number]))
-        update_copies[-1].start()
-    piece_copies = []
-    shard_rows = piece_refs[0].shape[1]
-    for number, (ref, (plane_bits, y_bits, with_x, c_bits)) in enumerate(zip(piece_refs, places)):
-        from_y, from_c = flipped(y, y_bits), flipped(c, c_bits)
-        if with_x:
-            from_y = joined_bits(joined_bits(from_y, x), from_c)
-        shard = flipped(plane, plane_bits) * 4 + from_y * 2 + from_c
-        start = pl.multiple_of(shard * shard_rows, 16)
-        piece_copies.append(
-            pltpu.make_async_copy(ref, weights.at[:, pl.ds(start, shard_rows), :], piece_sem.at[number])
-        )
-        piece_copies[-1].start()
-    for copy in token_copies(token_refs[0], token_refs[1]):
+    for copy in token_copies(block, near):
         copy.wait()
-    for copy in update_copies:
+
+    @pl.loop(0, current.shape[0] // BLOCK)
+    def _(number):
+        rows = pl.ds(pl.multiple_of(number * BLOCK, BLOCK), BLOCK)
+        widened = current[rows, :].astype(jnp.float32)
+        inverse = lax.rsqrt(jnp.mean(widened * widened, axis=-1, keepdims=True) + 1e-06)
+        store_normed(current, rows, inverse, extra_ref, normed)
+
+
+def project_kernel(places, *refs):
+    normed = refs[0]
+    piece_refs = refs[1 : 1 + len(places)]
+    out, weights, sem = refs[1 + len(places) :]
+    for copy in gather_pieces(piece_refs, places, 0, weights, sem):
         copy.wait()
-    for copy in scalar_copies:
+    out[...] = jnp.dot(normed[:, : weights.shape[0]], weights[...], preferred_element_type=jnp.float32)
+
+
+def assemble_kernel(places, *refs):
+    for copy in gather_pieces(refs[:-2], places, 0, refs[-2], refs[-1]):
         copy.wait()
-    for number, (plane_bits, y_bits) in enumerate(updates):
-        quarter = quarter_of(flipped(plane, plane_bits), flipped(y, y_bits))
-        spot = columns(quarter, width)
-        current[:, spot] = (
-            current[:, spot].astype(jnp.float32) + scale_ref[0] * parts[number].astype(jnp.float32)
-        ).astype(current.dtype)
-    widened = current[...].astype(jnp.float32)
-    inverse = lax.rsqrt(jnp.mean(widened * widened, axis=-1, keepdims=True) + 1e-06)
-    normed[...] = (widened * inverse * gain_ref[...]).astype(normed.dtype)
-    for copy in piece_copies:
-        copy.wait()
-    queries, keys, values = (
-        jnp.dot(normed[...], weights[number], preferred_element_type=jnp.float32).astype(jnp.bfloat16)
-        for number in range(3)
-    )
-    frame = (plane // 2) * 2 + c
-    entries = key_ref.shape[0] // lax.axis_size("frame")
+
+
+def attend_heads(projected, key_ref, value_ref, extra_ref, attended, head_count):
+    width = projected.shape[1] // 3
     head_size = width // head_count
     scale_dot = 1.0 / math.sqrt(head_size)
-    entry = lax.broadcasted_iota(jnp.int32, (1, key_ref.shape[0]), 1) % entries
-    live = entry < count_ref[frame]
+    mem_rows = key_ref.shape[0]
+    live = extra_ref[3:4, :mem_rows] > 0.5
     contract_last = (((1,), (1,)), ((), ()))
+    frame_rows = projected.shape[0]
+    half = frame_rows // 2
     for head in range(head_count):
         span = slice(head * head_size, (head + 1) * head_size)
-        frame_scores = (
-            lax.dot_general(queries[:, span], keys[:, span], contract_last, preferred_element_type=jnp.float32)
-            * scale_dot
-        )
-        mem_scores = (
-            lax.dot_general(queries[:, span], key_ref[:, span], contract_last, preferred_element_type=jnp.float32)
-            * scale_dot
-        )
-        mem_scores = jnp.where(live, mem_scores, -1e30)
-        largest = jnp.maximum(
-            jnp.max(frame_scores, axis=-1, keepdims=True), jnp.max(mem_scores, axis=-1, keepdims=True)
-        )
-        frame_weights = jnp.exp(frame_scores - largest)
-        mem_weights = jnp.exp(mem_scores - largest)
-        denominator = jnp.sum(frame_weights, axis=-1, keepdims=True) + jnp.sum(mem_weights, axis=-1, keepdims=True)
-        blended = jnp.dot(
-            frame_weights.astype(jnp.bfloat16), values[:, span], preferred_element_type=jnp.float32
-        ) + jnp.dot(mem_weights.astype(jnp.bfloat16), value_ref[:, span], preferred_element_type=jnp.float32)
-        attended[:, span] = (blended / denominator).astype(attended.dtype)
-    if not last:
-        outs[0][...] = attended[...]
-        return
+        keys = projected[:, width + head * head_size : width + (head + 1) * head_size]
+        values = projected[:, 2 * width + head * head_size : 2 * width + (head + 1) * head_size]
+        for start in range(0, frame_rows, half):
+            queries = projected[start : start + half, span]
+            frame_scores = (
+                lax.dot_general(queries, keys, contract_last, preferred_element_type=jnp.float32) * scale_dot
+            )
+            mem_scores = (
+                lax.dot_general(queries, key_ref[:, span], contract_last, preferred_element_type=jnp.float32)
+                * scale_dot
+            )
+            mem_scores = jnp.where(live, mem_scores, -1e30)
+            largest = jnp.maximum(
+                jnp.max(frame_scores, axis=-1, keepdims=True), jnp.max(mem_scores, axis=-1, keepdims=True)
+            )
+            frame_weights = jnp.exp(frame_scores - largest)
+            mem_weights = jnp.exp(mem_scores - largest)
+            denominator = jnp.sum(frame_weights, axis=-1, keepdims=True) + jnp.sum(
+                mem_weights, axis=-1, keepdims=True
+            )
+            blended = jnp.dot(
+                frame_weights.astype(jnp.bfloat16), values, preferred_element_type=jnp.float32
+            ) + jnp.dot(mem_weights.astype(jnp.bfloat16), value_ref[:, span], preferred_element_type=jnp.float32)
+            attended[start : start + half, span] = (blended / denominator).astype(attended.dtype)
+
+
+def step_kernel(places, first_plane, head_count, extra_ref, key_ref, value_ref, normed, part_ref, *refs):
+    piece_refs = refs[: len(places)]
+    attended, weights, projected, sem = refs[len(places) :]
+    for copy in gather_pieces(piece_refs, places, first_plane, weights, sem):
+        copy.wait()
+    early = normed.shape[1] - weights.shape[0]
+    projected[...] = (
+        part_ref[...] + jnp.dot(normed[:, early:], weights[...], preferred_element_type=jnp.float32)
+    ).astype(projected.dtype)
+    attend_heads(projected, key_ref, value_ref, extra_ref, attended, head_count)
+
+
+def last_step_kernel(
+    update_places, head_count, extra_ref, key_ref, value_ref, current_ref, weights, first_part, second_part, third_part,
+    fourth_part, keep, first, second, third, fourth, current, normed, projected, attended,
+):
+    _, _, plane, y, c = here()
+    width = first_part.shape[1]
+    at_home = plane % 2 == c
+
+    @pl.loop(0, current.shape[0] // BLOCK)
+    def _(number):
+        rows = pl.ds(pl.multiple_of(number * BLOCK, BLOCK), BLOCK)
+        total = jnp.zeros((BLOCK, 1), jnp.float32)
+        for part, (plane_bits, y_bits) in zip((first_part, second_part, third_part, fourth_part), update_places):
+            spot = columns(quarter_of(flipped(plane, plane_bits), flipped(y, y_bits)), width)
+            updated = (
+                current_ref[rows, spot].astype(jnp.float32)
+                + extra_ref[1:2, :width] * part[rows, :].astype(jnp.float32)
+            ).astype(current.dtype)
+            current[rows, spot] = updated
+            widened = updated.astype(jnp.float32)
+            total = total + jnp.sum(widened * widened, axis=-1, keepdims=True)
+        inverse = lax.rsqrt(total / current.shape[1] + 1e-06)
+        store_normed(current, rows, inverse, extra_ref, normed)
+
+    projected[...] = jnp.dot(normed[...], weights[...], preferred_element_type=jnp.float32).astype(projected.dtype)
+    attend_heads(projected, key_ref, value_ref, extra_ref, attended, head_count)
     spot = columns(quarter_of(plane, y), width)
     attended[...] = (
-        current[:, spot].astype(jnp.float32) + scale_ref[1] * attended[...].astype(jnp.float32)
+        current[:, spot].astype(jnp.float32) + extra_ref[2:3, :width] * attended[...].astype(jnp.float32)
     ).astype(attended.dtype)
+    chip_rows = attended.shape[0] // 2
     rows = chip_rows // 2
     here_rows, there_rows = y * chip_rows, (1 - y) * chip_rows
 
     def part(start):
         return attended[pl.ds(pl.multiple_of(start, rows), rows), :]
 
-    keep, first, second, third, fourth = outs
     keep[...] = part(here_rows)
     fourth[...] = part(there_rows + rows)
 
@@ -349,83 +403,119 @@
         third[...] = part(there_rows)
 
 
-def step(pieces, updates, last, counts, scales, norm_gain, keys, values, tokens):
-    _, width = pieces[0][0].shape[1:]
-    features = norm_gain.shape[0]
-    chip_rows = tokens[0].shape[0]
-    frame_rows = 2 * chip_rows
-    dtype = tokens[0].dtype
-    head_count = HEADS // SPATIAL
-    kernel = functools.partial(
-        step_kernel, tuple(place for _, place in pieces), tuple(bits for _, bits in updates), last, head_count
-    )
-    if last:
-        out_shape = tuple(jax.ShapeDtypeStruct((chip_rows // 2, width), dtype) for _ in range(5))
-    else:
-        out_shape = (jax.ShapeDtypeStruct((frame_rows, width), dtype),)
-    anywhere = pl.BlockSpec(memory_space=pl.ANY)
-    held = pl.BlockSpec(memory_space=pltpu.HBM)
+MIB = 1024 * 1024
+
+
+def kernel_call(kernel, out_shape, operands, anywhere, scratch_shapes, limit, flops):
     vectors = pl.BlockSpec(memory_space=pltpu.VMEM)
-    flops = 2 * frame_rows * width * (3 * features + 2 * (frame_rows + keys.shape[0]))
+    free = pl.BlockSpec(memory_space=pl.ANY)
+    moved_bytes = sum(operand.size * operand.dtype.itemsize for operand in operands)
     return pl.pallas_call(
         kernel,
         out_shape=out_shape,
-        in_specs=[held, held, vectors, vectors, vectors] + [anywhere] * (4 + len(pieces) + len(updates)),
-        out_specs=tuple(vectors for _ in out_shape),
-        scratch_shapes=[
-            pltpu.VMEM((frame_rows, features), dtype),
-            pltpu.VMEM((frame_rows, features), jnp.bfloat16),
-            pltpu.VMEM((3, features, width), jnp.bfloat16),
-            pltpu.VMEM((max(len(updates), 1), frame_rows, width), dtype),
-            pltpu.VMEM((frame_rows, width), dtype),
-            pltpu.SMEM(counts.shape, counts.dtype),
-            pltpu.SMEM(scales.shape, scales.dtype),
-            pltpu.SemaphoreType.DMA((2,)),
+        in_specs=[free if number in anywhere else vectors for number in range(len(operands))],
+        out_specs=jax.tree.map(lambda _: vectors, out_shape),
+        scratch_shapes=scratch_shapes,
+        compiler_params=pltpu.CompilerParams(vmem_limit_bytes=limit),
+        cost_estimate=pl.CostEstimate(flops=flops, transcendentals=0, bytes_accessed=moved_bytes),
+    )(*operands)
+
+
+def prepare(extra, tokens):
+    frame = jax.ShapeDtypeStruct((2 * tokens[0].shape[0], tokens[0].shape[1]), tokens[0].dtype)
+    return kernel_call(
+        prepare_kernel, (frame, frame), (extra, *tokens), range(1, 5), [pltpu.SemaphoreType.DMA((2,))],
+        8 * MIB, 0,
+    )
+
+
+def project(normed, pieces):
+    rows, width = pieces[0][0].shape
+    depth = rows * len(pieces)
+    return kernel_call(
+        functools.partial(project_kernel, tuple(place for _, place in pieces)),
+        jax.ShapeDtypeStruct((normed.shape[0], width), jnp.float32),
+        (normed, *[array for array, _ in pieces]),
+        range(1, 1 + len(pieces)),
+        [pltpu.VMEM((depth, width), normed.dtype), pltpu.SemaphoreType.DMA((len(pieces),))],
+        16 * MIB,
+        2 * normed.shape[0] * depth * width,
+    )
+
+
+def assemble(pieces):
+    rows, width = pieces[0][0].shape
+    return kernel_call(
+        functools.partial(assemble_kernel, tuple(place for _, place in pieces)),
+        jax.ShapeDtypeStruct((rows * len(pieces), width), pieces[0][0].dtype),
+        [array for array, _ in pieces],
+        range(len(pieces)),
+        [pltpu.SemaphoreType.DMA((len(pieces),))],
+        8 * MIB,
+        0,
+    )
+
+
+def step(extra, keys, values, normed, part, pieces):
+    rows, width = pieces[0][0].shape
+    depth = rows * len(pieces)
+    frame_rows = normed.shape[0]
+    return kernel_call(
+        functools.partial(step_kernel, tuple(place for _, place in pieces), pieces[0][1][0], HEADS // SPATIAL),
+        jax.ShapeDtypeStruct((frame_rows, width // 3), normed.dtype),
+        (extra, keys, values, normed, part, *[array for array, _ in pieces]),
+        range(5, 5 + len(pieces)),
+        [
+            pltpu.VMEM((depth, width), normed.dtype),
+            pltpu.VMEM((frame_rows, width), normed.dtype),
             pltpu.SemaphoreType.DMA((len(pieces),)),
-            pltpu.SemaphoreType.DMA((max(len(updates), 1),)),
-            pltpu.SemaphoreType.DMA((2,)),
         ],
-        compiler_params=pltpu.CompilerParams(vmem_limit_bytes=VMEM_LIMIT),
-        cost_estimate=pl.CostEstimate(
-            flops=flops, transcendentals=frame_rows * head_count * (frame_rows + keys.shape[0]), bytes_accessed=6 << 20
-        ),
-        name="last_step" if last else "step",
-    )(
-        counts,
-        scales,
-        norm_gain.reshape(1, -1),
-        keys,
-        values,
-        *tokens,
-        *[array for array, _ in pieces],
-        *[array for array, _ in updates],
-    )
-
-
-def join_kernel(keep, first, second, third, fourth, out, sem):
+        16 * MIB,
+        2 * frame_rows * width * (depth + frame_rows),
+    )
+
+
+def last_step(extra, keys, values, current, weights, updates):
+    frame_rows, features = current.shape
+    width = weights.shape[1] // 3
+    share = jax.ShapeDtypeStruct((frame_rows // 4, width), current.dtype)
+    return kernel_call(
+        functools.partial(last_step_kernel, tuple(place for _, place in updates), HEADS // SPATIAL),
+        (share,) * 5,
+        (extra, keys, values, current, weights, *[array for array, _ in updates]),
+        (),
+        [
+            pltpu.VMEM((frame_rows, features), current.dtype),
+            pltpu.VMEM((frame_rows, features), current.dtype),
+            pltpu.VMEM((frame_rows, 3 * width), current.dtype),
+            pltpu.VMEM((frame_rows, width), current.dtype),
+        ],
+        16 * MIB,
+        2 * frame_rows * 3 * width * (features + frame_rows),
+    )
+
+
+def join_kernel(keep, first, second, third, fourth, out):
     _, _, plane, y, c = here()
     low = plane % 2
     width = keep.shape[1]
 
-    def put(number, ref, plane_low, at_y):
-        return pltpu.make_async_copy(ref, out.at[:, columns(plane_low * 2 + at_y, width)], sem.at[number])
+    def put(ref, plane_low, at_y):
+        out[:, columns(plane_low * 2 + at_y, width)] = ref[...]
 
     @pl.when(low == c)
     def _():
-        put(0, keep, low, y).start()
-        put(1, first, low, 1 - y).start()
-        put(2, second, 1 - low, y).start()
-        put(3, third, 1 - low, 1 - y).start()
+        put(keep, low, y)
+        put(first, low, 1 - y)
+        put(second, 1 - low, y)
+        put(third, 1 - low, 1 - y)
 
     @pl.when(low != c)
     def _():
-        put(0, first, 1 - low, y).start()
-        put(1, second, low, 1 - y).start()
-        put(2, third, low, y).start()
-        put(3, fourth, 1 - low, 1 - y).start()
-
-    for number in range(4):
-        put(number, first, number // 2, number % 2).wait()
+        put(first, 1 - low, y)
+        put(second, low, 1 - y)
+        put(third, low, y)
+        put(fourth, 1 - low, 1 - y)
 
 
 def joined(keep, first, second, third, fourth):
@@ -437,31 +527,43 @@
     third = moved(third, lambda x, p, y, c: (x, p, y, 1 - c) if at_home(p, c) else (x, p ^ 1, 1 - y, c))
     fourth = moved(fourth, lambda x, p, y, c: None if at_home(p, c) else (x, p ^ 1, 1 - y, 1 - c))
     rows, width = keep.shape
-    anywhere = pl.BlockSpec(memory_space=pl.ANY)
-    return pl.pallas_call(
+    return kernel_call(
         join_kernel,
-        out_shape=jax.ShapeDtypeStruct((rows, width * SPATIAL), keep.dtype),
-        in_specs=[anywhere] * 5,
-        out_specs=anywhere,
-        scratch_shapes=[pltpu.SemaphoreType.DMA((4,))],
-        name="join",
-    )(keep, first, second, third, fourth)
+        jax.ShapeDtypeStruct((rows, width * SPATIAL), keep.dtype),
+        (keep, first, second, third, fourth),
+        (),
+        [],
+        4 * MIB,
+        0,
+    )
+
+
+def small_operands(norm_gain, step_scale, counts, entries):
+    features = norm_gain.shape[0]
+    _, _, plane, _, c = here()
+    live = jnp.arange(features, dtype=jnp.int32) % entries < counts[(plane // 2) * 2 + c]
+    scales = [jnp.full((features,), step_scale[number]) for number in range(STEPS)]
+    return jnp.stack([norm_gain, *scales, live.astype(jnp.float32)])
 
 
 def paired_planes(
     latent, norm_gain, w_query, w_key, w_value, mem_cache, intersection, counts, slot_of, step_scale
 ):
-    pieces = all_pieces(*pack_weights(w_query, w_key, w_value))
+    late = late_plane(lax.axis_size("frame"))
+    pieces = sorted(all_pieces(*pack_weights(w_query, w_key, w_value)), key=lambda piece: piece[1][0])
     tokens = all_tokens(latent)
     keys, values = all_memory(*pack_memory(mem_cache, intersection, slot_of))
-    (attended,) = step(pieces, [], False, counts, step_scale, norm_gain, keys, values, tokens)
+    extra = small_operands(norm_gain, step_scale, counts, intersection.shape[1])
+    current, normed = prepare(extra, tokens)
+    part = project(normed, [piece for piece in pieces if piece[1][0] < late])
+    attended = step(extra, keys, values, normed, part, [piece for piece in pieces if piece[1][0] == late])
     updates = [
         (attended, (0, 0)),
         (moved(attended, lambda x, p, y, c: (x, p ^ 1, 1 - y, c)), (1, 1)),
         (moved(attended, lambda x, p, y, c: (x, p ^ 1, y, c)), (1, 0)),
         (moved(attended, lambda x, p, y, c: (x, p, 1 - y, c)), (0, 1)),
     ]
-    shares = step(pieces, updates, True, counts, step_scale, norm_gain, keys, values, tokens)
+    shares = last_step(extra, keys, values, current, assemble(pieces), updates)
     return joined(*shares)
 
 

time: 105 us -> 100 us (0.952)
  starting transfers between devices: 42.6 us -> 35.4 us
  local copies, waits for them, and re-layouts: 2.02 us -> 4.35 us
  waiting for transfers between devices: 34.4 us -> 32.5 us
  other arithmetic: 1.12 us -> 2.68 us
    ppermute x4, waiting for transfers between devices: 18.4 us -> 11.5 us  [hop(): lax.ppermute(array, 'frame', [(i, i ^ 1 << bit) for i in range(lax.axis_s...]
    ppermute x26, waiting for transfers between devices: 16 us -> 21 us  [moved(): return lax.ppermute(array, AXES, pairs)]
    ppermute x26, starting transfers between devices: 39.6 us -> 34.8 us  [moved(): return lax.ppermute(array, AXES, pairs)]
    ppermute x4, starting transfers between devices: 2.93 us -> 0.56 us  [hop(): lax.ppermute(array, 'frame', [(i, i ^ 1 << bit) for i in range(lax.axis_s...]
    another operation x0 -> x3, local copies, waits for them, and re-layouts: none -> 1.47 us  [small_operands(): return jnp.stack([norm_gain, *scales, live.astype(jnp.float32)])]
    dynamic_slice x0 -> x1, local copies, waits for them, and re-layouts: none -> 1.24 us  [small_operands(): counts[plane // 2 * 2 + c]]
    pallas_call x3 -> x6, Pallas kernels: 18.7 us -> 19.6 us  [kernel_call(): pl.pallas_call(kernel, out_shape=out_shape, in_specs=[free if number in a...]
  transfers between devices with their start and end apart: 30 -> 30, of which waited for: 11 -> 8; matrix products, arithmetic and copies ran while one was open for 1% -> 7% of each run, Pallas kernels for 2% -> 14%
where the time goes in v3:
time: 100 us
  starting transfers between devices  35.4 us (35%)
  waiting for transfers between devices  32.5 us (32%)
  Pallas kernels  24.8 us (25%)
  local copies, waits for them, and re-layouts  4.35 us (4%)
  other arithmetic  2.68 us (3%)
    ppermute x26, starting transfers between devices, moved(): return lax.ppermute(array, AXES, pairs)  34.8 us
    ppermute x26, waiting for transfers between devices, moved(): return lax.ppermute(array, AXES, pairs)  21 us
    pallas_call x6, Pallas kernels, kernel_call(): pl.pallas_call(kernel, out_shape=out_shape, in_specs=[free if number in a...  19.6 us
    ppermute x4, waiting for transfers between devices, hop(): lax.ppermute(array, 'frame', [(i, i ^ 1 << bit) for i in range(lax.axis_s...  11.5 us
    pallas_call x1, Pallas kernels, pack_memory(): pl.pallas_call(pack_memory_kernel, out_shape=(half,) * 2, in_specs=[held]...  3.11 us
    pallas_call x1, Pallas kernels, pack_weights(): pl.pallas_call(pack_weights_kernel, out_shape=(piece,) * 4, in_specs=[hel...  2.08 us
  transfers between devices with their start and end apart: 30, of which 8 were waited for; matrix products, arithmetic and copies ran while one was open for 7% of the time, Pallas kernels for 14%

profile of v3, /device:TPU:1, one launch (start us, length us, event | category | flops | bytes accessed | tf_op | source)
XLA Modules:
  0.0 100.0 jit_solution(1581478875158063659)
XLA Ops:
  0.0 3.1 %pack_memory.1 = (bf16[8,8,2,384]{3,2,1,0:T(2,128)(2,1)}, bf16[8,8,2,384]{3,2,1,0:T(2,128)(2,1)}) custom-call(s32[4,8]{1,0:T(4,128)} %list_hbm.1, s32[128]{0:T(128)} %slot_hbm.1, bf16[128,1,2,1536]{3,2,1,0:T(2,128)(2,1)} %mem_ref.1), custom_call_target="tpu_custom_call" | custom-call | tf_op jit(solution)/shard_map/pack_memory/pallas_call | solution.py:166
  3.2 2.1 %pack_weights.1 = (bf16[96,1152]{1,0:T(8,128)(2,1)}, bf16[96,1152]{1,0:T(8,128)(2,1)}, bf16[96,1152]{1,0:T(8,128)(2,1)}, bf16[96,1152]{1,0:T(8,128)(2,1)}) custom-call(bf16[96,1536]{1,0:T(8,128)(2,1)} %w_query.1, bf16[96,1536]{1,0:T(8,128)(2,1)} %w_key.1, bf16[96,1536]{1,0:T(8,128)(2,1)} %w_value.1), custom_call_target="tpu_custom_call" | custom-call | tf_op jit(solution)/shard_map/pack_weights/pallas_call | solution.py:99
  5.3 5.8 %collective-permute-start.19 = (bf16[96,1152]{1,0:T(8,128)(2,1)}, bf16[96,1152]{1,0:T(8,128)(2,1)S(1)}, u32[]{:S(2)}, u32[]{:S(2)}) collective-permute-start(bf16[96,1152]{1,0:T(8,128)(2,1)} %get-tuple-element.23), channel_id=1, source_target_pairs={{0,12},{1,15},{2,14},{3,13},{4,8},{5,11},{6,10},{7,9},{8,4},{9,7},... | collective-permute-start | bytes 663560 | tf_op jit(solution)/shard_map/ppermute | solution.py:36
  11.1 1.3 %collective-permute-start.4 = (bf16[64,1536]{1,0:T(8,128)(2,1)}, bf16[64,1536]{1,0:T(8,128)(2,1)S(1)}, u32[]{:S(2)}, u32[]{:S(2)}) collective-permute-start(bf16[64,1536]{1,0:T(8,128)(2,1)} %param.10), channel_id=1, source_target_pairs={{1,0},{3,2},{4,5},{6,7},{9,8},{11,10},{12,13},{14,15},{17,16},{19,... | collective-permute-start | bytes 589832 | tf_op jit(solution)/shard_map/ppermute | solution.py:36
  12.4 1.3 %collective-permute-start.8 = (bf16[96,1152]{1,0:T(8,128)(2,1)}, bf16[96,1152]{1,0:T(8,128)(2,1)S(1)}, u32[]{:S(2)}, u32[]{:S(2)}) collective-permute-start(bf16[96,1152]{1,0:T(8,128)(2,1)} %get-tuple-element.22), channel_id=1, source_target_pairs={{0,2},{1,3},{2,0},{3,1},{4,6},{5,7},{6,4},{7,5},{8,10},{9,11},{10,... | collective-permute-start | bytes 663560 | tf_op jit(solution)/shard_map/ppermute | solution.py:36
  13.7 1.1 %fusion.2 = (bf16[2,4,8,2,384]{4,3,2,1,0:T(2,128)(2,1)S(1)}, bf16[2,4,8,2,384]{4,3,2,1,0:T(2,128)(2,1)S(1)}) fusion(bf16[1,8,8,2,384]{4,3,2,1,0:T(2,128)(2,1)} %bitcast.9, bf16[1,8,8,2,384]{4,3,2,1,0:T(2,128)(2,1)S(1)} %bitcast.10), kind=kLoop, calls=%fused_computation.10 | loop fusion | flops 98304 | bytes 393216 | tf_op jit(solution)/shard_map/stack | solution.py:202
  14.8 0.3 collective-permute-start.1
  15.1 0.9 constant_dynamic-update-slice_fusion.1
  16.1 1.2 %dynamic_slice.3 = s32[1]{0:T(128)} dynamic-slice(s32[4]{0:T(128)} %param.17, s32[]{:T(128)S(6)} %select_n.31), dynamic_slice_sizes={1} | dynamic-slice | bytes 12 | tf_op jit(solution)/shard_map/dynamic_slice | solution.py:544
  17.4 7.8 %collective-permute-done.1 = bf16[2,4,8,2,384]{4,3,2,1,0:T(2,128)(2,1)S(1)} collective-permute-done((bf16[2,4,8,2,384]{4,3,2,1,0:T(2,128)(2,1)S(1)}, bf16[2,4,8,2,384]{4,3,2,1,0:T(2,128)(2,1)S(1)}, u32[]{:S(2)}, u32[]{:S(2)}) %collective-permute-start.1) | collective-permute-done | bytes 98336 | tf_op jit(solution)/shard_map/ppermute | solution.py:211
  25.2 2.1 %collective-permute-start.15 = (bf16[96,1152]{1,0:T(8,128)(2,1)}, bf16[96,1152]{1,0:T(8,128)(2,1)S(1)}, u32[]{:S(2)}, u32[]{:S(2)}) collective-permute-start(bf16[96,1152]{1,0:T(8,128)(2,1)} %get-tuple-element.24), channel_id=1, source_target_pairs={{0,8},{1,11},{2,10},{3,9},{4,12},{5,15},{6,14},{7,13},{8,0},{9,3},... | collective-permute-start | bytes 663560 | tf_op jit(solution)/shard_map/ppermute | solution.py:36
  27.3 0.3 fusion.1
  27.7 1.3 %collective-permute-start.6 = (bf16[128,1536]{1,0:T(8,128)(2,1)S(1)}, bf16[128,1536]{1,0:T(8,128)(2,1)S(1)}, u32[]{:S(2)}, u32[]{:S(2)}) collective-permute-start(bf16[128,1536]{1,0:T(8,128)(2,1)S(1)} %constant_dynamic-update-slice_fusion.block), channel_id=1, source_target_pairs={{0,4},{2,6},{5,1},{7,3},{8,12},{10,14},{13,9},{15,11},{16,20},{18,... | collective-permute-start | bytes 1179656 | tf_op jit(solution)/shard_map/ppermute | solution.py:36
  29.0 0.7 compare_convert_fusion
  29.7 8.5 %collective-permute-done.15.refs_8_.refs_9_ = bf16[96,1152]{1,0:T(8,128)(2,1)S(1)} collective-permute-done((bf16[96,1152]{1,0:T(8,128)(2,1)}, bf16[96,1152]{1,0:T(8,128)(2,1)S(1)}, u32[]{:S(2)}, u32[]{:S(2)}) %collective-permute-start.15) | collective-permute-done | bytes 221216 | tf_op jit(solution)/shard_map/ppermute | solution.py:36
  38.1 1.4 %collective-permute-start.9 = (bf16[96,1152]{1,0:T(8,128)(2,1)}, bf16[96,1152]{1,0:T(8,128)(2,1)S(1)}, u32[]{:S(2)}, u32[]{:S(2)}) collective-permute-start(bf16[96,1152]{1,0:T(8,128)(2,1)} %get-tuple-element.21.refs_0_.refs_1_), channel_id=1, source_target_pairs={{0,1},{1,0},{2,3},{3,2},{4,5},{5,4},{6,7},{7,6},{8,9},{9,8},{10,11... | collective-permute-start | bytes 663560 | tf_op jit(solution)/shard_map/ppermute | solution.py:36
  39.6 0.5 collective-permute-start.17
  40.1 0.3 fusion
  40.4 0.6 fusion.3
  41.1 0.7 pad.9.clone
  41.8 0.7 pad.10.clone
  42.6 0.7 collective-permute-start.5
  43.2 3.7 %collective-permute-done.3 = bf16[8,1,8,2,384]{4,3,2,1,0:T(2,128)(2,1)S(1)} collective-permute-done((bf16[8,1,8,2,384]{4,3,2,1,0:T(2,128)(2,1)S(1)}, bf16[8,1,8,2,384]{4,3,2,1,0:T(2,128)(2,1)S(1)}, u32[]{:S(2)}, u32[]{:S(2)}) %collective-permute-start.3) | collective-permute-done | bytes 98336 | tf_op jit(solution)/shard_map/ppermute | solution.py:211
  46.9 0.7 collective-permute-start.16
  47.6 0.8 collective-permute-start.20
  48.4 0.7 collective-permute-start.12
  49.1 2.5 %collective-permute-start.7 = (bf16[128,1536]{1,0:T(8,128)(2,1)S(1)}, bf16[128,1536]{1,0:T(8,128)(2,1)S(1)}, u32[]{:S(2)}, u32[]{:S(2)}) collective-permute-start(bf16[128,1536]{1,0:T(8,128)(2,1)S(1)} %collective-permute-done.6.far), channel_id=1, source_target_pairs={{1,3},{3,1},{4,6},{6,4},{9,11},{11,9},{12,14},{14,12},{17,19},{19,... | collective-permute-start | bytes 1179656 | tf_op jit(solution)/shard_map/ppermute | solution.py:36
  51.7 0.3 pad_maximum_fusion
  52.0 1.5 %collective-permute-done.16.refs_9_.refs_10_ = bf16[96,1152]{1,0:T(8,128)(2,1)S(1)} collective-permute-done((bf16[96,1152]{1,0:T(8,128)(2,1)S(1)}, bf16[96,1152]{1,0:T(8,128)(2,1)S(1)}, u32[]{:S(2)}, u32[]{:S(2)}) %collective-permute-start.16) | collective-permute-done | bytes 221216 | tf_op jit(solution)/shard_map/ppermute | solution.py:36
  53.5 2.2 %collective-permute-start.21 = (bf16[96,1152]{1,0:T(8,128)(2,1)S(1)}, bf16[96,1152]{1,0:T(8,128)(2,1)S(1)}, u32[]{:S(2)}, u32[]{:S(2)}) collective-permute-start(bf16[96,1152]{1,0:T(8,128)(2,1)S(1)} %collective-permute-done.19.refs_12_.refs_0_), channel_id=1, source_target_pairs={{0,1},{1,0},{2,3},{3,2},{4,5},{5,4},{6,7},{7,6},{8,9},{9,8},{10,11... | collective-permute-start | bytes 663560 | tf_op jit(solution)/shard_map/ppermute | solution.py:36
  55.7 2.5 %collective-permute-done.20.refs_13_.refs_1_ = bf16[96,1152]{1,0:T(8,128)(2,1)S(1)} collective-permute-done((bf16[96,1152]{1,0:T(8,128)(2,1)S(1)}, bf16[96,1152]{1,0:T(8,128)(2,1)S(1)}, u32[]{:S(2)}, u32[]{:S(2)}) %collective-permute-start.20) | collective-permute-done | bytes 221216 | tf_op jit(solution)/shard_map/ppermute | solution.py:36
  58.2 2.2 %collective-permute-start.13 = (bf16[96,1152]{1,0:T(8,128)(2,1)S(1)}, bf16[96,1152]{1,0:T(8,128)(2,1)S(1)}, u32[]{:S(2)}, u32[]{:S(2)}) collective-permute-start(bf16[96,1152]{1,0:T(8,128)(2,1)S(1)} %collective-permute-done.11.refs_4_.refs_5_), channel_id=1, source_target_pairs={{0,1},{1,0},{2,3},{3,2},{4,5},{5,4},{6,7},{7,6},{8,9},{9,8},{10,11... | collective-permute-start | bytes 663560 | tf_op jit(solution)/shard_map/ppermute | solution.py:36
  60.4 2.5 %collective-permute-done.12.refs_5_.refs_6_ = bf16[96,1152]{1,0:T(8,128)(2,1)S(1)} collective-permute-done((bf16[96,1152]{1,0:T(8,128)(2,1)S(1)}, bf16[96,1152]{1,0:T(8,128)(2,1)S(1)}, u32[]{:S(2)}, u32[]{:S(2)}) %collective-permute-start.12) | collective-permute-done | bytes 221216 | tf_op jit(solution)/shard_map/ppermute | solution.py:36
  63.0 1.3 %collective-permute-start.18 = (bf16[96,1152]{1,0:T(8,128)(2,1)S(1)}, bf16[96,1152]{1,0:T(8,128)(2,1)S(1)}, u32[]{:S(2)}, u32[]{:S(2)}) collective-permute-start(bf16[96,1152]{1,0:T(8,128)(2,1)S(1)} %collective-permute-done.16.refs_9_.refs_10_), channel_id=1, source_target_pairs={{0,1},{1,0},{2,3},{3,2},{4,5},{5,4},{6,7},{7,6},{8,9},{9,8},{10,11... | collective-permute-start | bytes 663560 | tf_op jit(solution)/shard_map/ppermute | solution.py:36
  64.3 0.5 collective-permute-start.14
  64.8 1.4 %shard_map.100 = (bf16[256,1536]{1,0:T(8,128)(2,1)S(1)}, bf16[256,1536]{1,0:T(8,128)(2,1)S(1)}) custom-call(f32[4,1536]{1,0:T(4,128)S(1)} %pad_maximum_fusion.4.extra_ref, bf16[128,1536]{1,0:T(8,128)(2,1)S(1)} %constant_dynamic-update-slice_fusion.block, bf16[128,1536]{1,0:T(8,128)(2,1)S(1)} %collective-permute-done.5.near, ...), custom_call_target="tpu_custom_call" | custom-call | bytes 1597440 | tf_op jit(solution)/shard_map/pallas_call | solution.py:413
  66.3 4.8 %shard_map.102.part_ref = f32[256,1152]{1,0:T(8,128)S(1)} custom-call(bf16[256,1536]{1,0:T(8,128)(2,1)S(1)} %get-tuple-element.25.refs_0_.normed, bf16[96,1152]{1,0:T(8,128)(2,1)S(1)} %copy-done, bf16[96,1152]{1,0:T(8,128)(2,1)S(1)} %collective-permute-done.8.refs_1_.refs_2_, bf16[96,1152]{1,0:T(8,128)(2,1)S(1)} %collective-permute-done.9.refs_2_.refs_3_, ...), custom_call_target="tpu_custom_call" | custom-call | flops 679477248 | bytes 3440640 | tf_op jit(solution)/shard_map/pallas_call | solution.py:413
  71.1 3.3 %shard_map.103.first_part = bf16[256,384]{1,0:T(8,128)(2,1)S(1)} custom-call(f32[4,1536]{1,0:T(4,128)S(1)} %pad_maximum_fusion.4.extra_ref, bf16[128,384]{1,0:T(8,128)(2,1)S(1)} %get-tuple-element.42.key_ref, bf16[128,384]{1,0:T(8,128)(2,1)S(1)} %get-tuple-element.41.value_ref, bf16[256,1536]{1,0:T(8,128)(2,1)S(1)} %get-tuple-element.25.refs_0_.normed, ...), custom_call_target="tpu_custom_call" | custom-call | flops 377487360 | bytes 3072000 | tf_op jit(solution)/shard_map/pallas_call | solution.py:413
  74.4 0.9 collective-permute-start.25
  75.3 1.8 %collective-permute-start.23 = (bf16[256,384]{1,0:T(8,128)(2,1)S(1)}, bf16[256,384]{1,0:T(8,128)(2,1)S(1)}, u32[]{:S(2)}, u32[]{:S(2)}) collective-permute-start(bf16[256,384]{1,0:T(8,128)(2,1)S(1)} %shard_map.103.first_part), channel_id=1, source_target_pairs={{0,6},{1,7},{2,4},{3,5},{4,2},{5,3},{6,0},{7,1},{8,14},{9,15},{10,... | collective-permute-start | bytes 589832 | tf_op jit(solution)/shard_map/ppermute | solution.py:36
  77.1 5.3 %shard_map.101.weights = bf16[1536,1152]{1,0:T(8,128)(2,1)S(1)} custom-call(bf16[96,1152]{1,0:T(8,128)(2,1)S(1)} %copy-done, bf16[96,1152]{1,0:T(8,128)(2,1)S(1)} %collective-permute-done.8.refs_1_.refs_2_, bf16[96,1152]{1,0:T(8,128)(2,1)S(1)} %collective-permute-done.9.refs_2_.refs_3_, bf16[96,1152]{1,0:T(8,128)(2,1)S(1)} %collective-permute-done.10.refs_3_.refs_4_, ...), custom_call_target="tpu_custom_call" | custom-call | bytes 3538944 | tf_op jit(solution)/shard_map/pallas_call | solution.py:413
  82.5 3.5 %collective-permute-done.23.second_part = bf16[256,384]{1,0:T(8,128)(2,1)S(1)} collective-permute-done((bf16[256,384]{1,0:T(8,128)(2,1)S(1)}, bf16[256,384]{1,0:T(8,128)(2,1)S(1)}, u32[]{:S(2)}, u32[]{:S(2)}) %collective-permute-start.23) | collective-permute-done | bytes 196640 | tf_op jit(solution)/shard_map/ppermute | solution.py:36
  86.0 4.0 %shard_map.104 = (bf16[64,384]{1,0:T(8,128)(2,1)S(1)}, bf16[64,384]{1,0:T(8,128)(2,1)S(1)}, bf16[64,384]{1,0:T(8,128)(2,1)S(1)}, bf16[64,384]{1,0:T(8,128)(2,1)S(1)}, bf16[64,384]{1,0:T(8,128)(2,1)S(1)}) custom-call(f32[4,1536]{1,0:T(4,128)S(1)} %pad_maximum_fusion.4.extra_ref, bf16[128,384]{1,0:T(8,128)(2,1)S(1)} %get-tuple-element.42.key_ref, ...), custom_call_target="tpu_custom_call" | custom-call | flops 1056964608 | bytes 5332992 | tf_op jit(solution)/shard_map/pallas_call | solution.py:413
  90.0 1.2 %collective-permute-start.26 = (bf16[64,384]{1,0:T(8,128)(2,1)S(1)}, bf16[64,384]{1,0:T(8,128)(2,1)S(1)}, u32[]{:S(2)}, u32[]{:S(2)}) collective-permute-start(bf16[64,384]{1,0:T(8,128)(2,1)S(1)} %get-tuple-element.27), channel_id=1, source_target_pairs={{0,2},{1,4},{2,0},{3,6},{4,1},{5,7},{6,3},{7,5},{8,10},{9,12},{10,... | collective-permute-start | bytes 147464 | tf_op jit(solution)/shard_map/ppermute | solution.py:36
  91.2 1.8 %collective-permute-start.28 = (bf16[64,384]{1,0:T(8,128)(2,1)S(1)}, bf16[64,384]{1,0:T(8,128)(2,1)S(1)}, u32[]{:S(2)}, u32[]{:S(2)}) collective-permute-start(bf16[64,384]{1,0:T(8,128)(2,1)S(1)} %get-tuple-element.29), channel_id=1, source_target_pairs={{0,1},{1,7},{2,3},{3,5},{4,2},{5,4},{6,0},{7,6},{8,9},{9,15},{10,1... | collective-permute-start | bytes 147464 | tf_op jit(solution)/shard_map/ppermute | solution.py:36
  93.0 3.8 %collective-permute-start.29 = (bf16[64,384]{1,0:T(8,128)(2,1)S(1)}, bf16[64,384]{1,0:T(8,128)(2,1)S(1)}, u32[]{:S(2)}, u32[]{:S(2)}) collective-permute-start(bf16[64,384]{1,0:T(8,128)(2,1)S(1)} %get-tuple-element.30), channel_id=1, source_target_pairs={{1,6},{3,4},{4,3},{6,1},{9,14},{11,12},{12,11},{14,9},{17,22},{19,... | collective-permute-start | bytes 147464 | tf_op jit(solution)/shard_map/ppermute | solution.py:36
  96.9 2.4 %collective-permute-done.29.fourth = bf16[64,384]{1,0:T(8,128)(2,1)S(1)} collective-permute-done((bf16[64,384]{1,0:T(8,128)(2,1)S(1)}, bf16[64,384]{1,0:T(8,128)(2,1)S(1)}, u32[]{:S(2)}, u32[]{:S(2)}) %collective-permute-start.29) | collective-permute-done | bytes 49184 | tf_op jit(solution)/shard_map/ppermute | solution.py:36
  99.3 0.7 shard_map.105
  (40 shorter events, 0.5 us)
Async XLA Ops:
  0.0 40.4 %copy-start.2 = (f32[2]{0:T(128)S(1)}, f32[2]{0:T(128)}, u32[]{:S(2)}) copy-start(f32[2]{0:T(128)} %param.19) | copy-start | bytes 28
  0.0 42.5 %copy-start.1 = (f32[1536]{0:T(1024)S(1)}, f32[1536]{0:T(1024)}, u32[]{:S(2)}) copy-start(f32[1536]{0:T(1024)} %param.11) | copy-start | bytes 18436
  3.1 10.6 %collective-permute-start = (bf16[8,8,2,384]{3,2,1,0:T(2,128)(2,1)}, bf16[8,8,2,384]{3,2,1,0:T(2,128)(2,1)S(1)}, u32[]{:S(2)}, u32[]{:S(2)}) collective-permute-start(bf16[8,8,2,384]{3,2,1,0:T(2,128)(2,1)} %get-tuple-element.19), channel_id=1, source_target_pairs={{0,1},{1,0},{2,3},{3,2},{4,5},{5,4},{6,7},{7,6},{8,9},{9,8},{10,11... | collective-permute-start | bytes 294920 | tf_op jit(solution)/shard_map/ppermute | solution.py:211
  5.3 61.0 %copy-start = (bf16[96,1152]{1,0:T(8,128)(2,1)S(1)}, bf16[96,1152]{1,0:T(8,128)(2,1)}, u32[]{:S(2)}) copy-start(bf16[96,1152]{1,0:T(8,128)(2,1)} %get-tuple-element.21.refs_0_.refs_1_) | copy-start | bytes 663556
  5.3 34.3 %collective-permute-start.19 = (bf16[96,1152]{1,0:T(8,128)(2,1)}, bf16[96,1152]{1,0:T(8,128)(2,1)S(1)}, u32[]{:S(2)}, u32[]{:S(2)}) collective-permute-start(bf16[96,1152]{1,0:T(8,128)(2,1)} %get-tuple-element.23), channel_id=1, source_target_pairs={{0,12},{1,15},{2,14},{3,13},{4,8},{5,11},{6,10},{7,9},{8,4},{9,7},... | collective-permute-start | bytes 663560 | tf_op jit(solution)/shard_map/ppermute | solution.py:36
  11.1 29.2 %collective-permute-start.11 = (bf16[96,1152]{1,0:T(8,128)(2,1)}, bf16[96,1152]{1,0:T(8,128)(2,1)S(1)}, u32[]{:S(2)}, u32[]{:S(2)}) collective-permute-start(bf16[96,1152]{1,0:T(8,128)(2,1)} %get-tuple-element.23), channel_id=1, source_target_pairs={{0,4},{1,7},{2,6},{3,5},{4,0},{5,3},{6,2},{7,1},{8,12},{9,15},{10,... | collective-permute-start | bytes 663560 | tf_op jit(solution)/shard_map/ppermute | solution.py:36
  11.1 16.4 %collective-permute-start.4 = (bf16[64,1536]{1,0:T(8,128)(2,1)}, bf16[64,1536]{1,0:T(8,128)(2,1)S(1)}, u32[]{:S(2)}, u32[]{:S(2)}) collective-permute-start(bf16[64,1536]{1,0:T(8,128)(2,1)} %param.10), channel_id=1, source_target_pairs={{1,0},{3,2},{4,5},{6,7},{9,8},{11,10},{12,13},{14,15},{17,16},{19,... | collective-permute-start | bytes 589832 | tf_op jit(solution)/shard_map/ppermute | solution.py:36
  12.4 15.3 %collective-permute-start.8 = (bf16[96,1152]{1,0:T(8,128)(2,1)}, bf16[96,1152]{1,0:T(8,128)(2,1)S(1)}, u32[]{:S(2)}, u32[]{:S(2)}) collective-permute-start(bf16[96,1152]{1,0:T(8,128)(2,1)} %get-tuple-element.22), channel_id=1, source_target_pairs={{0,2},{1,3},{2,0},{3,1},{4,6},{5,7},{6,4},{7,5},{8,10},{9,11},{10,... | collective-permute-start | bytes 663560 | tf_op jit(solution)/shard_map/ppermute | solution.py:36
  14.8 10.4 %collective-permute-start.1 = (bf16[2,4,8,2,384]{4,3,2,1,0:T(2,128)(2,1)S(1)}, bf16[2,4,8,2,384]{4,3,2,1,0:T(2,128)(2,1)S(1)}, u32[]{:S(2)}, u32[]{:S(2)}) collective-permute-start(bf16[2,4,8,2,384]{4,3,2,1,0:T(2,128)(2,1)S(1)} %get-tuple-element.38), channel_id=1, source_target_pairs={{0,2},{1,3},{2,0},{3,1},{4,6},{5,7},{6,4},{7,5},{8,10},{9,11},{10,... | collective-permute-start | bytes 294920 | tf_op jit(solution)/shard_map/ppermute | solution.py:211
  25.2 12.9 %collective-permute-start.15 = (bf16[96,1152]{1,0:T(8,128)(2,1)}, bf16[96,1152]{1,0:T(8,128)(2,1)S(1)}, u32[]{:S(2)}, u32[]{:S(2)}) collective-permute-start(bf16[96,1152]{1,0:T(8,128)(2,1)} %get-tuple-element.24), channel_id=1, source_target_pairs={{0,8},{1,11},{2,10},{3,9},{4,12},{5,15},{6,14},{7,13},{8,0},{9,3},... | collective-permute-start | bytes 663560 | tf_op jit(solution)/shard_map/ppermute | solution.py:36
  27.6 12.0 %collective-permute-start.2 = (bf16[4,2,8,2,384]{4,3,2,1,0:T(2,128)(2,1)S(1)}, bf16[4,2,8,2,384]{4,3,2,1,0:T(2,128)(2,1)S(1)}, u32[]{:S(2)}, u32[]{:S(2)}) collective-permute-start(bf16[4,2,8,2,384]{4,3,2,1,0:T(2,128)(2,1)S(1)} %get-tuple-element.36), channel_id=1, source_target_pairs={{0,4},{1,5},{2,6},{3,7},{4,0},{5,1},{6,2},{7,3},{8,12},{9,13},{10,... | collective-permute-start | bytes 294920 | tf_op jit(solution)/shard_map/ppermute | solution.py:211
  27.7 21.4 %collective-permute-start.6 = (bf16[128,1536]{1,0:T(8,128)(2,1)S(1)}, bf16[128,1536]{1,0:T(8,128)(2,1)S(1)}, u32[]{:S(2)}, u32[]{:S(2)}) collective-permute-start(bf16[128,1536]{1,0:T(8,128)(2,1)S(1)} %constant_dynamic-update-slice_fusion.block), channel_id=1, source_target_pairs={{0,4},{2,6},{5,1},{7,3},{8,12},{10,14},{13,9},{15,11},{16,20},{18,... | collective-permute-start | bytes 1179656 | tf_op jit(solution)/shard_map/ppermute | solution.py:36
  38.1 4.4 %collective-permute-start.9 = (bf16[96,1152]{1,0:T(8,128)(2,1)}, bf16[96,1152]{1,0:T(8,128)(2,1)S(1)}, u32[]{:S(2)}, u32[]{:S(2)}) collective-permute-start(bf16[96,1152]{1,0:T(8,128)(2,1)} %get-tuple-element.21.refs_0_.refs_1_), channel_id=1, source_target_pairs={{0,1},{1,0},{2,3},{3,2},{4,5},{5,4},{6,7},{7,6},{8,9},{9,8},{10,11... | collective-permute-start | bytes 663560 | tf_op jit(solution)/shard_map/ppermute | solution.py:36
  39.6 8.1 %collective-permute-start.10 = (bf16[96,1152]{1,0:T(8,128)(2,1)S(1)}, bf16[96,1152]{1,0:T(8,128)(2,1)S(1)}, u32[]{:S(2)}, u32[]{:S(2)}) collective-permute-start(bf16[96,1152]{1,0:T(8,128)(2,1)S(1)} %collective-permute-done.8.refs_1_.refs_2_), channel_id=1, source_target_pairs={{0,1},{1,0},{2,3},{3,2},{4,5},{5,4},{6,7},{7,6},{8,9},{9,8},{10,11... | collective-permute-start | bytes 663560 | tf_op jit(solution)/shard_map/ppermute | solution.py:36
  39.6 8.8 %collective-permute-start.17 = (bf16[96,1152]{1,0:T(8,128)(2,1)S(1)}, bf16[96,1152]{1,0:T(8,128)(2,1)S(1)}, u32[]{:S(2)}, u32[]{:S(2)}) collective-permute-start(bf16[96,1152]{1,0:T(8,128)(2,1)S(1)} %collective-permute-done.15.refs_8_.refs_9_), channel_id=1, source_target_pairs={{0,1},{1,0},{2,3},{3,2},{4,5},{5,4},{6,7},{7,6},{8,9},{9,8},{10,11... | collective-permute-start | bytes 663560 | tf_op jit(solution)/shard_map/ppermute | solution.py:36
  40.3 6.6 %collective-permute-start.3 = (bf16[8,1,8,2,384]{4,3,2,1,0:T(2,128)(2,1)S(1)}, bf16[8,1,8,2,384]{4,3,2,1,0:T(2,128)(2,1)S(1)}, u32[]{:S(2)}, u32[]{:S(2)}) collective-permute-start(bf16[8,1,8,2,384]{4,3,2,1,0:T(2,128)(2,1)S(1)} %get-tuple-element.34), channel_id=1, source_target_pairs={{0,8},{1,9},{2,10},{3,11},{4,12},{5,13},{6,14},{7,15},{8,0},{9,1},... | collective-permute-start | bytes 294920 | tf_op jit(solution)/shard_map/ppermute | solution.py:211
  42.6 21.7 %collective-permute-start.5 = (bf16[128,1536]{1,0:T(8,128)(2,1)S(1)}, bf16[128,1536]{1,0:T(8,128)(2,1)S(1)}, u32[]{:S(2)}, u32[]{:S(2)}) collective-permute-start(bf16[128,1536]{1,0:T(8,128)(2,1)S(1)} %constant_dynamic-update-slice_fusion.block), channel_id=1, source_target_pairs={{0,2},{2,0},{5,7},{7,5},{8,10},{10,8},{13,15},{15,13},{16,18},{18,... | collective-permute-start | bytes 1179656 | tf_op jit(solution)/shard_map/ppermute | solution.py:36
  46.9 6.5 %collective-permute-start.16 = (bf16[96,1152]{1,0:T(8,128)(2,1)S(1)}, bf16[96,1152]{1,0:T(8,128)(2,1)S(1)}, u32[]{:S(2)}, u32[]{:S(2)}) collective-permute-start(bf16[96,1152]{1,0:T(8,128)(2,1)S(1)} %collective-permute-done.15.refs_8_.refs_9_), channel_id=1, source_target_pairs={{0,16},{1,17},{2,18},{3,19},{4,20},{5,21},{6,22},{7,23},{8,24},{9,... | collective-permute-start | bytes 663560 | tf_op jit(solution)/shard_map/ppermute | solution.py:36
  47.6 10.6 %collective-permute-start.20 = (bf16[96,1152]{1,0:T(8,128)(2,1)S(1)}, bf16[96,1152]{1,0:T(8,128)(2,1)S(1)}, u32[]{:S(2)}, u32[]{:S(2)}) collective-permute-start(bf16[96,1152]{1,0:T(8,128)(2,1)S(1)} %collective-permute-done.19.refs_12_.refs_0_), channel_id=1, source_target_pairs={{0,16},{1,17},{2,18},{3,19},{4,20},{5,21},{6,22},{7,23},{8,24},{9,... | collective-permute-start | bytes 663560 | tf_op jit(solution)/shard_map/ppermute | solution.py:36
  48.4 14.5 %collective-permute-start.12 = (bf16[96,1152]{1,0:T(8,128)(2,1)S(1)}, bf16[96,1152]{1,0:T(8,128)(2,1)S(1)}, u32[]{:S(2)}, u32[]{:S(2)}) collective-permute-start(bf16[96,1152]{1,0:T(8,128)(2,1)S(1)} %collective-permute-done.11.refs_4_.refs_5_), channel_id=1, source_target_pairs={{0,16},{1,17},{2,18},{3,19},{4,20},{5,21},{6,22},{7,23},{8,24},{9,... | collective-permute-start | bytes 663560 | tf_op jit(solution)/shard_map/ppermute | solution.py:36
  49.1 15.2 %collective-permute-start.7 = (bf16[128,1536]{1,0:T(8,128)(2,1)S(1)}, bf16[128,1536]{1,0:T(8,128)(2,1)S(1)}, u32[]{:S(2)}, u32[]{:S(2)}) collective-permute-start(bf16[128,1536]{1,0:T(8,128)(2,1)S(1)} %collective-permute-done.6.far), channel_id=1, source_target_pairs={{1,3},{3,1},{4,6},{6,4},{9,11},{11,9},{12,14},{14,12},{17,19},{19,... | collective-permute-start | bytes 1179656 | tf_op jit(solution)/shard_map/ppermute | solution.py:36
  53.5 17.6 %collective-permute-start.21 = (bf16[96,1152]{1,0:T(8,128)(2,1)S(1)}, bf16[96,1152]{1,0:T(8,128)(2,1)S(1)}, u32[]{:S(2)}, u32[]{:S(2)}) collective-permute-start(bf16[96,1152]{1,0:T(8,128)(2,1)S(1)} %collective-permute-done.19.refs_12_.refs_0_), channel_id=1, source_target_pairs={{0,1},{1,0},{2,3},{3,2},{4,5},{5,4},{6,7},{7,6},{8,9},{9,8},{10,11... | collective-permute-start | bytes 663560 | tf_op jit(solution)/shard_map/ppermute | solution.py:36
  58.2 8.0 %collective-permute-start.13 = (bf16[96,1152]{1,0:T(8,128)(2,1)S(1)}, bf16[96,1152]{1,0:T(8,128)(2,1)S(1)}, u32[]{:S(2)}, u32[]{:S(2)}) collective-permute-start(bf16[96,1152]{1,0:T(8,128)(2,1)S(1)} %collective-permute-done.11.refs_4_.refs_5_), channel_id=1, source_target_pairs={{0,1},{1,0},{2,3},{3,2},{4,5},{5,4},{6,7},{7,6},{8,9},{9,8},{10,11... | collective-permute-start | bytes 663560 | tf_op jit(solution)/shard_map/ppermute | solution.py:36
  63.0 3.3 %collective-permute-start.18 = (bf16[96,1152]{1,0:T(8,128)(2,1)S(1)}, bf16[96,1152]{1,0:T(8,128)(2,1)S(1)}, u32[]{:S(2)}, u32[]{:S(2)}) collective-permute-start(bf16[96,1152]{1,0:T(8,128)(2,1)S(1)} %collective-permute-done.16.refs_9_.refs_10_), channel_id=1, source_target_pairs={{0,1},{1,0},{2,3},{3,2},{4,5},{5,4},{6,7},{7,6},{8,9},{9,8},{10,11... | collective-permute-start | bytes 663560 | tf_op jit(solution)/shard_map/ppermute | solution.py:36
  64.3 6.8 %collective-permute-start.22 = (bf16[96,1152]{1,0:T(8,128)(2,1)S(1)}, bf16[96,1152]{1,0:T(8,128)(2,1)S(1)}, u32[]{:S(2)}, u32[]{:S(2)}) collective-permute-start(bf16[96,1152]{1,0:T(8,128)(2,1)S(1)} %collective-permute-done.20.refs_13_.refs_1_), channel_id=1, source_target_pairs={{0,1},{1,0},{2,3},{3,2},{4,5},{5,4},{6,7},{7,6},{8,9},{9,8},{10,11... | collective-permute-start | bytes 663560 | tf_op jit(solution)/shard_map/ppermute | solution.py:36
  64.3 2.0 %collective-permute-start.14 = (bf16[96,1152]{1,0:T(8,128)(2,1)S(1)}, bf16[96,1152]{1,0:T(8,128)(2,1)S(1)}, u32[]{:S(2)}, u32[]{:S(2)}) collective-permute-start(bf16[96,1152]{1,0:T(8,128)(2,1)S(1)} %collective-permute-done.12.refs_5_.refs_6_), channel_id=1, source_target_pairs={{0,1},{1,0},{2,3},{3,2},{4,5},{5,4},{6,7},{7,6},{8,9},{9,8},{10,11... | collective-permute-start | bytes 663560 | tf_op jit(solution)/shard_map/ppermute | solution.py:36
  74.4 8.0 %collective-permute-start.25 = (bf16[256,384]{1,0:T(8,128)(2,1)S(1)}, bf16[256,384]{1,0:T(8,128)(2,1)S(1)}, u32[]{:S(2)}, u32[]{:S(2)}) collective-permute-start(bf16[256,384]{1,0:T(8,128)(2,1)S(1)} %shard_map.103.first_part), channel_id=1, source_target_pairs={{0,2},{1,3},{2,0},{3,1},{4,6},{5,7},{6,4},{7,5},{8,10},{9,11},{10,... | collective-permute-start | bytes 589832 | tf_op jit(solution)/shard_map/ppermute | solution.py:36
  75.3 7.2 %collective-permute-start.24 = (bf16[256,384]{1,0:T(8,128)(2,1)S(1)}, bf16[256,384]{1,0:T(8,128)(2,1)S(1)}, u32[]{:S(2)}, u32[]{:S(2)}) collective-permute-start(bf16[256,384]{1,0:T(8,128)(2,1)S(1)} %shard_map.103.first_part), channel_id=1, source_target_pairs={{0,4},{1,5},{2,6},{3,7},{4,0},{5,1},{6,2},{7,3},{8,12},{9,13},{10,... | collective-permute-start | bytes 589832 | tf_op jit(solution)/shard_map/ppermute | solution.py:36
  75.3 10.7 %collective-permute-start.23 = (bf16[256,384]{1,0:T(8,128)(2,1)S(1)}, bf16[256,384]{1,0:T(8,128)(2,1)S(1)}, u32[]{:S(2)}, u32[]{:S(2)}) collective-permute-start(bf16[256,384]{1,0:T(8,128)(2,1)S(1)} %shard_map.103.first_part), channel_id=1, source_target_pairs={{0,6},{1,7},{2,4},{3,5},{4,2},{5,3},{6,0},{7,1},{8,14},{9,15},{10,... | collective-permute-start | bytes 589832 | tf_op jit(solution)/shard_map/ppermute | solution.py:36
  90.0 6.8 %collective-permute-start.26 = (bf16[64,384]{1,0:T(8,128)(2,1)S(1)}, bf16[64,384]{1,0:T(8,128)(2,1)S(1)}, u32[]{:S(2)}, u32[]{:S(2)}) collective-permute-start(bf16[64,384]{1,0:T(8,128)(2,1)S(1)} %get-tuple-element.27), channel_id=1, source_target_pairs={{0,2},{1,4},{2,0},{3,6},{4,1},{5,7},{6,3},{7,5},{8,10},{9,12},{10,... | collective-permute-start | bytes 147464 | tf_op jit(solution)/shard_map/ppermute | solution.py:36
  91.2 5.7 %collective-permute-start.27 = (bf16[64,384]{1,0:T(8,128)(2,1)S(1)}, bf16[64,384]{1,0:T(8,128)(2,1)S(1)}, u32[]{:S(2)}, u32[]{:S(2)}) collective-permute-start(bf16[64,384]{1,0:T(8,128)(2,1)S(1)} %get-tuple-element.28), channel_id=1, source_target_pairs={{0,3},{1,5},{2,1},{3,7},{4,0},{5,6},{6,2},{7,4},{8,11},{9,13},{10,... | collective-permute-start | bytes 147464 | tf_op jit(solution)/shard_map/ppermute | solution.py:36
  91.2 5.7 %collective-permute-start.28 = (bf16[64,384]{1,0:T(8,128)(2,1)S(1)}, bf16[64,384]{1,0:T(8,128)(2,1)S(1)}, u32[]{:S(2)}, u32[]{:S(2)}) collective-permute-start(bf16[64,384]{1,0:T(8,128)(2,1)S(1)} %get-tuple-element.29), channel_id=1, source_target_pairs={{0,1},{1,7},{2,3},{3,5},{4,2},{5,4},{6,0},{7,6},{8,9},{9,15},{10,1... | collective-permute-start | bytes 147464 | tf_op jit(solution)/shard_map/ppermute | solution.py:36
  93.0 6.3 %collective-permute-start.29 = (bf16[64,384]{1,0:T(8,128)(2,1)S(1)}, bf16[64,384]{1,0:T(8,128)(2,1)S(1)}, u32[]{:S(2)}, u32[]{:S(2)}) collective-permute-start(bf16[64,384]{1,0:T(8,128)(2,1)S(1)} %get-tuple-element.30), channel_id=1, source_target_pairs={{1,6},{3,4},{4,3},{6,1},{9,14},{11,12},{12,11},{14,9},{17,22},{19,... | collective-permute-start | bytes 147464 | tf_op jit(solution)/shard_map/ppermute | solution.py:36

commit v4 on v3

--- a/solution.py
+++ b/solution.py
@@ -111,19 +111,23 @@
 
 
 def pack_memory_kernel(
-    list_hbm, slot_hbm, mem_ref, kept_ref, sent_ref, list_ref, slot_ref, stored, scalar_sem, mem_sem, give_sem
+    list_hbm, slot_hbm, count_hbm, scale_hbm, gain_hbm, mem_ref, kept_ref, sent_ref, extra_ref,
+    list_ref, slot_ref, count_ref, scale_ref, stored, extra, scalar_sem, mem_sem, give_sem,
 ):
-    _, index, _, _, _ = here()
+    _, index, plane, _, c = here()
     devices = lax.axis_size("frame")
     frames, entries = list_ref.shape
     width = kept_ref.shape[-1]
     scalars = [
         pltpu.make_async_copy(list_hbm, list_ref, scalar_sem.at[0]),
         pltpu.make_async_copy(slot_hbm, slot_ref, scalar_sem.at[1]),
+        pltpu.make_async_copy(count_hbm, count_ref, scalar_sem.at[2]),
+        pltpu.make_async_copy(scale_hbm, scale_ref, scalar_sem.at[3]),
+        pltpu.make_async_copy(gain_hbm, extra.at[pl.ds(0, 1)], scalar_sem.at[4]),
     ]
     for copy in scalars:
         copy.start()
-    for copy in scalars:
+    for copy in scalars[:2]:
         copy.wait()
     picks = []
     for frame in range(frames):
@@ -132,9 +136,17 @@
             row = slot_ref[list_ref[frame, entry]]
             picks.append(pltpu.make_async_copy(mem_ref.at[row, 0], stored.at[number], mem_sem.at[number]))
             picks[-1].start()
+    for copy in scalars[2:]:
+        copy.wait()
+    row = (1, extra.shape[1])
+    for number in range(STEPS):
+        extra[1 + number : 2 + number, :] = jnp.full(row, scale_ref[number], jnp.float32)
+    live = lax.broadcasted_iota(jnp.int32, row, 1) % entries < count_ref[(plane // 2) * 2 + c]
+    extra[1 + STEPS : 2 + STEPS, :] = jnp.where(live, 1.0, 0.0)
     for pick in picks:
         pick.wait()
-    gives = []
+    gives = [pltpu.make_async_copy(extra, extra_ref, scalar_sem.at[5])]
+    gives[0].start()
     bits = devices.bit_length() - 1
     for away in range(devices):
         target = flipped(index, away)
@@ -156,7 +168,7 @@
         give.wait()
 
 
-def pack_memory(mem_cache, intersection, slot_of):
+def pack_memory(mem_cache, intersection, slot_of, counts, step_scale, norm_gain):
     devices = lax.axis_size("frame")
     features = mem_cache.shape[-1]
     frames, entries = intersection.shape
@@ -165,19 +177,22 @@
     held = pl.BlockSpec(memory_space=pltpu.HBM)
     return pl.pallas_call(
         pack_memory_kernel,
-        out_shape=(half,) * 2,
-        in_specs=[held] * 3,
-        out_specs=(anywhere,) * 2,
+        out_shape=(half, half, jax.ShapeDtypeStruct((2 + STEPS, features), jnp.float32)),
+        in_specs=[held] * 6,
+        out_specs=(anywhere,) * 3,
         scratch_shapes=[
             pltpu.SMEM(intersection.shape, intersection.dtype),
             pltpu.SMEM(slot_of.shape, slot_of.dtype),
+            pltpu.SMEM(counts.shape, counts.dtype),
+            pltpu.SMEM(step_scale.shape, step_scale.dtype),
             pltpu.VMEM((frames * entries, 2, features), mem_cache.dtype),
-            pltpu.SemaphoreType.DMA((2,)),
+            pltpu.VMEM((2 + STEPS, features), jnp.float32),
+            pltpu.SemaphoreType.DMA((6,)),
             pltpu.SemaphoreType.DMA((frames * entries,)),
             pltpu.SemaphoreType.DMA((devices,)),
         ],
         name="pack_memory",
-    )(intersection, slot_of, mem_cache)
+    )(intersection, slot_of, counts, step_scale, norm_gain.reshape(1, -1), mem_cache)
 
 
 def all_pieces(own, beside, even, odd):
@@ -233,13 +248,10 @@
     return pl.multiple_of((plane_number * 4 + from_y * 2 + from_c) * shard_rows, 16)
 
 
-def gather_pieces(piece_refs, places, first_plane, weights, sem):
-    copies = []
-    for number, (ref, place) in enumerate(zip(piece_refs, places)):
+def gather_pieces(piece_refs, places, first_plane, weights):
+    for ref, place in zip(piece_refs, places):
         start = piece_start(place, ref.shape[0], place[0] - first_plane)
-        copies.append(pltpu.make_async_copy(ref, weights.at[pl.ds(start, ref.shape[0])], sem.at[number]))
-        copies[-1].start()
-    return copies
+        weights[pl.ds(start, ref.shape[0]), :] = ref[...]
 
 
 def store_normed(current, rows, inverse, gain_ref, normed):
@@ -255,10 +267,12 @@
 BLOCK = 32
 
 
-def prepare_kernel(extra_ref, block, near, far, far_near, current, normed, token_sem):
+def prepare_kernel(extra_ref, block, near, far, far_near, extra, current, normed, token_sem):
     _, _, plane, y, c = here()
     chip_rows = block.shape[0]
     at_home = plane % 2 == c
+    extra_copy = pltpu.make_async_copy(extra_ref, extra, token_sem.at[2])
+    extra_copy.start()
 
     def token_copies(first, second):
         return (
@@ -278,27 +292,26 @@
 
     for copy in token_copies(block, near):
         copy.wait()
+    extra_copy.wait()
 
     @pl.loop(0, current.shape[0] // BLOCK)
     def _(number):
         rows = pl.ds(pl.multiple_of(number * BLOCK, BLOCK), BLOCK)
         widened = current[rows, :].astype(jnp.float32)
         inverse = lax.rsqrt(jnp.mean(widened * widened, axis=-1, keepdims=True) + 1e-06)
-        store_normed(current, rows, inverse, extra_ref, normed)
+        store_normed(current, rows, inverse, extra, normed)
 
 
 def project_kernel(places, *refs):
     normed = refs[0]
     piece_refs = refs[1 : 1 + len(places)]
-    out, weights, sem = refs[1 + len(places) :]
-    for copy in gather_pieces(piece_refs, places, 0, weights, sem):
-        copy.wait()
+    out, weights = refs[1 + len(places) :]
+    gather_pieces(piece_refs, places, 0, weights)
     out[...] = jnp.dot(normed[:, : weights.shape[0]], weights[...], preferred_element_type=jnp.float32)
 
 
 def assemble_kernel(places, *refs):
-    for copy in gather_pieces(refs[:-2], places, 0, refs[-2], refs[-1]):
-        copy.wait()
+    gather_pieces(refs[:-1], places, 0, refs[-1])
 
 
 def attend_heads(projected, key_ref, value_ref, extra_ref, attended, head_count):
@@ -340,9 +353,8 @@
 
 def step_kernel(places, first_plane, head_count, extra_ref, key_ref, value_ref, normed, part_ref, *refs):
     piece_refs = refs[: len(places)]
-    attended, weights, projected, sem = refs[len(places) :]
-    for copy in gather_pieces(piece_refs, places, first_plane, weights, sem):
-        copy.wait()
+    attended, weights, projected = refs[len(places) :]
+    gather_pieces(piece_refs, places, first_plane, weights)
     early = normed.shape[1] - weights.shape[0]
     projected[...] = (
         part_ref[...] + jnp.dot(normed[:, early:], weights[...], preferred_element_type=jnp.float32)
@@ -424,8 +436,13 @@
 def prepare(extra, tokens):
     frame = jax.ShapeDtypeStruct((2 * tokens[0].shape[0], tokens[0].shape[1]), tokens[0].dtype)
     return kernel_call(
-        prepare_kernel, (frame, frame), (extra, *tokens), range(1, 5), [pltpu.SemaphoreType.DMA((2,))],
-        8 * MIB, 0,
+        prepare_kernel,
+        (jax.ShapeDtypeStruct(extra.shape, extra.dtype), frame, frame),
+        (extra, *tokens),
+        range(5),
+        [pltpu.SemaphoreType.DMA((3,))],
+        8 * MIB,
+        0,
     )
 
 
@@ -436,8 +453,8 @@
         functools.partial(project_kernel, tuple(place for _, place in pieces)),
         jax.ShapeDtypeStruct((normed.shape[0], width), jnp.float32),
         (normed, *[array for array, _ in pieces]),
-        range(1, 1 + len(pieces)),
-        [pltpu.VMEM((depth, width), normed.dtype), pltpu.SemaphoreType.DMA((len(pieces),))],
+        (),
+        [pltpu.VMEM((depth, width), normed.dtype)],
         16 * MIB,
         2 * normed.shape[0] * depth * width,
     )
@@ -449,8 +466,8 @@
         functools.partial(assemble_kernel, tuple(place for _, place in pieces)),
         jax.ShapeDtypeStruct((rows * len(pieces), width), pieces[0][0].dtype),
         [array for array, _ in pieces],
-        range(len(pieces)),
-        [pltpu.SemaphoreType.DMA((len(pieces),))],
+        (),
+        [],
         8 * MIB,
         0,
     )
@@ -464,12 +481,8 @@
         functools.partial(step_kernel, tuple(place for _, place in pieces), pieces[0][1][0], HEADS // SPATIAL),
         jax.ShapeDtypeStruct((frame_rows, width // 3), normed.dtype),
         (extra, keys, values, normed, part, *[array for array, _ in pieces]),
-        range(5, 5 + len(pieces)),
-        [
-            pltpu.VMEM((depth, width), normed.dtype),
-            pltpu.VMEM((frame_rows, width), normed.dtype),
-            pltpu.SemaphoreType.DMA((len(pieces),)),
-        ],
+        (),
+        [pltpu.VMEM((depth, width), normed.dtype), pltpu.VMEM((frame_rows, width), normed.dtype)],
         16 * MIB,
         2 * frame_rows * width * (depth + frame_rows),
     )
@@ -538,23 +551,15 @@
     )
 
 
-def small_operands(norm_gain, step_scale, counts, entries):
-    features = norm_gain.shape[0]
-    _, _, plane, _, c = here()
-    live = jnp.arange(features, dtype=jnp.int32) % entries < counts[(plane // 2) * 2 + c]
-    scales = [jnp.full((features,), step_scale[number]) for number in range(STEPS)]
-    return jnp.stack([norm_gain, *scales, live.astype(jnp.float32)])
-
-
 def paired_planes(
     latent, norm_gain, w_query, w_key, w_value, mem_cache, intersection, counts, slot_of, step_scale
 ):
     late = late_plane(lax.axis_size("frame"))
     pieces = sorted(all_pieces(*pack_weights(w_query, w_key, w_value)), key=lambda piece: piece[1][0])
     tokens = all_tokens(latent)
-    keys, values = all_memory(*pack_memory(mem_cache, intersection, slot_of))
-    extra = small_operands(norm_gain, step_scale, counts, intersection.shape[1])
-    current, normed = prepare(extra, tokens)
+    kept, sent, extra = pack_memory(mem_cache, intersection, slot_of, counts, step_scale, norm_gain)
+    keys, values = all_memory(kept, sent)
+    extra, current, normed = prepare(extra, tokens)
     part = project(normed, [piece for piece in pieces if piece[1][0] < late])
     attended = step(extra, keys, values, normed, part, [piece for piece in pieces if piece[1][0] == late])
     updates = [

time: 100 us -> 99.1 us (level)
  starting transfers between devices: 35.4 us -> 57 us
  waiting for transfers between devices: 32.5 us -> 22.1 us
  Pallas kernels: 24.8 us -> 15 us
  local copies, waits for them, and re-layouts: 4.35 us -> 2.29 us
    ppermute x4, starting transfers between devices: 0.56 us -> 16.6 us  [hop(): lax.ppermute(array, 'frame', [(i, i ^ 1 << bit) for i in range(lax.axis_s...]
    pallas_call x6, Pallas kernels: 19.6 us -> 9.89 us  [kernel_call(): pl.pallas_call(kernel, out_shape=out_shape, in_specs=[free if number in a...]
    ppermute x4, waiting for transfers between devices: 11.5 us -> 5.68 us  [hop(): lax.ppermute(array, 'frame', [(i, i ^ 1 << bit) for i in range(lax.axis_s...]
    ppermute x26, starting transfers between devices: 34.8 us -> 40.3 us  [moved(): return lax.ppermute(array, AXES, pairs)]
    ppermute x26, waiting for transfers between devices: 21 us -> 16.4 us  [moved(): return lax.ppermute(array, AXES, pairs)]
    another operation x3 -> x0, local copies, waits for them, and re-layouts: 1.47 us -> none  [small_operands(): return jnp.stack([norm_gain, *scales, live.astype(jnp.float32)])]
    reshape x0 -> x1, local copies, waits for them, and re-layouts: none -> 1.3 us  [pack_memory(): norm_gain.reshape(1, -1)]
    dynamic_slice x1 -> x0, local copies, waits for them, and re-layouts: 1.24 us -> none  [small_operands(): counts[plane // 2 * 2 + c]]
  transfers between devices with their start and end apart: 30 -> 30, of which waited for: 8 -> 9; matrix products, arithmetic and copies ran while one was open for 7% -> 4% of each run, Pallas kernels for 14% -> 8%
where the time goes in v4:
time: 99.1 us; the launch traced here: 98.6 us
  starting transfers between devices  57 us (58%)
  waiting for transfers between devices  22.1 us (22%)
  Pallas kernels  15 us (15%)
  local copies, waits for them, and re-layouts  2.29 us (2%)
  other arithmetic  1.95 us (2%)
    ppermute x26, starting transfers between devices, moved(): return lax.ppermute(array, AXES, pairs)  40.3 us
    ppermute x4, starting transfers between devices, hop(): lax.ppermute(array, 'frame', [(i, i ^ 1 << bit) for i in range(lax.axis_s...  16.6 us
    ppermute x26, waiting for transfers between devices, moved(): return lax.ppermute(array, AXES, pairs)  16.4 us
    pallas_call x6, Pallas kernels, kernel_call(): pl.pallas_call(kernel, out_shape=out_shape, in_specs=[free if number in a...  9.89 us
    ppermute x4, waiting for transfers between devices, hop(): lax.ppermute(array, 'frame', [(i, i ^ 1 << bit) for i in range(lax.axis_s...  5.68 us
    pallas_call x1, Pallas kernels, pack_memory(): pl.pallas_call(pack_memory_kernel, out_shape=(half, half, jax.ShapeDtypeS...  3.03 us
    pallas_call x1, Pallas kernels, pack_weights(): pl.pallas_call(pack_weights_kernel, out_shape=(piece,) * 4, in_specs=[hel...  2.06 us
  transfers between devices with their start and end apart: 30, of which 9 were waited for; matrix products, arithmetic and copies ran while one was open for 4% of the time, Pallas kernels for 8%

profile of v4, /device:TPU:1, one launch (start us, length us, event | category | flops | bytes accessed | tf_op | source)
XLA Modules:
  0.0 98.6 jit_solution(906232673007892296)
XLA Ops:
  0.0 1.9 %collective-permute-start = (bf16[64,1536]{1,0:T(8,128)(2,1)}, bf16[64,1536]{1,0:T(8,128)(2,1)S(1)}, u32[]{:S(2)}, u32[]{:S(2)}) collective-permute-start(bf16[64,1536]{1,0:T(8,128)(2,1)} %param.10), channel_id=1, source_target_pairs={{1,0},{3,2},{4,5},{6,7},{9,8},{11,10},{12,13},{14,15},{17,16},{19,... | collective-permute-start | bytes 589832 | tf_op jit(solution)/shard_map/ppermute | solution.py:36
  1.9 1.3 %reshape.3.gain_hbm = f32[1,1536]{1,0:T(1,128)} reshape(f32[1536]{0:T(1024)} %param.11) | data formatting | bytes 12288 | tf_op jit(solution)/shard_map/reshape | solution.py:195
  3.2 3.0 %pack_memory.1 = (bf16[8,8,2,384]{3,2,1,0:T(2,128)(2,1)}, bf16[8,8,2,384]{3,2,1,0:T(2,128)(2,1)}, f32[4,1536]{1,0:T(4,128)}) custom-call(s32[4,8]{1,0:T(4,128)} %list_hbm.1, s32[128]{0:T(128)} %slot_hbm.1, s32[4]{0:T(128)} %count_hbm.1, f32[2]{0:T(128)} %scale_hbm.1, f32[1,1536]{1,0:T(1,128)} %reshape.3.gain_hbm, bf16[128,1,2,1536]{3,2,1,0:T(2,128)(2,1)} %mem_ref.1), custom_call_target="tpu_custom_call" | custom-call | tf_op jit(solution)/shard_map/pack_memory/pallas_call | solution.py:178
  6.3 0.1 collective-permute-start.4
  6.4 2.1 %pack_weights.1 = (bf16[96,1152]{1,0:T(8,128)(2,1)}, bf16[96,1152]{1,0:T(8,128)(2,1)}, bf16[96,1152]{1,0:T(8,128)(2,1)}, bf16[96,1152]{1,0:T(8,128)(2,1)}) custom-call(bf16[96,1536]{1,0:T(8,128)(2,1)} %w_query.1, bf16[96,1536]{1,0:T(8,128)(2,1)} %w_key.1, bf16[96,1536]{1,0:T(8,128)(2,1)} %w_value.1), custom_call_target="tpu_custom_call" | custom-call | tf_op jit(solution)/shard_map/pack_weights/pallas_call | solution.py:99
  8.4 2.8 %collective-permute-start.8 = (bf16[96,1152]{1,0:T(8,128)(2,1)}, bf16[96,1152]{1,0:T(8,128)(2,1)S(1)}, u32[]{:S(2)}, u32[]{:S(2)}) collective-permute-start(bf16[96,1152]{1,0:T(8,128)(2,1)} %get-tuple-element.26), channel_id=1, source_target_pairs={{0,2},{1,3},{2,0},{3,1},{4,6},{5,7},{6,4},{7,5},{8,10},{9,11},{10,... | collective-permute-start | bytes 663560 | tf_op jit(solution)/shard_map/ppermute | solution.py:36
  11.2 0.9 constant_dynamic-update-slice_fusion.1
  12.2 1.3 %collective-permute-start.2 = (bf16[128,1536]{1,0:T(8,128)(2,1)S(1)}, bf16[128,1536]{1,0:T(8,128)(2,1)S(1)}, u32[]{:S(2)}, u32[]{:S(2)}) collective-permute-start(bf16[128,1536]{1,0:T(8,128)(2,1)S(1)} %constant_dynamic-update-slice_fusion.block), channel_id=1, source_target_pairs={{0,4},{2,6},{5,1},{7,3},{8,12},{10,14},{13,9},{15,11},{16,20},{18,... | collective-permute-start | bytes 1179656 | tf_op jit(solution)/shard_map/ppermute | solution.py:36
  13.5 1.1 %fusion.2 = (bf16[2,4,8,2,384]{4,3,2,1,0:T(2,128)(2,1)S(1)}, bf16[2,4,8,2,384]{4,3,2,1,0:T(2,128)(2,1)S(1)}) fusion(bf16[1,8,8,2,384]{4,3,2,1,0:T(2,128)(2,1)} %bitcast.6, bf16[1,8,8,2,384]{4,3,2,1,0:T(2,128)(2,1)S(1)} %bitcast.7), kind=kLoop, calls=%fused_computation.10 | loop fusion | flops 98304 | bytes 393216 | tf_op jit(solution)/shard_map/stack | solution.py:217
  14.6 0.1 collective-permute-start.5
  14.7 3.4 %collective-permute-start.15 = (bf16[96,1152]{1,0:T(8,128)(2,1)}, bf16[96,1152]{1,0:T(8,128)(2,1)S(1)}, u32[]{:S(2)}, u32[]{:S(2)}) collective-permute-start(bf16[96,1152]{1,0:T(8,128)(2,1)} %get-tuple-element.28), channel_id=1, source_target_pairs={{0,8},{1,11},{2,10},{3,9},{4,12},{5,15},{6,14},{7,13},{8,0},{9,3},... | collective-permute-start | bytes 663560 | tf_op jit(solution)/shard_map/ppermute | solution.py:36
  18.2 1.8 %collective-permute-start.19 = (bf16[96,1152]{1,0:T(8,128)(2,1)}, bf16[96,1152]{1,0:T(8,128)(2,1)S(1)}, u32[]{:S(2)}, u32[]{:S(2)}) collective-permute-start(bf16[96,1152]{1,0:T(8,128)(2,1)} %get-tuple-element.27), channel_id=1, source_target_pairs={{0,12},{1,15},{2,14},{3,13},{4,8},{5,11},{6,10},{7,9},{8,4},{9,7},... | collective-permute-start | bytes 663560 | tf_op jit(solution)/shard_map/ppermute | solution.py:36
  20.0 1.4 %collective-permute-start.11 = (bf16[96,1152]{1,0:T(8,128)(2,1)}, bf16[96,1152]{1,0:T(8,128)(2,1)S(1)}, u32[]{:S(2)}, u32[]{:S(2)}) collective-permute-start(bf16[96,1152]{1,0:T(8,128)(2,1)} %get-tuple-element.27), channel_id=1, source_target_pairs={{0,4},{1,7},{2,6},{3,5},{4,0},{5,3},{6,2},{7,1},{8,12},{9,15},{10,... | collective-permute-start | bytes 663560 | tf_op jit(solution)/shard_map/ppermute | solution.py:36
  21.4 2.2 %collective-permute-start.9 = (bf16[96,1152]{1,0:T(8,128)(2,1)}, bf16[96,1152]{1,0:T(8,128)(2,1)S(1)}, u32[]{:S(2)}, u32[]{:S(2)}) collective-permute-start(bf16[96,1152]{1,0:T(8,128)(2,1)} %get-tuple-element.25.refs_0_.refs_1_), channel_id=1, source_target_pairs={{0,1},{1,0},{2,3},{3,2},{4,5},{5,4},{6,7},{7,6},{8,9},{9,8},{10,11... | collective-permute-start | bytes 663560 | tf_op jit(solution)/shard_map/ppermute | solution.py:36
  23.6 0.3 fusion.1
  23.8 11.1 %collective-permute-start.6 = (bf16[4,2,8,2,384]{4,3,2,1,0:T(2,128)(2,1)S(1)}, bf16[4,2,8,2,384]{4,3,2,1,0:T(2,128)(2,1)S(1)}, u32[]{:S(2)}, u32[]{:S(2)}) collective-permute-start(bf16[4,2,8,2,384]{4,3,2,1,0:T(2,128)(2,1)S(1)} %get-tuple-element.40), channel_id=1, source_target_pairs={{0,4},{1,5},{2,6},{3,7},{4,0},{5,1},{6,2},{7,3},{8,12},{9,13},{10,... | collective-permute-start | bytes 294920 | tf_op jit(solution)/shard_map/ppermute | solution.py:226
  34.9 0.9 collective-permute-start.10
  35.8 0.1 collective-permute-start.17
  35.9 1.0 collective-permute-done.6
  36.9 0.7 collective-permute-start.1
  37.6 2.1 %collective-permute-start.3 = (bf16[128,1536]{1,0:T(8,128)(2,1)S(1)}, bf16[128,1536]{1,0:T(8,128)(2,1)S(1)}, u32[]{:S(2)}, u32[]{:S(2)}) collective-permute-start(bf16[128,1536]{1,0:T(8,128)(2,1)S(1)} %collective-permute-done.2.far), channel_id=1, source_target_pairs={{1,3},{3,1},{4,6},{6,4},{9,11},{11,9},{12,14},{14,12},{17,19},{19,... | collective-permute-start | bytes 1179656 | tf_op jit(solution)/shard_map/ppermute | solution.py:36
  39.7 0.3 fusion
  40.0 5.4 %collective-permute-start.7 = (bf16[8,1,8,2,384]{4,3,2,1,0:T(2,128)(2,1)S(1)}, bf16[8,1,8,2,384]{4,3,2,1,0:T(2,128)(2,1)S(1)}, u32[]{:S(2)}, u32[]{:S(2)}) collective-permute-start(bf16[8,1,8,2,384]{4,3,2,1,0:T(2,128)(2,1)S(1)} %get-tuple-element.38), channel_id=1, source_target_pairs={{0,8},{1,9},{2,10},{3,11},{4,12},{5,13},{6,14},{7,15},{8,0},{9,1},... | collective-permute-start | bytes 294920 | tf_op jit(solution)/shard_map/ppermute | solution.py:226
  45.4 4.7 %collective-permute-done.7 = bf16[8,1,8,2,384]{4,3,2,1,0:T(2,128)(2,1)S(1)} collective-permute-done((bf16[8,1,8,2,384]{4,3,2,1,0:T(2,128)(2,1)S(1)}, bf16[8,1,8,2,384]{4,3,2,1,0:T(2,128)(2,1)S(1)}, u32[]{:S(2)}, u32[]{:S(2)}) %collective-permute-start.7) | collective-permute-done | bytes 98336 | tf_op jit(solution)/shard_map/ppermute | solution.py:226
  50.1 1.5 %collective-permute-start.20 = (bf16[96,1152]{1,0:T(8,128)(2,1)S(1)}, bf16[96,1152]{1,0:T(8,128)(2,1)S(1)}, u32[]{:S(2)}, u32[]{:S(2)}) collective-permute-start(bf16[96,1152]{1,0:T(8,128)(2,1)S(1)} %collective-permute-done.19.refs_12_.refs_0_), channel_id=1, source_target_pairs={{0,16},{1,17},{2,18},{3,19},{4,20},{5,21},{6,22},{7,23},{8,24},{9,... | collective-permute-start | bytes 663560 | tf_op jit(solution)/shard_map/ppermute | solution.py:36
  51.6 0.3 pad_maximum_fusion
  51.9 3.8 %collective-permute-done.16.refs_9_.refs_10_ = bf16[96,1152]{1,0:T(8,128)(2,1)S(1)} collective-permute-done((bf16[96,1152]{1,0:T(8,128)(2,1)S(1)}, bf16[96,1152]{1,0:T(8,128)(2,1)S(1)}, u32[]{:S(2)}, u32[]{:S(2)}) %collective-permute-start.16) | collective-permute-done | bytes 221216 | tf_op jit(solution)/shard_map/ppermute | solution.py:36
  55.8 3.9 %collective-permute-start.21 = (bf16[96,1152]{1,0:T(8,128)(2,1)S(1)}, bf16[96,1152]{1,0:T(8,128)(2,1)S(1)}, u32[]{:S(2)}, u32[]{:S(2)}) collective-permute-start(bf16[96,1152]{1,0:T(8,128)(2,1)S(1)} %collective-permute-done.19.refs_12_.refs_0_), channel_id=1, source_target_pairs={{0,1},{1,0},{2,3},{3,2},{4,5},{5,4},{6,7},{7,6},{8,9},{9,8},{10,11... | collective-permute-start | bytes 663560 | tf_op jit(solution)/shard_map/ppermute | solution.py:36
  59.7 0.8 collective-permute-done.20.refs_13_.refs_1_
  60.5 3.9 %collective-permute-start.13 = (bf16[96,1152]{1,0:T(8,128)(2,1)S(1)}, bf16[96,1152]{1,0:T(8,128)(2,1)S(1)}, u32[]{:S(2)}, u32[]{:S(2)}) collective-permute-start(bf16[96,1152]{1,0:T(8,128)(2,1)S(1)} %collective-permute-done.11.refs_4_.refs_5_), channel_id=1, source_target_pairs={{0,1},{1,0},{2,3},{3,2},{4,5},{5,4},{6,7},{7,6},{8,9},{9,8},{10,11... | collective-permute-start | bytes 663560 | tf_op jit(solution)/shard_map/ppermute | solution.py:36
  64.4 0.8 collective-permute-done.12.refs_5_.refs_6_
  65.2 2.1 %collective-permute-start.18 = (bf16[96,1152]{1,0:T(8,128)(2,1)S(1)}, bf16[96,1152]{1,0:T(8,128)(2,1)S(1)}, u32[]{:S(2)}, u32[]{:S(2)}) collective-permute-start(bf16[96,1152]{1,0:T(8,128)(2,1)S(1)} %collective-permute-done.16.refs_9_.refs_10_), channel_id=1, source_target_pairs={{0,1},{1,0},{2,3},{3,2},{4,5},{5,4},{6,7},{7,6},{8,9},{9,8},{10,11... | collective-permute-start | bytes 663560 | tf_op jit(solution)/shard_map/ppermute | solution.py:36
  67.4 0.5 collective-permute-start.14
  68.0 1.5 %shard_map.100 = (f32[4,1536]{1,0:T(4,128)S(1)}, bf16[256,1536]{1,0:T(8,128)(2,1)S(1)}, bf16[256,1536]{1,0:T(8,128)(2,1)S(1)}) custom-call(f32[4,1536]{1,0:T(4,128)S(1)} %copy-done.1, bf16[128,1536]{1,0:T(8,128)(2,1)S(1)} %constant_dynamic-update-slice_fusion.block, bf16[128,1536]{1,0:T(8,128)(2,1)S(1)} %collective-permute-done.1.near, ...), custom_call_target="tpu_custom_call" | custom-call | bytes 1597440 | tf_op jit(solution)/shard_map/pallas_call | solution.py:425
  69.5 1.2 %shard_map.102.part_ref = f32[256,1152]{1,0:T(8,128)S(1)} custom-call(bf16[256,1536]{1,0:T(8,128)(2,1)S(1)} %get-tuple-element.29.refs_0_.normed, bf16[96,1152]{1,0:T(8,128)(2,1)S(1)} %copy-done, bf16[96,1152]{1,0:T(8,128)(2,1)S(1)} %collective-permute-done.8.refs_1_.refs_2_, bf16[96,1152]{1,0:T(8,128)(2,1)S(1)} %collective-permute-done.9.refs_2_.refs_3_, ...), custom_call_target="tpu_custom_call" | custom-call | flops 679477248 | bytes 3440640 | tf_op jit(solution)/shard_map/pallas_call | solution.py:425
  70.7 2.2 %shard_map.103.first_part = bf16[256,384]{1,0:T(8,128)(2,1)S(1)} custom-call(f32[4,1536]{1,0:T(4,128)S(1)} %get-tuple-element.21.extra_ref, bf16[128,384]{1,0:T(8,128)(2,1)S(1)} %get-tuple-element.44.key_ref, bf16[128,384]{1,0:T(8,128)(2,1)S(1)} %get-tuple-element.43.value_ref, bf16[256,1536]{1,0:T(8,128)(2,1)S(1)} %get-tuple-element.29.refs_0_.normed, ...), custom_call_target="tpu_custom_call" | custom-call | flops 377487360 | bytes 3072000 | tf_op jit(solution)/shard_map/pallas_call | solution.py:425
  72.9 1.1 %collective-permute-start.25 = (bf16[256,384]{1,0:T(8,128)(2,1)S(1)}, bf16[256,384]{1,0:T(8,128)(2,1)S(1)}, u32[]{:S(2)}, u32[]{:S(2)}) collective-permute-start(bf16[256,384]{1,0:T(8,128)(2,1)S(1)} %shard_map.103.first_part), channel_id=1, source_target_pairs={{0,2},{1,3},{2,0},{3,1},{4,6},{5,7},{6,4},{7,5},{8,10},{9,11},{10,... | collective-permute-start | bytes 589832 | tf_op jit(solution)/shard_map/ppermute | solution.py:36
  74.0 1.6 %collective-permute-start.23 = (bf16[256,384]{1,0:T(8,128)(2,1)S(1)}, bf16[256,384]{1,0:T(8,128)(2,1)S(1)}, u32[]{:S(2)}, u32[]{:S(2)}) collective-permute-start(bf16[256,384]{1,0:T(8,128)(2,1)S(1)} %shard_map.103.first_part), channel_id=1, source_target_pairs={{0,6},{1,7},{2,4},{3,5},{4,2},{5,3},{6,0},{7,1},{8,14},{9,15},{10,... | collective-permute-start | bytes 589832 | tf_op jit(solution)/shard_map/ppermute | solution.py:36
  75.6 0.3 shard_map.101.weights
  75.9 3.5 %collective-permute-done.25.fourth_part = bf16[256,384]{1,0:T(8,128)(2,1)S(1)} collective-permute-done((bf16[256,384]{1,0:T(8,128)(2,1)S(1)}, bf16[256,384]{1,0:T(8,128)(2,1)S(1)}, u32[]{:S(2)}, u32[]{:S(2)}) %collective-permute-start.25) | collective-permute-done | bytes 196640 | tf_op jit(solution)/shard_map/ppermute | solution.py:36
  79.4 0.8 collective-permute-done.24.third_part
  80.1 4.4 %collective-permute-done.23.second_part = bf16[256,384]{1,0:T(8,128)(2,1)S(1)} collective-permute-done((bf16[256,384]{1,0:T(8,128)(2,1)S(1)}, bf16[256,384]{1,0:T(8,128)(2,1)S(1)}, u32[]{:S(2)}, u32[]{:S(2)}) %collective-permute-start.23) | collective-permute-done | bytes 196640 | tf_op jit(solution)/shard_map/ppermute | solution.py:36
  84.5 4.0 %shard_map.104 = (bf16[64,384]{1,0:T(8,128)(2,1)S(1)}, bf16[64,384]{1,0:T(8,128)(2,1)S(1)}, bf16[64,384]{1,0:T(8,128)(2,1)S(1)}, bf16[64,384]{1,0:T(8,128)(2,1)S(1)}, bf16[64,384]{1,0:T(8,128)(2,1)S(1)}) custom-call(f32[4,1536]{1,0:T(4,128)S(1)} %get-tuple-element.21.extra_ref, bf16[128,384]{1,0:T(8,128)(2,1)S(1)} %get-tuple-element.44.key_ref, ...), custom_call_target="tpu_custom_call" | custom-call | flops 1056964608 | bytes 5332992 | tf_op jit(solution)/shard_map/pallas_call | solution.py:425
  88.5 1.8 %collective-permute-start.26 = (bf16[64,384]{1,0:T(8,128)(2,1)S(1)}, bf16[64,384]{1,0:T(8,128)(2,1)S(1)}, u32[]{:S(2)}, u32[]{:S(2)}) collective-permute-start(bf16[64,384]{1,0:T(8,128)(2,1)S(1)} %get-tuple-element.31), channel_id=1, source_target_pairs={{0,2},{1,4},{2,0},{3,6},{4,1},{5,7},{6,3},{7,5},{8,10},{9,12},{10,... | collective-permute-start | bytes 147464 | tf_op jit(solution)/shard_map/ppermute | solution.py:36
  90.3 1.3 %collective-permute-start.28 = (bf16[64,384]{1,0:T(8,128)(2,1)S(1)}, bf16[64,384]{1,0:T(8,128)(2,1)S(1)}, u32[]{:S(2)}, u32[]{:S(2)}) collective-permute-start(bf16[64,384]{1,0:T(8,128)(2,1)S(1)} %get-tuple-element.33), channel_id=1, source_target_pairs={{0,1},{1,7},{2,3},{3,5},{4,2},{5,4},{6,0},{7,6},{8,9},{9,15},{10,1... | collective-permute-start | bytes 147464 | tf_op jit(solution)/shard_map/ppermute | solution.py:36
  91.6 4.0 %collective-permute-start.29 = (bf16[64,384]{1,0:T(8,128)(2,1)S(1)}, bf16[64,384]{1,0:T(8,128)(2,1)S(1)}, u32[]{:S(2)}, u32[]{:S(2)}) collective-permute-start(bf16[64,384]{1,0:T(8,128)(2,1)S(1)} %get-tuple-element.34), channel_id=1, source_target_pairs={{1,6},{3,4},{4,3},{6,1},{9,14},{11,12},{12,11},{14,9},{17,22},{19,... | collective-permute-start | bytes 147464 | tf_op jit(solution)/shard_map/ppermute | solution.py:36
  95.6 2.3 %collective-permute-done.29.fourth = bf16[64,384]{1,0:T(8,128)(2,1)S(1)} collective-permute-done((bf16[64,384]{1,0:T(8,128)(2,1)S(1)}, bf16[64,384]{1,0:T(8,128)(2,1)S(1)}, u32[]{:S(2)}, u32[]{:S(2)}) %collective-permute-start.29) | collective-permute-done | bytes 49184 | tf_op jit(solution)/shard_map/ppermute | solution.py:36
  97.9 0.7 shard_map.105
  (32 shorter events, 0.2 us)
Async XLA Ops:
  0.0 12.2 %collective-permute-start = (bf16[64,1536]{1,0:T(8,128)(2,1)}, bf16[64,1536]{1,0:T(8,128)(2,1)S(1)}, u32[]{:S(2)}, u32[]{:S(2)}) collective-permute-start(bf16[64,1536]{1,0:T(8,128)(2,1)} %param.10), channel_id=1, source_target_pairs={{1,0},{3,2},{4,5},{6,7},{9,8},{11,10},{12,13},{14,15},{17,16},{19,... | collective-permute-start | bytes 589832 | tf_op jit(solution)/shard_map/ppermute | solution.py:36
  6.3 61.7 %copy-start.1 = (f32[4,1536]{1,0:T(4,128)S(1)}, f32[4,1536]{1,0:T(4,128)}, u32[]{:S(2)}) copy-start(f32[4,1536]{1,0:T(4,128)} %get-tuple-element.20.extra_ref) | copy-start | bytes 73732
  6.3 7.2 %collective-permute-start.4 = (bf16[8,8,2,384]{3,2,1,0:T(2,128)(2,1)}, bf16[8,8,2,384]{3,2,1,0:T(2,128)(2,1)S(1)}, u32[]{:S(2)}, u32[]{:S(2)}) collective-permute-start(bf16[8,8,2,384]{3,2,1,0:T(2,128)(2,1)} %get-tuple-element.23), channel_id=1, source_target_pairs={{0,1},{1,0},{2,3},{3,2},{4,5},{5,4},{6,7},{7,6},{8,9},{9,8},{10,11... | collective-permute-start | bytes 294920 | tf_op jit(solution)/shard_map/ppermute | solution.py:226
  8.4 61.0 %copy-start = (bf16[96,1152]{1,0:T(8,128)(2,1)S(1)}, bf16[96,1152]{1,0:T(8,128)(2,1)}, u32[]{:S(2)}) copy-start(bf16[96,1152]{1,0:T(8,128)(2,1)} %get-tuple-element.25.refs_0_.refs_1_) | copy-start | bytes 663556
  8.4 12.9 %collective-permute-start.8 = (bf16[96,1152]{1,0:T(8,128)(2,1)}, bf16[96,1152]{1,0:T(8,128)(2,1)S(1)}, u32[]{:S(2)}, u32[]{:S(2)}) collective-permute-start(bf16[96,1152]{1,0:T(8,128)(2,1)} %get-tuple-element.26), channel_id=1, source_target_pairs={{0,2},{1,3},{2,0},{3,1},{4,6},{5,7},{6,4},{7,5},{8,10},{9,11},{10,... | collective-permute-start | bytes 663560 | tf_op jit(solution)/shard_map/ppermute | solution.py:36
  12.2 25.4 %collective-permute-start.2 = (bf16[128,1536]{1,0:T(8,128)(2,1)S(1)}, bf16[128,1536]{1,0:T(8,128)(2,1)S(1)}, u32[]{:S(2)}, u32[]{:S(2)}) collective-permute-start(bf16[128,1536]{1,0:T(8,128)(2,1)S(1)} %constant_dynamic-update-slice_fusion.block), channel_id=1, source_target_pairs={{0,4},{2,6},{5,1},{7,3},{8,12},{10,14},{13,9},{15,11},{16,20},{18,... | collective-permute-start | bytes 1179656 | tf_op jit(solution)/shard_map/ppermute | solution.py:36
  14.6 5.4 %collective-permute-start.5 = (bf16[2,4,8,2,384]{4,3,2,1,0:T(2,128)(2,1)S(1)}, bf16[2,4,8,2,384]{4,3,2,1,0:T(2,128)(2,1)S(1)}, u32[]{:S(2)}, u32[]{:S(2)}) collective-permute-start(bf16[2,4,8,2,384]{4,3,2,1,0:T(2,128)(2,1)S(1)} %get-tuple-element.42), channel_id=1, source_target_pairs={{0,2},{1,3},{2,0},{3,1},{4,6},{5,7},{6,4},{7,5},{8,10},{9,11},{10,... | collective-permute-start | bytes 294920 | tf_op jit(solution)/shard_map/ppermute | solution.py:226
  14.7 9.1 %collective-permute-start.15 = (bf16[96,1152]{1,0:T(8,128)(2,1)}, bf16[96,1152]{1,0:T(8,128)(2,1)S(1)}, u32[]{:S(2)}, u32[]{:S(2)}) collective-permute-start(bf16[96,1152]{1,0:T(8,128)(2,1)} %get-tuple-element.28), channel_id=1, source_target_pairs={{0,8},{1,11},{2,10},{3,9},{4,12},{5,15},{6,14},{7,13},{8,0},{9,3},... | collective-permute-start | bytes 663560 | tf_op jit(solution)/shard_map/ppermute | solution.py:36
  18.2 16.7 %collective-permute-start.19 = (bf16[96,1152]{1,0:T(8,128)(2,1)}, bf16[96,1152]{1,0:T(8,128)(2,1)S(1)}, u32[]{:S(2)}, u32[]{:S(2)}) collective-permute-start(bf16[96,1152]{1,0:T(8,128)(2,1)} %get-tuple-element.27), channel_id=1, source_target_pairs={{0,12},{1,15},{2,14},{3,13},{4,8},{5,11},{6,10},{7,9},{8,4},{9,7},... | collective-permute-start | bytes 663560 | tf_op jit(solution)/shard_map/ppermute | solution.py:36
  20.0 15.8 %collective-permute-start.11 = (bf16[96,1152]{1,0:T(8,128)(2,1)}, bf16[96,1152]{1,0:T(8,128)(2,1)S(1)}, u32[]{:S(2)}, u32[]{:S(2)}) collective-permute-start(bf16[96,1152]{1,0:T(8,128)(2,1)} %get-tuple-element.27), channel_id=1, source_target_pairs={{0,4},{1,7},{2,6},{3,5},{4,0},{5,3},{6,2},{7,1},{8,12},{9,15},{10,... | collective-permute-start | bytes 663560 | tf_op jit(solution)/shard_map/ppermute | solution.py:36
  21.4 18.6 %collective-permute-start.9 = (bf16[96,1152]{1,0:T(8,128)(2,1)}, bf16[96,1152]{1,0:T(8,128)(2,1)S(1)}, u32[]{:S(2)}, u32[]{:S(2)}) collective-permute-start(bf16[96,1152]{1,0:T(8,128)(2,1)} %get-tuple-element.25.refs_0_.refs_1_), channel_id=1, source_target_pairs={{0,1},{1,0},{2,3},{3,2},{4,5},{5,4},{6,7},{7,6},{8,9},{9,8},{10,11... | collective-permute-start | bytes 663560 | tf_op jit(solution)/shard_map/ppermute | solution.py:36
  23.8 13.1 %collective-permute-start.6 = (bf16[4,2,8,2,384]{4,3,2,1,0:T(2,128)(2,1)S(1)}, bf16[4,2,8,2,384]{4,3,2,1,0:T(2,128)(2,1)S(1)}, u32[]{:S(2)}, u32[]{:S(2)}) collective-permute-start(bf16[4,2,8,2,384]{4,3,2,1,0:T(2,128)(2,1)S(1)} %get-tuple-element.40), channel_id=1, source_target_pairs={{0,4},{1,5},{2,6},{3,7},{4,0},{5,1},{6,2},{7,3},{8,12},{9,13},{10,... | collective-permute-start | bytes 294920 | tf_op jit(solution)/shard_map/ppermute | solution.py:226
  34.9 15.2 %collective-permute-start.10 = (bf16[96,1152]{1,0:T(8,128)(2,1)S(1)}, bf16[96,1152]{1,0:T(8,128)(2,1)S(1)}, u32[]{:S(2)}, u32[]{:S(2)}) collective-permute-start(bf16[96,1152]{1,0:T(8,128)(2,1)S(1)} %collective-permute-done.8.refs_1_.refs_2_), channel_id=1, source_target_pairs={{0,1},{1,0},{2,3},{3,2},{4,5},{5,4},{6,7},{7,6},{8,9},{9,8},{10,11... | collective-permute-start | bytes 663560 | tf_op jit(solution)/shard_map/ppermute | solution.py:36
  35.8 15.7 %collective-permute-start.17 = (bf16[96,1152]{1,0:T(8,128)(2,1)S(1)}, bf16[96,1152]{1,0:T(8,128)(2,1)S(1)}, u32[]{:S(2)}, u32[]{:S(2)}) collective-permute-start(bf16[96,1152]{1,0:T(8,128)(2,1)S(1)} %collective-permute-done.15.refs_8_.refs_9_), channel_id=1, source_target_pairs={{0,1},{1,0},{2,3},{3,2},{4,5},{5,4},{6,7},{7,6},{8,9},{9,8},{10,11... | collective-permute-start | bytes 663560 | tf_op jit(solution)/shard_map/ppermute | solution.py:36
  36.9 30.5 %collective-permute-start.1 = (bf16[128,1536]{1,0:T(8,128)(2,1)S(1)}, bf16[128,1536]{1,0:T(8,128)(2,1)S(1)}, u32[]{:S(2)}, u32[]{:S(2)}) collective-permute-start(bf16[128,1536]{1,0:T(8,128)(2,1)S(1)} %constant_dynamic-update-slice_fusion.block), channel_id=1, source_target_pairs={{0,2},{2,0},{5,7},{7,5},{8,10},{10,8},{13,15},{15,13},{16,18},{18,... | collective-permute-start | bytes 1179656 | tf_op jit(solution)/shard_map/ppermute | solution.py:36
  37.6 29.8 %collective-permute-start.3 = (bf16[128,1536]{1,0:T(8,128)(2,1)S(1)}, bf16[128,1536]{1,0:T(8,128)(2,1)S(1)}, u32[]{:S(2)}, u32[]{:S(2)}) collective-permute-start(bf16[128,1536]{1,0:T(8,128)(2,1)S(1)} %collective-permute-done.2.far), channel_id=1, source_target_pairs={{1,3},{3,1},{4,6},{6,4},{9,11},{11,9},{12,14},{14,12},{17,19},{19,... | collective-permute-start | bytes 1179656 | tf_op jit(solution)/shard_map/ppermute | solution.py:36
  40.0 10.1 %collective-permute-start.7 = (bf16[8,1,8,2,384]{4,3,2,1,0:T(2,128)(2,1)S(1)}, bf16[8,1,8,2,384]{4,3,2,1,0:T(2,128)(2,1)S(1)}, u32[]{:S(2)}, u32[]{:S(2)}) collective-permute-start(bf16[8,1,8,2,384]{4,3,2,1,0:T(2,128)(2,1)S(1)} %get-tuple-element.38), channel_id=1, source_target_pairs={{0,8},{1,9},{2,10},{3,11},{4,12},{5,13},{6,14},{7,15},{8,0},{9,1},... | collective-permute-start | bytes 294920 | tf_op jit(solution)/shard_map/ppermute | solution.py:226
  50.1 5.7 %collective-permute-start.16 = (bf16[96,1152]{1,0:T(8,128)(2,1)S(1)}, bf16[96,1152]{1,0:T(8,128)(2,1)S(1)}, u32[]{:S(2)}, u32[]{:S(2)}) collective-permute-start(bf16[96,1152]{1,0:T(8,128)(2,1)S(1)} %collective-permute-done.15.refs_8_.refs_9_), channel_id=1, source_target_pairs={{0,16},{1,17},{2,18},{3,19},{4,20},{5,21},{6,22},{7,23},{8,24},{9,... | collective-permute-start | bytes 663560 | tf_op jit(solution)/shard_map/ppermute | solution.py:36
  50.1 10.4 %collective-permute-start.20 = (bf16[96,1152]{1,0:T(8,128)(2,1)S(1)}, bf16[96,1152]{1,0:T(8,128)(2,1)S(1)}, u32[]{:S(2)}, u32[]{:S(2)}) collective-permute-start(bf16[96,1152]{1,0:T(8,128)(2,1)S(1)} %collective-permute-done.19.refs_12_.refs_0_), channel_id=1, source_target_pairs={{0,16},{1,17},{2,18},{3,19},{4,20},{5,21},{6,22},{7,23},{8,24},{9,... | collective-permute-start | bytes 663560 | tf_op jit(solution)/shard_map/ppermute | solution.py:36
  51.5 13.7 %collective-permute-start.12 = (bf16[96,1152]{1,0:T(8,128)(2,1)S(1)}, bf16[96,1152]{1,0:T(8,128)(2,1)S(1)}, u32[]{:S(2)}, u32[]{:S(2)}) collective-permute-start(bf16[96,1152]{1,0:T(8,128)(2,1)S(1)} %collective-permute-done.11.refs_4_.refs_5_), channel_id=1, source_target_pairs={{0,16},{1,17},{2,18},{3,19},{4,20},{5,21},{6,22},{7,23},{8,24},{9,... | collective-permute-start | bytes 663560 | tf_op jit(solution)/shard_map/ppermute | solution.py:36
  55.8 14.9 %collective-permute-start.21 = (bf16[96,1152]{1,0:T(8,128)(2,1)S(1)}, bf16[96,1152]{1,0:T(8,128)(2,1)S(1)}, u32[]{:S(2)}, u32[]{:S(2)}) collective-permute-start(bf16[96,1152]{1,0:T(8,128)(2,1)S(1)} %collective-permute-done.19.refs_12_.refs_0_), channel_id=1, source_target_pairs={{0,1},{1,0},{2,3},{3,2},{4,5},{5,4},{6,7},{7,6},{8,9},{9,8},{10,11... | collective-permute-start | bytes 663560 | tf_op jit(solution)/shard_map/ppermute | solution.py:36
  60.5 8.9 %collective-permute-start.13 = (bf16[96,1152]{1,0:T(8,128)(2,1)S(1)}, bf16[96,1152]{1,0:T(8,128)(2,1)S(1)}, u32[]{:S(2)}, u32[]{:S(2)}) collective-permute-start(bf16[96,1152]{1,0:T(8,128)(2,1)S(1)} %collective-permute-done.11.refs_4_.refs_5_), channel_id=1, source_target_pairs={{0,1},{1,0},{2,3},{3,2},{4,5},{5,4},{6,7},{7,6},{8,9},{9,8},{10,11... | collective-permute-start | bytes 663560 | tf_op jit(solution)/shard_map/ppermute | solution.py:36
  65.2 4.2 %collective-permute-start.18 = (bf16[96,1152]{1,0:T(8,128)(2,1)S(1)}, bf16[96,1152]{1,0:T(8,128)(2,1)S(1)}, u32[]{:S(2)}, u32[]{:S(2)}) collective-permute-start(bf16[96,1152]{1,0:T(8,128)(2,1)S(1)} %collective-permute-done.16.refs_9_.refs_10_), channel_id=1, source_target_pairs={{0,1},{1,0},{2,3},{3,2},{4,5},{5,4},{6,7},{7,6},{8,9},{9,8},{10,11... | collective-permute-start | bytes 663560 | tf_op jit(solution)/shard_map/ppermute | solution.py:36
  67.4 3.3 %collective-permute-start.22 = (bf16[96,1152]{1,0:T(8,128)(2,1)S(1)}, bf16[96,1152]{1,0:T(8,128)(2,1)S(1)}, u32[]{:S(2)}, u32[]{:S(2)}) collective-permute-start(bf16[96,1152]{1,0:T(8,128)(2,1)S(1)} %collective-permute-done.20.refs_13_.refs_1_), channel_id=1, source_target_pairs={{0,1},{1,0},{2,3},{3,2},{4,5},{5,4},{6,7},{7,6},{8,9},{9,8},{10,11... | collective-permute-start | bytes 663560 | tf_op jit(solution)/shard_map/ppermute | solution.py:36
  67.4 2.1 %collective-permute-start.14 = (bf16[96,1152]{1,0:T(8,128)(2,1)S(1)}, bf16[96,1152]{1,0:T(8,128)(2,1)S(1)}, u32[]{:S(2)}, u32[]{:S(2)}) collective-permute-start(bf16[96,1152]{1,0:T(8,128)(2,1)S(1)} %collective-permute-done.12.refs_5_.refs_6_), channel_id=1, source_target_pairs={{0,1},{1,0},{2,3},{3,2},{4,5},{5,4},{6,7},{7,6},{8,9},{9,8},{10,11... | collective-permute-start | bytes 663560 | tf_op jit(solution)/shard_map/ppermute | solution.py:36
  72.9 6.5 %collective-permute-start.25 = (bf16[256,384]{1,0:T(8,128)(2,1)S(1)}, bf16[256,384]{1,0:T(8,128)(2,1)S(1)}, u32[]{:S(2)}, u32[]{:S(2)}) collective-permute-start(bf16[256,384]{1,0:T(8,128)(2,1)S(1)} %shard_map.103.first_part), channel_id=1, source_target_pairs={{0,2},{1,3},{2,0},{3,1},{4,6},{5,7},{6,4},{7,5},{8,10},{9,11},{10,... | collective-permute-start | bytes 589832 | tf_op jit(solution)/shard_map/ppermute | solution.py:36
  74.0 6.1 %collective-permute-start.24 = (bf16[256,384]{1,0:T(8,128)(2,1)S(1)}, bf16[256,384]{1,0:T(8,128)(2,1)S(1)}, u32[]{:S(2)}, u32[]{:S(2)}) collective-permute-start(bf16[256,384]{1,0:T(8,128)(2,1)S(1)} %shard_map.103.first_part), channel_id=1, source_target_pairs={{0,4},{1,5},{2,6},{3,7},{4,0},{5,1},{6,2},{7,3},{8,12},{9,13},{10,... | collective-permute-start | bytes 589832 | tf_op jit(solution)/shard_map/ppermute | solution.py:36
  74.0 10.5 %collective-permute-start.23 = (bf16[256,384]{1,0:T(8,128)(2,1)S(1)}, bf16[256,384]{1,0:T(8,128)(2,1)S(1)}, u32[]{:S(2)}, u32[]{:S(2)}) collective-permute-start(bf16[256,384]{1,0:T(8,128)(2,1)S(1)} %shard_map.103.first_part), channel_id=1, source_target_pairs={{0,6},{1,7},{2,4},{3,5},{4,2},{5,3},{6,0},{7,1},{8,14},{9,15},{10,... | collective-permute-start | bytes 589832 | tf_op jit(solution)/shard_map/ppermute | solution.py:36
  88.5 7.0 %collective-permute-start.26 = (bf16[64,384]{1,0:T(8,128)(2,1)S(1)}, bf16[64,384]{1,0:T(8,128)(2,1)S(1)}, u32[]{:S(2)}, u32[]{:S(2)}) collective-permute-start(bf16[64,384]{1,0:T(8,128)(2,1)S(1)} %get-tuple-element.31), channel_id=1, source_target_pairs={{0,2},{1,4},{2,0},{3,6},{4,1},{5,7},{6,3},{7,5},{8,10},{9,12},{10,... | collective-permute-start | bytes 147464 | tf_op jit(solution)/shard_map/ppermute | solution.py:36
  90.3 5.3 %collective-permute-start.27 = (bf16[64,384]{1,0:T(8,128)(2,1)S(1)}, bf16[64,384]{1,0:T(8,128)(2,1)S(1)}, u32[]{:S(2)}, u32[]{:S(2)}) collective-permute-start(bf16[64,384]{1,0:T(8,128)(2,1)S(1)} %get-tuple-element.32), channel_id=1, source_target_pairs={{0,3},{1,5},{2,1},{3,7},{4,0},{5,6},{6,2},{7,4},{8,11},{9,13},{10,... | collective-permute-start | bytes 147464 | tf_op jit(solution)/shard_map/ppermute | solution.py:36
  90.3 5.3 %collective-permute-start.28 = (bf16[64,384]{1,0:T(8,128)(2,1)S(1)}, bf16[64,384]{1,0:T(8,128)(2,1)S(1)}, u32[]{:S(2)}, u32[]{:S(2)}) collective-permute-start(bf16[64,384]{1,0:T(8,128)(2,1)S(1)} %get-tuple-element.33), channel_id=1, source_target_pairs={{0,1},{1,7},{2,3},{3,5},{4,2},{5,4},{6,0},{7,6},{8,9},{9,15},{10,1... | collective-permute-start | bytes 147464 | tf_op jit(solution)/shard_map/ppermute | solution.py:36
  91.6 6.3 %collective-permute-start.29 = (bf16[64,384]{1,0:T(8,128)(2,1)S(1)}, bf16[64,384]{1,0:T(8,128)(2,1)S(1)}, u32[]{:S(2)}, u32[]{:S(2)}) collective-permute-start(bf16[64,384]{1,0:T(8,128)(2,1)S(1)} %get-tuple-element.34), channel_id=1, source_target_pairs={{1,6},{3,4},{4,3},{6,1},{9,14},{11,12},{12,11},{14,9},{17,22},{19,... | collective-permute-start | bytes 147464 | tf_op jit(solution)/shard_map/ppermute | solution.py:36

commit v5 on v4

--- a/solution.py
+++ b/solution.py
@@ -63,15 +63,48 @@
     return pl.ds(pl.multiple_of(quarter * width, 128), width)
 
 
-def pack_weights_kernel(
-    w_query, w_key, w_value, own_ref, beside_ref, even_ref, odd_ref, rows, row_sem, out_sem
+def pack_kernel(
+    w_query, w_key, w_value, list_hbm, slot_hbm, count_hbm, scale_hbm, gain_hbm, mem_ref,
+    own_ref, beside_ref, even_ref, odd_ref, extra_ref, *refs,
 ):
-    x, _, plane, y, c = here()
+    near_count = SPATIAL
+    memory_refs = refs[:near_count]
+    (
+        list_ref, slot_ref, count_ref, scale_ref, gain, rows, stored, extra, row_sem, out_sem, scalar_sem, mem_sem, give_sem,
+    ) = refs[near_count:]
+    x, index, plane, y, c = here()
+    devices = lax.axis_size("frame")
+    frames, entries = list_ref.shape
     width = own_ref.shape[1] // 3
+    scalars = [
+        pltpu.make_async_copy(source, target, scalar_sem.at[number])
+        for number, (source, target) in enumerate(
+            (
+                (list_hbm, list_ref),
+                (slot_hbm, slot_ref),
+                (count_hbm, count_ref),
+                (scale_hbm, scale_ref),
+                (gain_hbm, gain),
+            )
+        )
+    ]
+    for copy in scalars[:2]:
+        copy.start()
     reads = []
     for number, weight in enumerate((w_query, w_key, w_value)):
         reads.append(pltpu.make_async_copy(weight, rows.at[number], row_sem.at[number]))
         reads[-1].start()
+    for copy in scalars[2:]:
+        copy.start()
+    for copy in scalars[:2]:
+        copy.wait()
+    picks = []
+    for frame in range(frames):
+        for entry in range(entries):
+            number = frame * entries + entry
+            row = slot_ref[list_ref[frame, entry]]
+            picks.append(pltpu.make_async_copy(mem_ref.at[row, 0], stored.at[number], mem_sem.at[number]))
+            picks[-1].start()
     across = joined_bits(joined_bits(x, y), c)
     low = plane % 2
     quarters = (low * 2 + across, (1 - low) * 2 + across, low * 2 + 1 - y, quarter_of(plane, y))
@@ -87,79 +120,25 @@
                 )
             )
             gives[-1].start()
-    for give in gives:
-        give.wait()
-
-
-def pack_weights(w_query, w_key, w_value):
-    shard_rows, features = w_query.shape
-    piece = jax.ShapeDtypeStruct((shard_rows, 3 * (features // SPATIAL)), w_query.dtype)
-    anywhere = pl.BlockSpec(memory_space=pl.ANY)
-    held = pl.BlockSpec(memory_space=pltpu.HBM)
-    return pl.pallas_call(
-        pack_weights_kernel,
-        out_shape=(piece,) * 4,
-        in_specs=[held] * 3,
-        out_specs=(anywhere,) * 4,
-        scratch_shapes=[
-            pltpu.VMEM((3, shard_rows, features), w_query.dtype),
-            pltpu.SemaphoreType.DMA((3,)),
-            pltpu.SemaphoreType.DMA((3, 4)),
-        ],
-        name="pack_weights",
-    )(w_query, w_key, w_value)
-
-
-def pack_memory_kernel(
-    list_hbm, slot_hbm, count_hbm, scale_hbm, gain_hbm, mem_ref, kept_ref, sent_ref, extra_ref,
-    list_ref, slot_ref, count_ref, scale_ref, stored, extra, scalar_sem, mem_sem, give_sem,
-):
-    _, index, plane, _, c = here()
-    devices = lax.axis_size("frame")
-    frames, entries = list_ref.shape
-    width = kept_ref.shape[-1]
-    scalars = [
-        pltpu.make_async_copy(list_hbm, list_ref, scalar_sem.at[0]),
-        pltpu.make_async_copy(slot_hbm, slot_ref, scalar_sem.at[1]),
-        pltpu.make_async_copy(count_hbm, count_ref, scalar_sem.at[2]),
-        pltpu.make_async_copy(scale_hbm, scale_ref, scalar_sem.at[3]),
-        pltpu.make_async_copy(gain_hbm, extra.at[pl.ds(0, 1)], scalar_sem.at[4]),
-    ]
-    for copy in scalars:
-        copy.start()
-    for copy in scalars[:2]:
-        copy.wait()
-    picks = []
-    for frame in range(frames):
-        for entry in range(entries):
-            number = frame * entries + entry
-            row = slot_ref[list_ref[frame, entry]]
-            picks.append(pltpu.make_async_copy(mem_ref.at[row, 0], stored.at[number], mem_sem.at[number]))
-            picks[-1].start()
     for copy in scalars[2:]:
         copy.wait()
     row = (1, extra.shape[1])
+    extra[0:1, :] = gain[...].reshape(row)
     for number in range(STEPS):
         extra[1 + number : 2 + number, :] = jnp.full(row, scale_ref[number], jnp.float32)
     live = lax.broadcasted_iota(jnp.int32, row, 1) % entries < count_ref[(plane // 2) * 2 + c]
     extra[1 + STEPS : 2 + STEPS, :] = jnp.where(live, 1.0, 0.0)
+    gives.append(pltpu.make_async_copy(extra, extra_ref, scalar_sem.at[5]))
+    gives[-1].start()
     for pick in picks:
         pick.wait()
-    gives = [pltpu.make_async_copy(extra, extra_ref, scalar_sem.at[5])]
-    gives[0].start()
-    bits = devices.bit_length() - 1
     for away in range(devices):
-        target = flipped(index, away)
-        to_plane, to_y, to_c = coords(target)
+        to_plane, to_y, to_c = coords(flipped(index, away))
         to_frame = (to_plane // 2) * 2 + to_c
-        place = 0
-        for bit in range(1, bits):
-            place = place * 2 + (away >> bit & 1)
-        out = sent_ref if away & 1 else kept_ref
         gives.append(
             pltpu.make_async_copy(
                 stored.at[pl.ds(to_frame * entries, entries), :, columns(quarter_of(to_plane, to_y), width)],
-                out.at[place],
+                memory_refs[away % SPATIAL].at[away // SPATIAL],
                 give_sem.at[away],
             )
         )
@@ -168,31 +147,39 @@
         give.wait()
 
 
-def pack_memory(mem_cache, intersection, slot_of, counts, step_scale, norm_gain):
+def pack(w_query, w_key, w_value, intersection, slot_of, counts, step_scale, norm_gain, mem_cache):
     devices = lax.axis_size("frame")
-    features = mem_cache.shape[-1]
+    shard_rows, features = w_query.shape
     frames, entries = intersection.shape
-    half = jax.ShapeDtypeStruct((devices // 2, entries, 2, features // SPATIAL), mem_cache.dtype)
+    piece = jax.ShapeDtypeStruct((shard_rows, 3 * (features // SPATIAL)), w_query.dtype)
+    small = jax.ShapeDtypeStruct((2 + STEPS, features), jnp.float32)
+    memory = jax.ShapeDtypeStruct((devices // SPATIAL, entries, 2, features // SPATIAL), mem_cache.dtype)
+    out_shape = (piece,) * 4 + (small,) + (memory,) * SPATIAL
     anywhere = pl.BlockSpec(memory_space=pl.ANY)
     held = pl.BlockSpec(memory_space=pltpu.HBM)
-    return pl.pallas_call(
-        pack_memory_kernel,
-        out_shape=(half, half, jax.ShapeDtypeStruct((2 + STEPS, features), jnp.float32)),
-        in_specs=[held] * 6,
-        out_specs=(anywhere,) * 3,
+    outs = pl.pallas_call(
+        pack_kernel,
+        out_shape=out_shape,
+        in_specs=[held] * 9,
+        out_specs=(anywhere,) * len(out_shape),
         scratch_shapes=[
             pltpu.SMEM(intersection.shape, intersection.dtype),
             pltpu.SMEM(slot_of.shape, slot_of.dtype),
             pltpu.SMEM(counts.shape, counts.dtype),
             pltpu.SMEM(step_scale.shape, step_scale.dtype),
+            pltpu.VMEM(norm_gain.shape, norm_gain.dtype),
+            pltpu.VMEM((3, shard_rows, features), w_query.dtype),
             pltpu.VMEM((frames * entries, 2, features), mem_cache.dtype),
-            pltpu.VMEM((2 + STEPS, features), jnp.float32),
+            pltpu.VMEM(small.shape, small.dtype),
+            pltpu.SemaphoreType.DMA((3,)),
+            pltpu.SemaphoreType.DMA((3, 4)),
             pltpu.SemaphoreType.DMA((6,)),
             pltpu.SemaphoreType.DMA((frames * entries,)),
             pltpu.SemaphoreType.DMA((devices,)),
         ],
-        name="pack_memory",
-    )(intersection, slot_of, counts, step_scale, norm_gain.reshape(1, -1), mem_cache)
+        name="pack",
+    )(w_query, w_key, w_value, intersection, slot_of, counts, step_scale, norm_gain, mem_cache)
+    return outs[:4], outs[4], outs[5:]
 
 
 def all_pieces(own, beside, even, odd):
@@ -212,18 +199,18 @@
     return places
 
 
-def all_memory(kept, sent):
-    devices = lax.axis_size("frame")
-    held = jnp.stack([kept, hop(sent, 0)])
-    for bit in range(1, devices.bit_length() - 1):
-        half = held.shape[1] // 2
-        held = jnp.concatenate([held[:, :half], hop(held[:, half:], bit)])
-    keys, values = held[:, 0, :, 0, :], held[:, 0, :, 1, :]
+def all_memory(parts):
+    planes = lax.axis_size("frame") // SPATIAL
+    near = [parts[0]] + [hop(part, place) for place, part in enumerate(parts) if place]
+    held = jnp.stack(near, axis=1)
+    arrived = [held[0]] + [hop(held[bits], bits * SPATIAL) for bits in range(1, planes)]
+    held = jnp.concatenate(arrived)
+    keys, values = held[:, :, 0, :], held[:, :, 1, :]
     return keys.reshape(-1, keys.shape[-1]), values.reshape(-1, values.shape[-1])
 
 
-def hop(array, bit):
-    return lax.ppermute(array, "frame", [(i, i ^ 1 << bit) for i in range(lax.axis_size("frame"))])
+def hop(array, bits):
+    return lax.ppermute(array, "frame", [(i, i ^ bits) for i in range(lax.axis_size("frame"))])
 
 
 def all_tokens(latent):
@@ -231,8 +218,8 @@
     block = jnp.concatenate([latent, other])
     near = moved(block, lambda x, p, y, c: (x, p, 1 - y, c) if c == p % 2 else None)
     far = moved(block, lambda x, p, y, c: (x, p ^ 1, y, c) if c == p % 2 else None)
-    far_near = moved(far, lambda x, p, y, c: (x, p, 1 - y, c) if c != p % 2 else None)
-    return block, near, far, far_near
+    both = moved(block, lambda x, p, y, c: (x, p ^ 1, 1 - y, c) if c == p % 2 else None)
+    return block, near, far, both
 
 
 def late_plane(devices):
@@ -555,10 +542,12 @@
     latent, norm_gain, w_query, w_key, w_value, mem_cache, intersection, counts, slot_of, step_scale
 ):
     late = late_plane(lax.axis_size("frame"))
-    pieces = sorted(all_pieces(*pack_weights(w_query, w_key, w_value)), key=lambda piece: piece[1][0])
+    weights, extra, memory = pack(
+        w_query, w_key, w_value, intersection, slot_of, counts, step_scale, norm_gain, mem_cache
+    )
+    pieces = sorted(all_pieces(*weights), key=lambda piece: piece[1][0])
     tokens = all_tokens(latent)
-    kept, sent, extra = pack_memory(mem_cache, intersection, slot_of, counts, step_scale, norm_gain)
-    keys, values = all_memory(kept, sent)
+    keys, values = all_memory(memory)
     extra, current, normed = prepare(extra, tokens)
     part = project(normed, [piece for piece in pieces if piece[1][0] < late])
     attended = step(extra, keys, values, normed, part, [piece for piece in pieces if piece[1][0] == late])

time: 99.1 us -> 98.4 us (level)
  waiting for transfers between devices: 22.1 us -> 42.4 us
  starting transfers between devices: 57 us -> 38.9 us
  Pallas kernels: 15 us -> 13 us
    ppermute x4 -> x6, waiting for transfers between devices: 5.68 us -> 23.8 us  [hop(): lax.ppermute(array, 'frame', [(i, i ^ bits) for i in range(lax.axis_size(...]
    ppermute x4 -> x6, starting transfers between devices: 16.6 us -> 7.37 us  [hop(): lax.ppermute(array, 'frame', [(i, i ^ bits) for i in range(lax.axis_size(...]
    ppermute x26, starting transfers between devices: 40.3 us -> 31.5 us  [moved(): return lax.ppermute(array, AXES, pairs)]
    ppermute x26, waiting for transfers between devices: 16.4 us -> 18.5 us  [moved(): return lax.ppermute(array, AXES, pairs)]
    pallas_call x2 -> x1, Pallas kernels: 5.09 us -> 3.18 us  [pack(): pl.pallas_call(pack_kernel, out_shape=out_shape, in_specs=[held] * 9, out...]
    reshape x1 -> x0, local copies, waits for them, and re-layouts: 1.3 us -> none  [pack_memory(): norm_gain.reshape(1, -1)]
  transfers between devices with their start and end apart: 30 -> 32, of which waited for: 9 -> 9; matrix products, arithmetic and copies ran while one was open for 4% -> 2% of each run, Pallas kernels for 8% -> 3%
where the time goes in v5:
time: 98.4 us; the launch traced here: 98.1 us
  waiting for transfers between devices  42.4 us (43%)
  starting transfers between devices  38.9 us (40%)
  Pallas kernels  13 us (13%)
  local copies, waits for them, and re-layouts  2.13 us (2%)
  other arithmetic  1.44 us (1%)
    ppermute x26, starting transfers between devices, moved(): return lax.ppermute(array, AXES, pairs)  31.5 us
    ppermute x6, waiting for transfers between devices, hop(): lax.ppermute(array, 'frame', [(i, i ^ bits) for i in range(lax.axis_size(...  23.8 us
    ppermute x26, waiting for transfers between devices, moved(): return lax.ppermute(array, AXES, pairs)  18.5 us
    pallas_call x6, Pallas kernels, kernel_call(): pl.pallas_call(kernel, out_shape=out_shape, in_specs=[free if number in a...  9.82 us
    ppermute x6, starting transfers between devices, hop(): lax.ppermute(array, 'frame', [(i, i ^ bits) for i in range(lax.axis_size(...  7.37 us
    pallas_call x1, Pallas kernels, pack(): pl.pallas_call(pack_kernel, out_shape=out_shape, in_specs=[held] * 9, out...  3.18 us
  transfers between devices with their start and end apart: 32, of which 9 were waited for; matrix products, arithmetic and copies ran while one was open for 2% of the time, Pallas kernels for 3%

profile of v5, /device:TPU:1, one launch (start us, length us, event | category | flops | bytes accessed | tf_op | source)
XLA Modules:
  0.0 98.1 jit_solution(8919552358197615323)
XLA Ops:
  0.0 3.2 %pack.1 = (bf16[96,1152]{1,0:T(8,128)(2,1)}, bf16[96,1152]{1,0:T(8,128)(2,1)}, bf16[96,1152]{1,0:T(8,128)(2,1)}, bf16[96,1152]{1,0:T(8,128)(2,1)}, f32[4,1536]{1...) custom-call(bf16[96,1536]{1,0:T(8,128)(2,1)} %w_query.1, ...), custom_call_target="tpu_custom_call" | custom-call | tf_op jit(solution)/shard_map/pack/pallas_call | solution.py:160
  3.2 0.1 collective-permute-start.4
  3.3 2.7 %collective-permute-start.5 = (bf16[4,8,2,384]{3,2,1,0:T(2,128)(2,1)}, bf16[4,8,2,384]{3,2,1,0:T(2,128)(2,1)S(1)}, u32[]{:S(2)}, u32[]{:S(2)}) collective-permute-start(bf16[4,8,2,384]{3,2,1,0:T(2,128)(2,1)} %get-tuple-element.26), channel_id=1, source_target_pairs={{0,2},{1,3},{2,0},{3,1},{4,6},{5,7},{6,4},{7,5},{8,10},{9,11},{10,... | collective-permute-start | bytes 147464 | tf_op jit(solution)/shard_map/ppermute | solution.py:213
  6.0 2.2 %collective-permute-done.5 = bf16[4,8,2,384]{3,2,1,0:T(2,128)(2,1)S(1)} collective-permute-done((bf16[4,8,2,384]{3,2,1,0:T(2,128)(2,1)}, bf16[4,8,2,384]{3,2,1,0:T(2,128)(2,1)S(1)}, u32[]{:S(2)}, u32[]{:S(2)}) %collective-permute-start.5) | collective-permute-done | bytes 49184 | tf_op jit(solution)/shard_map/ppermute | solution.py:213
  8.2 1.7 %collective-permute-done.6 = bf16[4,8,2,384]{3,2,1,0:T(2,128)(2,1)S(1)} collective-permute-done((bf16[4,8,2,384]{3,2,1,0:T(2,128)(2,1)}, bf16[4,8,2,384]{3,2,1,0:T(2,128)(2,1)S(1)}, u32[]{:S(2)}, u32[]{:S(2)}) %collective-permute-start.6) | collective-permute-done | bytes 49184 | tf_op jit(solution)/shard_map/ppermute | solution.py:213
  9.9 1.1 %pad_maximum_fusion = bf16[4,4,8,2,384]{4,3,2,0,1:T(2,128)(2,1)S(1)} fusion(bf16[4,1,8,2,384]{4,3,2,0,1:T(2,128)(2,1)S(1)} %bitcast.25, bf16[4,1,8,2,384]{4,3,2,0,1:T(2,128)(2,1)S(1)} %bitcast.24, bf16[4,1,8,2,384]{4,3,2,0,1:T(2,128)(2,1)S(1)} %bitcast.23, bf16[4,1,8,2,384]{4,3,2,0,1:T(2,128)(2,1)} %bitcast.22), kind=kLoop, calls=%fused_computation | loop fusion | flops 294912 | bytes 393216 | tf_op jit(solution)/shard_map/stack | solution.py:205
  11.1 0.1 slice_bitcast_fusion.3
  11.2 1.4 %collective-permute-start.7 = (bf16[4,8,2,384]{3,2,1,0:T(2,128)(2,1)S(1)}, bf16[4,8,2,384]{3,2,1,0:T(2,128)(2,1)S(1)}, u32[]{:S(2)}, u32[]{:S(2)}) collective-permute-start(bf16[4,8,2,384]{3,2,1,0:T(2,128)(2,1)S(1)} %get-tuple-element.42), channel_id=1, source_target_pairs={{0,4},{1,5},{2,6},{3,7},{4,0},{5,1},{6,2},{7,3},{8,12},{9,13},{10,... | collective-permute-start | bytes 147464 | tf_op jit(solution)/shard_map/ppermute | solution.py:213
  12.6 2.2 %collective-permute-start.9 = (bf16[4,8,2,384]{3,2,1,0:T(2,128)(2,1)S(1)}, bf16[4,8,2,384]{3,2,1,0:T(2,128)(2,1)S(1)}, u32[]{:S(2)}, u32[]{:S(2)}) collective-permute-start(bf16[4,8,2,384]{3,2,1,0:T(2,128)(2,1)S(1)} %get-tuple-element.43), channel_id=1, source_target_pairs={{0,12},{1,13},{2,14},{3,15},{4,8},{5,9},{6,10},{7,11},{8,4},{9,5},... | collective-permute-start | bytes 147464 | tf_op jit(solution)/shard_map/ppermute | solution.py:213
  14.8 2.8 %collective-permute-start = (bf16[64,1536]{1,0:T(8,128)(2,1)}, bf16[64,1536]{1,0:T(8,128)(2,1)S(1)}, u32[]{:S(2)}, u32[]{:S(2)}) collective-permute-start(bf16[64,1536]{1,0:T(8,128)(2,1)} %param.10), channel_id=1, source_target_pairs={{1,0},{3,2},{4,5},{6,7},{9,8},{11,10},{12,13},{14,15},{17,16},{19,... | collective-permute-start | bytes 589832 | tf_op jit(solution)/shard_map/ppermute | solution.py:36
  17.6 0.7 collective-permute-start.10
  18.3 0.4 collective-permute-start.17
  18.7 1.6 %collective-permute-start.21 = (bf16[96,1152]{1,0:T(8,128)(2,1)}, bf16[96,1152]{1,0:T(8,128)(2,1)S(1)}, u32[]{:S(2)}, u32[]{:S(2)}) collective-permute-start(bf16[96,1152]{1,0:T(8,128)(2,1)} %get-tuple-element.31), channel_id=1, source_target_pairs={{0,12},{1,15},{2,14},{3,13},{4,8},{5,11},{6,10},{7,9},{8,4},{9,7},... | collective-permute-start | bytes 663560 | tf_op jit(solution)/shard_map/ppermute | solution.py:36
  20.3 1.0 collective-permute-start.8
  21.3 0.9 constant_dynamic-update-slice_fusion.1
  22.2 20.0 %collective-permute-done.8 = bf16[4,8,2,384]{3,2,1,0:T(2,128)(2,1)S(1)} collective-permute-done((bf16[4,8,2,384]{3,2,1,0:T(2,128)(2,1)S(1)}, bf16[4,8,2,384]{3,2,1,0:T(2,128)(2,1)S(1)}, u32[]{:S(2)}, u32[]{:S(2)}) %collective-permute-start.8) | collective-permute-done | bytes 49184 | tf_op jit(solution)/shard_map/ppermute | solution.py:213
  42.2 0.4 collective-permute-start.11
  42.6 0.1 collective-permute-start.19
  42.7 0.9 collective-permute-start.18
  43.6 0.7 collective-permute-start.12
  44.4 5.5 %collective-permute-done.13.refs_4_.refs_5_ = bf16[96,1152]{1,0:T(8,128)(2,1)S(1)} collective-permute-done((bf16[96,1152]{1,0:T(8,128)(2,1)}, bf16[96,1152]{1,0:T(8,128)(2,1)S(1)}, u32[]{:S(2)}, u32[]{:S(2)}) %collective-permute-start.13) | collective-permute-done | bytes 221216 | tf_op jit(solution)/shard_map/ppermute | solution.py:36
  49.8 1.3 %collective-permute-start.3 = (bf16[128,1536]{1,0:T(8,128)(2,1)S(1)}, bf16[128,1536]{1,0:T(8,128)(2,1)S(1)}, u32[]{:S(2)}, u32[]{:S(2)}) collective-permute-start(bf16[128,1536]{1,0:T(8,128)(2,1)S(1)} %constant_dynamic-update-slice_fusion.block), channel_id=1, source_target_pairs={{0,6},{2,4},{5,3},{7,1},{8,14},{10,12},{13,11},{15,9},{16,22},{18,... | collective-permute-start | bytes 1179656 | tf_op jit(solution)/shard_map/ppermute | solution.py:36
  51.1 1.3 %collective-permute-start.2 = (bf16[128,1536]{1,0:T(8,128)(2,1)S(1)}, bf16[128,1536]{1,0:T(8,128)(2,1)S(1)}, u32[]{:S(2)}, u32[]{:S(2)}) collective-permute-start(bf16[128,1536]{1,0:T(8,128)(2,1)S(1)} %constant_dynamic-update-slice_fusion.block), channel_id=1, source_target_pairs={{0,4},{2,6},{5,1},{7,3},{8,12},{10,14},{13,9},{15,11},{16,20},{18,... | collective-permute-start | bytes 1179656 | tf_op jit(solution)/shard_map/ppermute | solution.py:36
  52.4 0.7 collective-permute-start.1
  53.1 0.3 pad_maximum_fusion.1
  53.5 1.4 %collective-permute-start.14 = (bf16[96,1152]{1,0:T(8,128)(2,1)S(1)}, bf16[96,1152]{1,0:T(8,128)(2,1)S(1)}, u32[]{:S(2)}, u32[]{:S(2)}) collective-permute-start(bf16[96,1152]{1,0:T(8,128)(2,1)S(1)} %collective-permute-done.13.refs_4_.refs_5_), channel_id=1, source_target_pairs={{0,16},{1,17},{2,18},{3,19},{4,20},{5,21},{6,22},{7,23},{8,24},{9,... | collective-permute-start | bytes 663560 | tf_op jit(solution)/shard_map/ppermute | solution.py:36
  55.0 0.3 fusion
  55.3 3.0 %collective-permute-done.22.refs_13_.refs_1_ = bf16[96,1152]{1,0:T(8,128)(2,1)S(1)} collective-permute-done((bf16[96,1152]{1,0:T(8,128)(2,1)S(1)}, bf16[96,1152]{1,0:T(8,128)(2,1)S(1)}, u32[]{:S(2)}, u32[]{:S(2)}) %collective-permute-start.22) | collective-permute-done | bytes 221216 | tf_op jit(solution)/shard_map/ppermute | solution.py:36
  58.3 5.4 %collective-permute-start.23 = (bf16[96,1152]{1,0:T(8,128)(2,1)S(1)}, bf16[96,1152]{1,0:T(8,128)(2,1)S(1)}, u32[]{:S(2)}, u32[]{:S(2)}) collective-permute-start(bf16[96,1152]{1,0:T(8,128)(2,1)S(1)} %collective-permute-done.21.refs_12_.refs_0_), channel_id=1, source_target_pairs={{0,1},{1,0},{2,3},{3,2},{4,5},{5,4},{6,7},{7,6},{8,9},{9,8},{10,11... | collective-permute-start | bytes 663560 | tf_op jit(solution)/shard_map/ppermute | solution.py:36
  63.7 2.4 %collective-permute-start.15 = (bf16[96,1152]{1,0:T(8,128)(2,1)S(1)}, bf16[96,1152]{1,0:T(8,128)(2,1)S(1)}, u32[]{:S(2)}, u32[]{:S(2)}) collective-permute-start(bf16[96,1152]{1,0:T(8,128)(2,1)S(1)} %collective-permute-done.13.refs_4_.refs_5_), channel_id=1, source_target_pairs={{0,1},{1,0},{2,3},{3,2},{4,5},{5,4},{6,7},{7,6},{8,9},{9,8},{10,11... | collective-permute-start | bytes 663560 | tf_op jit(solution)/shard_map/ppermute | solution.py:36
  66.1 0.5 collective-permute-start.24
  66.7 0.7 copy-done.1
  67.5 1.4 %shard_map.100 = (f32[4,1536]{1,0:T(4,128)S(1)}, bf16[256,1536]{1,0:T(8,128)(2,1)S(1)}, bf16[256,1536]{1,0:T(8,128)(2,1)S(1)}) custom-call(f32[4,1536]{1,0:T(4,128)S(1)} %copy-done.1, bf16[128,1536]{1,0:T(8,128)(2,1)S(1)} %constant_dynamic-update-slice_fusion.block, bf16[128,1536]{1,0:T(8,128)(2,1)S(1)} %collective-permute-done.1.near, ...), custom_call_target="tpu_custom_call" | custom-call | bytes 1597440 | tf_op jit(solution)/shard_map/pallas_call | solution.py:412
  68.9 1.2 %shard_map.102.part_ref = f32[256,1152]{1,0:T(8,128)S(1)} custom-call(bf16[256,1536]{1,0:T(8,128)(2,1)S(1)} %get-tuple-element.33.refs_0_.normed, bf16[96,1152]{1,0:T(8,128)(2,1)S(1)} %copy-done, bf16[96,1152]{1,0:T(8,128)(2,1)S(1)} %collective-permute-done.10.refs_1_.refs_2_, bf16[96,1152]{1,0:T(8,128)(2,1)S(1)} %collective-permute-done.11.refs_2_.refs_3_, ...), custom_call_target="tpu_custom_call" | custom-call | flops 679477248 | bytes 3440640 | tf_op jit(solution)/shard_map/pallas_call | solution.py:412
  70.2 2.2 %shard_map.103.first_part = bf16[256,384]{1,0:T(8,128)(2,1)S(1)} custom-call(f32[4,1536]{1,0:T(4,128)S(1)} %get-tuple-element.23.extra_ref, bf16[128,384]{1,0:T(8,128)(2,1)S(1)} %get-tuple-element.46.key_ref, bf16[128,384]{1,0:T(8,128)(2,1)S(1)} %get-tuple-element.45.value_ref, bf16[256,1536]{1,0:T(8,128)(2,1)S(1)} %get-tuple-element.33.refs_0_.normed, ...), custom_call_target="tpu_custom_call" | custom-call | flops 377487360 | bytes 3072000 | tf_op jit(solution)/shard_map/pallas_call | solution.py:412
  72.4 1.4 %collective-permute-start.27 = (bf16[256,384]{1,0:T(8,128)(2,1)S(1)}, bf16[256,384]{1,0:T(8,128)(2,1)S(1)}, u32[]{:S(2)}, u32[]{:S(2)}) collective-permute-start(bf16[256,384]{1,0:T(8,128)(2,1)S(1)} %shard_map.103.first_part), channel_id=1, source_target_pairs={{0,2},{1,3},{2,0},{3,1},{4,6},{5,7},{6,4},{7,5},{8,10},{9,11},{10,... | collective-permute-start | bytes 589832 | tf_op jit(solution)/shard_map/ppermute | solution.py:36
  73.8 0.2 collective-permute-start.26
  74.0 1.1 %collective-permute-start.25 = (bf16[256,384]{1,0:T(8,128)(2,1)S(1)}, bf16[256,384]{1,0:T(8,128)(2,1)S(1)}, u32[]{:S(2)}, u32[]{:S(2)}) collective-permute-start(bf16[256,384]{1,0:T(8,128)(2,1)S(1)} %shard_map.103.first_part), channel_id=1, source_target_pairs={{0,6},{1,7},{2,4},{3,5},{4,2},{5,3},{6,0},{7,1},{8,14},{9,15},{10,... | collective-permute-start | bytes 589832 | tf_op jit(solution)/shard_map/ppermute | solution.py:36
  75.1 0.3 shard_map.101.weights
  75.3 3.1 %collective-permute-done.27.fourth_part = bf16[256,384]{1,0:T(8,128)(2,1)S(1)} collective-permute-done((bf16[256,384]{1,0:T(8,128)(2,1)S(1)}, bf16[256,384]{1,0:T(8,128)(2,1)S(1)}, u32[]{:S(2)}, u32[]{:S(2)}) %collective-permute-start.27) | collective-permute-done | bytes 196640 | tf_op jit(solution)/shard_map/ppermute | solution.py:36
  78.4 1.1 %collective-permute-done.26.third_part = bf16[256,384]{1,0:T(8,128)(2,1)S(1)} collective-permute-done((bf16[256,384]{1,0:T(8,128)(2,1)S(1)}, bf16[256,384]{1,0:T(8,128)(2,1)S(1)}, u32[]{:S(2)}, u32[]{:S(2)}) %collective-permute-start.26) | collective-permute-done | bytes 196640 | tf_op jit(solution)/shard_map/ppermute | solution.py:36
  79.5 4.0 %collective-permute-done.25.second_part = bf16[256,384]{1,0:T(8,128)(2,1)S(1)} collective-permute-done((bf16[256,384]{1,0:T(8,128)(2,1)S(1)}, bf16[256,384]{1,0:T(8,128)(2,1)S(1)}, u32[]{:S(2)}, u32[]{:S(2)}) %collective-permute-start.25) | collective-permute-done | bytes 196640 | tf_op jit(solution)/shard_map/ppermute | solution.py:36
  83.6 4.0 %shard_map.104 = (bf16[64,384]{1,0:T(8,128)(2,1)S(1)}, bf16[64,384]{1,0:T(8,128)(2,1)S(1)}, bf16[64,384]{1,0:T(8,128)(2,1)S(1)}, bf16[64,384]{1,0:T(8,128)(2,1)S(1)}, bf16[64,384]{1,0:T(8,128)(2,1)S(1)}) custom-call(f32[4,1536]{1,0:T(4,128)S(1)} %get-tuple-element.23.extra_ref, bf16[128,384]{1,0:T(8,128)(2,1)S(1)} %get-tuple-element.46.key_ref, ...), custom_call_target="tpu_custom_call" | custom-call | flops 1056964608 | bytes 5332992 | tf_op jit(solution)/shard_map/pallas_call | solution.py:412
  87.6 2.2 %collective-permute-start.28 = (bf16[64,384]{1,0:T(8,128)(2,1)S(1)}, bf16[64,384]{1,0:T(8,128)(2,1)S(1)}, u32[]{:S(2)}, u32[]{:S(2)}) collective-permute-start(bf16[64,384]{1,0:T(8,128)(2,1)S(1)} %get-tuple-element.35), channel_id=1, source_target_pairs={{0,2},{1,4},{2,0},{3,6},{4,1},{5,7},{6,3},{7,5},{8,10},{9,12},{10,... | collective-permute-start | bytes 147464 | tf_op jit(solution)/shard_map/ppermute | solution.py:36
  89.8 1.3 %collective-permute-start.30 = (bf16[64,384]{1,0:T(8,128)(2,1)S(1)}, bf16[64,384]{1,0:T(8,128)(2,1)S(1)}, u32[]{:S(2)}, u32[]{:S(2)}) collective-permute-start(bf16[64,384]{1,0:T(8,128)(2,1)S(1)} %get-tuple-element.37), channel_id=1, source_target_pairs={{0,1},{1,7},{2,3},{3,5},{4,2},{5,4},{6,0},{7,6},{8,9},{9,15},{10,1... | collective-permute-start | bytes 147464 | tf_op jit(solution)/shard_map/ppermute | solution.py:36
  91.1 4.5 %collective-permute-start.31 = (bf16[64,384]{1,0:T(8,128)(2,1)S(1)}, bf16[64,384]{1,0:T(8,128)(2,1)S(1)}, u32[]{:S(2)}, u32[]{:S(2)}) collective-permute-start(bf16[64,384]{1,0:T(8,128)(2,1)S(1)} %get-tuple-element.38), channel_id=1, source_target_pairs={{1,6},{3,4},{4,3},{6,1},{9,14},{11,12},{12,11},{14,9},{17,22},{19,... | collective-permute-start | bytes 147464 | tf_op jit(solution)/shard_map/ppermute | solution.py:36
  95.6 1.8 %collective-permute-done.31.fourth = bf16[64,384]{1,0:T(8,128)(2,1)S(1)} collective-permute-done((bf16[64,384]{1,0:T(8,128)(2,1)S(1)}, bf16[64,384]{1,0:T(8,128)(2,1)S(1)}, u32[]{:S(2)}, u32[]{:S(2)}) %collective-permute-start.31) | collective-permute-done | bytes 49184 | tf_op jit(solution)/shard_map/ppermute | solution.py:36
  97.4 0.7 shard_map.105
  (34 shorter events, 0.3 us)
Async XLA Ops:
  3.2 65.7 %copy-start = (bf16[96,1152]{1,0:T(8,128)(2,1)S(1)}, bf16[96,1152]{1,0:T(8,128)(2,1)}, u32[]{:S(2)}) copy-start(bf16[96,1152]{1,0:T(8,128)(2,1)} %get-tuple-element.29.refs_0_.refs_1_) | copy-start | bytes 663556
  3.2 2.8 %collective-permute-start.4 = (bf16[4,8,2,384]{3,2,1,0:T(2,128)(2,1)}, bf16[4,8,2,384]{3,2,1,0:T(2,128)(2,1)S(1)}, u32[]{:S(2)}, u32[]{:S(2)}) collective-permute-start(bf16[4,8,2,384]{3,2,1,0:T(2,128)(2,1)} %get-tuple-element.25), channel_id=1, source_target_pairs={{0,1},{1,0},{2,3},{3,2},{4,5},{5,4},{6,7},{7,6},{8,9},{9,8},{10,11... | collective-permute-start | bytes 147464 | tf_op jit(solution)/shard_map/ppermute | solution.py:213
  3.3 5.0 %collective-permute-start.5 = (bf16[4,8,2,384]{3,2,1,0:T(2,128)(2,1)}, bf16[4,8,2,384]{3,2,1,0:T(2,128)(2,1)S(1)}, u32[]{:S(2)}, u32[]{:S(2)}) collective-permute-start(bf16[4,8,2,384]{3,2,1,0:T(2,128)(2,1)} %get-tuple-element.26), channel_id=1, source_target_pairs={{0,2},{1,3},{2,0},{3,1},{4,6},{5,7},{6,4},{7,5},{8,10},{9,11},{10,... | collective-permute-start | bytes 147464 | tf_op jit(solution)/shard_map/ppermute | solution.py:213
  6.0 3.9 %collective-permute-start.6 = (bf16[4,8,2,384]{3,2,1,0:T(2,128)(2,1)}, bf16[4,8,2,384]{3,2,1,0:T(2,128)(2,1)S(1)}, u32[]{:S(2)}, u32[]{:S(2)}) collective-permute-start(bf16[4,8,2,384]{3,2,1,0:T(2,128)(2,1)} %get-tuple-element.27), channel_id=1, source_target_pairs={{0,3},{1,2},{2,1},{3,0},{4,7},{5,6},{6,5},{7,4},{8,11},{9,10},{10,... | collective-permute-start | bytes 147464 | tf_op jit(solution)/shard_map/ppermute | solution.py:213
  11.2 7.5 %collective-permute-start.7 = (bf16[4,8,2,384]{3,2,1,0:T(2,128)(2,1)S(1)}, bf16[4,8,2,384]{3,2,1,0:T(2,128)(2,1)S(1)}, u32[]{:S(2)}, u32[]{:S(2)}) collective-permute-start(bf16[4,8,2,384]{3,2,1,0:T(2,128)(2,1)S(1)} %get-tuple-element.42), channel_id=1, source_target_pairs={{0,4},{1,5},{2,6},{3,7},{4,0},{5,1},{6,2},{7,3},{8,12},{9,13},{10,... | collective-permute-start | bytes 147464 | tf_op jit(solution)/shard_map/ppermute | solution.py:213
  12.6 7.7 %collective-permute-start.9 = (bf16[4,8,2,384]{3,2,1,0:T(2,128)(2,1)S(1)}, bf16[4,8,2,384]{3,2,1,0:T(2,128)(2,1)S(1)}, u32[]{:S(2)}, u32[]{:S(2)}) collective-permute-start(bf16[4,8,2,384]{3,2,1,0:T(2,128)(2,1)S(1)} %get-tuple-element.43), channel_id=1, source_target_pairs={{0,12},{1,13},{2,14},{3,15},{4,8},{5,9},{6,10},{7,11},{8,4},{9,5},... | collective-permute-start | bytes 147464 | tf_op jit(solution)/shard_map/ppermute | solution.py:213
  14.8 27.4 %collective-permute-start = (bf16[64,1536]{1,0:T(8,128)(2,1)}, bf16[64,1536]{1,0:T(8,128)(2,1)S(1)}, u32[]{:S(2)}, u32[]{:S(2)}) collective-permute-start(bf16[64,1536]{1,0:T(8,128)(2,1)} %param.10), channel_id=1, source_target_pairs={{1,0},{3,2},{4,5},{6,7},{9,8},{11,10},{12,13},{14,15},{17,16},{19,... | collective-permute-start | bytes 589832 | tf_op jit(solution)/shard_map/ppermute | solution.py:36
  17.6 25.1 %collective-permute-start.10 = (bf16[96,1152]{1,0:T(8,128)(2,1)}, bf16[96,1152]{1,0:T(8,128)(2,1)S(1)}, u32[]{:S(2)}, u32[]{:S(2)}) collective-permute-start(bf16[96,1152]{1,0:T(8,128)(2,1)} %get-tuple-element.30), channel_id=1, source_target_pairs={{0,2},{1,3},{2,0},{3,1},{4,6},{5,7},{6,4},{7,5},{8,10},{9,11},{10,... | collective-permute-start | bytes 663560 | tf_op jit(solution)/shard_map/ppermute | solution.py:36
  18.3 24.3 %collective-permute-start.17 = (bf16[96,1152]{1,0:T(8,128)(2,1)}, bf16[96,1152]{1,0:T(8,128)(2,1)S(1)}, u32[]{:S(2)}, u32[]{:S(2)}) collective-permute-start(bf16[96,1152]{1,0:T(8,128)(2,1)} %get-tuple-element.32), channel_id=1, source_target_pairs={{0,8},{1,11},{2,10},{3,9},{4,12},{5,15},{6,14},{7,13},{8,0},{9,3},... | collective-permute-start | bytes 663560 | tf_op jit(solution)/shard_map/ppermute | solution.py:36
  18.7 24.9 %collective-permute-start.21 = (bf16[96,1152]{1,0:T(8,128)(2,1)}, bf16[96,1152]{1,0:T(8,128)(2,1)S(1)}, u32[]{:S(2)}, u32[]{:S(2)}) collective-permute-start(bf16[96,1152]{1,0:T(8,128)(2,1)} %get-tuple-element.31), channel_id=1, source_target_pairs={{0,12},{1,15},{2,14},{3,13},{4,8},{5,11},{6,10},{7,9},{8,4},{9,7},... | collective-permute-start | bytes 663560 | tf_op jit(solution)/shard_map/ppermute | solution.py:36
  20.3 21.9 %collective-permute-start.8 = (bf16[4,8,2,384]{3,2,1,0:T(2,128)(2,1)S(1)}, bf16[4,8,2,384]{3,2,1,0:T(2,128)(2,1)S(1)}, u32[]{:S(2)}, u32[]{:S(2)}) collective-permute-start(bf16[4,8,2,384]{3,2,1,0:T(2,128)(2,1)S(1)} %get-tuple-element.44), channel_id=1, source_target_pairs={{0,8},{1,9},{2,10},{3,11},{4,12},{5,13},{6,14},{7,15},{8,0},{9,1},... | collective-permute-start | bytes 147464 | tf_op jit(solution)/shard_map/ppermute | solution.py:213
  42.2 7.6 %collective-permute-start.13 = (bf16[96,1152]{1,0:T(8,128)(2,1)}, bf16[96,1152]{1,0:T(8,128)(2,1)S(1)}, u32[]{:S(2)}, u32[]{:S(2)}) collective-permute-start(bf16[96,1152]{1,0:T(8,128)(2,1)} %get-tuple-element.31), channel_id=1, source_target_pairs={{0,4},{1,7},{2,6},{3,5},{4,0},{5,3},{6,2},{7,1},{8,12},{9,15},{10,... | collective-permute-start | bytes 663560 | tf_op jit(solution)/shard_map/ppermute | solution.py:36
  42.2 8.9 %collective-permute-start.11 = (bf16[96,1152]{1,0:T(8,128)(2,1)}, bf16[96,1152]{1,0:T(8,128)(2,1)S(1)}, u32[]{:S(2)}, u32[]{:S(2)}) collective-permute-start(bf16[96,1152]{1,0:T(8,128)(2,1)} %get-tuple-element.29.refs_0_.refs_1_), channel_id=1, source_target_pairs={{0,1},{1,0},{2,3},{3,2},{4,5},{5,4},{6,7},{7,6},{8,9},{9,8},{10,11... | collective-permute-start | bytes 663560 | tf_op jit(solution)/shard_map/ppermute | solution.py:36
  42.6 10.8 %collective-permute-start.19 = (bf16[96,1152]{1,0:T(8,128)(2,1)S(1)}, bf16[96,1152]{1,0:T(8,128)(2,1)S(1)}, u32[]{:S(2)}, u32[]{:S(2)}) collective-permute-start(bf16[96,1152]{1,0:T(8,128)(2,1)S(1)} %collective-permute-done.17.refs_8_.refs_9_), channel_id=1, source_target_pairs={{0,1},{1,0},{2,3},{3,2},{4,5},{5,4},{6,7},{7,6},{8,9},{9,8},{10,11... | collective-permute-start | bytes 663560 | tf_op jit(solution)/shard_map/ppermute | solution.py:36
  42.7 10.8 %collective-permute-start.18 = (bf16[96,1152]{1,0:T(8,128)(2,1)S(1)}, bf16[96,1152]{1,0:T(8,128)(2,1)S(1)}, u32[]{:S(2)}, u32[]{:S(2)}) collective-permute-start(bf16[96,1152]{1,0:T(8,128)(2,1)S(1)} %collective-permute-done.17.refs_8_.refs_9_), channel_id=1, source_target_pairs={{0,16},{1,17},{2,18},{3,19},{4,20},{5,21},{6,22},{7,23},{8,24},{9,... | collective-permute-start | bytes 663560 | tf_op jit(solution)/shard_map/ppermute | solution.py:36
  43.6 8.8 %collective-permute-start.12 = (bf16[96,1152]{1,0:T(8,128)(2,1)S(1)}, bf16[96,1152]{1,0:T(8,128)(2,1)S(1)}, u32[]{:S(2)}, u32[]{:S(2)}) collective-permute-start(bf16[96,1152]{1,0:T(8,128)(2,1)S(1)} %collective-permute-done.10.refs_1_.refs_2_), channel_id=1, source_target_pairs={{0,1},{1,0},{2,3},{3,2},{4,5},{5,4},{6,7},{7,6},{8,9},{9,8},{10,11... | collective-permute-start | bytes 663560 | tf_op jit(solution)/shard_map/ppermute | solution.py:36
  49.8 16.3 %collective-permute-start.3 = (bf16[128,1536]{1,0:T(8,128)(2,1)S(1)}, bf16[128,1536]{1,0:T(8,128)(2,1)S(1)}, u32[]{:S(2)}, u32[]{:S(2)}) collective-permute-start(bf16[128,1536]{1,0:T(8,128)(2,1)S(1)} %constant_dynamic-update-slice_fusion.block), channel_id=1, source_target_pairs={{0,6},{2,4},{5,3},{7,1},{8,14},{10,12},{13,11},{15,9},{16,22},{18,... | collective-permute-start | bytes 1179656 | tf_op jit(solution)/shard_map/ppermute | solution.py:36
  51.1 15.0 %collective-permute-start.2 = (bf16[128,1536]{1,0:T(8,128)(2,1)S(1)}, bf16[128,1536]{1,0:T(8,128)(2,1)S(1)}, u32[]{:S(2)}, u32[]{:S(2)}) collective-permute-start(bf16[128,1536]{1,0:T(8,128)(2,1)S(1)} %constant_dynamic-update-slice_fusion.block), channel_id=1, source_target_pairs={{0,4},{2,6},{5,1},{7,3},{8,12},{10,14},{13,9},{15,11},{16,20},{18,... | collective-permute-start | bytes 1179656 | tf_op jit(solution)/shard_map/ppermute | solution.py:36
  52.4 14.2 %collective-permute-start.1 = (bf16[128,1536]{1,0:T(8,128)(2,1)S(1)}, bf16[128,1536]{1,0:T(8,128)(2,1)S(1)}, u32[]{:S(2)}, u32[]{:S(2)}) collective-permute-start(bf16[128,1536]{1,0:T(8,128)(2,1)S(1)} %constant_dynamic-update-slice_fusion.block), channel_id=1, source_target_pairs={{0,2},{2,0},{5,7},{7,5},{8,10},{10,8},{13,15},{15,13},{16,18},{18,... | collective-permute-start | bytes 1179656 | tf_op jit(solution)/shard_map/ppermute | solution.py:36
  53.4 4.8 %collective-permute-start.22 = (bf16[96,1152]{1,0:T(8,128)(2,1)S(1)}, bf16[96,1152]{1,0:T(8,128)(2,1)S(1)}, u32[]{:S(2)}, u32[]{:S(2)}) collective-permute-start(bf16[96,1152]{1,0:T(8,128)(2,1)S(1)} %collective-permute-done.21.refs_12_.refs_0_), channel_id=1, source_target_pairs={{0,16},{1,17},{2,18},{3,19},{4,20},{5,21},{6,22},{7,23},{8,24},{9,... | collective-permute-start | bytes 663560 | tf_op jit(solution)/shard_map/ppermute | solution.py:36
  53.5 10.2 %collective-permute-start.14 = (bf16[96,1152]{1,0:T(8,128)(2,1)S(1)}, bf16[96,1152]{1,0:T(8,128)(2,1)S(1)}, u32[]{:S(2)}, u32[]{:S(2)}) collective-permute-start(bf16[96,1152]{1,0:T(8,128)(2,1)S(1)} %collective-permute-done.13.refs_4_.refs_5_), channel_id=1, source_target_pairs={{0,16},{1,17},{2,18},{3,19},{4,20},{5,21},{6,22},{7,23},{8,24},{9,... | collective-permute-start | bytes 663560 | tf_op jit(solution)/shard_map/ppermute | solution.py:36
  58.3 11.9 %collective-permute-start.23 = (bf16[96,1152]{1,0:T(8,128)(2,1)S(1)}, bf16[96,1152]{1,0:T(8,128)(2,1)S(1)}, u32[]{:S(2)}, u32[]{:S(2)}) collective-permute-start(bf16[96,1152]{1,0:T(8,128)(2,1)S(1)} %collective-permute-done.21.refs_12_.refs_0_), channel_id=1, source_target_pairs={{0,1},{1,0},{2,3},{3,2},{4,5},{5,4},{6,7},{7,6},{8,9},{9,8},{10,11... | collective-permute-start | bytes 663560 | tf_op jit(solution)/shard_map/ppermute | solution.py:36
  63.7 5.2 %collective-permute-start.15 = (bf16[96,1152]{1,0:T(8,128)(2,1)S(1)}, bf16[96,1152]{1,0:T(8,128)(2,1)S(1)}, u32[]{:S(2)}, u32[]{:S(2)}) collective-permute-start(bf16[96,1152]{1,0:T(8,128)(2,1)S(1)} %collective-permute-done.13.refs_4_.refs_5_), channel_id=1, source_target_pairs={{0,1},{1,0},{2,3},{3,2},{4,5},{5,4},{6,7},{7,6},{8,9},{9,8},{10,11... | collective-permute-start | bytes 663560 | tf_op jit(solution)/shard_map/ppermute | solution.py:36
  66.1 2.8 %collective-permute-start.20 = (bf16[96,1152]{1,0:T(8,128)(2,1)S(1)}, bf16[96,1152]{1,0:T(8,128)(2,1)S(1)}, u32[]{:S(2)}, u32[]{:S(2)}) collective-permute-start(bf16[96,1152]{1,0:T(8,128)(2,1)S(1)} %collective-permute-done.18.refs_9_.refs_10_), channel_id=1, source_target_pairs={{0,1},{1,0},{2,3},{3,2},{4,5},{5,4},{6,7},{7,6},{8,9},{9,8},{10,11... | collective-permute-start | bytes 663560 | tf_op jit(solution)/shard_map/ppermute | solution.py:36
  66.1 4.1 %collective-permute-start.24 = (bf16[96,1152]{1,0:T(8,128)(2,1)S(1)}, bf16[96,1152]{1,0:T(8,128)(2,1)S(1)}, u32[]{:S(2)}, u32[]{:S(2)}) collective-permute-start(bf16[96,1152]{1,0:T(8,128)(2,1)S(1)} %collective-permute-done.22.refs_13_.refs_1_), channel_id=1, source_target_pairs={{0,1},{1,0},{2,3},{3,2},{4,5},{5,4},{6,7},{7,6},{8,9},{9,8},{10,11... | collective-permute-start | bytes 663560 | tf_op jit(solution)/shard_map/ppermute | solution.py:36
  66.6 2.3 %collective-permute-start.16 = (bf16[96,1152]{1,0:T(8,128)(2,1)S(1)}, bf16[96,1152]{1,0:T(8,128)(2,1)S(1)}, u32[]{:S(2)}, u32[]{:S(2)}) collective-permute-start(bf16[96,1152]{1,0:T(8,128)(2,1)S(1)} %collective-permute-done.14.refs_5_.refs_6_), channel_id=1, source_target_pairs={{0,1},{1,0},{2,3},{3,2},{4,5},{5,4},{6,7},{7,6},{8,9},{9,8},{10,11... | collective-permute-start | bytes 663560 | tf_op jit(solution)/shard_map/ppermute | solution.py:36
  66.7 0.7 copy-start.1
  72.4 6.1 %collective-permute-start.27 = (bf16[256,384]{1,0:T(8,128)(2,1)S(1)}, bf16[256,384]{1,0:T(8,128)(2,1)S(1)}, u32[]{:S(2)}, u32[]{:S(2)}) collective-permute-start(bf16[256,384]{1,0:T(8,128)(2,1)S(1)} %shard_map.103.first_part), channel_id=1, source_target_pairs={{0,2},{1,3},{2,0},{3,1},{4,6},{5,7},{6,4},{7,5},{8,10},{9,11},{10,... | collective-permute-start | bytes 589832 | tf_op jit(solution)/shard_map/ppermute | solution.py:36
  73.8 5.7 %collective-permute-start.26 = (bf16[256,384]{1,0:T(8,128)(2,1)S(1)}, bf16[256,384]{1,0:T(8,128)(2,1)S(1)}, u32[]{:S(2)}, u32[]{:S(2)}) collective-permute-start(bf16[256,384]{1,0:T(8,128)(2,1)S(1)} %shard_map.103.first_part), channel_id=1, source_target_pairs={{0,4},{1,5},{2,6},{3,7},{4,0},{5,1},{6,2},{7,3},{8,12},{9,13},{10,... | collective-permute-start | bytes 589832 | tf_op jit(solution)/shard_map/ppermute | solution.py:36
  74.0 9.6 %collective-permute-start.25 = (bf16[256,384]{1,0:T(8,128)(2,1)S(1)}, bf16[256,384]{1,0:T(8,128)(2,1)S(1)}, u32[]{:S(2)}, u32[]{:S(2)}) collective-permute-start(bf16[256,384]{1,0:T(8,128)(2,1)S(1)} %shard_map.103.first_part), channel_id=1, source_target_pairs={{0,6},{1,7},{2,4},{3,5},{4,2},{5,3},{6,0},{7,1},{8,14},{9,15},{10,... | collective-permute-start | bytes 589832 | tf_op jit(solution)/shard_map/ppermute | solution.py:36
  87.6 8.0 %collective-permute-start.28 = (bf16[64,384]{1,0:T(8,128)(2,1)S(1)}, bf16[64,384]{1,0:T(8,128)(2,1)S(1)}, u32[]{:S(2)}, u32[]{:S(2)}) collective-permute-start(bf16[64,384]{1,0:T(8,128)(2,1)S(1)} %get-tuple-element.35), channel_id=1, source_target_pairs={{0,2},{1,4},{2,0},{3,6},{4,1},{5,7},{6,3},{7,5},{8,10},{9,12},{10,... | collective-permute-start | bytes 147464 | tf_op jit(solution)/shard_map/ppermute | solution.py:36
  89.8 5.8 %collective-permute-start.29 = (bf16[64,384]{1,0:T(8,128)(2,1)S(1)}, bf16[64,384]{1,0:T(8,128)(2,1)S(1)}, u32[]{:S(2)}, u32[]{:S(2)}) collective-permute-start(bf16[64,384]{1,0:T(8,128)(2,1)S(1)} %get-tuple-element.36), channel_id=1, source_target_pairs={{0,3},{1,5},{2,1},{3,7},{4,0},{5,6},{6,2},{7,4},{8,11},{9,13},{10,... | collective-permute-start | bytes 147464 | tf_op jit(solution)/shard_map/ppermute | solution.py:36
  89.8 5.8 %collective-permute-start.30 = (bf16[64,384]{1,0:T(8,128)(2,1)S(1)}, bf16[64,384]{1,0:T(8,128)(2,1)S(1)}, u32[]{:S(2)}, u32[]{:S(2)}) collective-permute-start(bf16[64,384]{1,0:T(8,128)(2,1)S(1)} %get-tuple-element.37), channel_id=1, source_target_pairs={{0,1},{1,7},{2,3},{3,5},{4,2},{5,4},{6,0},{7,6},{8,9},{9,15},{10,1... | collective-permute-start | bytes 147464 | tf_op jit(solution)/shard_map/ppermute | solution.py:36
  91.1 6.3 %collective-permute-start.31 = (bf16[64,384]{1,0:T(8,128)(2,1)S(1)}, bf16[64,384]{1,0:T(8,128)(2,1)S(1)}, u32[]{:S(2)}, u32[]{:S(2)}) collective-permute-start(bf16[64,384]{1,0:T(8,128)(2,1)S(1)} %get-tuple-element.38), channel_id=1, source_target_pairs={{1,6},{3,4},{4,3},{6,1},{9,14},{11,12},{12,11},{14,9},{17,22},{19,... | collective-permute-start | bytes 147464 | tf_op jit(solution)/shard_map/ppermute | solution.py:36

commit v6 on v5

--- a/solution.py
+++ b/solution.py
@@ -132,13 +132,17 @@
     gives[-1].start()
     for pick in picks:
         pick.wait()
+    bits = devices.bit_length() - 1
     for away in range(devices):
         to_plane, to_y, to_c = coords(flipped(index, away))
         to_frame = (to_plane // 2) * 2 + to_c
+        place = 0
+        for bit in range(2, bits):
+            place = place * 2 + (away >> bit & 1)
         gives.append(
             pltpu.make_async_copy(
                 stored.at[pl.ds(to_frame * entries, entries), :, columns(quarter_of(to_plane, to_y), width)],
-                memory_refs[away % SPATIAL].at[away // SPATIAL],
+                memory_refs[away % SPATIAL].at[place],
                 give_sem.at[away],
             )
         )
@@ -200,12 +204,14 @@
 
 
 def all_memory(parts):
-    planes = lax.axis_size("frame") // SPATIAL
+    devices = lax.axis_size("frame")
     near = [parts[0]] + [hop(part, place) for place, part in enumerate(parts) if place]
-    held = jnp.stack(near, axis=1)
-    arrived = [held[0]] + [hop(held[bits], bits * SPATIAL) for bits in range(1, planes)]
-    held = jnp.concatenate(arrived)
-    keys, values = held[:, :, 0, :], held[:, :, 1, :]
+    held = jnp.stack(near)
+    for bit in range(2, devices.bit_length() - 1):
+        half = held.shape[1] // 2
+        arrived = hop(held[:, half:], 1 << bit)
+        held = jnp.concatenate([held[:, :half], arrived])
+    keys, values = held[:, 0, :, 0, :], held[:, 0, :, 1, :]
     return keys.reshape(-1, keys.shape[-1]), values.reshape(-1, values.shape[-1])
 
 
@@ -218,8 +224,8 @@
     block = jnp.concatenate([latent, other])
     near = moved(block, lambda x, p, y, c: (x, p, 1 - y, c) if c == p % 2 else None)
     far = moved(block, lambda x, p, y, c: (x, p ^ 1, y, c) if c == p % 2 else None)
-    both = moved(block, lambda x, p, y, c: (x, p ^ 1, 1 - y, c) if c == p % 2 else None)
-    return block, near, far, both
+    far_near = moved(far, lambda x, p, y, c: (x, p, 1 - y, c) if c != p % 2 else None)
+    return block, near, far, far_near
 
 
 def late_plane(devices):

time: 98.4 us -> 102 us (1.037)
  starting transfers between devices: 38.9 us -> 42.2 us
    ppermute x26, waiting for transfers between devices: 18.5 us -> 26.7 us  [moved(): return lax.ppermute(array, AXES, pairs)]
    ppermute x6 -> x5, waiting for transfers between devices: 23.8 us -> 15.8 us  [hop(): lax.ppermute(array, 'frame', [(i, i ^ bits) for i in range(lax.axis_size(...]
    ppermute x26, starting transfers between devices: 31.5 us -> 34.1 us  [moved(): return lax.ppermute(array, AXES, pairs)]
    ppermute x6 -> x5, starting transfers between devices: 7.37 us -> 8.07 us  [hop(): lax.ppermute(array, 'frame', [(i, i ^ bits) for i in range(lax.axis_size(...]
  transfers between devices with their start and end apart: 32 -> 31, of which waited for: 9 -> 12; matrix products, arithmetic and copies ran while one was open for 2% -> 3% of each run, Pallas kernels for 3% -> 6%
where the time goes in v6:
time: 102 us
  waiting for transfers between devices  42.5 us (42%)
  starting transfers between devices  42.2 us (41%)
  Pallas kernels  13 us (13%)
  local copies, waits for them, and re-layouts  1.86 us (2%)
  other arithmetic  1.73 us (2%)
    ppermute x26, starting transfers between devices, moved(): return lax.ppermute(array, AXES, pairs)  34.1 us
    ppermute x26, waiting for transfers between devices, moved(): return lax.ppermute(array, AXES, pairs)  26.7 us
    ppermute x5, waiting for transfers between devices, hop(): lax.ppermute(array, 'frame', [(i, i ^ bits) for i in range(lax.axis_size(...  15.8 us
    pallas_call x6, Pallas kernels, kernel_call(): pl.pallas_call(kernel, out_shape=out_shape, in_specs=[free if number in a...  9.81 us
    ppermute x5, starting transfers between devices, hop(): lax.ppermute(array, 'frame', [(i, i ^ bits) for i in range(lax.axis_size(...  8.07 us
    pallas_call x1, Pallas kernels, pack(): pl.pallas_call(pack_kernel, out_shape=out_shape, in_specs=[held] * 9, out...  3.19 us
  transfers between devices with their start and end apart: 31, of which 12 were waited for; matrix products, arithmetic and copies ran while one was open for 3% of the time, Pallas kernels for 6%

profile of v6, /device:TPU:1, one launch (start us, length us, event | category | flops | bytes accessed | tf_op | source)
XLA Modules:
  0.0 101.5 jit_solution(11867550883290126473)
XLA Ops:
  0.0 1.9 %collective-permute-start = (bf16[64,1536]{1,0:T(8,128)(2,1)}, bf16[64,1536]{1,0:T(8,128)(2,1)S(1)}, u32[]{:S(2)}, u32[]{:S(2)}) collective-permute-start(bf16[64,1536]{1,0:T(8,128)(2,1)} %param.10), channel_id=1, source_target_pairs={{1,0},{3,2},{4,5},{6,7},{9,8},{11,10},{12,13},{14,15},{17,16},{19,... | collective-permute-start | bytes 589832 | tf_op jit(solution)/shard_map/ppermute | solution.py:36
  1.9 3.2 %pack.1 = (bf16[96,1152]{1,0:T(8,128)(2,1)}, bf16[96,1152]{1,0:T(8,128)(2,1)}, bf16[96,1152]{1,0:T(8,128)(2,1)}, bf16[96,1152]{1,0:T(8,128)(2,1)}, f32[4,1536]{1...) custom-call(bf16[96,1536]{1,0:T(8,128)(2,1)} %w_query.1, ...), custom_call_target="tpu_custom_call" | custom-call | tf_op jit(solution)/shard_map/pack/pallas_call | solution.py:164
  5.2 2.8 %collective-permute-start.5 = (bf16[4,8,2,384]{3,2,1,0:T(2,128)(2,1)}, bf16[4,8,2,384]{3,2,1,0:T(2,128)(2,1)S(1)}, u32[]{:S(2)}, u32[]{:S(2)}) collective-permute-start(bf16[4,8,2,384]{3,2,1,0:T(2,128)(2,1)} %get-tuple-element.26), channel_id=1, source_target_pairs={{0,2},{1,3},{2,0},{3,1},{4,6},{5,7},{6,4},{7,5},{8,10},{9,11},{10,... | collective-permute-start | bytes 147464 | tf_op jit(solution)/shard_map/ppermute | solution.py:219
  8.0 0.3 collective-permute-start.6
  8.3 1.7 %collective-permute-start.9 = (bf16[96,1152]{1,0:T(8,128)(2,1)}, bf16[96,1152]{1,0:T(8,128)(2,1)S(1)}, u32[]{:S(2)}, u32[]{:S(2)}) collective-permute-start(bf16[96,1152]{1,0:T(8,128)(2,1)} %get-tuple-element.30), channel_id=1, source_target_pairs={{0,2},{1,3},{2,0},{3,1},{4,6},{5,7},{6,4},{7,5},{8,10},{9,11},{10,... | collective-permute-start | bytes 663560 | tf_op jit(solution)/shard_map/ppermute | solution.py:36
  10.1 0.9 constant_dynamic-update-slice_fusion.1
  11.0 1.5 %collective-permute-done.6 = bf16[4,8,2,384]{3,2,1,0:T(2,128)(2,1)S(1)} collective-permute-done((bf16[4,8,2,384]{3,2,1,0:T(2,128)(2,1)}, bf16[4,8,2,384]{3,2,1,0:T(2,128)(2,1)S(1)}, u32[]{:S(2)}, u32[]{:S(2)}) %collective-permute-start.6) | collective-permute-done | bytes 49184 | tf_op jit(solution)/shard_map/ppermute | solution.py:219
  12.5 1.1 %pad_maximum_fusion.1 = bf16[4,4,8,2,384]{4,3,2,1,0:T(2,128)(2,1)S(1)} fusion(bf16[1,4,8,2,384]{4,3,2,1,0:T(2,128)(2,1)S(1)} %bitcast.11, bf16[1,4,8,2,384]{4,3,2,1,0:T(2,128)(2,1)S(1)} %bitcast.10, bf16[1,4,8,2,384]{4,3,2,1,0:T(2,128)(2,1)S(1)} %bitcast.9, bf16[1,4,8,2,384]{4,3,2,1,0:T(2,128)(2,1)} %bitcast.8), kind=kLoop, calls=%fused_computation.2 | loop fusion | flops 294912 | bytes 393216 | tf_op jit(solution)/shard_map/stack | solution.py:209
  13.7 1.3 %collective-permute-start.2 = (bf16[128,1536]{1,0:T(8,128)(2,1)S(1)}, bf16[128,1536]{1,0:T(8,128)(2,1)S(1)}, u32[]{:S(2)}, u32[]{:S(2)}) collective-permute-start(bf16[128,1536]{1,0:T(8,128)(2,1)S(1)} %constant_dynamic-update-slice_fusion.block), channel_id=1, source_target_pairs={{0,4},{2,6},{5,1},{7,3},{8,12},{10,14},{13,9},{15,11},{16,20},{18,... | collective-permute-start | bytes 1179656 | tf_op jit(solution)/shard_map/ppermute | solution.py:36
  15.0 0.1 fusion.1
  15.2 2.2 %collective-permute-start.7 = (bf16[4,2,8,2,384]{4,3,2,1,0:T(2,128)(2,1)S(1)}, bf16[4,2,8,2,384]{4,3,2,1,0:T(2,128)(2,1)S(1)}, u32[]{:S(2)}, u32[]{:S(2)}) collective-permute-start(bf16[4,2,8,2,384]{4,3,2,1,0:T(2,128)(2,1)S(1)} %get-tuple-element.44), channel_id=1, source_target_pairs={{0,4},{1,5},{2,6},{3,7},{4,0},{5,1},{6,2},{7,3},{8,12},{9,13},{10,... | collective-permute-start | bytes 294920 | tf_op jit(solution)/shard_map/ppermute | solution.py:219
  17.3 2.9 %collective-permute-start.16 = (bf16[96,1152]{1,0:T(8,128)(2,1)}, bf16[96,1152]{1,0:T(8,128)(2,1)S(1)}, u32[]{:S(2)}, u32[]{:S(2)}) collective-permute-start(bf16[96,1152]{1,0:T(8,128)(2,1)} %get-tuple-element.32), channel_id=1, source_target_pairs={{0,8},{1,11},{2,10},{3,9},{4,12},{5,15},{6,14},{7,13},{8,0},{9,3},... | collective-permute-start | bytes 663560 | tf_op jit(solution)/shard_map/ppermute | solution.py:36
  20.2 0.2 collective-permute-start.20
  20.4 9.3 %collective-permute-done.7 = bf16[4,2,8,2,384]{4,3,2,1,0:T(2,128)(2,1)S(1)} collective-permute-done((bf16[4,2,8,2,384]{4,3,2,1,0:T(2,128)(2,1)S(1)}, bf16[4,2,8,2,384]{4,3,2,1,0:T(2,128)(2,1)S(1)}, u32[]{:S(2)}, u32[]{:S(2)}) %collective-permute-start.7) | collective-permute-done | bytes 98336 | tf_op jit(solution)/shard_map/ppermute | solution.py:219
  29.7 2.1 %collective-permute-start.11 = (bf16[96,1152]{1,0:T(8,128)(2,1)S(1)}, bf16[96,1152]{1,0:T(8,128)(2,1)S(1)}, u32[]{:S(2)}, u32[]{:S(2)}) collective-permute-start(bf16[96,1152]{1,0:T(8,128)(2,1)S(1)} %collective-permute-done.9.refs_1_.refs_2_), channel_id=1, source_target_pairs={{0,1},{1,0},{2,3},{3,2},{4,5},{5,4},{6,7},{7,6},{8,9},{9,8},{10,11... | collective-permute-start | bytes 663560 | tf_op jit(solution)/shard_map/ppermute | solution.py:36
  31.8 4.7 %collective-permute-done.20.refs_12_.refs_0_ = bf16[96,1152]{1,0:T(8,128)(2,1)S(1)} collective-permute-done((bf16[96,1152]{1,0:T(8,128)(2,1)}, bf16[96,1152]{1,0:T(8,128)(2,1)S(1)}, u32[]{:S(2)}, u32[]{:S(2)}) %collective-permute-start.20) | collective-permute-done | bytes 221216 | tf_op jit(solution)/shard_map/ppermute | solution.py:36
  36.5 2.9 %collective-permute-done.12.refs_4_.refs_5_ = bf16[96,1152]{1,0:T(8,128)(2,1)S(1)} collective-permute-done((bf16[96,1152]{1,0:T(8,128)(2,1)}, bf16[96,1152]{1,0:T(8,128)(2,1)S(1)}, u32[]{:S(2)}, u32[]{:S(2)}) %collective-permute-start.12) | collective-permute-done | bytes 221216 | tf_op jit(solution)/shard_map/ppermute | solution.py:36
  39.4 0.7 collective-permute-start.1
  40.1 2.8 %collective-permute-start.3 = (bf16[128,1536]{1,0:T(8,128)(2,1)S(1)}, bf16[128,1536]{1,0:T(8,128)(2,1)S(1)}, u32[]{:S(2)}, u32[]{:S(2)}) collective-permute-start(bf16[128,1536]{1,0:T(8,128)(2,1)S(1)} %collective-permute-done.2.far), channel_id=1, source_target_pairs={{1,3},{3,1},{4,6},{6,4},{9,11},{11,9},{12,14},{14,12},{17,19},{19,... | collective-permute-start | bytes 1179656 | tf_op jit(solution)/shard_map/ppermute | solution.py:36
  42.9 0.3 fusion
  43.2 2.7 %collective-permute-start.8 = (bf16[8,1,8,2,384]{4,3,2,1,0:T(2,128)(2,1)S(1)}, bf16[8,1,8,2,384]{4,3,2,1,0:T(2,128)(2,1)S(1)}, u32[]{:S(2)}, u32[]{:S(2)}) collective-permute-start(bf16[8,1,8,2,384]{4,3,2,1,0:T(2,128)(2,1)S(1)} %get-tuple-element.42), channel_id=1, source_target_pairs={{0,8},{1,9},{2,10},{3,11},{4,12},{5,13},{6,14},{7,15},{8,0},{9,1},... | collective-permute-start | bytes 294920 | tf_op jit(solution)/shard_map/ppermute | solution.py:219
  45.9 5.0 %collective-permute-done.8 = bf16[8,1,8,2,384]{4,3,2,1,0:T(2,128)(2,1)S(1)} collective-permute-done((bf16[8,1,8,2,384]{4,3,2,1,0:T(2,128)(2,1)S(1)}, bf16[8,1,8,2,384]{4,3,2,1,0:T(2,128)(2,1)S(1)}, u32[]{:S(2)}, u32[]{:S(2)}) %collective-permute-start.8) | collective-permute-done | bytes 98336 | tf_op jit(solution)/shard_map/ppermute | solution.py:219
  50.9 3.0 %collective-permute-start.17 = (bf16[96,1152]{1,0:T(8,128)(2,1)S(1)}, bf16[96,1152]{1,0:T(8,128)(2,1)S(1)}, u32[]{:S(2)}, u32[]{:S(2)}) collective-permute-start(bf16[96,1152]{1,0:T(8,128)(2,1)S(1)} %collective-permute-done.16.refs_8_.refs_9_), channel_id=1, source_target_pairs={{0,16},{1,17},{2,18},{3,19},{4,20},{5,21},{6,22},{7,23},{8,24},{9,... | collective-permute-start | bytes 663560 | tf_op jit(solution)/shard_map/ppermute | solution.py:36
  53.9 1.4 %collective-permute-start.13 = (bf16[96,1152]{1,0:T(8,128)(2,1)S(1)}, bf16[96,1152]{1,0:T(8,128)(2,1)S(1)}, u32[]{:S(2)}, u32[]{:S(2)}) collective-permute-start(bf16[96,1152]{1,0:T(8,128)(2,1)S(1)} %collective-permute-done.12.refs_4_.refs_5_), channel_id=1, source_target_pairs={{0,16},{1,17},{2,18},{3,19},{4,20},{5,21},{6,22},{7,23},{8,24},{9,... | collective-permute-start | bytes 663560 | tf_op jit(solution)/shard_map/ppermute | solution.py:36
  55.4 0.3 pad_maximum_fusion
  55.7 3.1 %collective-permute-done.17.refs_9_.refs_10_ = bf16[96,1152]{1,0:T(8,128)(2,1)S(1)} collective-permute-done((bf16[96,1152]{1,0:T(8,128)(2,1)S(1)}, bf16[96,1152]{1,0:T(8,128)(2,1)S(1)}, u32[]{:S(2)}, u32[]{:S(2)}) %collective-permute-start.17) | collective-permute-done | bytes 221216 | tf_op jit(solution)/shard_map/ppermute | solution.py:36
  58.8 2.5 %collective-permute-start.22 = (bf16[96,1152]{1,0:T(8,128)(2,1)S(1)}, bf16[96,1152]{1,0:T(8,128)(2,1)S(1)}, u32[]{:S(2)}, u32[]{:S(2)}) collective-permute-start(bf16[96,1152]{1,0:T(8,128)(2,1)S(1)} %collective-permute-done.20.refs_12_.refs_0_), channel_id=1, source_target_pairs={{0,1},{1,0},{2,3},{3,2},{4,5},{5,4},{6,7},{7,6},{8,9},{9,8},{10,11... | collective-permute-start | bytes 663560 | tf_op jit(solution)/shard_map/ppermute | solution.py:36
  61.3 2.2 %collective-permute-done.21.refs_13_.refs_1_ = bf16[96,1152]{1,0:T(8,128)(2,1)S(1)} collective-permute-done((bf16[96,1152]{1,0:T(8,128)(2,1)S(1)}, bf16[96,1152]{1,0:T(8,128)(2,1)S(1)}, u32[]{:S(2)}, u32[]{:S(2)}) %collective-permute-start.21) | collective-permute-done | bytes 221216 | tf_op jit(solution)/shard_map/ppermute | solution.py:36
  63.6 2.5 %collective-permute-start.14 = (bf16[96,1152]{1,0:T(8,128)(2,1)S(1)}, bf16[96,1152]{1,0:T(8,128)(2,1)S(1)}, u32[]{:S(2)}, u32[]{:S(2)}) collective-permute-start(bf16[96,1152]{1,0:T(8,128)(2,1)S(1)} %collective-permute-done.12.refs_4_.refs_5_), channel_id=1, source_target_pairs={{0,1},{1,0},{2,3},{3,2},{4,5},{5,4},{6,7},{7,6},{8,9},{9,8},{10,11... | collective-permute-start | bytes 663560 | tf_op jit(solution)/shard_map/ppermute | solution.py:36
  66.1 2.2 %collective-permute-done.13.refs_5_.refs_6_ = bf16[96,1152]{1,0:T(8,128)(2,1)S(1)} collective-permute-done((bf16[96,1152]{1,0:T(8,128)(2,1)S(1)}, bf16[96,1152]{1,0:T(8,128)(2,1)S(1)}, u32[]{:S(2)}, u32[]{:S(2)}) %collective-permute-start.13) | collective-permute-done | bytes 221216 | tf_op jit(solution)/shard_map/ppermute | solution.py:36
  68.3 1.5 %collective-permute-start.19 = (bf16[96,1152]{1,0:T(8,128)(2,1)S(1)}, bf16[96,1152]{1,0:T(8,128)(2,1)S(1)}, u32[]{:S(2)}, u32[]{:S(2)}) collective-permute-start(bf16[96,1152]{1,0:T(8,128)(2,1)S(1)} %collective-permute-done.17.refs_9_.refs_10_), channel_id=1, source_target_pairs={{0,1},{1,0},{2,3},{3,2},{4,5},{5,4},{6,7},{7,6},{8,9},{9,8},{10,11... | collective-permute-start | bytes 663560 | tf_op jit(solution)/shard_map/ppermute | solution.py:36
  69.8 0.5 collective-permute-start.15
  70.3 0.7 copy-done.1
  71.0 1.4 %shard_map.100 = (f32[4,1536]{1,0:T(4,128)S(1)}, bf16[256,1536]{1,0:T(8,128)(2,1)S(1)}, bf16[256,1536]{1,0:T(8,128)(2,1)S(1)}) custom-call(f32[4,1536]{1,0:T(4,128)S(1)} %copy-done.1, bf16[128,1536]{1,0:T(8,128)(2,1)S(1)} %constant_dynamic-update-slice_fusion.block, bf16[128,1536]{1,0:T(8,128)(2,1)S(1)} %collective-permute-done.1.near, ...), custom_call_target="tpu_custom_call" | custom-call | bytes 1597440 | tf_op jit(solution)/shard_map/pallas_call | solution.py:418
  72.5 1.2 %shard_map.102.part_ref = f32[256,1152]{1,0:T(8,128)S(1)} custom-call(bf16[256,1536]{1,0:T(8,128)(2,1)S(1)} %get-tuple-element.33.refs_0_.normed, bf16[96,1152]{1,0:T(8,128)(2,1)S(1)} %copy-done, bf16[96,1152]{1,0:T(8,128)(2,1)S(1)} %collective-permute-done.9.refs_1_.refs_2_, bf16[96,1152]{1,0:T(8,128)(2,1)S(1)} %collective-permute-done.10.refs_2_.refs_3_, ...), custom_call_target="tpu_custom_call" | custom-call | flops 679477248 | bytes 3440640 | tf_op jit(solution)/shard_map/pallas_call | solution.py:418
  73.8 2.2 %shard_map.103.first_part = bf16[256,384]{1,0:T(8,128)(2,1)S(1)} custom-call(f32[4,1536]{1,0:T(4,128)S(1)} %get-tuple-element.23.extra_ref, bf16[128,384]{1,0:T(8,128)(2,1)S(1)} %get-tuple-element.46.key_ref, bf16[128,384]{1,0:T(8,128)(2,1)S(1)} %get-tuple-element.45.value_ref, bf16[256,1536]{1,0:T(8,128)(2,1)S(1)} %get-tuple-element.33.refs_0_.normed, ...), custom_call_target="tpu_custom_call" | custom-call | flops 377487360 | bytes 3072000 | tf_op jit(solution)/shard_map/pallas_call | solution.py:418
  75.9 0.5 collective-permute-start.26
  76.4 2.3 %collective-permute-start.24 = (bf16[256,384]{1,0:T(8,128)(2,1)S(1)}, bf16[256,384]{1,0:T(8,128)(2,1)S(1)}, u32[]{:S(2)}, u32[]{:S(2)}) collective-permute-start(bf16[256,384]{1,0:T(8,128)(2,1)S(1)} %shard_map.103.first_part), channel_id=1, source_target_pairs={{0,6},{1,7},{2,4},{3,5},{4,2},{5,3},{6,0},{7,1},{8,14},{9,15},{10,... | collective-permute-start | bytes 589832 | tf_op jit(solution)/shard_map/ppermute | solution.py:36
  78.6 0.3 shard_map.101.weights
  78.9 3.5 %collective-permute-done.26.fourth_part = bf16[256,384]{1,0:T(8,128)(2,1)S(1)} collective-permute-done((bf16[256,384]{1,0:T(8,128)(2,1)S(1)}, bf16[256,384]{1,0:T(8,128)(2,1)S(1)}, u32[]{:S(2)}, u32[]{:S(2)}) %collective-permute-start.26) | collective-permute-done | bytes 196640 | tf_op jit(solution)/shard_map/ppermute | solution.py:36
  82.4 0.1 collective-permute-done.25.third_part
  82.5 5.0 %collective-permute-done.24.second_part = bf16[256,384]{1,0:T(8,128)(2,1)S(1)} collective-permute-done((bf16[256,384]{1,0:T(8,128)(2,1)S(1)}, bf16[256,384]{1,0:T(8,128)(2,1)S(1)}, u32[]{:S(2)}, u32[]{:S(2)}) %collective-permute-start.24) | collective-permute-done | bytes 196640 | tf_op jit(solution)/shard_map/ppermute | solution.py:36
  87.5 4.0 %shard_map.104 = (bf16[64,384]{1,0:T(8,128)(2,1)S(1)}, bf16[64,384]{1,0:T(8,128)(2,1)S(1)}, bf16[64,384]{1,0:T(8,128)(2,1)S(1)}, bf16[64,384]{1,0:T(8,128)(2,1)S(1)}, bf16[64,384]{1,0:T(8,128)(2,1)S(1)}) custom-call(f32[4,1536]{1,0:T(4,128)S(1)} %get-tuple-element.23.extra_ref, bf16[128,384]{1,0:T(8,128)(2,1)S(1)} %get-tuple-element.46.key_ref, ...), custom_call_target="tpu_custom_call" | custom-call | flops 1056964608 | bytes 5332992 | tf_op jit(solution)/shard_map/pallas_call | solution.py:418
  91.5 1.2 %collective-permute-start.27 = (bf16[64,384]{1,0:T(8,128)(2,1)S(1)}, bf16[64,384]{1,0:T(8,128)(2,1)S(1)}, u32[]{:S(2)}, u32[]{:S(2)}) collective-permute-start(bf16[64,384]{1,0:T(8,128)(2,1)S(1)} %get-tuple-element.35), channel_id=1, source_target_pairs={{0,2},{1,4},{2,0},{3,6},{4,1},{5,7},{6,3},{7,5},{8,10},{9,12},{10,... | collective-permute-start | bytes 147464 | tf_op jit(solution)/shard_map/ppermute | solution.py:36
  92.7 1.8 %collective-permute-start.29 = (bf16[64,384]{1,0:T(8,128)(2,1)S(1)}, bf16[64,384]{1,0:T(8,128)(2,1)S(1)}, u32[]{:S(2)}, u32[]{:S(2)}) collective-permute-start(bf16[64,384]{1,0:T(8,128)(2,1)S(1)} %get-tuple-element.37), channel_id=1, source_target_pairs={{0,1},{1,7},{2,3},{3,5},{4,2},{5,4},{6,0},{7,6},{8,9},{9,15},{10,1... | collective-permute-start | bytes 147464 | tf_op jit(solution)/shard_map/ppermute | solution.py:36
  94.5 3.4 %collective-permute-start.30 = (bf16[64,384]{1,0:T(8,128)(2,1)S(1)}, bf16[64,384]{1,0:T(8,128)(2,1)S(1)}, u32[]{:S(2)}, u32[]{:S(2)}) collective-permute-start(bf16[64,384]{1,0:T(8,128)(2,1)S(1)} %get-tuple-element.38), channel_id=1, source_target_pairs={{1,6},{3,4},{4,3},{6,1},{9,14},{11,12},{12,11},{14,9},{17,22},{19,... | collective-permute-start | bytes 147464 | tf_op jit(solution)/shard_map/ppermute | solution.py:36
  98.0 2.9 %collective-permute-done.30.fourth = bf16[64,384]{1,0:T(8,128)(2,1)S(1)} collective-permute-done((bf16[64,384]{1,0:T(8,128)(2,1)S(1)}, bf16[64,384]{1,0:T(8,128)(2,1)S(1)}, u32[]{:S(2)}, u32[]{:S(2)}) %collective-permute-start.30) | collective-permute-done | bytes 49184 | tf_op jit(solution)/shard_map/ppermute | solution.py:36
  100.8 0.7 shard_map.105
  (32 shorter events, 0.2 us)
Async XLA Ops:
  0.0 13.7 %collective-permute-start = (bf16[64,1536]{1,0:T(8,128)(2,1)}, bf16[64,1536]{1,0:T(8,128)(2,1)S(1)}, u32[]{:S(2)}, u32[]{:S(2)}) collective-permute-start(bf16[64,1536]{1,0:T(8,128)(2,1)} %param.10), channel_id=1, source_target_pairs={{1,0},{3,2},{4,5},{6,7},{9,8},{11,10},{12,13},{14,15},{17,16},{19,... | collective-permute-start | bytes 589832 | tf_op jit(solution)/shard_map/ppermute | solution.py:36
  5.1 67.4 %copy-start = (bf16[96,1152]{1,0:T(8,128)(2,1)S(1)}, bf16[96,1152]{1,0:T(8,128)(2,1)}, u32[]{:S(2)}) copy-start(bf16[96,1152]{1,0:T(8,128)(2,1)} %get-tuple-element.29.refs_0_.refs_1_) | copy-start | bytes 663556
  5.1 5.9 %collective-permute-start.4 = (bf16[4,8,2,384]{3,2,1,0:T(2,128)(2,1)}, bf16[4,8,2,384]{3,2,1,0:T(2,128)(2,1)S(1)}, u32[]{:S(2)}, u32[]{:S(2)}) collective-permute-start(bf16[4,8,2,384]{3,2,1,0:T(2,128)(2,1)} %get-tuple-element.25), channel_id=1, source_target_pairs={{0,1},{1,0},{2,3},{3,2},{4,5},{5,4},{6,7},{7,6},{8,9},{9,8},{10,11... | collective-permute-start | bytes 147464 | tf_op jit(solution)/shard_map/ppermute | solution.py:219
  5.2 5.8 %collective-permute-start.5 = (bf16[4,8,2,384]{3,2,1,0:T(2,128)(2,1)}, bf16[4,8,2,384]{3,2,1,0:T(2,128)(2,1)S(1)}, u32[]{:S(2)}, u32[]{:S(2)}) collective-permute-start(bf16[4,8,2,384]{3,2,1,0:T(2,128)(2,1)} %get-tuple-element.26), channel_id=1, source_target_pairs={{0,2},{1,3},{2,0},{3,1},{4,6},{5,7},{6,4},{7,5},{8,10},{9,11},{10,... | collective-permute-start | bytes 147464 | tf_op jit(solution)/shard_map/ppermute | solution.py:219
  8.0 4.5 %collective-permute-start.6 = (bf16[4,8,2,384]{3,2,1,0:T(2,128)(2,1)}, bf16[4,8,2,384]{3,2,1,0:T(2,128)(2,1)S(1)}, u32[]{:S(2)}, u32[]{:S(2)}) collective-permute-start(bf16[4,8,2,384]{3,2,1,0:T(2,128)(2,1)} %get-tuple-element.27), channel_id=1, source_target_pairs={{0,3},{1,2},{2,1},{3,0},{4,7},{5,6},{6,5},{7,4},{8,11},{9,10},{10,... | collective-permute-start | bytes 147464 | tf_op jit(solution)/shard_map/ppermute | solution.py:219
  8.3 21.3 %collective-permute-start.9 = (bf16[96,1152]{1,0:T(8,128)(2,1)}, bf16[96,1152]{1,0:T(8,128)(2,1)S(1)}, u32[]{:S(2)}, u32[]{:S(2)}) collective-permute-start(bf16[96,1152]{1,0:T(8,128)(2,1)} %get-tuple-element.30), channel_id=1, source_target_pairs={{0,2},{1,3},{2,0},{3,1},{4,6},{5,7},{6,4},{7,5},{8,10},{9,11},{10,... | collective-permute-start | bytes 663560 | tf_op jit(solution)/shard_map/ppermute | solution.py:36
  13.7 26.4 %collective-permute-start.2 = (bf16[128,1536]{1,0:T(8,128)(2,1)S(1)}, bf16[128,1536]{1,0:T(8,128)(2,1)S(1)}, u32[]{:S(2)}, u32[]{:S(2)}) collective-permute-start(bf16[128,1536]{1,0:T(8,128)(2,1)S(1)} %constant_dynamic-update-slice_fusion.block), channel_id=1, source_target_pairs={{0,4},{2,6},{5,1},{7,3},{8,12},{10,14},{13,9},{15,11},{16,20},{18,... | collective-permute-start | bytes 1179656 | tf_op jit(solution)/shard_map/ppermute | solution.py:36
  15.2 14.5 %collective-permute-start.7 = (bf16[4,2,8,2,384]{4,3,2,1,0:T(2,128)(2,1)S(1)}, bf16[4,2,8,2,384]{4,3,2,1,0:T(2,128)(2,1)S(1)}, u32[]{:S(2)}, u32[]{:S(2)}) collective-permute-start(bf16[4,2,8,2,384]{4,3,2,1,0:T(2,128)(2,1)S(1)} %get-tuple-element.44), channel_id=1, source_target_pairs={{0,4},{1,5},{2,6},{3,7},{4,0},{5,1},{6,2},{7,3},{8,12},{9,13},{10,... | collective-permute-start | bytes 294920 | tf_op jit(solution)/shard_map/ppermute | solution.py:219
  17.3 12.3 %collective-permute-start.16 = (bf16[96,1152]{1,0:T(8,128)(2,1)}, bf16[96,1152]{1,0:T(8,128)(2,1)S(1)}, u32[]{:S(2)}, u32[]{:S(2)}) collective-permute-start(bf16[96,1152]{1,0:T(8,128)(2,1)} %get-tuple-element.32), channel_id=1, source_target_pairs={{0,8},{1,11},{2,10},{3,9},{4,12},{5,15},{6,14},{7,13},{8,0},{9,3},... | collective-permute-start | bytes 663560 | tf_op jit(solution)/shard_map/ppermute | solution.py:36
  20.2 16.3 %collective-permute-start.20 = (bf16[96,1152]{1,0:T(8,128)(2,1)}, bf16[96,1152]{1,0:T(8,128)(2,1)S(1)}, u32[]{:S(2)}, u32[]{:S(2)}) collective-permute-start(bf16[96,1152]{1,0:T(8,128)(2,1)} %get-tuple-element.31), channel_id=1, source_target_pairs={{0,12},{1,15},{2,14},{3,13},{4,8},{5,11},{6,10},{7,9},{8,4},{9,7},... | collective-permute-start | bytes 663560 | tf_op jit(solution)/shard_map/ppermute | solution.py:36
  29.7 9.8 %collective-permute-start.12 = (bf16[96,1152]{1,0:T(8,128)(2,1)}, bf16[96,1152]{1,0:T(8,128)(2,1)S(1)}, u32[]{:S(2)}, u32[]{:S(2)}) collective-permute-start(bf16[96,1152]{1,0:T(8,128)(2,1)} %get-tuple-element.31), channel_id=1, source_target_pairs={{0,4},{1,7},{2,6},{3,5},{4,0},{5,3},{6,2},{7,1},{8,12},{9,15},{10,... | collective-permute-start | bytes 663560 | tf_op jit(solution)/shard_map/ppermute | solution.py:36
  29.7 13.5 %collective-permute-start.10 = (bf16[96,1152]{1,0:T(8,128)(2,1)}, bf16[96,1152]{1,0:T(8,128)(2,1)S(1)}, u32[]{:S(2)}, u32[]{:S(2)}) collective-permute-start(bf16[96,1152]{1,0:T(8,128)(2,1)} %get-tuple-element.29.refs_0_.refs_1_), channel_id=1, source_target_pairs={{0,1},{1,0},{2,3},{3,2},{4,5},{5,4},{6,7},{7,6},{8,9},{9,8},{10,11... | collective-permute-start | bytes 663560 | tf_op jit(solution)/shard_map/ppermute | solution.py:36
  29.7 24.2 %collective-permute-start.11 = (bf16[96,1152]{1,0:T(8,128)(2,1)S(1)}, bf16[96,1152]{1,0:T(8,128)(2,1)S(1)}, u32[]{:S(2)}, u32[]{:S(2)}) collective-permute-start(bf16[96,1152]{1,0:T(8,128)(2,1)S(1)} %collective-permute-done.9.refs_1_.refs_2_), channel_id=1, source_target_pairs={{0,1},{1,0},{2,3},{3,2},{4,5},{5,4},{6,7},{7,6},{8,9},{9,8},{10,11... | collective-permute-start | bytes 663560 | tf_op jit(solution)/shard_map/ppermute | solution.py:36
  36.5 17.4 %collective-permute-start.18 = (bf16[96,1152]{1,0:T(8,128)(2,1)S(1)}, bf16[96,1152]{1,0:T(8,128)(2,1)S(1)}, u32[]{:S(2)}, u32[]{:S(2)}) collective-permute-start(bf16[96,1152]{1,0:T(8,128)(2,1)S(1)} %collective-permute-done.16.refs_8_.refs_9_), channel_id=1, source_target_pairs={{0,1},{1,0},{2,3},{3,2},{4,5},{5,4},{6,7},{7,6},{8,9},{9,8},{10,11... | collective-permute-start | bytes 663560 | tf_op jit(solution)/shard_map/ppermute | solution.py:36
  39.4 30.3 %collective-permute-start.1 = (bf16[128,1536]{1,0:T(8,128)(2,1)S(1)}, bf16[128,1536]{1,0:T(8,128)(2,1)S(1)}, u32[]{:S(2)}, u32[]{:S(2)}) collective-permute-start(bf16[128,1536]{1,0:T(8,128)(2,1)S(1)} %constant_dynamic-update-slice_fusion.block), channel_id=1, source_target_pairs={{0,2},{2,0},{5,7},{7,5},{8,10},{10,8},{13,15},{15,13},{16,18},{18,... | collective-permute-start | bytes 1179656 | tf_op jit(solution)/shard_map/ppermute | solution.py:36
  40.1 29.6 %collective-permute-start.3 = (bf16[128,1536]{1,0:T(8,128)(2,1)S(1)}, bf16[128,1536]{1,0:T(8,128)(2,1)S(1)}, u32[]{:S(2)}, u32[]{:S(2)}) collective-permute-start(bf16[128,1536]{1,0:T(8,128)(2,1)S(1)} %collective-permute-done.2.far), channel_id=1, source_target_pairs={{1,3},{3,1},{4,6},{6,4},{9,11},{11,9},{12,14},{14,12},{17,19},{19,... | collective-permute-start | bytes 1179656 | tf_op jit(solution)/shard_map/ppermute | solution.py:36
  43.2 7.7 %collective-permute-start.8 = (bf16[8,1,8,2,384]{4,3,2,1,0:T(2,128)(2,1)S(1)}, bf16[8,1,8,2,384]{4,3,2,1,0:T(2,128)(2,1)S(1)}, u32[]{:S(2)}, u32[]{:S(2)}) collective-permute-start(bf16[8,1,8,2,384]{4,3,2,1,0:T(2,128)(2,1)S(1)} %get-tuple-element.42), channel_id=1, source_target_pairs={{0,8},{1,9},{2,10},{3,11},{4,12},{5,13},{6,14},{7,15},{8,0},{9,1},... | collective-permute-start | bytes 294920 | tf_op jit(solution)/shard_map/ppermute | solution.py:219
  50.9 7.9 %collective-permute-start.17 = (bf16[96,1152]{1,0:T(8,128)(2,1)S(1)}, bf16[96,1152]{1,0:T(8,128)(2,1)S(1)}, u32[]{:S(2)}, u32[]{:S(2)}) collective-permute-start(bf16[96,1152]{1,0:T(8,128)(2,1)S(1)} %collective-permute-done.16.refs_8_.refs_9_), channel_id=1, source_target_pairs={{0,16},{1,17},{2,18},{3,19},{4,20},{5,21},{6,22},{7,23},{8,24},{9,... | collective-permute-start | bytes 663560 | tf_op jit(solution)/shard_map/ppermute | solution.py:36
  53.9 9.7 %collective-permute-start.21 = (bf16[96,1152]{1,0:T(8,128)(2,1)S(1)}, bf16[96,1152]{1,0:T(8,128)(2,1)S(1)}, u32[]{:S(2)}, u32[]{:S(2)}) collective-permute-start(bf16[96,1152]{1,0:T(8,128)(2,1)S(1)} %collective-permute-done.20.refs_12_.refs_0_), channel_id=1, source_target_pairs={{0,16},{1,17},{2,18},{3,19},{4,20},{5,21},{6,22},{7,23},{8,24},{9,... | collective-permute-start | bytes 663560 | tf_op jit(solution)/shard_map/ppermute | solution.py:36
  53.9 14.4 %collective-permute-start.13 = (bf16[96,1152]{1,0:T(8,128)(2,1)S(1)}, bf16[96,1152]{1,0:T(8,128)(2,1)S(1)}, u32[]{:S(2)}, u32[]{:S(2)}) collective-permute-start(bf16[96,1152]{1,0:T(8,128)(2,1)S(1)} %collective-permute-done.12.refs_4_.refs_5_), channel_id=1, source_target_pairs={{0,16},{1,17},{2,18},{3,19},{4,20},{5,21},{6,22},{7,23},{8,24},{9,... | collective-permute-start | bytes 663560 | tf_op jit(solution)/shard_map/ppermute | solution.py:36
  58.8 14.9 %collective-permute-start.22 = (bf16[96,1152]{1,0:T(8,128)(2,1)S(1)}, bf16[96,1152]{1,0:T(8,128)(2,1)S(1)}, u32[]{:S(2)}, u32[]{:S(2)}) collective-permute-start(bf16[96,1152]{1,0:T(8,128)(2,1)S(1)} %collective-permute-done.20.refs_12_.refs_0_), channel_id=1, source_target_pairs={{0,1},{1,0},{2,3},{3,2},{4,5},{5,4},{6,7},{7,6},{8,9},{9,8},{10,11... | collective-permute-start | bytes 663560 | tf_op jit(solution)/shard_map/ppermute | solution.py:36
  63.6 8.9 %collective-permute-start.14 = (bf16[96,1152]{1,0:T(8,128)(2,1)S(1)}, bf16[96,1152]{1,0:T(8,128)(2,1)S(1)}, u32[]{:S(2)}, u32[]{:S(2)}) collective-permute-start(bf16[96,1152]{1,0:T(8,128)(2,1)S(1)} %collective-permute-done.12.refs_4_.refs_5_), channel_id=1, source_target_pairs={{0,1},{1,0},{2,3},{3,2},{4,5},{5,4},{6,7},{7,6},{8,9},{9,8},{10,11... | collective-permute-start | bytes 663560 | tf_op jit(solution)/shard_map/ppermute | solution.py:36
  68.3 4.2 %collective-permute-start.19 = (bf16[96,1152]{1,0:T(8,128)(2,1)S(1)}, bf16[96,1152]{1,0:T(8,128)(2,1)S(1)}, u32[]{:S(2)}, u32[]{:S(2)}) collective-permute-start(bf16[96,1152]{1,0:T(8,128)(2,1)S(1)} %collective-permute-done.17.refs_9_.refs_10_), channel_id=1, source_target_pairs={{0,1},{1,0},{2,3},{3,2},{4,5},{5,4},{6,7},{7,6},{8,9},{9,8},{10,11... | collective-permute-start | bytes 663560 | tf_op jit(solution)/shard_map/ppermute | solution.py:36
  69.8 4.0 %collective-permute-start.23 = (bf16[96,1152]{1,0:T(8,128)(2,1)S(1)}, bf16[96,1152]{1,0:T(8,128)(2,1)S(1)}, u32[]{:S(2)}, u32[]{:S(2)}) collective-permute-start(bf16[96,1152]{1,0:T(8,128)(2,1)S(1)} %collective-permute-done.21.refs_13_.refs_1_), channel_id=1, source_target_pairs={{0,1},{1,0},{2,3},{3,2},{4,5},{5,4},{6,7},{7,6},{8,9},{9,8},{10,11... | collective-permute-start | bytes 663560 | tf_op jit(solution)/shard_map/ppermute | solution.py:36
  69.8 2.7 %collective-permute-start.15 = (bf16[96,1152]{1,0:T(8,128)(2,1)S(1)}, bf16[96,1152]{1,0:T(8,128)(2,1)S(1)}, u32[]{:S(2)}, u32[]{:S(2)}) collective-permute-start(bf16[96,1152]{1,0:T(8,128)(2,1)S(1)} %collective-permute-done.13.refs_5_.refs_6_), channel_id=1, source_target_pairs={{0,1},{1,0},{2,3},{3,2},{4,5},{5,4},{6,7},{7,6},{8,9},{9,8},{10,11... | collective-permute-start | bytes 663560 | tf_op jit(solution)/shard_map/ppermute | solution.py:36
  70.3 0.7 copy-start.1
  75.9 6.4 %collective-permute-start.26 = (bf16[256,384]{1,0:T(8,128)(2,1)S(1)}, bf16[256,384]{1,0:T(8,128)(2,1)S(1)}, u32[]{:S(2)}, u32[]{:S(2)}) collective-permute-start(bf16[256,384]{1,0:T(8,128)(2,1)S(1)} %shard_map.103.first_part), channel_id=1, source_target_pairs={{0,2},{1,3},{2,0},{3,1},{4,6},{5,7},{6,4},{7,5},{8,10},{9,11},{10,... | collective-permute-start | bytes 589832 | tf_op jit(solution)/shard_map/ppermute | solution.py:36
  76.4 6.1 %collective-permute-start.25 = (bf16[256,384]{1,0:T(8,128)(2,1)S(1)}, bf16[256,384]{1,0:T(8,128)(2,1)S(1)}, u32[]{:S(2)}, u32[]{:S(2)}) collective-permute-start(bf16[256,384]{1,0:T(8,128)(2,1)S(1)} %shard_map.103.first_part), channel_id=1, source_target_pairs={{0,4},{1,5},{2,6},{3,7},{4,0},{5,1},{6,2},{7,3},{8,12},{9,13},{10,... | collective-permute-start | bytes 589832 | tf_op jit(solution)/shard_map/ppermute | solution.py:36
  76.4 11.1 %collective-permute-start.24 = (bf16[256,384]{1,0:T(8,128)(2,1)S(1)}, bf16[256,384]{1,0:T(8,128)(2,1)S(1)}, u32[]{:S(2)}, u32[]{:S(2)}) collective-permute-start(bf16[256,384]{1,0:T(8,128)(2,1)S(1)} %shard_map.103.first_part), channel_id=1, source_target_pairs={{0,6},{1,7},{2,4},{3,5},{4,2},{5,3},{6,0},{7,1},{8,14},{9,15},{10,... | collective-permute-start | bytes 589832 | tf_op jit(solution)/shard_map/ppermute | solution.py:36
  91.5 6.4 %collective-permute-start.27 = (bf16[64,384]{1,0:T(8,128)(2,1)S(1)}, bf16[64,384]{1,0:T(8,128)(2,1)S(1)}, u32[]{:S(2)}, u32[]{:S(2)}) collective-permute-start(bf16[64,384]{1,0:T(8,128)(2,1)S(1)} %get-tuple-element.35), channel_id=1, source_target_pairs={{0,2},{1,4},{2,0},{3,6},{4,1},{5,7},{6,3},{7,5},{8,10},{9,12},{10,... | collective-permute-start | bytes 147464 | tf_op jit(solution)/shard_map/ppermute | solution.py:36
  92.7 5.2 %collective-permute-start.28 = (bf16[64,384]{1,0:T(8,128)(2,1)S(1)}, bf16[64,384]{1,0:T(8,128)(2,1)S(1)}, u32[]{:S(2)}, u32[]{:S(2)}) collective-permute-start(bf16[64,384]{1,0:T(8,128)(2,1)S(1)} %get-tuple-element.36), channel_id=1, source_target_pairs={{0,3},{1,5},{2,1},{3,7},{4,0},{5,6},{6,2},{7,4},{8,11},{9,13},{10,... | collective-permute-start | bytes 147464 | tf_op jit(solution)/shard_map/ppermute | solution.py:36
  92.7 5.2 %collective-permute-start.29 = (bf16[64,384]{1,0:T(8,128)(2,1)S(1)}, bf16[64,384]{1,0:T(8,128)(2,1)S(1)}, u32[]{:S(2)}, u32[]{:S(2)}) collective-permute-start(bf16[64,384]{1,0:T(8,128)(2,1)S(1)} %get-tuple-element.37), channel_id=1, source_target_pairs={{0,1},{1,7},{2,3},{3,5},{4,2},{5,4},{6,0},{7,6},{8,9},{9,15},{10,1... | collective-permute-start | bytes 147464 | tf_op jit(solution)/shard_map/ppermute | solution.py:36
  94.5 6.3 %collective-permute-start.30 = (bf16[64,384]{1,0:T(8,128)(2,1)S(1)}, bf16[64,384]{1,0:T(8,128)(2,1)S(1)}, u32[]{:S(2)}, u32[]{:S(2)}) collective-permute-start(bf16[64,384]{1,0:T(8,128)(2,1)S(1)} %get-tuple-element.38), channel_id=1, source_target_pairs={{1,6},{3,4},{4,3},{6,1},{9,14},{11,12},{12,11},{14,9},{17,22},{19,... | collective-permute-start | bytes 147464 | tf_op jit(solution)/shard_map/ppermute | solution.py:36

commit v7 on v6

--- a/solution.py
+++ b/solution.py
@@ -187,20 +187,29 @@
 
 
 def all_pieces(own, beside, even, odd):
-    planes = lax.axis_size("frame") // 4
-    pieces = [("own", own, (0, 0, False))]
-    pieces.append(("near", moved(beside, lambda x, p, y, c: (x, p, 1 - y, c)), (0, 1, False)))
-    for bits in range(1, planes):
-        name = f"plane{bits}"
+    late = late_plane(lax.axis_size("frame"))
+
+    def direct(bits):
         sent = even if bits % 2 == 0 else odd
-        direct = moved(sent, lambda x, p, y, c, bits=bits: (x, p ^ bits, y ^ x ^ c, c))
-        pieces.append((name, direct, (bits, 0, True)))
-        name = f"cross{bits}"
-        pieces.append((name, moved(direct, lambda x, p, y, c: (1 - x, p, y, c)), (bits, 1, True)))
-    places = [(array, place + (0,)) for _, array, place in pieces]
-    for name, array, place in pieces:
-        places.append((moved(array, lambda x, p, y, c: (x, p, y, 1 - c)), place + (1,)))
-    return places
+        return moved(sent, lambda x, p, y, c: (x, p ^ bits, y ^ x ^ c, c))
+
+    near = moved(beside, lambda x, p, y, c: (x, p, 1 - y, c))
+    pieces = [("own", own, [(0, 0, False)]), ("near", near, [(0, 1, False)])]
+    early = list(range(1, late))
+    for name, bits_list in (("early", early), ("late", [late])):
+        if not bits_list:
+            continue
+        arrays = [direct(bits) for bits in bits_list]
+        if len(arrays) > 1:
+            arrays = [jnp.concatenate(arrays)]
+        pieces.append((name, arrays[0], [(bits, 0, True) for bits in bits_list]))
+        crossed = moved(arrays[0], lambda x, p, y, c: (1 - x, p, y, c))
+        pieces.append((f"cross_{name}", crossed, [(bits, 1, True) for bits in bits_list]))
+    found = [(array, tuple(place + (0,) for place in places)) for _, array, places in pieces]
+    for name, array, places in pieces:
+        swapped = moved(array, lambda x, p, y, c: (x, p, y, 1 - c))
+        found.append((swapped, tuple(place + (1,) for place in places)))
+    return found
 
 
 def all_memory(parts):
@@ -242,9 +251,11 @@
 
 
 def gather_pieces(piece_refs, places, first_plane, weights):
-    for ref, place in zip(piece_refs, places):
-        start = piece_start(place, ref.shape[0], place[0] - first_plane)
-        weights[pl.ds(start, ref.shape[0]), :] = ref[...]
+    for ref, shards in zip(piece_refs, places):
+        rows = ref.shape[0] // len(shards)
+        for number, place in enumerate(shards):
+            start = piece_start(place, rows, place[0] - first_plane)
+            weights[pl.ds(start, rows), :] = ref[number * rows : (number + 1) * rows, :]
 
 
 def store_normed(current, rows, inverse, gain_ref, normed):
@@ -260,39 +271,25 @@
 BLOCK = 32
 
 
-def prepare_kernel(extra_ref, block, near, far, far_near, extra, current, normed, token_sem):
+def prepare_kernel(extra_ref, block, near, far, far_near, extra, current, normed):
     _, _, plane, y, c = here()
     chip_rows = block.shape[0]
-    at_home = plane % 2 == c
-    extra_copy = pltpu.make_async_copy(extra_ref, extra, token_sem.at[2])
-    extra_copy.start()
-
-    def token_copies(first, second):
-        return (
-            pltpu.make_async_copy(first, current.at[pl.ds(y * chip_rows, chip_rows)], token_sem.at[0]),
-            pltpu.make_async_copy(second, current.at[pl.ds((1 - y) * chip_rows, chip_rows)], token_sem.at[1]),
-        )
-
-    @pl.when(at_home)
-    def _():
-        for copy in token_copies(block, near):
-            copy.start()
-
-    @pl.when(jnp.logical_not(at_home))
-    def _():
-        for copy in token_copies(far, far_near):
-            copy.start()
-
-    for copy in token_copies(block, near):
-        copy.wait()
-    extra_copy.wait()
-
-    @pl.loop(0, current.shape[0] // BLOCK)
-    def _(number):
-        rows = pl.ds(pl.multiple_of(number * BLOCK, BLOCK), BLOCK)
-        widened = current[rows, :].astype(jnp.float32)
-        inverse = lax.rsqrt(jnp.mean(widened * widened, axis=-1, keepdims=True) + 1e-06)
-        store_normed(current, rows, inverse, extra, normed)
+    blocks = chip_rows // BLOCK
+    extra[...] = extra_ref[...]
+
+    def fill(first, second):
+        @pl.loop(0, blocks)
+        def _(number):
+            for ref, base in ((first, y * chip_rows), (second, (1 - y) * chip_rows)):
+                tokens = ref[pl.ds(pl.multiple_of(number * BLOCK, BLOCK), BLOCK), :]
+                rows = pl.ds(pl.multiple_of(base + number * BLOCK, BLOCK), BLOCK)
+                current[rows, :] = tokens
+                widened = tokens.astype(jnp.float32)
+                inverse = lax.rsqrt(jnp.mean(widened * widened, axis=-1, keepdims=True) + 1e-06)
+                store_normed(current, rows, inverse, extra, normed)
+
+    pl.when(plane % 2 == c)(lambda: fill(block, near))
+    pl.when(plane % 2 != c)(lambda: fill(far, far_near))
 
 
 def project_kernel(places, *refs):
@@ -329,18 +326,13 @@
                 lax.dot_general(queries, key_ref[:, span], contract_last, preferred_element_type=jnp.float32)
                 * scale_dot
             )
-            mem_scores = jnp.where(live, mem_scores, -1e30)
-            largest = jnp.maximum(
-                jnp.max(frame_scores, axis=-1, keepdims=True), jnp.max(mem_scores, axis=-1, keepdims=True)
-            )
-            frame_weights = jnp.exp(frame_scores - largest)
-            mem_weights = jnp.exp(mem_scores - largest)
-            denominator = jnp.sum(frame_weights, axis=-1, keepdims=True) + jnp.sum(
-                mem_weights, axis=-1, keepdims=True
-            )
+            scores = jnp.concatenate([frame_scores, jnp.where(live, mem_scores, -1e30)], axis=1)
+            weights = jnp.exp(scores - jnp.max(scores, axis=-1, keepdims=True))
+            denominator = jnp.sum(weights, axis=-1, keepdims=True)
+            rounded = weights.astype(jnp.bfloat16)
             blended = jnp.dot(
-                frame_weights.astype(jnp.bfloat16), values, preferred_element_type=jnp.float32
-            ) + jnp.dot(mem_weights.astype(jnp.bfloat16), value_ref[:, span], preferred_element_type=jnp.float32)
+                rounded[:, :frame_rows], values, preferred_element_type=jnp.float32
+            ) + jnp.dot(rounded[:, frame_rows:], value_ref[:, span], preferred_element_type=jnp.float32)
             attended[start : start + half, span] = (blended / denominator).astype(attended.dtype)
 
 
@@ -432,16 +424,16 @@
         prepare_kernel,
         (jax.ShapeDtypeStruct(extra.shape, extra.dtype), frame, frame),
         (extra, *tokens),
-        range(5),
-        [pltpu.SemaphoreType.DMA((3,))],
+        (),
+        [],
         8 * MIB,
         0,
     )
 
 
 def project(normed, pieces):
-    rows, width = pieces[0][0].shape
-    depth = rows * len(pieces)
+    width = pieces[0][0].shape[1]
+    depth = sum(array.shape[0] for array, _ in pieces)
     return kernel_call(
         functools.partial(project_kernel, tuple(place for _, place in pieces)),
         jax.ShapeDtypeStruct((normed.shape[0], width), jnp.float32),
@@ -454,10 +446,11 @@
 
 
 def assemble(pieces):
-    rows, width = pieces[0][0].shape
+    width = pieces[0][0].shape[1]
+    depth = sum(array.shape[0] for array, _ in pieces)
     return kernel_call(
         functools.partial(assemble_kernel, tuple(place for _, place in pieces)),
-        jax.ShapeDtypeStruct((rows * len(pieces), width), pieces[0][0].dtype),
+        jax.ShapeDtypeStruct((depth, width), pieces[0][0].dtype),
         [array for array, _ in pieces],
         (),
         [],
@@ -467,11 +460,11 @@
 
 
 def step(extra, keys, values, normed, part, pieces):
-    rows, width = pieces[0][0].shape
-    depth = rows * len(pieces)
+    width = pieces[0][0].shape[1]
+    depth = sum(array.shape[0] for array, _ in pieces)
     frame_rows = normed.shape[0]
     return kernel_call(
-        functools.partial(step_kernel, tuple(place for _, place in pieces), pieces[0][1][0], HEADS // SPATIAL),
+        functools.partial(step_kernel, tuple(place for _, place in pieces), pieces[0][1][0][0], HEADS // SPATIAL),
         jax.ShapeDtypeStruct((frame_rows, width // 3), normed.dtype),
         (extra, keys, values, normed, part, *[array for array, _ in pieces]),
         (),
@@ -551,12 +544,12 @@
     weights, extra, memory = pack(
         w_query, w_key, w_value, intersection, slot_of, counts, step_scale, norm_gain, mem_cache
     )
-    pieces = sorted(all_pieces(*weights), key=lambda piece: piece[1][0])
+    pieces = all_pieces(*weights)
     tokens = all_tokens(latent)
     keys, values = all_memory(memory)
     extra, current, normed = prepare(extra, tokens)
-    part = project(normed, [piece for piece in pieces if piece[1][0] < late])
-    attended = step(extra, keys, values, normed, part, [piece for piece in pieces if piece[1][0] == late])
+    part = project(normed, [piece for piece in pieces if piece[1][0][0] < late])
+    attended = step(extra, keys, values, normed, part, [piece for piece in pieces if piece[1][0][0] == late])
     updates = [
         (attended, (0, 0)),
         (moved(attended, lambda x, p, y, c: (x, p ^ 1, 1 - y, c)), (1, 1)),

time: 102 us -> 82.1 us (0.80)
  waiting for transfers between devices: 42.5 us -> 28.7 us
  starting transfers between devices: 42.2 us -> 37.6 us
    ppermute x26 -> x23, waiting for transfers between devices: 26.7 us -> 18.8 us  [moved(): return lax.ppermute(array, AXES, pairs)]
    ppermute x5, waiting for transfers between devices: 15.8 us -> 9.9 us  [hop(): lax.ppermute(array, 'frame', [(i, i ^ bits) for i in range(lax.axis_size(...]
    ppermute x5, starting transfers between devices: 8.07 us -> 4.22 us  [hop(): lax.ppermute(array, 'frame', [(i, i ^ bits) for i in range(lax.axis_size(...]
    ppermute x26 -> x23, starting transfers between devices: 34.1 us -> 33.4 us  [moved(): return lax.ppermute(array, AXES, pairs)]
  transfers between devices with their start and end apart: 31 -> 28, of which waited for: 12 -> 8; matrix products, arithmetic and copies ran while one was open for 3% -> 4% of each run, Pallas kernels for 6% -> 7%
where the time goes in v7:
time: 82.1 us; the launch traced here: 81.8 us
  starting transfers between devices  37.6 us (46%)
  waiting for transfers between devices  28.7 us (35%)
  Pallas kernels  12.3 us (15%)
  other arithmetic  1.73 us (2%)
  local copies, waits for them, and re-layouts  1.17 us (1%)
    ppermute x23, starting transfers between devices, moved(): return lax.ppermute(array, AXES, pairs)  33.4 us
    ppermute x23, waiting for transfers between devices, moved(): return lax.ppermute(array, AXES, pairs)  18.8 us
    ppermute x5, waiting for transfers between devices, hop(): lax.ppermute(array, 'frame', [(i, i ^ bits) for i in range(lax.axis_size(...  9.9 us
    pallas_call x6, Pallas kernels, kernel_call(): pl.pallas_call(kernel, out_shape=out_shape, in_specs=[free if number in a...  9.07 us
    ppermute x5, starting transfers between devices, hop(): lax.ppermute(array, 'frame', [(i, i ^ bits) for i in range(lax.axis_size(...  4.22 us
    pallas_call x1, Pallas kernels, pack(): pl.pallas_call(pack_kernel, out_shape=out_shape, in_specs=[held] * 9, out...  3.2 us
  transfers between devices with their start and end apart: 28, of which 8 were waited for; matrix products, arithmetic and copies ran while one was open for 4% of the time, Pallas kernels for 7%

profile of v7, /device:TPU:1, one launch (start us, length us, event | category | flops | bytes accessed | tf_op | source)
XLA Modules:
  0.0 81.8 jit_solution(7941939361630135745)
XLA Ops:
  0.0 1.9 %collective-permute-start = (bf16[64,1536]{1,0:T(8,128)(2,1)}, bf16[64,1536]{1,0:T(8,128)(2,1)S(1)}, u32[]{:S(2)}, u32[]{:S(2)}) collective-permute-start(bf16[64,1536]{1,0:T(8,128)(2,1)} %param.10), channel_id=1, source_target_pairs={{1,0},{3,2},{4,5},{6,7},{9,8},{11,10},{12,13},{14,15},{17,16},{19,... | collective-permute-start | bytes 589832 | tf_op jit(solution)/shard_map/ppermute | solution.py:36
  1.9 3.2 %pack.1 = (bf16[96,1152]{1,0:T(8,128)(2,1)}, bf16[96,1152]{1,0:T(8,128)(2,1)}, bf16[96,1152]{1,0:T(8,128)(2,1)}, bf16[96,1152]{1,0:T(8,128)(2,1)}, f32[4,1536]{1...) custom-call(bf16[96,1536]{1,0:T(8,128)(2,1)} %w_query.1, ...), custom_call_target="tpu_custom_call" | custom-call | tf_op jit(solution)/shard_map/pack/pallas_call | solution.py:164
  5.2 0.1 collective-permute-start.4
  5.2 2.8 %collective-permute-start.5 = (bf16[4,8,2,384]{3,2,1,0:T(2,128)(2,1)}, bf16[4,8,2,384]{3,2,1,0:T(2,128)(2,1)S(1)}, u32[]{:S(2)}, u32[]{:S(2)}) collective-permute-start(bf16[4,8,2,384]{3,2,1,0:T(2,128)(2,1)} %get-tuple-element.26), channel_id=1, source_target_pairs={{0,2},{1,3},{2,0},{3,1},{4,6},{5,7},{6,4},{7,5},{8,10},{9,11},{10,... | collective-permute-start | bytes 147464 | tf_op jit(solution)/shard_map/ppermute | solution.py:228
  8.0 0.3 collective-permute-start.6
  8.3 1.7 %collective-permute-start.9 = (bf16[96,1152]{1,0:T(8,128)(2,1)}, bf16[96,1152]{1,0:T(8,128)(2,1)S(1)}, u32[]{:S(2)}, u32[]{:S(2)}) collective-permute-start(bf16[96,1152]{1,0:T(8,128)(2,1)} %get-tuple-element.30), channel_id=1, source_target_pairs={{0,2},{1,3},{2,0},{3,1},{4,6},{5,7},{6,4},{7,5},{8,10},{9,11},{10,... | collective-permute-start | bytes 663560 | tf_op jit(solution)/shard_map/ppermute | solution.py:36
  10.1 0.9 %constant_dynamic-update-slice_fusion.1 = bf16[128,1536]{1,0:T(8,128)(2,1)S(1)} fusion(bf16[64,1536]{1,0:T(8,128)(2,1)} %param.10), kind=kLoop, calls=%fused_computation.10 | loop fusion | bytes 393216
  11.0 2.3 %collective-permute-start.11 = (bf16[96,1152]{1,0:T(8,128)(2,1)}, bf16[96,1152]{1,0:T(8,128)(2,1)S(1)}, u32[]{:S(2)}, u32[]{:S(2)}) collective-permute-start(bf16[96,1152]{1,0:T(8,128)(2,1)} %get-tuple-element.32), channel_id=1, source_target_pairs={{0,8},{1,11},{2,10},{3,9},{4,12},{5,15},{6,14},{7,13},{8,0},{9,3},... | collective-permute-start | bytes 663560 | tf_op jit(solution)/shard_map/ppermute | solution.py:36
  13.4 1.7 %collective-permute-start.10 = (bf16[96,1152]{1,0:T(8,128)(2,1)}, bf16[96,1152]{1,0:T(8,128)(2,1)S(1)}, u32[]{:S(2)}, u32[]{:S(2)}) collective-permute-start(bf16[96,1152]{1,0:T(8,128)(2,1)} %get-tuple-element.31), channel_id=1, source_target_pairs={{0,4},{1,7},{2,6},{3,5},{4,0},{5,3},{6,2},{7,1},{8,12},{9,15},{10,... | collective-permute-start | bytes 663560 | tf_op jit(solution)/shard_map/ppermute | solution.py:36
  15.0 0.0 collective-permute-done.6
  15.0 1.1 %pad_maximum_fusion.1 = bf16[4,4,8,2,384]{4,3,2,1,0:T(2,128)(2,1)S(1)} fusion(bf16[1,4,8,2,384]{4,3,2,1,0:T(2,128)(2,1)S(1)} %bitcast.11, bf16[1,4,8,2,384]{4,3,2,1,0:T(2,128)(2,1)S(1)} %bitcast.10, bf16[1,4,8,2,384]{4,3,2,1,0:T(2,128)(2,1)S(1)} %bitcast.9, bf16[1,4,8,2,384]{4,3,2,1,0:T(2,128)(2,1)} %bitcast.8), kind=kLoop, calls=%fused_computation.2 | loop fusion | flops 294912 | bytes 393216 | tf_op jit(solution)/shard_map/stack | solution.py:218
  16.2 1.3 %collective-permute-start.2 = (bf16[128,1536]{1,0:T(8,128)(2,1)S(1)}, bf16[128,1536]{1,0:T(8,128)(2,1)S(1)}, u32[]{:S(2)}, u32[]{:S(2)}) collective-permute-start(bf16[128,1536]{1,0:T(8,128)(2,1)S(1)} %constant_dynamic-update-slice_fusion.block), channel_id=1, source_target_pairs={{0,4},{2,6},{5,1},{7,3},{8,12},{10,14},{13,9},{15,11},{16,20},{18,... | collective-permute-start | bytes 1179656 | tf_op jit(solution)/shard_map/ppermute | solution.py:36
  17.5 8.1 %collective-permute-done.10 = bf16[96,1152]{1,0:T(8,128)(2,1)S(1)} collective-permute-done((bf16[96,1152]{1,0:T(8,128)(2,1)}, bf16[96,1152]{1,0:T(8,128)(2,1)S(1)}, u32[]{:S(2)}, u32[]{:S(2)}) %collective-permute-start.10) | collective-permute-done | bytes 221216 | tf_op jit(solution)/shard_map/ppermute | solution.py:36
  25.6 0.1 collective-permute-start.12
  25.7 0.1 fusion.1
  25.9 1.0 %collective-permute-start.7 = (bf16[4,2,8,2,384]{4,3,2,1,0:T(2,128)(2,1)S(1)}, bf16[4,2,8,2,384]{4,3,2,1,0:T(2,128)(2,1)S(1)}, u32[]{:S(2)}, u32[]{:S(2)}) collective-permute-start(bf16[4,2,8,2,384]{4,3,2,1,0:T(2,128)(2,1)S(1)} %get-tuple-element.44), channel_id=1, source_target_pairs={{0,4},{1,5},{2,6},{3,7},{4,0},{5,1},{6,2},{7,3},{8,12},{9,13},{10,... | collective-permute-start | bytes 294920 | tf_op jit(solution)/shard_map/ppermute | solution.py:228
  26.8 1.3 %collective-permute-start.13 = (bf16[96,1152]{1,0:T(8,128)(2,1)}, bf16[96,1152]{1,0:T(8,128)(2,1)S(1)}, u32[]{:S(2)}, u32[]{:S(2)}) collective-permute-start(bf16[96,1152]{1,0:T(8,128)(2,1)} %get-tuple-element.31), channel_id=1, source_target_pairs={{0,12},{1,15},{2,14},{3,13},{4,8},{5,11},{6,10},{7,9},{8,4},{9,7},... | collective-permute-start | bytes 663560 | tf_op jit(solution)/shard_map/ppermute | solution.py:36
  28.1 3.3 %collective-permute-done.7 = bf16[4,2,8,2,384]{4,3,2,1,0:T(2,128)(2,1)S(1)} collective-permute-done((bf16[4,2,8,2,384]{4,3,2,1,0:T(2,128)(2,1)S(1)}, bf16[4,2,8,2,384]{4,3,2,1,0:T(2,128)(2,1)S(1)}, u32[]{:S(2)}, u32[]{:S(2)}) %collective-permute-start.7) | collective-permute-done | bytes 98336 | tf_op jit(solution)/shard_map/ppermute | solution.py:228
  31.4 6.9 %collective-permute-start.15 = (bf16[96,1152]{1,0:T(8,128)(2,1)}, bf16[96,1152]{1,0:T(8,128)(2,1)S(1)}, u32[]{:S(2)}, u32[]{:S(2)}) collective-permute-start(bf16[96,1152]{1,0:T(8,128)(2,1)} %get-tuple-element.29.refs_0_.refs_1_), channel_id=1, source_target_pairs={{0,1},{1,0},{2,3},{3,2},{4,5},{5,4},{6,7},{7,6},{8,9},{9,8},{10,11... | collective-permute-start | bytes 663560 | tf_op jit(solution)/shard_map/ppermute | solution.py:36
  38.3 0.7 collective-permute-start.1
  39.0 0.0 collective-permute-done.2.far
  39.0 2.8 %collective-permute-start.3 = (bf16[128,1536]{1,0:T(8,128)(2,1)S(1)}, bf16[128,1536]{1,0:T(8,128)(2,1)S(1)}, u32[]{:S(2)}, u32[]{:S(2)}) collective-permute-start(bf16[128,1536]{1,0:T(8,128)(2,1)S(1)} %collective-permute-done.2.far), channel_id=1, source_target_pairs={{1,3},{3,1},{4,6},{6,4},{9,11},{11,9},{12,14},{14,12},{17,19},{19,... | collective-permute-start | bytes 1179656 | tf_op jit(solution)/shard_map/ppermute | solution.py:36
  41.8 0.3 fusion
  42.1 0.1 collective-permute-start.8
  42.2 0.1 collective-permute-start.14
  42.3 6.6 %collective-permute-done.8 = bf16[8,1,8,2,384]{4,3,2,1,0:T(2,128)(2,1)S(1)} collective-permute-done((bf16[8,1,8,2,384]{4,3,2,1,0:T(2,128)(2,1)S(1)}, bf16[8,1,8,2,384]{4,3,2,1,0:T(2,128)(2,1)S(1)}, u32[]{:S(2)}, u32[]{:S(2)}) %collective-permute-start.8) | collective-permute-done | bytes 98336 | tf_op jit(solution)/shard_map/ppermute | solution.py:228
  48.9 0.5 collective-permute-start.17
  49.4 0.0 collective-permute-start.18
  49.4 0.3 pad_maximum_fusion
  49.7 0.5 collective-permute-start.19
  50.3 1.6 %collective-permute-start.16 = (bf16[96,1152]{1,0:T(8,128)(2,1)S(1)}, bf16[96,1152]{1,0:T(8,128)(2,1)S(1)}, u32[]{:S(2)}, u32[]{:S(2)}) collective-permute-start(bf16[96,1152]{1,0:T(8,128)(2,1)S(1)} %collective-permute-done.9.refs_1_.refs_2_), channel_id=1, source_target_pairs={{0,1},{1,0},{2,3},{3,2},{4,5},{5,4},{6,7},{7,6},{8,9},{9,8},{10,11... | collective-permute-start | bytes 663560 | tf_op jit(solution)/shard_map/ppermute | solution.py:36
  51.9 0.0 collective-permute-start.20
  52.0 0.6 shard_map.100
  52.6 0.4 collective-permute-done.16.refs_7_.refs_6_
  53.0 1.2 %shard_map.102.part_ref = f32[256,1152]{1,0:T(8,128)S(1)} custom-call(bf16[256,1536]{1,0:T(8,128)(2,1)S(1)} %get-tuple-element.33.refs_0_.normed, bf16[96,1152]{1,0:T(8,128)(2,1)S(1)} %copy-done, bf16[96,1152]{1,0:T(8,128)(2,1)S(1)} %collective-permute-done.9.refs_1_.refs_2_, bf16[192,1152]{1,0:T(8,128)(2,1)S(1)} %constant_dynamic-update-slice_fusion.2.refs_2_.refs_3_, ...), custom_call_target="tpu_custom_call" | custom-call | flops 679477248 | bytes 3440640 | tf_op jit(solution)/shard_map/pallas_call | solution.py:410
  54.3 2.2 %shard_map.103.first_part = bf16[256,384]{1,0:T(8,128)(2,1)S(1)} custom-call(f32[4,1536]{1,0:T(4,128)S(1)} %get-tuple-element.23.extra_ref, bf16[128,384]{1,0:T(8,128)(2,1)S(1)} %get-tuple-element.46.key_ref, bf16[128,384]{1,0:T(8,128)(2,1)S(1)} %get-tuple-element.45.value_ref, bf16[256,1536]{1,0:T(8,128)(2,1)S(1)} %get-tuple-element.33.refs_0_.normed, ...), custom_call_target="tpu_custom_call" | custom-call | flops 377487360 | bytes 3072000 | tf_op jit(solution)/shard_map/pallas_call | solution.py:410
  56.5 1.0 %collective-permute-start.23 = (bf16[256,384]{1,0:T(8,128)(2,1)S(1)}, bf16[256,384]{1,0:T(8,128)(2,1)S(1)}, u32[]{:S(2)}, u32[]{:S(2)}) collective-permute-start(bf16[256,384]{1,0:T(8,128)(2,1)S(1)} %shard_map.103.first_part), channel_id=1, source_target_pairs={{0,2},{1,3},{2,0},{3,1},{4,6},{5,7},{6,4},{7,5},{8,10},{9,11},{10,... | collective-permute-start | bytes 589832 | tf_op jit(solution)/shard_map/ppermute | solution.py:36
  57.5 1.7 %collective-permute-start.21 = (bf16[256,384]{1,0:T(8,128)(2,1)S(1)}, bf16[256,384]{1,0:T(8,128)(2,1)S(1)}, u32[]{:S(2)}, u32[]{:S(2)}) collective-permute-start(bf16[256,384]{1,0:T(8,128)(2,1)S(1)} %shard_map.103.first_part), channel_id=1, source_target_pairs={{0,6},{1,7},{2,4},{3,5},{4,2},{5,3},{6,0},{7,1},{8,14},{9,15},{10,... | collective-permute-start | bytes 589832 | tf_op jit(solution)/shard_map/ppermute | solution.py:36
  59.2 0.3 shard_map.101.weights
  59.5 3.1 %collective-permute-done.23.fourth_part = bf16[256,384]{1,0:T(8,128)(2,1)S(1)} collective-permute-done((bf16[256,384]{1,0:T(8,128)(2,1)S(1)}, bf16[256,384]{1,0:T(8,128)(2,1)S(1)}, u32[]{:S(2)}, u32[]{:S(2)}) %collective-permute-start.23) | collective-permute-done | bytes 196640 | tf_op jit(solution)/shard_map/ppermute | solution.py:36
  62.6 0.6 collective-permute-done.22.third_part
  63.3 4.5 %collective-permute-done.21.second_part = bf16[256,384]{1,0:T(8,128)(2,1)S(1)} collective-permute-done((bf16[256,384]{1,0:T(8,128)(2,1)S(1)}, bf16[256,384]{1,0:T(8,128)(2,1)S(1)}, u32[]{:S(2)}, u32[]{:S(2)}) %collective-permute-start.21) | collective-permute-done | bytes 196640 | tf_op jit(solution)/shard_map/ppermute | solution.py:36
  67.7 4.0 %shard_map.104 = (bf16[64,384]{1,0:T(8,128)(2,1)S(1)}, bf16[64,384]{1,0:T(8,128)(2,1)S(1)}, bf16[64,384]{1,0:T(8,128)(2,1)S(1)}, bf16[64,384]{1,0:T(8,128)(2,1)S(1)}, bf16[64,384]{1,0:T(8,128)(2,1)S(1)}) custom-call(f32[4,1536]{1,0:T(4,128)S(1)} %get-tuple-element.23.extra_ref, bf16[128,384]{1,0:T(8,128)(2,1)S(1)} %get-tuple-element.46.key_ref, ...), custom_call_target="tpu_custom_call" | custom-call | flops 1056964608 | bytes 5332992 | tf_op jit(solution)/shard_map/pallas_call | solution.py:410
  71.8 1.5 %collective-permute-start.24 = (bf16[64,384]{1,0:T(8,128)(2,1)S(1)}, bf16[64,384]{1,0:T(8,128)(2,1)S(1)}, u32[]{:S(2)}, u32[]{:S(2)}) collective-permute-start(bf16[64,384]{1,0:T(8,128)(2,1)S(1)} %get-tuple-element.35), channel_id=1, source_target_pairs={{0,2},{1,4},{2,0},{3,6},{4,1},{5,7},{6,3},{7,5},{8,10},{9,12},{10,... | collective-permute-start | bytes 147464 | tf_op jit(solution)/shard_map/ppermute | solution.py:36
  73.2 1.5 %collective-permute-start.26 = (bf16[64,384]{1,0:T(8,128)(2,1)S(1)}, bf16[64,384]{1,0:T(8,128)(2,1)S(1)}, u32[]{:S(2)}, u32[]{:S(2)}) collective-permute-start(bf16[64,384]{1,0:T(8,128)(2,1)S(1)} %get-tuple-element.37), channel_id=1, source_target_pairs={{0,1},{1,7},{2,3},{3,5},{4,2},{5,4},{6,0},{7,6},{8,9},{9,15},{10,1... | collective-permute-start | bytes 147464 | tf_op jit(solution)/shard_map/ppermute | solution.py:36
  74.8 4.2 %collective-permute-start.27 = (bf16[64,384]{1,0:T(8,128)(2,1)S(1)}, bf16[64,384]{1,0:T(8,128)(2,1)S(1)}, u32[]{:S(2)}, u32[]{:S(2)}) collective-permute-start(bf16[64,384]{1,0:T(8,128)(2,1)S(1)} %get-tuple-element.38), channel_id=1, source_target_pairs={{1,6},{3,4},{4,3},{6,1},{9,14},{11,12},{12,11},{14,9},{17,22},{19,... | collective-permute-start | bytes 147464 | tf_op jit(solution)/shard_map/ppermute | solution.py:36
  79.0 2.0 %collective-permute-done.27.fourth = bf16[64,384]{1,0:T(8,128)(2,1)S(1)} collective-permute-done((bf16[64,384]{1,0:T(8,128)(2,1)S(1)}, bf16[64,384]{1,0:T(8,128)(2,1)S(1)}, u32[]{:S(2)}, u32[]{:S(2)}) %collective-permute-start.27) | collective-permute-done | bytes 49184 | tf_op jit(solution)/shard_map/ppermute | solution.py:36
  81.1 0.7 shard_map.105
  (28 shorter events, 0.1 us)
Async XLA Ops:
  0.0 16.2 %collective-permute-start = (bf16[64,1536]{1,0:T(8,128)(2,1)}, bf16[64,1536]{1,0:T(8,128)(2,1)S(1)}, u32[]{:S(2)}, u32[]{:S(2)}) collective-permute-start(bf16[64,1536]{1,0:T(8,128)(2,1)} %param.10), channel_id=1, source_target_pairs={{1,0},{3,2},{4,5},{6,7},{9,8},{11,10},{12,13},{14,15},{17,16},{19,... | collective-permute-start | bytes 589832 | tf_op jit(solution)/shard_map/ppermute | solution.py:36
  5.1 46.8 %copy-start.1 = (f32[4,1536]{1,0:T(4,128)S(1)}, f32[4,1536]{1,0:T(4,128)}, u32[]{:S(2)}) copy-start(f32[4,1536]{1,0:T(4,128)} %get-tuple-element.22.extra_ref) | copy-start | bytes 73732
  5.1 47.9 %copy-start = (bf16[96,1152]{1,0:T(8,128)(2,1)S(1)}, bf16[96,1152]{1,0:T(8,128)(2,1)}, u32[]{:S(2)}) copy-start(bf16[96,1152]{1,0:T(8,128)(2,1)} %get-tuple-element.29.refs_0_.refs_1_) | copy-start | bytes 663556
  5.2 5.9 %collective-permute-start.4 = (bf16[4,8,2,384]{3,2,1,0:T(2,128)(2,1)}, bf16[4,8,2,384]{3,2,1,0:T(2,128)(2,1)S(1)}, u32[]{:S(2)}, u32[]{:S(2)}) collective-permute-start(bf16[4,8,2,384]{3,2,1,0:T(2,128)(2,1)} %get-tuple-element.25), channel_id=1, source_target_pairs={{0,1},{1,0},{2,3},{3,2},{4,5},{5,4},{6,7},{7,6},{8,9},{9,8},{10,11... | collective-permute-start | bytes 147464 | tf_op jit(solution)/shard_map/ppermute | solution.py:228
  5.2 8.1 %collective-permute-start.5 = (bf16[4,8,2,384]{3,2,1,0:T(2,128)(2,1)}, bf16[4,8,2,384]{3,2,1,0:T(2,128)(2,1)S(1)}, u32[]{:S(2)}, u32[]{:S(2)}) collective-permute-start(bf16[4,8,2,384]{3,2,1,0:T(2,128)(2,1)} %get-tuple-element.26), channel_id=1, source_target_pairs={{0,2},{1,3},{2,0},{3,1},{4,6},{5,7},{6,4},{7,5},{8,10},{9,11},{10,... | collective-permute-start | bytes 147464 | tf_op jit(solution)/shard_map/ppermute | solution.py:228
  8.0 7.0 %collective-permute-start.6 = (bf16[4,8,2,384]{3,2,1,0:T(2,128)(2,1)}, bf16[4,8,2,384]{3,2,1,0:T(2,128)(2,1)S(1)}, u32[]{:S(2)}, u32[]{:S(2)}) collective-permute-start(bf16[4,8,2,384]{3,2,1,0:T(2,128)(2,1)} %get-tuple-element.27), channel_id=1, source_target_pairs={{0,3},{1,2},{2,1},{3,0},{4,7},{5,6},{6,5},{7,4},{8,11},{9,10},{10,... | collective-permute-start | bytes 147464 | tf_op jit(solution)/shard_map/ppermute | solution.py:228
  8.3 29.9 %collective-permute-start.9 = (bf16[96,1152]{1,0:T(8,128)(2,1)}, bf16[96,1152]{1,0:T(8,128)(2,1)S(1)}, u32[]{:S(2)}, u32[]{:S(2)}) collective-permute-start(bf16[96,1152]{1,0:T(8,128)(2,1)} %get-tuple-element.30), channel_id=1, source_target_pairs={{0,2},{1,3},{2,0},{3,1},{4,6},{5,7},{6,4},{7,5},{8,10},{9,11},{10,... | collective-permute-start | bytes 663560 | tf_op jit(solution)/shard_map/ppermute | solution.py:36
  11.0 14.6 %collective-permute-start.11 = (bf16[96,1152]{1,0:T(8,128)(2,1)}, bf16[96,1152]{1,0:T(8,128)(2,1)S(1)}, u32[]{:S(2)}, u32[]{:S(2)}) collective-permute-start(bf16[96,1152]{1,0:T(8,128)(2,1)} %get-tuple-element.32), channel_id=1, source_target_pairs={{0,8},{1,11},{2,10},{3,9},{4,12},{5,15},{6,14},{7,13},{8,0},{9,3},... | collective-permute-start | bytes 663560 | tf_op jit(solution)/shard_map/ppermute | solution.py:36
  13.4 12.2 %collective-permute-start.10 = (bf16[96,1152]{1,0:T(8,128)(2,1)}, bf16[96,1152]{1,0:T(8,128)(2,1)S(1)}, u32[]{:S(2)}, u32[]{:S(2)}) collective-permute-start(bf16[96,1152]{1,0:T(8,128)(2,1)} %get-tuple-element.31), channel_id=1, source_target_pairs={{0,4},{1,7},{2,6},{3,5},{4,0},{5,3},{6,2},{7,1},{8,12},{9,15},{10,... | collective-permute-start | bytes 663560 | tf_op jit(solution)/shard_map/ppermute | solution.py:36
  16.2 22.8 %collective-permute-start.2 = (bf16[128,1536]{1,0:T(8,128)(2,1)S(1)}, bf16[128,1536]{1,0:T(8,128)(2,1)S(1)}, u32[]{:S(2)}, u32[]{:S(2)}) collective-permute-start(bf16[128,1536]{1,0:T(8,128)(2,1)S(1)} %constant_dynamic-update-slice_fusion.block), channel_id=1, source_target_pairs={{0,4},{2,6},{5,1},{7,3},{8,12},{10,14},{13,9},{15,11},{16,20},{18,... | collective-permute-start | bytes 1179656 | tf_op jit(solution)/shard_map/ppermute | solution.py:36
  25.6 23.7 %collective-permute-start.12 = (bf16[192,1152]{1,0:T(8,128)(2,1)S(1)}, bf16[192,1152]{1,0:T(8,128)(2,1)S(1)}, u32[]{:S(2)}, u32[]{:S(2)}) collective-permute-start(bf16[192,1152]{1,0:T(8,128)(2,1)S(1)} %constant_dynamic-update-slice_fusion.2.refs_2_.refs_3_), channel_id=1, source_target_pairs={{0,16},{1,17},{2,18},{3,19},{4,20},{5,21},{6,22},{7,23},{8,24},{9,... | collective-permute-start | bytes 1327112 | tf_op jit(solution)/shard_map/ppermute | solution.py:36
  25.9 5.5 %collective-permute-start.7 = (bf16[4,2,8,2,384]{4,3,2,1,0:T(2,128)(2,1)S(1)}, bf16[4,2,8,2,384]{4,3,2,1,0:T(2,128)(2,1)S(1)}, u32[]{:S(2)}, u32[]{:S(2)}) collective-permute-start(bf16[4,2,8,2,384]{4,3,2,1,0:T(2,128)(2,1)S(1)} %get-tuple-element.44), channel_id=1, source_target_pairs={{0,4},{1,5},{2,6},{3,7},{4,0},{5,1},{6,2},{7,3},{8,12},{9,13},{10,... | collective-permute-start | bytes 294920 | tf_op jit(solution)/shard_map/ppermute | solution.py:228
  26.8 15.3 %collective-permute-start.13 = (bf16[96,1152]{1,0:T(8,128)(2,1)}, bf16[96,1152]{1,0:T(8,128)(2,1)S(1)}, u32[]{:S(2)}, u32[]{:S(2)}) collective-permute-start(bf16[96,1152]{1,0:T(8,128)(2,1)} %get-tuple-element.31), channel_id=1, source_target_pairs={{0,12},{1,15},{2,14},{3,13},{4,8},{5,11},{6,10},{7,9},{8,4},{9,7},... | collective-permute-start | bytes 663560 | tf_op jit(solution)/shard_map/ppermute | solution.py:36
  31.4 10.8 %collective-permute-start.15 = (bf16[96,1152]{1,0:T(8,128)(2,1)}, bf16[96,1152]{1,0:T(8,128)(2,1)S(1)}, u32[]{:S(2)}, u32[]{:S(2)}) collective-permute-start(bf16[96,1152]{1,0:T(8,128)(2,1)} %get-tuple-element.29.refs_0_.refs_1_), channel_id=1, source_target_pairs={{0,1},{1,0},{2,3},{3,2},{4,5},{5,4},{6,7},{7,6},{8,9},{9,8},{10,11... | collective-permute-start | bytes 663560 | tf_op jit(solution)/shard_map/ppermute | solution.py:36
  38.3 12.0 %collective-permute-start.1 = (bf16[128,1536]{1,0:T(8,128)(2,1)S(1)}, bf16[128,1536]{1,0:T(8,128)(2,1)S(1)}, u32[]{:S(2)}, u32[]{:S(2)}) collective-permute-start(bf16[128,1536]{1,0:T(8,128)(2,1)S(1)} %constant_dynamic-update-slice_fusion.block), channel_id=1, source_target_pairs={{0,2},{2,0},{5,7},{7,5},{8,10},{10,8},{13,15},{15,13},{16,18},{18,... | collective-permute-start | bytes 1179656 | tf_op jit(solution)/shard_map/ppermute | solution.py:36
  39.0 12.9 %collective-permute-start.3 = (bf16[128,1536]{1,0:T(8,128)(2,1)S(1)}, bf16[128,1536]{1,0:T(8,128)(2,1)S(1)}, u32[]{:S(2)}, u32[]{:S(2)}) collective-permute-start(bf16[128,1536]{1,0:T(8,128)(2,1)S(1)} %collective-permute-done.2.far), channel_id=1, source_target_pairs={{1,3},{3,1},{4,6},{6,4},{9,11},{11,9},{12,14},{14,12},{17,19},{19,... | collective-permute-start | bytes 1179656 | tf_op jit(solution)/shard_map/ppermute | solution.py:36
  42.1 6.8 %collective-permute-start.8 = (bf16[8,1,8,2,384]{4,3,2,1,0:T(2,128)(2,1)S(1)}, bf16[8,1,8,2,384]{4,3,2,1,0:T(2,128)(2,1)S(1)}, u32[]{:S(2)}, u32[]{:S(2)}) collective-permute-start(bf16[8,1,8,2,384]{4,3,2,1,0:T(2,128)(2,1)S(1)} %get-tuple-element.42), channel_id=1, source_target_pairs={{0,8},{1,9},{2,10},{3,11},{4,12},{5,13},{6,14},{7,15},{8,0},{9,1},... | collective-permute-start | bytes 294920 | tf_op jit(solution)/shard_map/ppermute | solution.py:228
  42.2 7.5 %collective-permute-start.14 = (bf16[96,1152]{1,0:T(8,128)(2,1)S(1)}, bf16[96,1152]{1,0:T(8,128)(2,1)S(1)}, u32[]{:S(2)}, u32[]{:S(2)}) collective-permute-start(bf16[96,1152]{1,0:T(8,128)(2,1)S(1)} %collective-permute-done.13.refs_4_.refs_0_), channel_id=1, source_target_pairs={{0,16},{1,17},{2,18},{3,19},{4,20},{5,21},{6,22},{7,23},{8,24},{9,... | collective-permute-start | bytes 663560 | tf_op jit(solution)/shard_map/ppermute | solution.py:36
  48.9 4.1 %collective-permute-start.17 = (bf16[192,1152]{1,0:T(8,128)(2,1)S(1)}, bf16[192,1152]{1,0:T(8,128)(2,1)S(1)}, u32[]{:S(2)}, u32[]{:S(2)}) collective-permute-start(bf16[192,1152]{1,0:T(8,128)(2,1)S(1)} %constant_dynamic-update-slice_fusion.2.refs_2_.refs_3_), channel_id=1, source_target_pairs={{0,1},{1,0},{2,3},{3,2},{4,5},{5,4},{6,7},{7,6},{8,9},{9,8},{10,11... | collective-permute-start | bytes 1327112 | tf_op jit(solution)/shard_map/ppermute | solution.py:36
  49.4 3.7 %collective-permute-start.18 = (bf16[192,1152]{1,0:T(8,128)(2,1)S(1)}, bf16[192,1152]{1,0:T(8,128)(2,1)S(1)}, u32[]{:S(2)}, u32[]{:S(2)}) collective-permute-start(bf16[192,1152]{1,0:T(8,128)(2,1)S(1)} %collective-permute-done.12.refs_3_.refs_4_), channel_id=1, source_target_pairs={{0,1},{1,0},{2,3},{3,2},{4,5},{5,4},{6,7},{7,6},{8,9},{9,8},{10,11... | collective-permute-start | bytes 1327112 | tf_op jit(solution)/shard_map/ppermute | solution.py:36
  49.7 4.5 %collective-permute-start.19 = (bf16[96,1152]{1,0:T(8,128)(2,1)S(1)}, bf16[96,1152]{1,0:T(8,128)(2,1)S(1)}, u32[]{:S(2)}, u32[]{:S(2)}) collective-permute-start(bf16[96,1152]{1,0:T(8,128)(2,1)S(1)} %collective-permute-done.13.refs_4_.refs_0_), channel_id=1, source_target_pairs={{0,1},{1,0},{2,3},{3,2},{4,5},{5,4},{6,7},{7,6},{8,9},{9,8},{10,11... | collective-permute-start | bytes 663560 | tf_op jit(solution)/shard_map/ppermute | solution.py:36
  50.3 2.8 %collective-permute-start.16 = (bf16[96,1152]{1,0:T(8,128)(2,1)S(1)}, bf16[96,1152]{1,0:T(8,128)(2,1)S(1)}, u32[]{:S(2)}, u32[]{:S(2)}) collective-permute-start(bf16[96,1152]{1,0:T(8,128)(2,1)S(1)} %collective-permute-done.9.refs_1_.refs_2_), channel_id=1, source_target_pairs={{0,1},{1,0},{2,3},{3,2},{4,5},{5,4},{6,7},{7,6},{8,9},{9,8},{10,11... | collective-permute-start | bytes 663560 | tf_op jit(solution)/shard_map/ppermute | solution.py:36
  51.9 2.4 %collective-permute-start.20 = (bf16[96,1152]{1,0:T(8,128)(2,1)S(1)}, bf16[96,1152]{1,0:T(8,128)(2,1)S(1)}, u32[]{:S(2)}, u32[]{:S(2)}) collective-permute-start(bf16[96,1152]{1,0:T(8,128)(2,1)S(1)} %collective-permute-done.14.refs_5_.refs_1_), channel_id=1, source_target_pairs={{0,1},{1,0},{2,3},{3,2},{4,5},{5,4},{6,7},{7,6},{8,9},{9,8},{10,11... | collective-permute-start | bytes 663560 | tf_op jit(solution)/shard_map/ppermute | solution.py:36
  56.5 6.2 %collective-permute-start.23 = (bf16[256,384]{1,0:T(8,128)(2,1)S(1)}, bf16[256,384]{1,0:T(8,128)(2,1)S(1)}, u32[]{:S(2)}, u32[]{:S(2)}) collective-permute-start(bf16[256,384]{1,0:T(8,128)(2,1)S(1)} %shard_map.103.first_part), channel_id=1, source_target_pairs={{0,2},{1,3},{2,0},{3,1},{4,6},{5,7},{6,4},{7,5},{8,10},{9,11},{10,... | collective-permute-start | bytes 589832 | tf_op jit(solution)/shard_map/ppermute | solution.py:36
  57.5 5.8 %collective-permute-start.22 = (bf16[256,384]{1,0:T(8,128)(2,1)S(1)}, bf16[256,384]{1,0:T(8,128)(2,1)S(1)}, u32[]{:S(2)}, u32[]{:S(2)}) collective-permute-start(bf16[256,384]{1,0:T(8,128)(2,1)S(1)} %shard_map.103.first_part), channel_id=1, source_target_pairs={{0,4},{1,5},{2,6},{3,7},{4,0},{5,1},{6,2},{7,3},{8,12},{9,13},{10,... | collective-permute-start | bytes 589832 | tf_op jit(solution)/shard_map/ppermute | solution.py:36
  57.5 10.3 %collective-permute-start.21 = (bf16[256,384]{1,0:T(8,128)(2,1)S(1)}, bf16[256,384]{1,0:T(8,128)(2,1)S(1)}, u32[]{:S(2)}, u32[]{:S(2)}) collective-permute-start(bf16[256,384]{1,0:T(8,128)(2,1)S(1)} %shard_map.103.first_part), channel_id=1, source_target_pairs={{0,6},{1,7},{2,4},{3,5},{4,2},{5,3},{6,0},{7,1},{8,14},{9,15},{10,... | collective-permute-start | bytes 589832 | tf_op jit(solution)/shard_map/ppermute | solution.py:36
  71.8 7.2 %collective-permute-start.24 = (bf16[64,384]{1,0:T(8,128)(2,1)S(1)}, bf16[64,384]{1,0:T(8,128)(2,1)S(1)}, u32[]{:S(2)}, u32[]{:S(2)}) collective-permute-start(bf16[64,384]{1,0:T(8,128)(2,1)S(1)} %get-tuple-element.35), channel_id=1, source_target_pairs={{0,2},{1,4},{2,0},{3,6},{4,1},{5,7},{6,3},{7,5},{8,10},{9,12},{10,... | collective-permute-start | bytes 147464 | tf_op jit(solution)/shard_map/ppermute | solution.py:36
  73.2 5.8 %collective-permute-start.25 = (bf16[64,384]{1,0:T(8,128)(2,1)S(1)}, bf16[64,384]{1,0:T(8,128)(2,1)S(1)}, u32[]{:S(2)}, u32[]{:S(2)}) collective-permute-start(bf16[64,384]{1,0:T(8,128)(2,1)S(1)} %get-tuple-element.36), channel_id=1, source_target_pairs={{0,3},{1,5},{2,1},{3,7},{4,0},{5,6},{6,2},{7,4},{8,11},{9,13},{10,... | collective-permute-start | bytes 147464 | tf_op jit(solution)/shard_map/ppermute | solution.py:36
  73.2 5.8 %collective-permute-start.26 = (bf16[64,384]{1,0:T(8,128)(2,1)S(1)}, bf16[64,384]{1,0:T(8,128)(2,1)S(1)}, u32[]{:S(2)}, u32[]{:S(2)}) collective-permute-start(bf16[64,384]{1,0:T(8,128)(2,1)S(1)} %get-tuple-element.37), channel_id=1, source_target_pairs={{0,1},{1,7},{2,3},{3,5},{4,2},{5,4},{6,0},{7,6},{8,9},{9,15},{10,1... | collective-permute-start | bytes 147464 | tf_op jit(solution)/shard_map/ppermute | solution.py:36
  74.8 6.3 %collective-permute-start.27 = (bf16[64,384]{1,0:T(8,128)(2,1)S(1)}, bf16[64,384]{1,0:T(8,128)(2,1)S(1)}, u32[]{:S(2)}, u32[]{:S(2)}) collective-permute-start(bf16[64,384]{1,0:T(8,128)(2,1)S(1)} %get-tuple-element.38), channel_id=1, source_target_pairs={{1,6},{3,4},{4,3},{6,1},{9,14},{11,12},{12,11},{14,9},{17,22},{19,... | collective-permute-start | bytes 147464 | tf_op jit(solution)/shard_map/ppermute | solution.py:36

commit v8 on v7

--- a/solution.py
+++ b/solution.py
@@ -229,12 +229,17 @@
 
 
 def all_tokens(latent):
-    other = moved(latent, lambda x, p, y, c: (x, p, y, 1 - c) if c != p % 2 else None)
-    block = jnp.concatenate([latent, other])
-    near = moved(block, lambda x, p, y, c: (x, p, 1 - y, c) if c == p % 2 else None)
-    far = moved(block, lambda x, p, y, c: (x, p ^ 1, y, c) if c == p % 2 else None)
-    far_near = moved(far, lambda x, p, y, c: (x, p, 1 - y, c) if c != p % 2 else None)
-    return block, near, far, far_near
+    def to_home(array):
+        return moved(array, lambda x, p, y, c: (x, p, y, 1 - c) if c != p % 2 else None)
+
+    def from_home(array):
+        return moved(array, lambda x, p, y, c: (x, p, y, 1 - c) if c == p % 2 else None)
+
+    far = moved(latent, lambda x, p, y, c: (x, p ^ 1, y, c))
+    near = moved(latent, lambda x, p, y, c: (x, p, 1 - y, c))
+    far_near = moved(far, lambda x, p, y, c: (x, p, 1 - y, c))
+    home = (latent, near, to_home(latent), to_home(near))
+    return home + (far, far_near, from_home(far), from_home(far_near))
 
 
 def late_plane(devices):
@@ -271,25 +276,26 @@
 BLOCK = 32
 
 
-def prepare_kernel(extra_ref, block, near, far, far_near, extra, current, normed):
+def prepare_kernel(extra_ref, *refs):
+    token_refs, (extra, current, normed) = refs[:8], refs[8:]
     _, _, plane, y, c = here()
-    chip_rows = block.shape[0]
-    blocks = chip_rows // BLOCK
+    rows = token_refs[0].shape[0]
     extra[...] = extra_ref[...]
-
-    def fill(first, second):
-        @pl.loop(0, blocks)
+    bases = [at_y * 2 * rows + core * rows for core in (0, 1) for at_y in (y, 1 - y)]
+
+    def fill(refs):
+        @pl.loop(0, rows // BLOCK)
         def _(number):
-            for ref, base in ((first, y * chip_rows), (second, (1 - y) * chip_rows)):
+            for ref, base in zip(refs, bases):
                 tokens = ref[pl.ds(pl.multiple_of(number * BLOCK, BLOCK), BLOCK), :]
-                rows = pl.ds(pl.multiple_of(base + number * BLOCK, BLOCK), BLOCK)
-                current[rows, :] = tokens
+                spot = pl.ds(pl.multiple_of(base + number * BLOCK, BLOCK), BLOCK)
+                current[spot, :] = tokens
                 widened = tokens.astype(jnp.float32)
                 inverse = lax.rsqrt(jnp.mean(widened * widened, axis=-1, keepdims=True) + 1e-06)
-                store_normed(current, rows, inverse, extra, normed)
-
-    pl.when(plane % 2 == c)(lambda: fill(block, near))
-    pl.when(plane % 2 != c)(lambda: fill(far, far_near))
+                store_normed(current, spot, inverse, extra, normed)
+
+    pl.when(plane % 2 == c)(lambda: fill(token_refs[:4]))
+    pl.when(plane % 2 != c)(lambda: fill(token_refs[4:]))
 
 
 def project_kernel(places, *refs):
@@ -419,7 +425,7 @@
 
 
 def prepare(extra, tokens):
-    frame = jax.ShapeDtypeStruct((2 * tokens[0].shape[0], tokens[0].shape[1]), tokens[0].dtype)
+    frame = jax.ShapeDtypeStruct((4 * tokens[0].shape[0], tokens[0].shape[1]), tokens[0].dtype)
     return kernel_call(
         prepare_kernel,
         (jax.ShapeDtypeStruct(extra.shape, extra.dtype), frame, frame),

time: 82.1 us -> 85.5 us (1.041)
  waiting for transfers between devices: 28.7 us -> 36.3 us
  starting transfers between devices: 37.6 us -> 33.6 us
    ppermute x23 -> x26, waiting for transfers between devices: 18.8 us -> 29.8 us  [moved(): return lax.ppermute(array, AXES, pairs)]
    ppermute x23 -> x26, starting transfers between devices: 33.4 us -> 29.7 us  [moved(): return lax.ppermute(array, AXES, pairs)]
    ppermute x5, waiting for transfers between devices: 9.9 us -> 6.55 us  [hop(): lax.ppermute(array, 'frame', [(i, i ^ bits) for i in range(lax.axis_size(...]
  transfers between devices with their start and end apart: 28 -> 31, of which waited for: 8 -> 8; matrix products, arithmetic and copies ran while one was open for 4% -> 2% of each run, Pallas kernels for 7% -> 2%
where the time goes in v8:
time: 85.5 us; the launch traced here: 85.1 us
  waiting for transfers between devices  36.3 us (42%)
  starting transfers between devices  33.6 us (39%)
  Pallas kernels  12.2 us (14%)
  other arithmetic  1.73 us (2%)
  local copies, waits for them, and re-layouts  0.95 us (1%)
    ppermute x26, waiting for transfers between devices, moved(): return lax.ppermute(array, AXES, pairs)  29.8 us
    ppermute x26, starting transfers between devices, moved(): return lax.ppermute(array, AXES, pairs)  29.7 us
    pallas_call x6, Pallas kernels, kernel_call(): pl.pallas_call(kernel, out_shape=out_shape, in_specs=[free if number in a...  8.88 us
    ppermute x5, waiting for transfers between devices, hop(): lax.ppermute(array, 'frame', [(i, i ^ bits) for i in range(lax.axis_size(...  6.55 us
    ppermute x5, starting transfers between devices, hop(): lax.ppermute(array, 'frame', [(i, i ^ bits) for i in range(lax.axis_size(...  3.92 us
    pallas_call x1, Pallas kernels, pack(): pl.pallas_call(pack_kernel, out_shape=out_shape, in_specs=[held] * 9, out...  3.33 us
  transfers between devices with their start and end apart: 31, of which 8 were waited for; matrix products, arithmetic and copies ran while one was open for 2% of the time, Pallas kernels for 2%

profile of v8, /device:TPU:1, one launch (start us, length us, event | category | flops | bytes accessed | tf_op | source)
XLA Modules:
  0.0 85.1 jit_solution(5553967603196189878)
XLA Ops:
  0.0 3.3 %pack.1 = (bf16[96,1152]{1,0:T(8,128)(2,1)}, bf16[96,1152]{1,0:T(8,128)(2,1)}, bf16[96,1152]{1,0:T(8,128)(2,1)}, bf16[96,1152]{1,0:T(8,128)(2,1)}, f32[4,1536]{1...) custom-call(bf16[96,1536]{1,0:T(8,128)(2,1)} %w_query.1, ...), custom_call_target="tpu_custom_call" | custom-call | tf_op jit(solution)/shard_map/pack/pallas_call | solution.py:164
  3.4 0.1 collective-permute-start.7
  3.4 2.7 %collective-permute-start.8 = (bf16[4,8,2,384]{3,2,1,0:T(2,128)(2,1)}, bf16[4,8,2,384]{3,2,1,0:T(2,128)(2,1)S(1)}, u32[]{:S(2)}, u32[]{:S(2)}) collective-permute-start(bf16[4,8,2,384]{3,2,1,0:T(2,128)(2,1)} %get-tuple-element.26), channel_id=1, source_target_pairs={{0,2},{1,3},{2,0},{3,1},{4,6},{5,7},{6,4},{7,5},{8,10},{9,11},{10,... | collective-permute-start | bytes 147464 | tf_op jit(solution)/shard_map/ppermute | solution.py:228
  6.2 0.0 collective-permute-start.9
  6.2 2.3 %collective-permute-start.1 = (bf16[64,1536]{1,0:T(8,128)(2,1)}, bf16[64,1536]{1,0:T(8,128)(2,1)S(1)}, u32[]{:S(2)}, u32[]{:S(2)}) collective-permute-start(bf16[64,1536]{1,0:T(8,128)(2,1)} %refs_0_.1), channel_id=1, source_target_pairs={{1,0},{3,2},{4,5},{6,7},{9,8},{11,10},{12,13},{14,15},{17,16},{19,... | collective-permute-start | bytes 589832 | tf_op jit(solution)/shard_map/ppermute | solution.py:36
  8.5 3.6 %collective-permute-start.14 = (bf16[96,1152]{1,0:T(8,128)(2,1)}, bf16[96,1152]{1,0:T(8,128)(2,1)S(1)}, u32[]{:S(2)}, u32[]{:S(2)}) collective-permute-start(bf16[96,1152]{1,0:T(8,128)(2,1)} %get-tuple-element.32), channel_id=1, source_target_pairs={{0,8},{1,11},{2,10},{3,9},{4,12},{5,15},{6,14},{7,13},{8,0},{9,3},... | collective-permute-start | bytes 663560 | tf_op jit(solution)/shard_map/ppermute | solution.py:36
  12.0 0.5 collective-permute-start.13
  12.5 1.1 %pad_maximum_fusion.1 = bf16[4,4,8,2,384]{4,3,2,1,0:T(2,128)(2,1)S(1)} fusion(bf16[1,4,8,2,384]{4,3,2,1,0:T(2,128)(2,1)S(1)} %bitcast.11, bf16[1,4,8,2,384]{4,3,2,1,0:T(2,128)(2,1)S(1)} %bitcast.10, bf16[1,4,8,2,384]{4,3,2,1,0:T(2,128)(2,1)S(1)} %bitcast.9, bf16[1,4,8,2,384]{4,3,2,1,0:T(2,128)(2,1)} %bitcast.8), kind=kLoop, calls=%fused_computation.2 | loop fusion | flops 294912 | bytes 393216 | tf_op jit(solution)/shard_map/stack | solution.py:218
  13.6 0.1 fusion.1
  13.8 1.0 %collective-permute-start.10 = (bf16[4,2,8,2,384]{4,3,2,1,0:T(2,128)(2,1)S(1)}, bf16[4,2,8,2,384]{4,3,2,1,0:T(2,128)(2,1)S(1)}, u32[]{:S(2)}, u32[]{:S(2)}) collective-permute-start(bf16[4,2,8,2,384]{4,3,2,1,0:T(2,128)(2,1)S(1)} %get-tuple-element.44), channel_id=1, source_target_pairs={{0,4},{1,5},{2,6},{3,7},{4,0},{5,1},{6,2},{7,3},{8,12},{9,13},{10,... | collective-permute-start | bytes 294920 | tf_op jit(solution)/shard_map/ppermute | solution.py:228
  14.8 9.8 %collective-permute-done.13 = bf16[96,1152]{1,0:T(8,128)(2,1)S(1)} collective-permute-done((bf16[96,1152]{1,0:T(8,128)(2,1)}, bf16[96,1152]{1,0:T(8,128)(2,1)S(1)}, u32[]{:S(2)}, u32[]{:S(2)}) %collective-permute-start.13) | collective-permute-done | bytes 221216 | tf_op jit(solution)/shard_map/ppermute | solution.py:36
  24.6 0.1 collective-permute-start.15
  24.7 0.1 collective-permute-start.12
  24.8 1.5 %collective-permute-start = (bf16[64,1536]{1,0:T(8,128)(2,1)}, bf16[64,1536]{1,0:T(8,128)(2,1)S(1)}, u32[]{:S(2)}, u32[]{:S(2)}) collective-permute-start(bf16[64,1536]{1,0:T(8,128)(2,1)} %refs_0_.1), channel_id=1, source_target_pairs={{0,2},{1,3},{2,0},{3,1},{4,6},{5,7},{6,4},{7,5},{8,10},{9,11},{10,... | collective-permute-start | bytes 589832 | tf_op jit(solution)/shard_map/ppermute | solution.py:36
  26.3 1.6 %collective-permute-start.16 = (bf16[96,1152]{1,0:T(8,128)(2,1)}, bf16[96,1152]{1,0:T(8,128)(2,1)S(1)}, u32[]{:S(2)}, u32[]{:S(2)}) collective-permute-start(bf16[96,1152]{1,0:T(8,128)(2,1)} %get-tuple-element.31), channel_id=1, source_target_pairs={{0,12},{1,15},{2,14},{3,13},{4,8},{5,11},{6,10},{7,9},{8,4},{9,7},... | collective-permute-start | bytes 663560 | tf_op jit(solution)/shard_map/ppermute | solution.py:36
  27.9 8.2 %collective-permute-done.refs_1_ = bf16[64,1536]{1,0:T(8,128)(2,1)S(1)} collective-permute-done((bf16[64,1536]{1,0:T(8,128)(2,1)}, bf16[64,1536]{1,0:T(8,128)(2,1)S(1)}, u32[]{:S(2)}, u32[]{:S(2)}) %collective-permute-start) | collective-permute-done | bytes 196640 | tf_op jit(solution)/shard_map/ppermute | solution.py:36
  36.1 3.3 %collective-permute-start.18 = (bf16[96,1152]{1,0:T(8,128)(2,1)}, bf16[96,1152]{1,0:T(8,128)(2,1)S(1)}, u32[]{:S(2)}, u32[]{:S(2)}) collective-permute-start(bf16[96,1152]{1,0:T(8,128)(2,1)} %get-tuple-element.29.refs_0_.refs_1_), channel_id=1, source_target_pairs={{0,1},{1,0},{2,3},{3,2},{4,5},{5,4},{6,7},{7,6},{8,9},{9,8},{10,11... | collective-permute-start | bytes 663560 | tf_op jit(solution)/shard_map/ppermute | solution.py:36
  39.4 1.9 %collective-permute-start.2 = (bf16[64,1536]{1,0:T(8,128)(2,1)S(1)}, bf16[64,1536]{1,0:T(8,128)(2,1)S(1)}, u32[]{:S(2)}, u32[]{:S(2)}) collective-permute-start(bf16[64,1536]{1,0:T(8,128)(2,1)S(1)} %collective-permute-done.refs_1_), channel_id=1, source_target_pairs={{1,0},{3,2},{4,5},{6,7},{9,8},{11,10},{12,13},{14,15},{17,16},{19,... | collective-permute-start | bytes 589832 | tf_op jit(solution)/shard_map/ppermute | solution.py:36
  41.3 0.4 collective-permute-start.4
  41.7 0.3 fusion
  42.0 0.1 collective-permute-start.11
  42.1 1.1 %collective-permute-start.17 = (bf16[96,1152]{1,0:T(8,128)(2,1)S(1)}, bf16[96,1152]{1,0:T(8,128)(2,1)S(1)}, u32[]{:S(2)}, u32[]{:S(2)}) collective-permute-start(bf16[96,1152]{1,0:T(8,128)(2,1)S(1)} %collective-permute-done.16.refs_4_.refs_0_), channel_id=1, source_target_pairs={{0,16},{1,17},{2,18},{3,19},{4,20},{5,21},{6,22},{7,23},{8,24},{9,... | collective-permute-start | bytes 663560 | tf_op jit(solution)/shard_map/ppermute | solution.py:36
  43.2 6.5 %collective-permute-done.11 = bf16[8,1,8,2,384]{4,3,2,1,0:T(2,128)(2,1)S(1)} collective-permute-done((bf16[8,1,8,2,384]{4,3,2,1,0:T(2,128)(2,1)S(1)}, bf16[8,1,8,2,384]{4,3,2,1,0:T(2,128)(2,1)S(1)}, u32[]{:S(2)}, u32[]{:S(2)}) %collective-permute-start.11) | collective-permute-done | bytes 98336 | tf_op jit(solution)/shard_map/ppermute | solution.py:228
  49.8 0.5 collective-permute-start.20
  50.3 0.0 collective-permute-start.21
  50.3 1.3 %collective-permute-start.5 = (bf16[64,1536]{1,0:T(8,128)(2,1)S(1)}, bf16[64,1536]{1,0:T(8,128)(2,1)S(1)}, u32[]{:S(2)}, u32[]{:S(2)}) collective-permute-start(bf16[64,1536]{1,0:T(8,128)(2,1)S(1)} %collective-permute-done.3.refs_4_), channel_id=1, source_target_pairs={{0,1},{2,3},{5,4},{7,6},{8,9},{10,11},{13,12},{15,14},{16,17},{18,... | collective-permute-start | bytes 589832 | tf_op jit(solution)/shard_map/ppermute | solution.py:36
  51.6 1.3 %collective-permute-start.6 = (bf16[64,1536]{1,0:T(8,128)(2,1)S(1)}, bf16[64,1536]{1,0:T(8,128)(2,1)S(1)}, u32[]{:S(2)}, u32[]{:S(2)}) collective-permute-start(bf16[64,1536]{1,0:T(8,128)(2,1)S(1)} %collective-permute-done.4.refs_5_), channel_id=1, source_target_pairs={{0,1},{2,3},{5,4},{7,6},{8,9},{10,11},{13,12},{15,14},{16,17},{18,... | collective-permute-start | bytes 589832 | tf_op jit(solution)/shard_map/ppermute | solution.py:36
  52.9 0.3 pad_maximum_fusion
  53.2 0.4 collective-permute-done.5.refs_6_
  53.6 0.8 collective-permute-start.22
  54.5 0.1 collective-permute-start.19
  54.6 0.4 collective-permute-done.6.refs_7_
  55.0 0.1 collective-permute-start.23
  55.2 0.7 copy-done.2
  55.9 0.5 shard_map.100
  56.4 1.2 %shard_map.102.part_ref = f32[256,1152]{1,0:T(8,128)S(1)} custom-call(bf16[256,1536]{1,0:T(8,128)(2,1)S(1)} %get-tuple-element.33.refs_0_.normed, bf16[96,1152]{1,0:T(8,128)(2,1)S(1)} %copy-done, bf16[96,1152]{1,0:T(8,128)(2,1)S(1)} %collective-permute-done.12.refs_1_.refs_2_, bf16[192,1152]{1,0:T(8,128)(2,1)S(1)} %constant_dynamic-update-slice_fusion.refs_2_.refs_3_, ...), custom_call_target="tpu_custom_call" | custom-call | flops 679477248 | bytes 3440640 | tf_op jit(solution)/shard_map/pallas_call | solution.py:416
  57.6 2.2 %shard_map.103.first_part = bf16[256,384]{1,0:T(8,128)(2,1)S(1)} custom-call(f32[4,1536]{1,0:T(4,128)S(1)} %get-tuple-element.23.extra_ref, bf16[128,384]{1,0:T(8,128)(2,1)S(1)} %get-tuple-element.46.key_ref, bf16[128,384]{1,0:T(8,128)(2,1)S(1)} %get-tuple-element.45.value_ref, bf16[256,1536]{1,0:T(8,128)(2,1)S(1)} %get-tuple-element.33.refs_0_.normed, ...), custom_call_target="tpu_custom_call" | custom-call | flops 377487360 | bytes 3072000 | tf_op jit(solution)/shard_map/pallas_call | solution.py:416
  59.8 0.1 collective-permute-start.26
  60.0 2.6 %collective-permute-start.24 = (bf16[256,384]{1,0:T(8,128)(2,1)S(1)}, bf16[256,384]{1,0:T(8,128)(2,1)S(1)}, u32[]{:S(2)}, u32[]{:S(2)}) collective-permute-start(bf16[256,384]{1,0:T(8,128)(2,1)S(1)} %shard_map.103.first_part), channel_id=1, source_target_pairs={{0,6},{1,7},{2,4},{3,5},{4,2},{5,3},{6,0},{7,1},{8,14},{9,15},{10,... | collective-permute-start | bytes 589832 | tf_op jit(solution)/shard_map/ppermute | solution.py:36
  62.5 0.3 shard_map.101.weights
  62.8 3.1 %collective-permute-done.26.fourth_part = bf16[256,384]{1,0:T(8,128)(2,1)S(1)} collective-permute-done((bf16[256,384]{1,0:T(8,128)(2,1)S(1)}, bf16[256,384]{1,0:T(8,128)(2,1)S(1)}, u32[]{:S(2)}, u32[]{:S(2)}) %collective-permute-start.26) | collective-permute-done | bytes 196640 | tf_op jit(solution)/shard_map/ppermute | solution.py:36
  66.0 5.1 %collective-permute-done.24.second_part = bf16[256,384]{1,0:T(8,128)(2,1)S(1)} collective-permute-done((bf16[256,384]{1,0:T(8,128)(2,1)S(1)}, bf16[256,384]{1,0:T(8,128)(2,1)S(1)}, u32[]{:S(2)}, u32[]{:S(2)}) %collective-permute-start.24) | collective-permute-done | bytes 196640 | tf_op jit(solution)/shard_map/ppermute | solution.py:36
  71.1 4.0 %shard_map.104 = (bf16[64,384]{1,0:T(8,128)(2,1)S(1)}, bf16[64,384]{1,0:T(8,128)(2,1)S(1)}, bf16[64,384]{1,0:T(8,128)(2,1)S(1)}, bf16[64,384]{1,0:T(8,128)(2,1)S(1)}, bf16[64,384]{1,0:T(8,128)(2,1)S(1)}) custom-call(f32[4,1536]{1,0:T(4,128)S(1)} %get-tuple-element.23.extra_ref, bf16[128,384]{1,0:T(8,128)(2,1)S(1)} %get-tuple-element.46.key_ref, ...), custom_call_target="tpu_custom_call" | custom-call | flops 1056964608 | bytes 5332992 | tf_op jit(solution)/shard_map/pallas_call | solution.py:416
  75.1 1.5 %collective-permute-start.27 = (bf16[64,384]{1,0:T(8,128)(2,1)S(1)}, bf16[64,384]{1,0:T(8,128)(2,1)S(1)}, u32[]{:S(2)}, u32[]{:S(2)}) collective-permute-start(bf16[64,384]{1,0:T(8,128)(2,1)S(1)} %get-tuple-element.35), channel_id=1, source_target_pairs={{0,2},{1,4},{2,0},{3,6},{4,1},{5,7},{6,3},{7,5},{8,10},{9,12},{10,... | collective-permute-start | bytes 147464 | tf_op jit(solution)/shard_map/ppermute | solution.py:36
  76.6 1.5 %collective-permute-start.29 = (bf16[64,384]{1,0:T(8,128)(2,1)S(1)}, bf16[64,384]{1,0:T(8,128)(2,1)S(1)}, u32[]{:S(2)}, u32[]{:S(2)}) collective-permute-start(bf16[64,384]{1,0:T(8,128)(2,1)S(1)} %get-tuple-element.37), channel_id=1, source_target_pairs={{0,1},{1,7},{2,3},{3,5},{4,2},{5,4},{6,0},{7,6},{8,9},{9,15},{10,1... | collective-permute-start | bytes 147464 | tf_op jit(solution)/shard_map/ppermute | solution.py:36
  78.1 3.6 %collective-permute-start.30 = (bf16[64,384]{1,0:T(8,128)(2,1)S(1)}, bf16[64,384]{1,0:T(8,128)(2,1)S(1)}, u32[]{:S(2)}, u32[]{:S(2)}) collective-permute-start(bf16[64,384]{1,0:T(8,128)(2,1)S(1)} %get-tuple-element.38), channel_id=1, source_target_pairs={{1,6},{3,4},{4,3},{6,1},{9,14},{11,12},{12,11},{14,9},{17,22},{19,... | collective-permute-start | bytes 147464 | tf_op jit(solution)/shard_map/ppermute | solution.py:36
  81.7 2.7 %collective-permute-done.30.fourth = bf16[64,384]{1,0:T(8,128)(2,1)S(1)} collective-permute-done((bf16[64,384]{1,0:T(8,128)(2,1)S(1)}, bf16[64,384]{1,0:T(8,128)(2,1)S(1)}, u32[]{:S(2)}, u32[]{:S(2)}) %collective-permute-start.30) | collective-permute-done | bytes 49184 | tf_op jit(solution)/shard_map/ppermute | solution.py:36
  84.4 0.7 shard_map.105
  (34 shorter events, 0.2 us)
Async XLA Ops:
  0.0 55.1 %copy-start.1 = (bf16[64,1536]{1,0:T(8,128)(2,1)S(1)}, bf16[64,1536]{1,0:T(8,128)(2,1)}, u32[]{:S(2)}) copy-start(bf16[64,1536]{1,0:T(8,128)(2,1)} %refs_0_.1) | copy-start | bytes 589828
  3.3 53.0 %copy-start = (bf16[96,1152]{1,0:T(8,128)(2,1)S(1)}, bf16[96,1152]{1,0:T(8,128)(2,1)}, u32[]{:S(2)}) copy-start(bf16[96,1152]{1,0:T(8,128)(2,1)} %get-tuple-element.29.refs_0_.refs_1_) | copy-start | bytes 663556
  3.4 8.7 %collective-permute-start.7 = (bf16[4,8,2,384]{3,2,1,0:T(2,128)(2,1)}, bf16[4,8,2,384]{3,2,1,0:T(2,128)(2,1)S(1)}, u32[]{:S(2)}, u32[]{:S(2)}) collective-permute-start(bf16[4,8,2,384]{3,2,1,0:T(2,128)(2,1)} %get-tuple-element.25), channel_id=1, source_target_pairs={{0,1},{1,0},{2,3},{3,2},{4,5},{5,4},{6,7},{7,6},{8,9},{9,8},{10,11... | collective-permute-start | bytes 147464 | tf_op jit(solution)/shard_map/ppermute | solution.py:228
  3.4 9.1 %collective-permute-start.8 = (bf16[4,8,2,384]{3,2,1,0:T(2,128)(2,1)}, bf16[4,8,2,384]{3,2,1,0:T(2,128)(2,1)S(1)}, u32[]{:S(2)}, u32[]{:S(2)}) collective-permute-start(bf16[4,8,2,384]{3,2,1,0:T(2,128)(2,1)} %get-tuple-element.26), channel_id=1, source_target_pairs={{0,2},{1,3},{2,0},{3,1},{4,6},{5,7},{6,4},{7,5},{8,10},{9,11},{10,... | collective-permute-start | bytes 147464 | tf_op jit(solution)/shard_map/ppermute | solution.py:228
  6.2 6.3 %collective-permute-start.9 = (bf16[4,8,2,384]{3,2,1,0:T(2,128)(2,1)}, bf16[4,8,2,384]{3,2,1,0:T(2,128)(2,1)S(1)}, u32[]{:S(2)}, u32[]{:S(2)}) collective-permute-start(bf16[4,8,2,384]{3,2,1,0:T(2,128)(2,1)} %get-tuple-element.27), channel_id=1, source_target_pairs={{0,3},{1,2},{2,1},{3,0},{4,7},{5,6},{6,5},{7,4},{8,11},{9,10},{10,... | collective-permute-start | bytes 147464 | tf_op jit(solution)/shard_map/ppermute | solution.py:228
  6.2 20.1 %collective-permute-start.1 = (bf16[64,1536]{1,0:T(8,128)(2,1)}, bf16[64,1536]{1,0:T(8,128)(2,1)S(1)}, u32[]{:S(2)}, u32[]{:S(2)}) collective-permute-start(bf16[64,1536]{1,0:T(8,128)(2,1)} %refs_0_.1), channel_id=1, source_target_pairs={{1,0},{3,2},{4,5},{6,7},{9,8},{11,10},{12,13},{14,15},{17,16},{19,... | collective-permute-start | bytes 589832 | tf_op jit(solution)/shard_map/ppermute | solution.py:36
  8.5 16.1 %collective-permute-start.14 = (bf16[96,1152]{1,0:T(8,128)(2,1)}, bf16[96,1152]{1,0:T(8,128)(2,1)S(1)}, u32[]{:S(2)}, u32[]{:S(2)}) collective-permute-start(bf16[96,1152]{1,0:T(8,128)(2,1)} %get-tuple-element.32), channel_id=1, source_target_pairs={{0,8},{1,11},{2,10},{3,9},{4,12},{5,15},{6,14},{7,13},{8,0},{9,3},... | collective-permute-start | bytes 663560 | tf_op jit(solution)/shard_map/ppermute | solution.py:36
  12.0 12.5 %collective-permute-start.13 = (bf16[96,1152]{1,0:T(8,128)(2,1)}, bf16[96,1152]{1,0:T(8,128)(2,1)S(1)}, u32[]{:S(2)}, u32[]{:S(2)}) collective-permute-start(bf16[96,1152]{1,0:T(8,128)(2,1)} %get-tuple-element.31), channel_id=1, source_target_pairs={{0,4},{1,7},{2,6},{3,5},{4,0},{5,3},{6,2},{7,1},{8,12},{9,15},{10,... | collective-permute-start | bytes 663560 | tf_op jit(solution)/shard_map/ppermute | solution.py:36
  13.8 12.5 %collective-permute-start.10 = (bf16[4,2,8,2,384]{4,3,2,1,0:T(2,128)(2,1)S(1)}, bf16[4,2,8,2,384]{4,3,2,1,0:T(2,128)(2,1)S(1)}, u32[]{:S(2)}, u32[]{:S(2)}) collective-permute-start(bf16[4,2,8,2,384]{4,3,2,1,0:T(2,128)(2,1)S(1)} %get-tuple-element.44), channel_id=1, source_target_pairs={{0,4},{1,5},{2,6},{3,7},{4,0},{5,1},{6,2},{7,3},{8,12},{9,13},{10,... | collective-permute-start | bytes 294920 | tf_op jit(solution)/shard_map/ppermute | solution.py:228
  24.6 25.7 %collective-permute-start.15 = (bf16[192,1152]{1,0:T(8,128)(2,1)S(1)}, bf16[192,1152]{1,0:T(8,128)(2,1)S(1)}, u32[]{:S(2)}, u32[]{:S(2)}) collective-permute-start(bf16[192,1152]{1,0:T(8,128)(2,1)S(1)} %constant_dynamic-update-slice_fusion.refs_2_.refs_3_), channel_id=1, source_target_pairs={{0,16},{1,17},{2,18},{3,19},{4,20},{5,21},{6,22},{7,23},{8,24},{9,... | collective-permute-start | bytes 1327112 | tf_op jit(solution)/shard_map/ppermute | solution.py:36
  24.7 16.6 %collective-permute-start.12 = (bf16[96,1152]{1,0:T(8,128)(2,1)}, bf16[96,1152]{1,0:T(8,128)(2,1)S(1)}, u32[]{:S(2)}, u32[]{:S(2)}) collective-permute-start(bf16[96,1152]{1,0:T(8,128)(2,1)} %get-tuple-element.30), channel_id=1, source_target_pairs={{0,2},{1,3},{2,0},{3,1},{4,6},{5,7},{6,4},{7,5},{8,10},{9,11},{10,... | collective-permute-start | bytes 663560 | tf_op jit(solution)/shard_map/ppermute | solution.py:36
  24.8 11.3 %collective-permute-start = (bf16[64,1536]{1,0:T(8,128)(2,1)}, bf16[64,1536]{1,0:T(8,128)(2,1)S(1)}, u32[]{:S(2)}, u32[]{:S(2)}) collective-permute-start(bf16[64,1536]{1,0:T(8,128)(2,1)} %refs_0_.1), channel_id=1, source_target_pairs={{0,2},{1,3},{2,0},{3,1},{4,6},{5,7},{6,4},{7,5},{8,10},{9,11},{10,... | collective-permute-start | bytes 589832 | tf_op jit(solution)/shard_map/ppermute | solution.py:36
  26.2 13.2 %collective-permute-start.3 = (bf16[64,1536]{1,0:T(8,128)(2,1)}, bf16[64,1536]{1,0:T(8,128)(2,1)S(1)}, u32[]{:S(2)}, u32[]{:S(2)}) collective-permute-start(bf16[64,1536]{1,0:T(8,128)(2,1)} %refs_0_.1), channel_id=1, source_target_pairs={{0,4},{1,5},{2,6},{3,7},{4,0},{5,1},{6,2},{7,3},{8,12},{9,13},{10,... | collective-permute-start | bytes 589832 | tf_op jit(solution)/shard_map/ppermute | solution.py:36
  26.3 15.7 %collective-permute-start.16 = (bf16[96,1152]{1,0:T(8,128)(2,1)}, bf16[96,1152]{1,0:T(8,128)(2,1)S(1)}, u32[]{:S(2)}, u32[]{:S(2)}) collective-permute-start(bf16[96,1152]{1,0:T(8,128)(2,1)} %get-tuple-element.31), channel_id=1, source_target_pairs={{0,12},{1,15},{2,14},{3,13},{4,8},{5,11},{6,10},{7,9},{8,4},{9,7},... | collective-permute-start | bytes 663560 | tf_op jit(solution)/shard_map/ppermute | solution.py:36
  36.1 6.0 %collective-permute-start.18 = (bf16[96,1152]{1,0:T(8,128)(2,1)}, bf16[96,1152]{1,0:T(8,128)(2,1)S(1)}, u32[]{:S(2)}, u32[]{:S(2)}) collective-permute-start(bf16[96,1152]{1,0:T(8,128)(2,1)} %get-tuple-element.29.refs_0_.refs_1_), channel_id=1, source_target_pairs={{0,1},{1,0},{2,3},{3,2},{4,5},{5,4},{6,7},{7,6},{8,9},{9,8},{10,11... | collective-permute-start | bytes 663560 | tf_op jit(solution)/shard_map/ppermute | solution.py:36
  39.4 10.9 %collective-permute-start.2 = (bf16[64,1536]{1,0:T(8,128)(2,1)S(1)}, bf16[64,1536]{1,0:T(8,128)(2,1)S(1)}, u32[]{:S(2)}, u32[]{:S(2)}) collective-permute-start(bf16[64,1536]{1,0:T(8,128)(2,1)S(1)} %collective-permute-done.refs_1_), channel_id=1, source_target_pairs={{1,0},{3,2},{4,5},{6,7},{9,8},{11,10},{12,13},{14,15},{17,16},{19,... | collective-permute-start | bytes 589832 | tf_op jit(solution)/shard_map/ppermute | solution.py:36
  41.3 10.3 %collective-permute-start.4 = (bf16[64,1536]{1,0:T(8,128)(2,1)S(1)}, bf16[64,1536]{1,0:T(8,128)(2,1)S(1)}, u32[]{:S(2)}, u32[]{:S(2)}) collective-permute-start(bf16[64,1536]{1,0:T(8,128)(2,1)S(1)} %collective-permute-done.3.refs_4_), channel_id=1, source_target_pairs={{0,2},{1,3},{2,0},{3,1},{4,6},{5,7},{6,4},{7,5},{8,10},{9,11},{10,... | collective-permute-start | bytes 589832 | tf_op jit(solution)/shard_map/ppermute | solution.py:36
  42.0 7.8 %collective-permute-start.11 = (bf16[8,1,8,2,384]{4,3,2,1,0:T(2,128)(2,1)S(1)}, bf16[8,1,8,2,384]{4,3,2,1,0:T(2,128)(2,1)S(1)}, u32[]{:S(2)}, u32[]{:S(2)}) collective-permute-start(bf16[8,1,8,2,384]{4,3,2,1,0:T(2,128)(2,1)S(1)} %get-tuple-element.42), channel_id=1, source_target_pairs={{0,8},{1,9},{2,10},{3,11},{4,12},{5,13},{6,14},{7,15},{8,0},{9,1},... | collective-permute-start | bytes 294920 | tf_op jit(solution)/shard_map/ppermute | solution.py:228
  42.1 12.4 %collective-permute-start.17 = (bf16[96,1152]{1,0:T(8,128)(2,1)S(1)}, bf16[96,1152]{1,0:T(8,128)(2,1)S(1)}, u32[]{:S(2)}, u32[]{:S(2)}) collective-permute-start(bf16[96,1152]{1,0:T(8,128)(2,1)S(1)} %collective-permute-done.16.refs_4_.refs_0_), channel_id=1, source_target_pairs={{0,16},{1,17},{2,18},{3,19},{4,20},{5,21},{6,22},{7,23},{8,24},{9,... | collective-permute-start | bytes 663560 | tf_op jit(solution)/shard_map/ppermute | solution.py:36
  49.8 6.6 %collective-permute-start.20 = (bf16[192,1152]{1,0:T(8,128)(2,1)S(1)}, bf16[192,1152]{1,0:T(8,128)(2,1)S(1)}, u32[]{:S(2)}, u32[]{:S(2)}) collective-permute-start(bf16[192,1152]{1,0:T(8,128)(2,1)S(1)} %constant_dynamic-update-slice_fusion.refs_2_.refs_3_), channel_id=1, source_target_pairs={{0,1},{1,0},{2,3},{3,2},{4,5},{5,4},{6,7},{7,6},{8,9},{9,8},{10,11... | collective-permute-start | bytes 1327112 | tf_op jit(solution)/shard_map/ppermute | solution.py:36
  50.3 6.1 %collective-permute-start.21 = (bf16[192,1152]{1,0:T(8,128)(2,1)S(1)}, bf16[192,1152]{1,0:T(8,128)(2,1)S(1)}, u32[]{:S(2)}, u32[]{:S(2)}) collective-permute-start(bf16[192,1152]{1,0:T(8,128)(2,1)S(1)} %collective-permute-done.15.refs_3_.refs_4_), channel_id=1, source_target_pairs={{0,1},{1,0},{2,3},{3,2},{4,5},{5,4},{6,7},{7,6},{8,9},{9,8},{10,11... | collective-permute-start | bytes 1327112 | tf_op jit(solution)/shard_map/ppermute | solution.py:36
  50.3 3.3 %collective-permute-start.5 = (bf16[64,1536]{1,0:T(8,128)(2,1)S(1)}, bf16[64,1536]{1,0:T(8,128)(2,1)S(1)}, u32[]{:S(2)}, u32[]{:S(2)}) collective-permute-start(bf16[64,1536]{1,0:T(8,128)(2,1)S(1)} %collective-permute-done.3.refs_4_), channel_id=1, source_target_pairs={{0,1},{2,3},{5,4},{7,6},{8,9},{10,11},{13,12},{15,14},{16,17},{18,... | collective-permute-start | bytes 589832 | tf_op jit(solution)/shard_map/ppermute | solution.py:36
  51.6 3.3 %collective-permute-start.6 = (bf16[64,1536]{1,0:T(8,128)(2,1)S(1)}, bf16[64,1536]{1,0:T(8,128)(2,1)S(1)}, u32[]{:S(2)}, u32[]{:S(2)}) collective-permute-start(bf16[64,1536]{1,0:T(8,128)(2,1)S(1)} %collective-permute-done.4.refs_5_), channel_id=1, source_target_pairs={{0,1},{2,3},{5,4},{7,6},{8,9},{10,11},{13,12},{15,14},{16,17},{18,... | collective-permute-start | bytes 589832 | tf_op jit(solution)/shard_map/ppermute | solution.py:36
  53.6 4.0 %collective-permute-start.22 = (bf16[96,1152]{1,0:T(8,128)(2,1)S(1)}, bf16[96,1152]{1,0:T(8,128)(2,1)S(1)}, u32[]{:S(2)}, u32[]{:S(2)}) collective-permute-start(bf16[96,1152]{1,0:T(8,128)(2,1)S(1)} %collective-permute-done.16.refs_4_.refs_0_), channel_id=1, source_target_pairs={{0,1},{1,0},{2,3},{3,2},{4,5},{5,4},{6,7},{7,6},{8,9},{9,8},{10,11... | collective-permute-start | bytes 663560 | tf_op jit(solution)/shard_map/ppermute | solution.py:36
  54.5 1.9 %collective-permute-start.19 = (bf16[96,1152]{1,0:T(8,128)(2,1)S(1)}, bf16[96,1152]{1,0:T(8,128)(2,1)S(1)}, u32[]{:S(2)}, u32[]{:S(2)}) collective-permute-start(bf16[96,1152]{1,0:T(8,128)(2,1)S(1)} %collective-permute-done.12.refs_1_.refs_2_), channel_id=1, source_target_pairs={{0,1},{1,0},{2,3},{3,2},{4,5},{5,4},{6,7},{7,6},{8,9},{9,8},{10,11... | collective-permute-start | bytes 663560 | tf_op jit(solution)/shard_map/ppermute | solution.py:36
  55.0 2.7 %collective-permute-start.23 = (bf16[96,1152]{1,0:T(8,128)(2,1)S(1)}, bf16[96,1152]{1,0:T(8,128)(2,1)S(1)}, u32[]{:S(2)}, u32[]{:S(2)}) collective-permute-start(bf16[96,1152]{1,0:T(8,128)(2,1)S(1)} %collective-permute-done.17.refs_5_.refs_1_), channel_id=1, source_target_pairs={{0,1},{1,0},{2,3},{3,2},{4,5},{5,4},{6,7},{7,6},{8,9},{9,8},{10,11... | collective-permute-start | bytes 663560 | tf_op jit(solution)/shard_map/ppermute | solution.py:36
  55.1 0.7 copy-start.2
  59.8 6.2 %collective-permute-start.26 = (bf16[256,384]{1,0:T(8,128)(2,1)S(1)}, bf16[256,384]{1,0:T(8,128)(2,1)S(1)}, u32[]{:S(2)}, u32[]{:S(2)}) collective-permute-start(bf16[256,384]{1,0:T(8,128)(2,1)S(1)} %shard_map.103.first_part), channel_id=1, source_target_pairs={{0,2},{1,3},{2,0},{3,1},{4,6},{5,7},{6,4},{7,5},{8,10},{9,11},{10,... | collective-permute-start | bytes 589832 | tf_op jit(solution)/shard_map/ppermute | solution.py:36
  60.0 6.0 %collective-permute-start.25 = (bf16[256,384]{1,0:T(8,128)(2,1)S(1)}, bf16[256,384]{1,0:T(8,128)(2,1)S(1)}, u32[]{:S(2)}, u32[]{:S(2)}) collective-permute-start(bf16[256,384]{1,0:T(8,128)(2,1)S(1)} %shard_map.103.first_part), channel_id=1, source_target_pairs={{0,4},{1,5},{2,6},{3,7},{4,0},{5,1},{6,2},{7,3},{8,12},{9,13},{10,... | collective-permute-start | bytes 589832 | tf_op jit(solution)/shard_map/ppermute | solution.py:36
  60.0 11.1 %collective-permute-start.24 = (bf16[256,384]{1,0:T(8,128)(2,1)S(1)}, bf16[256,384]{1,0:T(8,128)(2,1)S(1)}, u32[]{:S(2)}, u32[]{:S(2)}) collective-permute-start(bf16[256,384]{1,0:T(8,128)(2,1)S(1)} %shard_map.103.first_part), channel_id=1, source_target_pairs={{0,6},{1,7},{2,4},{3,5},{4,2},{5,3},{6,0},{7,1},{8,14},{9,15},{10,... | collective-permute-start | bytes 589832 | tf_op jit(solution)/shard_map/ppermute | solution.py:36
  75.1 6.6 %collective-permute-start.27 = (bf16[64,384]{1,0:T(8,128)(2,1)S(1)}, bf16[64,384]{1,0:T(8,128)(2,1)S(1)}, u32[]{:S(2)}, u32[]{:S(2)}) collective-permute-start(bf16[64,384]{1,0:T(8,128)(2,1)S(1)} %get-tuple-element.35), channel_id=1, source_target_pairs={{0,2},{1,4},{2,0},{3,6},{4,1},{5,7},{6,3},{7,5},{8,10},{9,12},{10,... | collective-permute-start | bytes 147464 | tf_op jit(solution)/shard_map/ppermute | solution.py:36
  76.6 5.1 %collective-permute-start.28 = (bf16[64,384]{1,0:T(8,128)(2,1)S(1)}, bf16[64,384]{1,0:T(8,128)(2,1)S(1)}, u32[]{:S(2)}, u32[]{:S(2)}) collective-permute-start(bf16[64,384]{1,0:T(8,128)(2,1)S(1)} %get-tuple-element.36), channel_id=1, source_target_pairs={{0,3},{1,5},{2,1},{3,7},{4,0},{5,6},{6,2},{7,4},{8,11},{9,13},{10,... | collective-permute-start | bytes 147464 | tf_op jit(solution)/shard_map/ppermute | solution.py:36
  76.6 5.1 %collective-permute-start.29 = (bf16[64,384]{1,0:T(8,128)(2,1)S(1)}, bf16[64,384]{1,0:T(8,128)(2,1)S(1)}, u32[]{:S(2)}, u32[]{:S(2)}) collective-permute-start(bf16[64,384]{1,0:T(8,128)(2,1)S(1)} %get-tuple-element.37), channel_id=1, source_target_pairs={{0,1},{1,7},{2,3},{3,5},{4,2},{5,4},{6,0},{7,6},{8,9},{9,15},{10,1... | collective-permute-start | bytes 147464 | tf_op jit(solution)/shard_map/ppermute | solution.py:36
  78.1 6.3 %collective-permute-start.30 = (bf16[64,384]{1,0:T(8,128)(2,1)S(1)}, bf16[64,384]{1,0:T(8,128)(2,1)S(1)}, u32[]{:S(2)}, u32[]{:S(2)}) collective-permute-start(bf16[64,384]{1,0:T(8,128)(2,1)S(1)} %get-tuple-element.38), channel_id=1, source_target_pairs={{1,6},{3,4},{4,3},{6,1},{9,14},{11,12},{12,11},{14,9},{17,22},{19,... | collective-permute-start | bytes 147464 | tf_op jit(solution)/shard_map/ppermute | solution.py:36

commit v9 on v8

--- a/solution.py
+++ b/solution.py
@@ -229,17 +229,14 @@
 
 
 def all_tokens(latent):
-    def to_home(array):
-        return moved(array, lambda x, p, y, c: (x, p, y, 1 - c) if c != p % 2 else None)
-
-    def from_home(array):
-        return moved(array, lambda x, p, y, c: (x, p, y, 1 - c) if c == p % 2 else None)
+    def swapped(array):
+        return moved(array, lambda x, p, y, c: (x, p, y, 1 - c))
 
     far = moved(latent, lambda x, p, y, c: (x, p ^ 1, y, c))
     near = moved(latent, lambda x, p, y, c: (x, p, 1 - y, c))
     far_near = moved(far, lambda x, p, y, c: (x, p, 1 - y, c))
-    home = (latent, near, to_home(latent), to_home(near))
-    return home + (far, far_near, from_home(far), from_home(far_near))
+    home = (latent, near, swapped(latent), swapped(near))
+    return home + (far, far_near, swapped(far), swapped(far_near))
 
 
 def late_plane(devices):

time: 85.5 us -> 79.3 us (0.927)
  waiting for transfers between devices: 36.3 us -> 28.5 us
  starting transfers between devices: 33.6 us -> 35.4 us
    ppermute x26, waiting for transfers between devices: 29.8 us -> 24.8 us  [moved(): return lax.ppermute(array, AXES, pairs)]
    ppermute x5, waiting for transfers between devices: 6.55 us -> 3.75 us  [hop(): lax.ppermute(array, 'frame', [(i, i ^ bits) for i in range(lax.axis_size(...]
    ppermute x26, starting transfers between devices: 29.7 us -> 31.2 us  [moved(): return lax.ppermute(array, AXES, pairs)]
where the time goes in v9:
time: 79.3 us; the launch traced here: 79 us
  starting transfers between devices  35.4 us (45%)
  waiting for transfers between devices  28.5 us (36%)
  Pallas kernels  12.2 us (15%)
  other arithmetic  1.73 us (2%)
  local copies, waits for them, and re-layouts  0.95 us (1%)
    ppermute x26, starting transfers between devices, moved(): return lax.ppermute(array, AXES, pairs)  31.2 us
    ppermute x26, waiting for transfers between devices, moved(): return lax.ppermute(array, AXES, pairs)  24.8 us
    pallas_call x6, Pallas kernels, kernel_call(): pl.pallas_call(kernel, out_shape=out_shape, in_specs=[free if number in a...  8.88 us
    ppermute x5, starting transfers between devices, hop(): lax.ppermute(array, 'frame', [(i, i ^ bits) for i in range(lax.axis_size(...  4.21 us
    ppermute x5, waiting for transfers between devices, hop(): lax.ppermute(array, 'frame', [(i, i ^ bits) for i in range(lax.axis_size(...  3.75 us
    pallas_call x1, Pallas kernels, pack(): pl.pallas_call(pack_kernel, out_shape=out_shape, in_specs=[held] * 9, out...  3.33 us
  transfers between devices with their start and end apart: 31, of which 8 were waited for; matrix products, arithmetic and copies ran while one was open for 2% of the time, Pallas kernels for 2%

profile of v9, /device:TPU:1, one launch (start us, length us, event | category | flops | bytes accessed | tf_op | source)
XLA Modules:
  0.0 79.0 jit_solution(11216000482824207855)
XLA Ops:
  0.0 3.3 %pack.1 = (bf16[96,1152]{1,0:T(8,128)(2,1)}, bf16[96,1152]{1,0:T(8,128)(2,1)}, bf16[96,1152]{1,0:T(8,128)(2,1)}, bf16[96,1152]{1,0:T(8,128)(2,1)}, f32[4,1536]{1...) custom-call(bf16[96,1536]{1,0:T(8,128)(2,1)} %w_query.1, ...), custom_call_target="tpu_custom_call" | custom-call | tf_op jit(solution)/shard_map/pack/pallas_call | solution.py:164
  3.4 0.1 collective-permute-start.7
  3.4 2.7 %collective-permute-start.8 = (bf16[4,8,2,384]{3,2,1,0:T(2,128)(2,1)}, bf16[4,8,2,384]{3,2,1,0:T(2,128)(2,1)S(1)}, u32[]{:S(2)}, u32[]{:S(2)}) collective-permute-start(bf16[4,8,2,384]{3,2,1,0:T(2,128)(2,1)} %get-tuple-element.26), channel_id=1, source_target_pairs={{0,2},{1,3},{2,0},{3,1},{4,6},{5,7},{6,4},{7,5},{8,10},{9,11},{10,... | collective-permute-start | bytes 147464 | tf_op jit(solution)/shard_map/ppermute | solution.py:228
  6.2 0.0 collective-permute-start.9
  6.2 0.4 collective-permute-start.1
  6.6 3.5 %collective-permute-start.14 = (bf16[96,1152]{1,0:T(8,128)(2,1)}, bf16[96,1152]{1,0:T(8,128)(2,1)S(1)}, u32[]{:S(2)}, u32[]{:S(2)}) collective-permute-start(bf16[96,1152]{1,0:T(8,128)(2,1)} %get-tuple-element.32), channel_id=1, source_target_pairs={{0,8},{1,11},{2,10},{3,9},{4,12},{5,15},{6,14},{7,13},{8,0},{9,3},... | collective-permute-start | bytes 663560 | tf_op jit(solution)/shard_map/ppermute | solution.py:36
  10.0 1.2 %collective-permute-start.13 = (bf16[96,1152]{1,0:T(8,128)(2,1)}, bf16[96,1152]{1,0:T(8,128)(2,1)S(1)}, u32[]{:S(2)}, u32[]{:S(2)}) collective-permute-start(bf16[96,1152]{1,0:T(8,128)(2,1)} %get-tuple-element.31), channel_id=1, source_target_pairs={{0,4},{1,7},{2,6},{3,5},{4,0},{5,3},{6,2},{7,1},{8,12},{9,15},{10,... | collective-permute-start | bytes 663560 | tf_op jit(solution)/shard_map/ppermute | solution.py:36
  11.3 1.1 %pad_maximum_fusion.1 = bf16[4,4,8,2,384]{4,3,2,1,0:T(2,128)(2,1)S(1)} fusion(bf16[1,4,8,2,384]{4,3,2,1,0:T(2,128)(2,1)S(1)} %bitcast.11, bf16[1,4,8,2,384]{4,3,2,1,0:T(2,128)(2,1)S(1)} %bitcast.10, bf16[1,4,8,2,384]{4,3,2,1,0:T(2,128)(2,1)S(1)} %bitcast.9, bf16[1,4,8,2,384]{4,3,2,1,0:T(2,128)(2,1)} %bitcast.8), kind=kLoop, calls=%fused_computation.2 | loop fusion | flops 294912 | bytes 393216 | tf_op jit(solution)/shard_map/stack | solution.py:218
  12.4 0.1 fusion.1
  12.6 0.2 collective-permute-start.10
  12.8 8.9 %collective-permute-done.13 = bf16[96,1152]{1,0:T(8,128)(2,1)S(1)} collective-permute-done((bf16[96,1152]{1,0:T(8,128)(2,1)}, bf16[96,1152]{1,0:T(8,128)(2,1)S(1)}, u32[]{:S(2)}, u32[]{:S(2)}) %collective-permute-start.13) | collective-permute-done | bytes 221216 | tf_op jit(solution)/shard_map/ppermute | solution.py:36
  21.8 0.1 collective-permute-start.15
  21.9 0.1 collective-permute-start.12
  22.0 1.5 %collective-permute-start = (bf16[64,1536]{1,0:T(8,128)(2,1)}, bf16[64,1536]{1,0:T(8,128)(2,1)S(1)}, u32[]{:S(2)}, u32[]{:S(2)}) collective-permute-start(bf16[64,1536]{1,0:T(8,128)(2,1)} %refs_0_.1), channel_id=1, source_target_pairs={{0,2},{1,3},{2,0},{3,1},{4,6},{5,7},{6,4},{7,5},{8,10},{9,11},{10,... | collective-permute-start | bytes 589832 | tf_op jit(solution)/shard_map/ppermute | solution.py:36
  23.4 0.9 %collective-permute-start.3 = (bf16[64,1536]{1,0:T(8,128)(2,1)}, bf16[64,1536]{1,0:T(8,128)(2,1)S(1)}, u32[]{:S(2)}, u32[]{:S(2)}) collective-permute-start(bf16[64,1536]{1,0:T(8,128)(2,1)} %refs_0_.1), channel_id=1, source_target_pairs={{0,4},{1,5},{2,6},{3,7},{4,0},{5,1},{6,2},{7,3},{8,12},{9,13},{10,... | collective-permute-start | bytes 589832 | tf_op jit(solution)/shard_map/ppermute | solution.py:36
  24.3 2.7 %collective-permute-start.16 = (bf16[96,1152]{1,0:T(8,128)(2,1)}, bf16[96,1152]{1,0:T(8,128)(2,1)S(1)}, u32[]{:S(2)}, u32[]{:S(2)}) collective-permute-start(bf16[96,1152]{1,0:T(8,128)(2,1)} %get-tuple-element.31), channel_id=1, source_target_pairs={{0,12},{1,15},{2,14},{3,13},{4,8},{5,11},{6,10},{7,9},{8,4},{9,7},... | collective-permute-start | bytes 663560 | tf_op jit(solution)/shard_map/ppermute | solution.py:36
  27.1 4.1 %collective-permute-done.refs_1_ = bf16[64,1536]{1,0:T(8,128)(2,1)S(1)} collective-permute-done((bf16[64,1536]{1,0:T(8,128)(2,1)}, bf16[64,1536]{1,0:T(8,128)(2,1)S(1)}, u32[]{:S(2)}, u32[]{:S(2)}) %collective-permute-start) | collective-permute-done | bytes 196640 | tf_op jit(solution)/shard_map/ppermute | solution.py:36
  31.1 5.5 %collective-permute-start.18 = (bf16[96,1152]{1,0:T(8,128)(2,1)}, bf16[96,1152]{1,0:T(8,128)(2,1)S(1)}, u32[]{:S(2)}, u32[]{:S(2)}) collective-permute-start(bf16[96,1152]{1,0:T(8,128)(2,1)} %get-tuple-element.29.refs_0_.refs_1_), channel_id=1, source_target_pairs={{0,1},{1,0},{2,3},{3,2},{4,5},{5,4},{6,7},{7,6},{8,9},{9,8},{10,11... | collective-permute-start | bytes 663560 | tf_op jit(solution)/shard_map/ppermute | solution.py:36
  36.6 0.4 collective-permute-start.2
  36.9 0.3 fusion
  37.2 1.1 %collective-permute-start.11 = (bf16[8,1,8,2,384]{4,3,2,1,0:T(2,128)(2,1)S(1)}, bf16[8,1,8,2,384]{4,3,2,1,0:T(2,128)(2,1)S(1)}, u32[]{:S(2)}, u32[]{:S(2)}) collective-permute-start(bf16[8,1,8,2,384]{4,3,2,1,0:T(2,128)(2,1)S(1)} %get-tuple-element.42), channel_id=1, source_target_pairs={{0,8},{1,9},{2,10},{3,11},{4,12},{5,13},{6,14},{7,15},{8,0},{9,1},... | collective-permute-start | bytes 294920 | tf_op jit(solution)/shard_map/ppermute | solution.py:228
  38.4 3.7 %collective-permute-done.11 = bf16[8,1,8,2,384]{4,3,2,1,0:T(2,128)(2,1)S(1)} collective-permute-done((bf16[8,1,8,2,384]{4,3,2,1,0:T(2,128)(2,1)S(1)}, bf16[8,1,8,2,384]{4,3,2,1,0:T(2,128)(2,1)S(1)}, u32[]{:S(2)}, u32[]{:S(2)}) %collective-permute-start.11) | collective-permute-done | bytes 98336 | tf_op jit(solution)/shard_map/ppermute | solution.py:228
  42.1 3.4 %collective-permute-start.20 = (bf16[192,1152]{1,0:T(8,128)(2,1)S(1)}, bf16[192,1152]{1,0:T(8,128)(2,1)S(1)}, u32[]{:S(2)}, u32[]{:S(2)}) collective-permute-start(bf16[192,1152]{1,0:T(8,128)(2,1)S(1)} %constant_dynamic-update-slice_fusion.refs_2_.refs_3_), channel_id=1, source_target_pairs={{0,1},{1,0},{2,3},{3,2},{4,5},{5,4},{6,7},{7,6},{8,9},{9,8},{10,11... | collective-permute-start | bytes 1327112 | tf_op jit(solution)/shard_map/ppermute | solution.py:36
  45.5 0.0 collective-permute-start.21
  45.5 0.5 collective-permute-start.5
  46.0 0.1 collective-permute-start.6
  46.1 0.3 pad_maximum_fusion
  46.4 1.4 %collective-permute-done.5.refs_6_ = bf16[64,1536]{1,0:T(8,128)(2,1)S(1)} collective-permute-done((bf16[64,1536]{1,0:T(8,128)(2,1)S(1)}, bf16[64,1536]{1,0:T(8,128)(2,1)S(1)}, u32[]{:S(2)}, u32[]{:S(2)}) %collective-permute-start.5) | collective-permute-done | bytes 196640 | tf_op jit(solution)/shard_map/ppermute | solution.py:36
  47.8 0.4 collective-permute-start.22
  48.2 0.1 collective-permute-start.19
  48.3 0.4 collective-permute-start.23
  48.8 0.7 copy-done.2
  49.5 0.5 shard_map.100
  50.0 1.2 %shard_map.102.part_ref = f32[256,1152]{1,0:T(8,128)S(1)} custom-call(bf16[256,1536]{1,0:T(8,128)(2,1)S(1)} %get-tuple-element.33.refs_0_.normed, bf16[96,1152]{1,0:T(8,128)(2,1)S(1)} %copy-done, bf16[96,1152]{1,0:T(8,128)(2,1)S(1)} %collective-permute-done.12.refs_1_.refs_2_, bf16[192,1152]{1,0:T(8,128)(2,1)S(1)} %constant_dynamic-update-slice_fusion.refs_2_.refs_3_, ...), custom_call_target="tpu_custom_call" | custom-call | flops 679477248 | bytes 3440640 | tf_op jit(solution)/shard_map/pallas_call | solution.py:413
  51.3 2.2 %shard_map.103.first_part = bf16[256,384]{1,0:T(8,128)(2,1)S(1)} custom-call(f32[4,1536]{1,0:T(4,128)S(1)} %get-tuple-element.23.extra_ref, bf16[128,384]{1,0:T(8,128)(2,1)S(1)} %get-tuple-element.46.key_ref, bf16[128,384]{1,0:T(8,128)(2,1)S(1)} %get-tuple-element.45.value_ref, bf16[256,1536]{1,0:T(8,128)(2,1)S(1)} %get-tuple-element.33.refs_0_.normed, ...), custom_call_target="tpu_custom_call" | custom-call | flops 377487360 | bytes 3072000 | tf_op jit(solution)/shard_map/pallas_call | solution.py:413
  53.4 1.5 %collective-permute-start.26 = (bf16[256,384]{1,0:T(8,128)(2,1)S(1)}, bf16[256,384]{1,0:T(8,128)(2,1)S(1)}, u32[]{:S(2)}, u32[]{:S(2)}) collective-permute-start(bf16[256,384]{1,0:T(8,128)(2,1)S(1)} %shard_map.103.first_part), channel_id=1, source_target_pairs={{0,2},{1,3},{2,0},{3,1},{4,6},{5,7},{6,4},{7,5},{8,10},{9,11},{10,... | collective-permute-start | bytes 589832 | tf_op jit(solution)/shard_map/ppermute | solution.py:36
  54.9 1.3 %collective-permute-start.24 = (bf16[256,384]{1,0:T(8,128)(2,1)S(1)}, bf16[256,384]{1,0:T(8,128)(2,1)S(1)}, u32[]{:S(2)}, u32[]{:S(2)}) collective-permute-start(bf16[256,384]{1,0:T(8,128)(2,1)S(1)} %shard_map.103.first_part), channel_id=1, source_target_pairs={{0,6},{1,7},{2,4},{3,5},{4,2},{5,3},{6,0},{7,1},{8,14},{9,15},{10,... | collective-permute-start | bytes 589832 | tf_op jit(solution)/shard_map/ppermute | solution.py:36
  56.2 0.3 shard_map.101.weights
  56.5 3.4 %collective-permute-done.26.fourth_part = bf16[256,384]{1,0:T(8,128)(2,1)S(1)} collective-permute-done((bf16[256,384]{1,0:T(8,128)(2,1)S(1)}, bf16[256,384]{1,0:T(8,128)(2,1)S(1)}, u32[]{:S(2)}, u32[]{:S(2)}) %collective-permute-start.26) | collective-permute-done | bytes 196640 | tf_op jit(solution)/shard_map/ppermute | solution.py:36
  59.8 1.1 %collective-permute-done.25.third_part = bf16[256,384]{1,0:T(8,128)(2,1)S(1)} collective-permute-done((bf16[256,384]{1,0:T(8,128)(2,1)S(1)}, bf16[256,384]{1,0:T(8,128)(2,1)S(1)}, u32[]{:S(2)}, u32[]{:S(2)}) %collective-permute-start.25) | collective-permute-done | bytes 196640 | tf_op jit(solution)/shard_map/ppermute | solution.py:36
  60.9 4.0 %collective-permute-done.24.second_part = bf16[256,384]{1,0:T(8,128)(2,1)S(1)} collective-permute-done((bf16[256,384]{1,0:T(8,128)(2,1)S(1)}, bf16[256,384]{1,0:T(8,128)(2,1)S(1)}, u32[]{:S(2)}, u32[]{:S(2)}) %collective-permute-start.24) | collective-permute-done | bytes 196640 | tf_op jit(solution)/shard_map/ppermute | solution.py:36
  65.0 4.0 %shard_map.104 = (bf16[64,384]{1,0:T(8,128)(2,1)S(1)}, bf16[64,384]{1,0:T(8,128)(2,1)S(1)}, bf16[64,384]{1,0:T(8,128)(2,1)S(1)}, bf16[64,384]{1,0:T(8,128)(2,1)S(1)}, bf16[64,384]{1,0:T(8,128)(2,1)S(1)}) custom-call(f32[4,1536]{1,0:T(4,128)S(1)} %get-tuple-element.23.extra_ref, bf16[128,384]{1,0:T(8,128)(2,1)S(1)} %get-tuple-element.46.key_ref, ...), custom_call_target="tpu_custom_call" | custom-call | flops 1056964608 | bytes 5332992 | tf_op jit(solution)/shard_map/pallas_call | solution.py:413
  69.0 1.5 %collective-permute-start.27 = (bf16[64,384]{1,0:T(8,128)(2,1)S(1)}, bf16[64,384]{1,0:T(8,128)(2,1)S(1)}, u32[]{:S(2)}, u32[]{:S(2)}) collective-permute-start(bf16[64,384]{1,0:T(8,128)(2,1)S(1)} %get-tuple-element.35), channel_id=1, source_target_pairs={{0,2},{1,4},{2,0},{3,6},{4,1},{5,7},{6,3},{7,5},{8,10},{9,12},{10,... | collective-permute-start | bytes 147464 | tf_op jit(solution)/shard_map/ppermute | solution.py:36
  70.5 0.2 collective-permute-start.28
  70.7 1.3 %collective-permute-start.29 = (bf16[64,384]{1,0:T(8,128)(2,1)S(1)}, bf16[64,384]{1,0:T(8,128)(2,1)S(1)}, u32[]{:S(2)}, u32[]{:S(2)}) collective-permute-start(bf16[64,384]{1,0:T(8,128)(2,1)S(1)} %get-tuple-element.37), channel_id=1, source_target_pairs={{0,1},{1,7},{2,3},{3,5},{4,2},{5,4},{6,0},{7,6},{8,9},{9,15},{10,1... | collective-permute-start | bytes 147464 | tf_op jit(solution)/shard_map/ppermute | solution.py:36
  72.0 4.4 %collective-permute-start.30 = (bf16[64,384]{1,0:T(8,128)(2,1)S(1)}, bf16[64,384]{1,0:T(8,128)(2,1)S(1)}, u32[]{:S(2)}, u32[]{:S(2)}) collective-permute-start(bf16[64,384]{1,0:T(8,128)(2,1)S(1)} %get-tuple-element.38), channel_id=1, source_target_pairs={{1,6},{3,4},{4,3},{6,1},{9,14},{11,12},{12,11},{14,9},{17,22},{19,... | collective-permute-start | bytes 147464 | tf_op jit(solution)/shard_map/ppermute | solution.py:36
  76.5 1.8 %collective-permute-done.30.fourth = bf16[64,384]{1,0:T(8,128)(2,1)S(1)} collective-permute-done((bf16[64,384]{1,0:T(8,128)(2,1)S(1)}, bf16[64,384]{1,0:T(8,128)(2,1)S(1)}, u32[]{:S(2)}, u32[]{:S(2)}) %collective-permute-start.30) | collective-permute-done | bytes 49184 | tf_op jit(solution)/shard_map/ppermute | solution.py:36
  78.3 0.7 shard_map.105
  (34 shorter events, 0.2 us)
Async XLA Ops:
  0.0 48.8 %copy-start.1 = (bf16[64,1536]{1,0:T(8,128)(2,1)S(1)}, bf16[64,1536]{1,0:T(8,128)(2,1)}, u32[]{:S(2)}) copy-start(bf16[64,1536]{1,0:T(8,128)(2,1)} %refs_0_.1) | copy-start | bytes 589828
  3.3 46.7 %copy-start = (bf16[96,1152]{1,0:T(8,128)(2,1)S(1)}, bf16[96,1152]{1,0:T(8,128)(2,1)}, u32[]{:S(2)}) copy-start(bf16[96,1152]{1,0:T(8,128)(2,1)} %get-tuple-element.29.refs_0_.refs_1_) | copy-start | bytes 663556
  3.4 6.7 %collective-permute-start.7 = (bf16[4,8,2,384]{3,2,1,0:T(2,128)(2,1)}, bf16[4,8,2,384]{3,2,1,0:T(2,128)(2,1)S(1)}, u32[]{:S(2)}, u32[]{:S(2)}) collective-permute-start(bf16[4,8,2,384]{3,2,1,0:T(2,128)(2,1)} %get-tuple-element.25), channel_id=1, source_target_pairs={{0,1},{1,0},{2,3},{3,2},{4,5},{5,4},{6,7},{7,6},{8,9},{9,8},{10,11... | collective-permute-start | bytes 147464 | tf_op jit(solution)/shard_map/ppermute | solution.py:228
  3.4 7.8 %collective-permute-start.8 = (bf16[4,8,2,384]{3,2,1,0:T(2,128)(2,1)}, bf16[4,8,2,384]{3,2,1,0:T(2,128)(2,1)S(1)}, u32[]{:S(2)}, u32[]{:S(2)}) collective-permute-start(bf16[4,8,2,384]{3,2,1,0:T(2,128)(2,1)} %get-tuple-element.26), channel_id=1, source_target_pairs={{0,2},{1,3},{2,0},{3,1},{4,6},{5,7},{6,4},{7,5},{8,10},{9,11},{10,... | collective-permute-start | bytes 147464 | tf_op jit(solution)/shard_map/ppermute | solution.py:228
  6.2 5.1 %collective-permute-start.9 = (bf16[4,8,2,384]{3,2,1,0:T(2,128)(2,1)}, bf16[4,8,2,384]{3,2,1,0:T(2,128)(2,1)S(1)}, u32[]{:S(2)}, u32[]{:S(2)}) collective-permute-start(bf16[4,8,2,384]{3,2,1,0:T(2,128)(2,1)} %get-tuple-element.27), channel_id=1, source_target_pairs={{0,3},{1,2},{2,1},{3,0},{4,7},{5,6},{6,5},{7,4},{8,11},{9,10},{10,... | collective-permute-start | bytes 147464 | tf_op jit(solution)/shard_map/ppermute | solution.py:228
  6.2 18.1 %collective-permute-start.1 = (bf16[64,1536]{1,0:T(8,128)(2,1)}, bf16[64,1536]{1,0:T(8,128)(2,1)S(1)}, u32[]{:S(2)}, u32[]{:S(2)}) collective-permute-start(bf16[64,1536]{1,0:T(8,128)(2,1)} %refs_0_.1), channel_id=1, source_target_pairs={{0,1},{1,0},{2,3},{3,2},{4,5},{5,4},{6,7},{7,6},{8,9},{9,8},{10,11... | collective-permute-start | bytes 589832 | tf_op jit(solution)/shard_map/ppermute | solution.py:36
  6.6 15.2 %collective-permute-start.14 = (bf16[96,1152]{1,0:T(8,128)(2,1)}, bf16[96,1152]{1,0:T(8,128)(2,1)S(1)}, u32[]{:S(2)}, u32[]{:S(2)}) collective-permute-start(bf16[96,1152]{1,0:T(8,128)(2,1)} %get-tuple-element.32), channel_id=1, source_target_pairs={{0,8},{1,11},{2,10},{3,9},{4,12},{5,15},{6,14},{7,13},{8,0},{9,3},... | collective-permute-start | bytes 663560 | tf_op jit(solution)/shard_map/ppermute | solution.py:36
  10.0 11.7 %collective-permute-start.13 = (bf16[96,1152]{1,0:T(8,128)(2,1)}, bf16[96,1152]{1,0:T(8,128)(2,1)S(1)}, u32[]{:S(2)}, u32[]{:S(2)}) collective-permute-start(bf16[96,1152]{1,0:T(8,128)(2,1)} %get-tuple-element.31), channel_id=1, source_target_pairs={{0,4},{1,7},{2,6},{3,5},{4,0},{5,3},{6,2},{7,1},{8,12},{9,15},{10,... | collective-permute-start | bytes 663560 | tf_op jit(solution)/shard_map/ppermute | solution.py:36
  12.6 10.8 %collective-permute-start.10 = (bf16[4,2,8,2,384]{4,3,2,1,0:T(2,128)(2,1)S(1)}, bf16[4,2,8,2,384]{4,3,2,1,0:T(2,128)(2,1)S(1)}, u32[]{:S(2)}, u32[]{:S(2)}) collective-permute-start(bf16[4,2,8,2,384]{4,3,2,1,0:T(2,128)(2,1)S(1)} %get-tuple-element.44), channel_id=1, source_target_pairs={{0,4},{1,5},{2,6},{3,7},{4,0},{5,1},{6,2},{7,3},{8,12},{9,13},{10,... | collective-permute-start | bytes 294920 | tf_op jit(solution)/shard_map/ppermute | solution.py:228
  21.8 23.7 %collective-permute-start.15 = (bf16[192,1152]{1,0:T(8,128)(2,1)S(1)}, bf16[192,1152]{1,0:T(8,128)(2,1)S(1)}, u32[]{:S(2)}, u32[]{:S(2)}) collective-permute-start(bf16[192,1152]{1,0:T(8,128)(2,1)S(1)} %constant_dynamic-update-slice_fusion.refs_2_.refs_3_), channel_id=1, source_target_pairs={{0,16},{1,17},{2,18},{3,19},{4,20},{5,21},{6,22},{7,23},{8,24},{9,... | collective-permute-start | bytes 1327112 | tf_op jit(solution)/shard_map/ppermute | solution.py:36
  21.9 15.1 %collective-permute-start.12 = (bf16[96,1152]{1,0:T(8,128)(2,1)}, bf16[96,1152]{1,0:T(8,128)(2,1)S(1)}, u32[]{:S(2)}, u32[]{:S(2)}) collective-permute-start(bf16[96,1152]{1,0:T(8,128)(2,1)} %get-tuple-element.30), channel_id=1, source_target_pairs={{0,2},{1,3},{2,0},{3,1},{4,6},{5,7},{6,4},{7,5},{8,10},{9,11},{10,... | collective-permute-start | bytes 663560 | tf_op jit(solution)/shard_map/ppermute | solution.py:36
  22.0 9.2 %collective-permute-start = (bf16[64,1536]{1,0:T(8,128)(2,1)}, bf16[64,1536]{1,0:T(8,128)(2,1)S(1)}, u32[]{:S(2)}, u32[]{:S(2)}) collective-permute-start(bf16[64,1536]{1,0:T(8,128)(2,1)} %refs_0_.1), channel_id=1, source_target_pairs={{0,2},{1,3},{2,0},{3,1},{4,6},{5,7},{6,4},{7,5},{8,10},{9,11},{10,... | collective-permute-start | bytes 589832 | tf_op jit(solution)/shard_map/ppermute | solution.py:36
  23.4 13.2 %collective-permute-start.3 = (bf16[64,1536]{1,0:T(8,128)(2,1)}, bf16[64,1536]{1,0:T(8,128)(2,1)S(1)}, u32[]{:S(2)}, u32[]{:S(2)}) collective-permute-start(bf16[64,1536]{1,0:T(8,128)(2,1)} %refs_0_.1), channel_id=1, source_target_pairs={{0,4},{1,5},{2,6},{3,7},{4,0},{5,1},{6,2},{7,3},{8,12},{9,13},{10,... | collective-permute-start | bytes 589832 | tf_op jit(solution)/shard_map/ppermute | solution.py:36
  24.3 12.9 %collective-permute-start.16 = (bf16[96,1152]{1,0:T(8,128)(2,1)}, bf16[96,1152]{1,0:T(8,128)(2,1)S(1)}, u32[]{:S(2)}, u32[]{:S(2)}) collective-permute-start(bf16[96,1152]{1,0:T(8,128)(2,1)} %get-tuple-element.31), channel_id=1, source_target_pairs={{0,12},{1,15},{2,14},{3,13},{4,8},{5,11},{6,10},{7,9},{8,4},{9,7},... | collective-permute-start | bytes 663560 | tf_op jit(solution)/shard_map/ppermute | solution.py:36
  31.1 7.2 %collective-permute-start.18 = (bf16[96,1152]{1,0:T(8,128)(2,1)}, bf16[96,1152]{1,0:T(8,128)(2,1)S(1)}, u32[]{:S(2)}, u32[]{:S(2)}) collective-permute-start(bf16[96,1152]{1,0:T(8,128)(2,1)} %get-tuple-element.29.refs_0_.refs_1_), channel_id=1, source_target_pairs={{0,1},{1,0},{2,3},{3,2},{4,5},{5,4},{6,7},{7,6},{8,9},{9,8},{10,11... | collective-permute-start | bytes 663560 | tf_op jit(solution)/shard_map/ppermute | solution.py:36
  36.6 8.9 %collective-permute-start.2 = (bf16[64,1536]{1,0:T(8,128)(2,1)S(1)}, bf16[64,1536]{1,0:T(8,128)(2,1)S(1)}, u32[]{:S(2)}, u32[]{:S(2)}) collective-permute-start(bf16[64,1536]{1,0:T(8,128)(2,1)S(1)} %collective-permute-done.refs_1_), channel_id=1, source_target_pairs={{0,1},{1,0},{2,3},{3,2},{4,5},{5,4},{6,7},{7,6},{8,9},{9,8},{10,11... | collective-permute-start | bytes 589832 | tf_op jit(solution)/shard_map/ppermute | solution.py:36
  36.9 9.1 %collective-permute-start.4 = (bf16[64,1536]{1,0:T(8,128)(2,1)S(1)}, bf16[64,1536]{1,0:T(8,128)(2,1)S(1)}, u32[]{:S(2)}, u32[]{:S(2)}) collective-permute-start(bf16[64,1536]{1,0:T(8,128)(2,1)S(1)} %collective-permute-done.3.refs_4_), channel_id=1, source_target_pairs={{0,2},{1,3},{2,0},{3,1},{4,6},{5,7},{6,4},{7,5},{8,10},{9,11},{10,... | collective-permute-start | bytes 589832 | tf_op jit(solution)/shard_map/ppermute | solution.py:36
  37.2 4.9 %collective-permute-start.11 = (bf16[8,1,8,2,384]{4,3,2,1,0:T(2,128)(2,1)S(1)}, bf16[8,1,8,2,384]{4,3,2,1,0:T(2,128)(2,1)S(1)}, u32[]{:S(2)}, u32[]{:S(2)}) collective-permute-start(bf16[8,1,8,2,384]{4,3,2,1,0:T(2,128)(2,1)S(1)} %get-tuple-element.42), channel_id=1, source_target_pairs={{0,8},{1,9},{2,10},{3,11},{4,12},{5,13},{6,14},{7,15},{8,0},{9,1},... | collective-permute-start | bytes 294920 | tf_op jit(solution)/shard_map/ppermute | solution.py:228
  38.4 9.9 %collective-permute-start.17 = (bf16[96,1152]{1,0:T(8,128)(2,1)S(1)}, bf16[96,1152]{1,0:T(8,128)(2,1)S(1)}, u32[]{:S(2)}, u32[]{:S(2)}) collective-permute-start(bf16[96,1152]{1,0:T(8,128)(2,1)S(1)} %collective-permute-done.16.refs_4_.refs_0_), channel_id=1, source_target_pairs={{0,16},{1,17},{2,18},{3,19},{4,20},{5,21},{6,22},{7,23},{8,24},{9,... | collective-permute-start | bytes 663560 | tf_op jit(solution)/shard_map/ppermute | solution.py:36
  42.1 7.9 %collective-permute-start.20 = (bf16[192,1152]{1,0:T(8,128)(2,1)S(1)}, bf16[192,1152]{1,0:T(8,128)(2,1)S(1)}, u32[]{:S(2)}, u32[]{:S(2)}) collective-permute-start(bf16[192,1152]{1,0:T(8,128)(2,1)S(1)} %constant_dynamic-update-slice_fusion.refs_2_.refs_3_), channel_id=1, source_target_pairs={{0,1},{1,0},{2,3},{3,2},{4,5},{5,4},{6,7},{7,6},{8,9},{9,8},{10,11... | collective-permute-start | bytes 1327112 | tf_op jit(solution)/shard_map/ppermute | solution.py:36
  45.5 4.5 %collective-permute-start.21 = (bf16[192,1152]{1,0:T(8,128)(2,1)S(1)}, bf16[192,1152]{1,0:T(8,128)(2,1)S(1)}, u32[]{:S(2)}, u32[]{:S(2)}) collective-permute-start(bf16[192,1152]{1,0:T(8,128)(2,1)S(1)} %collective-permute-done.15.refs_3_.refs_4_), channel_id=1, source_target_pairs={{0,1},{1,0},{2,3},{3,2},{4,5},{5,4},{6,7},{7,6},{8,9},{9,8},{10,11... | collective-permute-start | bytes 1327112 | tf_op jit(solution)/shard_map/ppermute | solution.py:36
  45.5 2.3 %collective-permute-start.5 = (bf16[64,1536]{1,0:T(8,128)(2,1)S(1)}, bf16[64,1536]{1,0:T(8,128)(2,1)S(1)}, u32[]{:S(2)}, u32[]{:S(2)}) collective-permute-start(bf16[64,1536]{1,0:T(8,128)(2,1)S(1)} %collective-permute-done.3.refs_4_), channel_id=1, source_target_pairs={{0,1},{1,0},{2,3},{3,2},{4,5},{5,4},{6,7},{7,6},{8,9},{9,8},{10,11... | collective-permute-start | bytes 589832 | tf_op jit(solution)/shard_map/ppermute | solution.py:36
  46.0 2.3 %collective-permute-start.6 = (bf16[64,1536]{1,0:T(8,128)(2,1)S(1)}, bf16[64,1536]{1,0:T(8,128)(2,1)S(1)}, u32[]{:S(2)}, u32[]{:S(2)}) collective-permute-start(bf16[64,1536]{1,0:T(8,128)(2,1)S(1)} %collective-permute-done.4.refs_5_), channel_id=1, source_target_pairs={{0,1},{1,0},{2,3},{3,2},{4,5},{5,4},{6,7},{7,6},{8,9},{9,8},{10,11... | collective-permute-start | bytes 589832 | tf_op jit(solution)/shard_map/ppermute | solution.py:36
  47.8 3.4 %collective-permute-start.22 = (bf16[96,1152]{1,0:T(8,128)(2,1)S(1)}, bf16[96,1152]{1,0:T(8,128)(2,1)S(1)}, u32[]{:S(2)}, u32[]{:S(2)}) collective-permute-start(bf16[96,1152]{1,0:T(8,128)(2,1)S(1)} %collective-permute-done.16.refs_4_.refs_0_), channel_id=1, source_target_pairs={{0,1},{1,0},{2,3},{3,2},{4,5},{5,4},{6,7},{7,6},{8,9},{9,8},{10,11... | collective-permute-start | bytes 663560 | tf_op jit(solution)/shard_map/ppermute | solution.py:36
  48.2 1.8 %collective-permute-start.19 = (bf16[96,1152]{1,0:T(8,128)(2,1)S(1)}, bf16[96,1152]{1,0:T(8,128)(2,1)S(1)}, u32[]{:S(2)}, u32[]{:S(2)}) collective-permute-start(bf16[96,1152]{1,0:T(8,128)(2,1)S(1)} %collective-permute-done.12.refs_1_.refs_2_), channel_id=1, source_target_pairs={{0,1},{1,0},{2,3},{3,2},{4,5},{5,4},{6,7},{7,6},{8,9},{9,8},{10,11... | collective-permute-start | bytes 663560 | tf_op jit(solution)/shard_map/ppermute | solution.py:36
  48.3 2.9 %collective-permute-start.23 = (bf16[96,1152]{1,0:T(8,128)(2,1)S(1)}, bf16[96,1152]{1,0:T(8,128)(2,1)S(1)}, u32[]{:S(2)}, u32[]{:S(2)}) collective-permute-start(bf16[96,1152]{1,0:T(8,128)(2,1)S(1)} %collective-permute-done.17.refs_5_.refs_1_), channel_id=1, source_target_pairs={{0,1},{1,0},{2,3},{3,2},{4,5},{5,4},{6,7},{7,6},{8,9},{9,8},{10,11... | collective-permute-start | bytes 663560 | tf_op jit(solution)/shard_map/ppermute | solution.py:36
  48.8 0.7 copy-start.2
  53.4 6.4 %collective-permute-start.26 = (bf16[256,384]{1,0:T(8,128)(2,1)S(1)}, bf16[256,384]{1,0:T(8,128)(2,1)S(1)}, u32[]{:S(2)}, u32[]{:S(2)}) collective-permute-start(bf16[256,384]{1,0:T(8,128)(2,1)S(1)} %shard_map.103.first_part), channel_id=1, source_target_pairs={{0,2},{1,3},{2,0},{3,1},{4,6},{5,7},{6,4},{7,5},{8,10},{9,11},{10,... | collective-permute-start | bytes 589832 | tf_op jit(solution)/shard_map/ppermute | solution.py:36
  54.9 6.0 %collective-permute-start.25 = (bf16[256,384]{1,0:T(8,128)(2,1)S(1)}, bf16[256,384]{1,0:T(8,128)(2,1)S(1)}, u32[]{:S(2)}, u32[]{:S(2)}) collective-permute-start(bf16[256,384]{1,0:T(8,128)(2,1)S(1)} %shard_map.103.first_part), channel_id=1, source_target_pairs={{0,4},{1,5},{2,6},{3,7},{4,0},{5,1},{6,2},{7,3},{8,12},{9,13},{10,... | collective-permute-start | bytes 589832 | tf_op jit(solution)/shard_map/ppermute | solution.py:36
  54.9 10.1 %collective-permute-start.24 = (bf16[256,384]{1,0:T(8,128)(2,1)S(1)}, bf16[256,384]{1,0:T(8,128)(2,1)S(1)}, u32[]{:S(2)}, u32[]{:S(2)}) collective-permute-start(bf16[256,384]{1,0:T(8,128)(2,1)S(1)} %shard_map.103.first_part), channel_id=1, source_target_pairs={{0,6},{1,7},{2,4},{3,5},{4,2},{5,3},{6,0},{7,1},{8,14},{9,15},{10,... | collective-permute-start | bytes 589832 | tf_op jit(solution)/shard_map/ppermute | solution.py:36
  69.0 7.4 %collective-permute-start.27 = (bf16[64,384]{1,0:T(8,128)(2,1)S(1)}, bf16[64,384]{1,0:T(8,128)(2,1)S(1)}, u32[]{:S(2)}, u32[]{:S(2)}) collective-permute-start(bf16[64,384]{1,0:T(8,128)(2,1)S(1)} %get-tuple-element.35), channel_id=1, source_target_pairs={{0,2},{1,4},{2,0},{3,6},{4,1},{5,7},{6,3},{7,5},{8,10},{9,12},{10,... | collective-permute-start | bytes 147464 | tf_op jit(solution)/shard_map/ppermute | solution.py:36
  70.5 6.0 %collective-permute-start.28 = (bf16[64,384]{1,0:T(8,128)(2,1)S(1)}, bf16[64,384]{1,0:T(8,128)(2,1)S(1)}, u32[]{:S(2)}, u32[]{:S(2)}) collective-permute-start(bf16[64,384]{1,0:T(8,128)(2,1)S(1)} %get-tuple-element.36), channel_id=1, source_target_pairs={{0,3},{1,5},{2,1},{3,7},{4,0},{5,6},{6,2},{7,4},{8,11},{9,13},{10,... | collective-permute-start | bytes 147464 | tf_op jit(solution)/shard_map/ppermute | solution.py:36
  70.7 5.7 %collective-permute-start.29 = (bf16[64,384]{1,0:T(8,128)(2,1)S(1)}, bf16[64,384]{1,0:T(8,128)(2,1)S(1)}, u32[]{:S(2)}, u32[]{:S(2)}) collective-permute-start(bf16[64,384]{1,0:T(8,128)(2,1)S(1)} %get-tuple-element.37), channel_id=1, source_target_pairs={{0,1},{1,7},{2,3},{3,5},{4,2},{5,4},{6,0},{7,6},{8,9},{9,15},{10,1... | collective-permute-start | bytes 147464 | tf_op jit(solution)/shard_map/ppermute | solution.py:36
  72.0 6.3 %collective-permute-start.30 = (bf16[64,384]{1,0:T(8,128)(2,1)S(1)}, bf16[64,384]{1,0:T(8,128)(2,1)S(1)}, u32[]{:S(2)}, u32[]{:S(2)}) collective-permute-start(bf16[64,384]{1,0:T(8,128)(2,1)S(1)} %get-tuple-element.38), channel_id=1, source_target_pairs={{1,6},{3,4},{4,3},{6,1},{9,14},{11,12},{12,11},{14,9},{17,22},{19,... | collective-permute-start | bytes 147464 | tf_op jit(solution)/shard_map/ppermute | solution.py:36

commit v10 on v9

--- a/solution.py
+++ b/solution.py
@@ -126,7 +126,7 @@
     extra[0:1, :] = gain[...].reshape(row)
     for number in range(STEPS):
         extra[1 + number : 2 + number, :] = jnp.full(row, scale_ref[number], jnp.float32)
-    live = lax.broadcasted_iota(jnp.int32, row, 1) % entries < count_ref[(plane // 2) * 2 + c]
+    live = lax.broadcasted_iota(jnp.int32, row, 1) % entries < count_ref[(plane // 2) * 2 + 1 - c]
     extra[1 + STEPS : 2 + STEPS, :] = jnp.where(live, 1.0, 0.0)
     gives.append(pltpu.make_async_copy(extra, extra_ref, scalar_sem.at[5]))
     gives[-1].start()
@@ -271,6 +271,7 @@
 
 
 BLOCK = 32
+ATTENTION_BLOCKS = 1
 
 
 def prepare_kernel(extra_ref, *refs):
@@ -315,7 +316,7 @@
     live = extra_ref[3:4, :mem_rows] > 0.5
     contract_last = (((1,), (1,)), ((), ()))
     frame_rows = projected.shape[0]
-    half = frame_rows // 2
+    half = frame_rows // ATTENTION_BLOCKS
     for head in range(head_count):
         span = slice(head * head_size, (head + 1) * head_size)
         keys = projected[:, width + head * head_size : width + (head + 1) * head_size]
@@ -352,7 +353,7 @@
 
 def last_step_kernel(
     update_places, head_count, extra_ref, key_ref, value_ref, current_ref, weights, first_part, second_part, third_part,
-    fourth_part, keep, first, second, third, fourth, current, normed, projected, attended,
+    fourth_part, keep, first, second, current, normed, projected, attended,
 ):
     _, _, plane, y, c = here()
     width = first_part.shape[1]
@@ -381,26 +382,20 @@
         current[:, spot].astype(jnp.float32) + extra_ref[2:3, :width] * attended[...].astype(jnp.float32)
     ).astype(attended.dtype)
     chip_rows = attended.shape[0] // 2
-    rows = chip_rows // 2
-    here_rows, there_rows = y * chip_rows, (1 - y) * chip_rows
-
-    def part(start):
-        return attended[pl.ds(pl.multiple_of(start, rows), rows), :]
-
-    keep[...] = part(here_rows)
-    fourth[...] = part(there_rows + rows)
+
+    def part(at_y):
+        return attended[pl.ds(pl.multiple_of(at_y * chip_rows, chip_rows), chip_rows), :]
+
+    keep[...] = part(y)
+    second[...] = part(1 - y)
 
     @pl.when(at_home)
     def _():
-        first[...] = part(there_rows)
-        second[...] = part(there_rows + rows)
-        third[...] = part(here_rows + rows)
+        first[...] = part(1 - y)
 
     @pl.when(jnp.logical_not(at_home))
     def _():
-        first[...] = part(here_rows + rows)
-        second[...] = part(here_rows)
-        third[...] = part(there_rows)
+        first[...] = part(y)
 
 
 MIB = 1024 * 1024
@@ -480,10 +475,10 @@
 def last_step(extra, keys, values, current, weights, updates):
     frame_rows, features = current.shape
     width = weights.shape[1] // 3
-    share = jax.ShapeDtypeStruct((frame_rows // 4, width), current.dtype)
+    share = jax.ShapeDtypeStruct((frame_rows // 2, width), current.dtype)
     return kernel_call(
         functools.partial(last_step_kernel, tuple(place for _, place in updates), HEADS // SPATIAL),
-        (share,) * 5,
+        (share,) * 3,
         (extra, keys, values, current, weights, *[array for array, _ in updates]),
         (),
         [
@@ -497,42 +492,44 @@
     )
 
 
-def join_kernel(keep, first, second, third, fourth, out):
+def join_kernel(keep, first, second, other_keep, other_first, other_second, out):
     _, _, plane, y, c = here()
     low = plane % 2
-    width = keep.shape[1]
-
-    def put(ref, plane_low, at_y):
-        out[:, columns(plane_low * 2 + at_y, width)] = ref[...]
+    rows, width = out.shape[0], keep.shape[1]
+
+    def put(ref, start, plane_low, at_y):
+        out[:, columns(plane_low * 2 + at_y, width)] = ref[start : start + rows, :]
 
     @pl.when(low == c)
     def _():
-        put(keep, low, y)
-        put(first, low, 1 - y)
-        put(second, 1 - low, y)
-        put(third, 1 - low, 1 - y)
+        put(keep, 0, low, y)
+        put(first, 0, low, 1 - y)
+        put(other_first, 0, 1 - low, y)
+        put(other_second, 0, 1 - low, 1 - y)
 
     @pl.when(low != c)
     def _():
-        put(first, 1 - low, y)
-        put(second, low, 1 - y)
-        put(third, low, y)
-        put(fourth, 1 - low, 1 - y)
-
-
-def joined(keep, first, second, third, fourth):
+        put(other_keep, rows, low, y)
+        put(other_first, rows, low, 1 - y)
+        put(first, rows, 1 - low, y)
+        put(second, rows, 1 - low, 1 - y)
+
+
+def joined(keep, first, second):
     def at_home(p, c):
         return c == p % 2
 
+    def swapped(array):
+        return moved(array, lambda x, p, y, c: (x, p, y, 1 - c))
+
     first = moved(first, lambda x, p, y, c: (x, p, 1 - y, c) if at_home(p, c) else (x, p ^ 1, y, 1 - c))
-    second = moved(second, lambda x, p, y, c: (x, p, 1 - y, 1 - c) if at_home(p, c) else (x, p ^ 1, y, c))
-    third = moved(third, lambda x, p, y, c: (x, p, y, 1 - c) if at_home(p, c) else (x, p ^ 1, 1 - y, c))
-    fourth = moved(fourth, lambda x, p, y, c: None if at_home(p, c) else (x, p ^ 1, 1 - y, 1 - c))
+    second = moved(second, lambda x, p, y, c: None if at_home(p, c) else (x, p ^ 1, 1 - y, 1 - c))
+    others = (swapped(keep), swapped(first), swapped(second))
     rows, width = keep.shape
     return kernel_call(
         join_kernel,
-        jax.ShapeDtypeStruct((rows, width * SPATIAL), keep.dtype),
-        (keep, first, second, third, fourth),
+        jax.ShapeDtypeStruct((rows // 2, width * SPATIAL), keep.dtype),
+        (keep, first, second, *others),
         (),
         [],
         4 * MIB,
@@ -547,6 +544,7 @@
     weights, extra, memory = pack(
         w_query, w_key, w_value, intersection, slot_of, counts, step_scale, norm_gain, mem_cache
     )
+    extra = moved(extra, lambda x, p, y, c: (x, p, y, 1 - c))
     pieces = all_pieces(*weights)
     tokens = all_tokens(latent)
     keys, values = all_memory(memory)

time: 79.3 us -> 78.6 us (level)
  waiting for transfers between devices: 28.5 us -> 31.3 us
  starting transfers between devices: 35.4 us -> 33.8 us
  Pallas kernels: 12.2 us -> 11 us
    ppermute x26 -> x28, waiting for transfers between devices: 24.8 us -> 29.1 us  [moved(): return lax.ppermute(array, AXES, pairs)]
    ppermute x26 -> x28, starting transfers between devices: 31.2 us -> 29.5 us  [moved(): return lax.ppermute(array, AXES, pairs)]
    ppermute x5, waiting for transfers between devices: 3.75 us -> 2.2 us  [hop(): lax.ppermute(array, 'frame', [(i, i ^ bits) for i in range(lax.axis_size(...]
    pallas_call x6, Pallas kernels: 8.88 us -> 7.63 us  [kernel_call(): pl.pallas_call(kernel, out_shape=out_shape, in_specs=[free if number in a...]
  transfers between devices with their start and end apart: 31 -> 33, of which waited for: 8 -> 10; matrix products, arithmetic and copies ran while one was open for 2% -> 2% of each run, Pallas kernels for 2% -> 3%
where the time goes in v10:
time: 78.6 us; the launch traced here: 78.2 us
  starting transfers between devices  33.8 us (43%)
  waiting for transfers between devices  31.3 us (40%)
  Pallas kernels  11 us (14%)
  other arithmetic  1.73 us (2%)
    ppermute x28, starting transfers between devices, moved(): return lax.ppermute(array, AXES, pairs)  29.5 us
    ppermute x28, waiting for transfers between devices, moved(): return lax.ppermute(array, AXES, pairs)  29.1 us
    pallas_call x6, Pallas kernels, kernel_call(): pl.pallas_call(kernel, out_shape=out_shape, in_specs=[free if number in a...  7.63 us
    ppermute x5, starting transfers between devices, hop(): lax.ppermute(array, 'frame', [(i, i ^ bits) for i in range(lax.axis_size(...  4.36 us
    pallas_call x1, Pallas kernels, pack(): pl.pallas_call(pack_kernel, out_shape=out_shape, in_specs=[held] * 9, out...  3.33 us
    ppermute x5, waiting for transfers between devices, hop(): lax.ppermute(array, 'frame', [(i, i ^ bits) for i in range(lax.axis_size(...  2.2 us
  transfers between devices with their start and end apart: 33, of which 10 were waited for; matrix products, arithmetic and copies ran while one was open for 2% of the time, Pallas kernels for 3%

profile of v10, /device:TPU:1, one launch (start us, length us, event | category | flops | bytes accessed | tf_op | source)
XLA Modules:
  0.0 78.2 jit_solution(784604643012925677)
XLA Ops:
  0.0 3.3 %pack.1 = (bf16[96,1152]{1,0:T(8,128)(2,1)}, bf16[96,1152]{1,0:T(8,128)(2,1)}, bf16[96,1152]{1,0:T(8,128)(2,1)}, bf16[96,1152]{1,0:T(8,128)(2,1)}, f32[4,1536]{1...) custom-call(bf16[96,1536]{1,0:T(8,128)(2,1)} %w_query.1, ...), custom_call_target="tpu_custom_call" | custom-call | tf_op jit(solution)/shard_map/pack/pallas_call | solution.py:164
  3.3 0.1 collective-permute-start.8
  3.4 2.7 %collective-permute-start.9 = (bf16[4,8,2,384]{3,2,1,0:T(2,128)(2,1)}, bf16[4,8,2,384]{3,2,1,0:T(2,128)(2,1)S(1)}, u32[]{:S(2)}, u32[]{:S(2)}) collective-permute-start(bf16[4,8,2,384]{3,2,1,0:T(2,128)(2,1)} %get-tuple-element.24), channel_id=1, source_target_pairs={{0,2},{1,3},{2,0},{3,1},{4,6},{5,7},{6,4},{7,5},{8,10},{9,11},{10,... | collective-permute-start | bytes 147464 | tf_op jit(solution)/shard_map/ppermute | solution.py:228
  6.2 0.4 collective-permute-start.2
  6.5 0.2 collective-permute-start
  6.7 3.7 %collective-permute-start.15 = (bf16[96,1152]{1,0:T(8,128)(2,1)}, bf16[96,1152]{1,0:T(8,128)(2,1)S(1)}, u32[]{:S(2)}, u32[]{:S(2)}) collective-permute-start(bf16[96,1152]{1,0:T(8,128)(2,1)} %get-tuple-element.30), channel_id=1, source_target_pairs={{0,8},{1,11},{2,10},{3,9},{4,12},{5,15},{6,14},{7,13},{8,0},{9,3},... | collective-permute-start | bytes 663560 | tf_op jit(solution)/shard_map/ppermute | solution.py:36
  10.4 1.2 %collective-permute-start.14 = (bf16[96,1152]{1,0:T(8,128)(2,1)}, bf16[96,1152]{1,0:T(8,128)(2,1)S(1)}, u32[]{:S(2)}, u32[]{:S(2)}) collective-permute-start(bf16[96,1152]{1,0:T(8,128)(2,1)} %get-tuple-element.29), channel_id=1, source_target_pairs={{0,4},{1,7},{2,6},{3,5},{4,0},{5,3},{6,2},{7,1},{8,12},{9,15},{10,... | collective-permute-start | bytes 663560 | tf_op jit(solution)/shard_map/ppermute | solution.py:36
  11.6 1.1 %pad_maximum_fusion.1 = bf16[4,4,8,2,384]{4,3,2,1,0:T(2,128)(2,1)S(1)} fusion(bf16[1,4,8,2,384]{4,3,2,1,0:T(2,128)(2,1)S(1)} %bitcast.11, bf16[1,4,8,2,384]{4,3,2,1,0:T(2,128)(2,1)S(1)} %bitcast.10, bf16[1,4,8,2,384]{4,3,2,1,0:T(2,128)(2,1)S(1)} %bitcast.9, bf16[1,4,8,2,384]{4,3,2,1,0:T(2,128)(2,1)} %bitcast.8), kind=kLoop, calls=%fused_computation.2 | loop fusion | flops 294912 | bytes 393216 | tf_op jit(solution)/shard_map/stack | solution.py:218
  12.8 0.1 fusion.1
  12.9 0.2 collective-permute-start.11
  13.2 9.1 %collective-permute-done.14 = bf16[96,1152]{1,0:T(8,128)(2,1)S(1)} collective-permute-done((bf16[96,1152]{1,0:T(8,128)(2,1)}, bf16[96,1152]{1,0:T(8,128)(2,1)S(1)}, u32[]{:S(2)}, u32[]{:S(2)}) %collective-permute-start.14) | collective-permute-done | bytes 221216 | tf_op jit(solution)/shard_map/ppermute | solution.py:36
  22.4 0.1 collective-permute-start.16
  22.4 0.1 collective-permute-start.13
  22.5 1.4 %collective-permute-start.1 = (bf16[64,1536]{1,0:T(8,128)(2,1)}, bf16[64,1536]{1,0:T(8,128)(2,1)S(1)}, u32[]{:S(2)}, u32[]{:S(2)}) collective-permute-start(bf16[64,1536]{1,0:T(8,128)(2,1)} %refs_0_.1), channel_id=1, source_target_pairs={{0,2},{1,3},{2,0},{3,1},{4,6},{5,7},{6,4},{7,5},{8,10},{9,11},{10,... | collective-permute-start | bytes 589832 | tf_op jit(solution)/shard_map/ppermute | solution.py:36
  24.0 0.3 collective-permute-start.4
  24.3 3.1 %collective-permute-start.17 = (bf16[96,1152]{1,0:T(8,128)(2,1)}, bf16[96,1152]{1,0:T(8,128)(2,1)S(1)}, u32[]{:S(2)}, u32[]{:S(2)}) collective-permute-start(bf16[96,1152]{1,0:T(8,128)(2,1)} %get-tuple-element.29), channel_id=1, source_target_pairs={{0,12},{1,15},{2,14},{3,13},{4,8},{5,11},{6,10},{7,9},{8,4},{9,7},... | collective-permute-start | bytes 663560 | tf_op jit(solution)/shard_map/ppermute | solution.py:36
  27.4 6.0 %collective-permute-done.1.refs_1_ = bf16[64,1536]{1,0:T(8,128)(2,1)S(1)} collective-permute-done((bf16[64,1536]{1,0:T(8,128)(2,1)}, bf16[64,1536]{1,0:T(8,128)(2,1)S(1)}, u32[]{:S(2)}, u32[]{:S(2)}) %collective-permute-start.1) | collective-permute-done | bytes 196640 | tf_op jit(solution)/shard_map/ppermute | solution.py:36
  33.4 3.7 %collective-permute-start.19 = (bf16[96,1152]{1,0:T(8,128)(2,1)}, bf16[96,1152]{1,0:T(8,128)(2,1)S(1)}, u32[]{:S(2)}, u32[]{:S(2)}) collective-permute-start(bf16[96,1152]{1,0:T(8,128)(2,1)} %get-tuple-element.27.refs_0_.refs_1_), channel_id=1, source_target_pairs={{0,1},{1,0},{2,3},{3,2},{4,5},{5,4},{6,7},{7,6},{8,9},{9,8},{10,11... | collective-permute-start | bytes 663560 | tf_op jit(solution)/shard_map/ppermute | solution.py:36
  37.1 0.1 collective-permute-start.5
  37.2 0.3 fusion
  37.5 1.3 %collective-permute-start.12 = (bf16[8,1,8,2,384]{4,3,2,1,0:T(2,128)(2,1)S(1)}, bf16[8,1,8,2,384]{4,3,2,1,0:T(2,128)(2,1)S(1)}, u32[]{:S(2)}, u32[]{:S(2)}) collective-permute-start(bf16[8,1,8,2,384]{4,3,2,1,0:T(2,128)(2,1)S(1)} %get-tuple-element.38), channel_id=1, source_target_pairs={{0,8},{1,9},{2,10},{3,11},{4,12},{5,13},{6,14},{7,15},{8,0},{9,1},... | collective-permute-start | bytes 294920 | tf_op jit(solution)/shard_map/ppermute | solution.py:228
  38.8 1.0 %collective-permute-start.18 = (bf16[96,1152]{1,0:T(8,128)(2,1)S(1)}, bf16[96,1152]{1,0:T(8,128)(2,1)S(1)}, u32[]{:S(2)}, u32[]{:S(2)}) collective-permute-start(bf16[96,1152]{1,0:T(8,128)(2,1)S(1)} %collective-permute-done.17.refs_4_.refs_0_), channel_id=1, source_target_pairs={{0,16},{1,17},{2,18},{3,19},{4,20},{5,21},{6,22},{7,23},{8,24},{9,... | collective-permute-start | bytes 663560 | tf_op jit(solution)/shard_map/ppermute | solution.py:36
  39.7 2.2 %collective-permute-done.12 = bf16[8,1,8,2,384]{4,3,2,1,0:T(2,128)(2,1)S(1)} collective-permute-done((bf16[8,1,8,2,384]{4,3,2,1,0:T(2,128)(2,1)S(1)}, bf16[8,1,8,2,384]{4,3,2,1,0:T(2,128)(2,1)S(1)}, u32[]{:S(2)}, u32[]{:S(2)}) %collective-permute-start.12) | collective-permute-done | bytes 98336 | tf_op jit(solution)/shard_map/ppermute | solution.py:228
  41.9 4.0 %collective-permute-start.21 = (bf16[192,1152]{1,0:T(8,128)(2,1)S(1)}, bf16[192,1152]{1,0:T(8,128)(2,1)S(1)}, u32[]{:S(2)}, u32[]{:S(2)}) collective-permute-start(bf16[192,1152]{1,0:T(8,128)(2,1)S(1)} %constant_dynamic-update-slice_fusion.refs_2_.refs_3_), channel_id=1, source_target_pairs={{0,1},{1,0},{2,3},{3,2},{4,5},{5,4},{6,7},{7,6},{8,9},{9,8},{10,11... | collective-permute-start | bytes 1327112 | tf_op jit(solution)/shard_map/ppermute | solution.py:36
  45.9 0.5 collective-permute-start.6
  46.5 0.3 pad_maximum_fusion
  46.8 1.4 %collective-permute-done.6.refs_6_ = bf16[64,1536]{1,0:T(8,128)(2,1)S(1)} collective-permute-done((bf16[64,1536]{1,0:T(8,128)(2,1)S(1)}, bf16[64,1536]{1,0:T(8,128)(2,1)S(1)}, u32[]{:S(2)}, u32[]{:S(2)}) %collective-permute-start.6) | collective-permute-done | bytes 196640 | tf_op jit(solution)/shard_map/ppermute | solution.py:36
  48.2 0.4 collective-permute-start.23
  48.6 0.1 collective-permute-start.20
  48.8 0.4 collective-permute-start.24
  49.2 0.5 shard_map.100
  49.7 0.4 collective-permute-done.20.refs_7_.refs_6_
  50.1 1.2 %shard_map.102.part_ref = f32[256,1152]{1,0:T(8,128)S(1)} custom-call(bf16[256,1536]{1,0:T(8,128)(2,1)S(1)} %get-tuple-element.31.refs_0_.normed, bf16[96,1152]{1,0:T(8,128)(2,1)S(1)} %copy-done, bf16[96,1152]{1,0:T(8,128)(2,1)S(1)} %collective-permute-done.13.refs_1_.refs_2_, bf16[192,1152]{1,0:T(8,128)(2,1)S(1)} %constant_dynamic-update-slice_fusion.refs_2_.refs_3_, ...), custom_call_target="tpu_custom_call" | custom-call | flops 679477248 | bytes 3440640 | tf_op jit(solution)/shard_map/pallas_call | solution.py:408
  51.4 1.5 %shard_map.103.first_part = bf16[256,384]{1,0:T(8,128)(2,1)S(1)} custom-call(f32[4,1536]{1,0:T(4,128)S(1)} %get-tuple-element.21.extra_ref, bf16[128,384]{1,0:T(8,128)(2,1)S(1)} %get-tuple-element.42.key_ref, bf16[128,384]{1,0:T(8,128)(2,1)S(1)} %get-tuple-element.41.value_ref, bf16[256,1536]{1,0:T(8,128)(2,1)S(1)} %get-tuple-element.31.refs_0_.normed, ...), custom_call_target="tpu_custom_call" | custom-call | flops 377487360 | bytes 3072000 | tf_op jit(solution)/shard_map/pallas_call | solution.py:408
  52.9 1.4 %collective-permute-start.27 = (bf16[256,384]{1,0:T(8,128)(2,1)S(1)}, bf16[256,384]{1,0:T(8,128)(2,1)S(1)}, u32[]{:S(2)}, u32[]{:S(2)}) collective-permute-start(bf16[256,384]{1,0:T(8,128)(2,1)S(1)} %shard_map.103.first_part), channel_id=1, source_target_pairs={{0,2},{1,3},{2,0},{3,1},{4,6},{5,7},{6,4},{7,5},{8,10},{9,11},{10,... | collective-permute-start | bytes 589832 | tf_op jit(solution)/shard_map/ppermute | solution.py:36
  54.3 1.3 %collective-permute-start.25 = (bf16[256,384]{1,0:T(8,128)(2,1)S(1)}, bf16[256,384]{1,0:T(8,128)(2,1)S(1)}, u32[]{:S(2)}, u32[]{:S(2)}) collective-permute-start(bf16[256,384]{1,0:T(8,128)(2,1)S(1)} %shard_map.103.first_part), channel_id=1, source_target_pairs={{0,6},{1,7},{2,4},{3,5},{4,2},{5,3},{6,0},{7,1},{8,14},{9,15},{10,... | collective-permute-start | bytes 589832 | tf_op jit(solution)/shard_map/ppermute | solution.py:36
  55.6 0.3 shard_map.101.weights
  55.9 3.2 %collective-permute-done.27.fourth_part = bf16[256,384]{1,0:T(8,128)(2,1)S(1)} collective-permute-done((bf16[256,384]{1,0:T(8,128)(2,1)S(1)}, bf16[256,384]{1,0:T(8,128)(2,1)S(1)}, u32[]{:S(2)}, u32[]{:S(2)}) %collective-permute-start.27) | collective-permute-done | bytes 196640 | tf_op jit(solution)/shard_map/ppermute | solution.py:36
  59.1 1.0 %collective-permute-done.26.third_part = bf16[256,384]{1,0:T(8,128)(2,1)S(1)} collective-permute-done((bf16[256,384]{1,0:T(8,128)(2,1)S(1)}, bf16[256,384]{1,0:T(8,128)(2,1)S(1)}, u32[]{:S(2)}, u32[]{:S(2)}) %collective-permute-start.26) | collective-permute-done | bytes 196640 | tf_op jit(solution)/shard_map/ppermute | solution.py:36
  60.1 4.1 %collective-permute-done.25.second_part = bf16[256,384]{1,0:T(8,128)(2,1)S(1)} collective-permute-done((bf16[256,384]{1,0:T(8,128)(2,1)S(1)}, bf16[256,384]{1,0:T(8,128)(2,1)S(1)}, u32[]{:S(2)}, u32[]{:S(2)}) %collective-permute-start.25) | collective-permute-done | bytes 196640 | tf_op jit(solution)/shard_map/ppermute | solution.py:36
  64.2 3.4 %shard_map.104 = (bf16[128,384]{1,0:T(8,128)(2,1)S(1)}, bf16[128,384]{1,0:T(8,128)(2,1)S(1)}, bf16[128,384]{1,0:T(8,128)(2,1)S(1)}) custom-call(f32[4,1536]{1,0:T(4,128)S(1)} %get-tuple-element.21.extra_ref, bf16[128,384]{1,0:T(8,128)(2,1)S(1)} %get-tuple-element.42.key_ref, bf16[128,384]{1,0:T(8,128)(2,1)S(1)} %get-tuple-element.41.value_ref, ...), custom_call_target="tpu_custom_call" | custom-call | flops 1056964608 | bytes 5332992 | tf_op jit(solution)/shard_map/pallas_call | solution.py:408
  67.6 1.8 %collective-permute-start.28 = (bf16[128,384]{1,0:T(8,128)(2,1)S(1)}, bf16[128,384]{1,0:T(8,128)(2,1)S(1)}, u32[]{:S(2)}, u32[]{:S(2)}) collective-permute-start(bf16[128,384]{1,0:T(8,128)(2,1)S(1)} %get-tuple-element.33), channel_id=1, source_target_pairs={{0,2},{1,4},{2,0},{3,6},{4,1},{5,7},{6,3},{7,5},{8,10},{9,12},{10,... | collective-permute-start | bytes 294920 | tf_op jit(solution)/shard_map/ppermute | solution.py:36
  69.4 3.0 %collective-permute-start.29 = (bf16[128,384]{1,0:T(8,128)(2,1)S(1)}, bf16[128,384]{1,0:T(8,128)(2,1)S(1)}, u32[]{:S(2)}, u32[]{:S(2)}) collective-permute-start(bf16[128,384]{1,0:T(8,128)(2,1)S(1)} %get-tuple-element.34), channel_id=1, source_target_pairs={{1,6},{3,4},{4,3},{6,1},{9,14},{11,12},{12,11},{14,9},{17,22},{19,... | collective-permute-start | bytes 294920 | tf_op jit(solution)/shard_map/ppermute | solution.py:36
  72.4 0.1 collective-permute-start.30
  72.5 1.3 %collective-permute-start.31 = (bf16[128,384]{1,0:T(8,128)(2,1)S(1)}, bf16[128,384]{1,0:T(8,128)(2,1)S(1)}, u32[]{:S(2)}, u32[]{:S(2)}) collective-permute-start(bf16[128,384]{1,0:T(8,128)(2,1)S(1)} %collective-permute-done.28.first), channel_id=1, source_target_pairs={{0,1},{1,0},{2,3},{3,2},{4,5},{5,4},{6,7},{7,6},{8,9},{9,8},{10,11... | collective-permute-start | bytes 294920 | tf_op jit(solution)/shard_map/ppermute | solution.py:36
  73.8 2.5 %collective-permute-done.29.second = bf16[128,384]{1,0:T(8,128)(2,1)S(1)} collective-permute-done((bf16[128,384]{1,0:T(8,128)(2,1)S(1)}, bf16[128,384]{1,0:T(8,128)(2,1)S(1)}, u32[]{:S(2)}, u32[]{:S(2)}) %collective-permute-start.29) | collective-permute-done | bytes 98336 | tf_op jit(solution)/shard_map/ppermute | solution.py:36
  76.2 1.3 %collective-permute-done.32.other_second = bf16[128,384]{1,0:T(8,128)(2,1)S(1)} collective-permute-done((bf16[128,384]{1,0:T(8,128)(2,1)S(1)}, bf16[128,384]{1,0:T(8,128)(2,1)S(1)}, u32[]{:S(2)}, u32[]{:S(2)}) %collective-permute-start.32) | collective-permute-done | bytes 98336 | tf_op jit(solution)/shard_map/ppermute | solution.py:36
  77.5 0.7 shard_map.105
  (36 shorter events, 0.3 us)
Async XLA Ops:
  0.0 49.2 %copy-start.1 = (bf16[64,1536]{1,0:T(8,128)(2,1)S(1)}, bf16[64,1536]{1,0:T(8,128)(2,1)}, u32[]{:S(2)}) copy-start(bf16[64,1536]{1,0:T(8,128)(2,1)} %refs_0_.1) | copy-start | bytes 589828
  3.3 46.8 %copy-start = (bf16[96,1152]{1,0:T(8,128)(2,1)S(1)}, bf16[96,1152]{1,0:T(8,128)(2,1)}, u32[]{:S(2)}) copy-start(bf16[96,1152]{1,0:T(8,128)(2,1)} %get-tuple-element.27.refs_0_.refs_1_) | copy-start | bytes 663556
  3.3 3.4 %collective-permute-start.8 = (bf16[4,8,2,384]{3,2,1,0:T(2,128)(2,1)}, bf16[4,8,2,384]{3,2,1,0:T(2,128)(2,1)S(1)}, u32[]{:S(2)}, u32[]{:S(2)}) collective-permute-start(bf16[4,8,2,384]{3,2,1,0:T(2,128)(2,1)} %get-tuple-element.23), channel_id=1, source_target_pairs={{0,1},{1,0},{2,3},{3,2},{4,5},{5,4},{6,7},{7,6},{8,9},{9,8},{10,11... | collective-permute-start | bytes 147464 | tf_op jit(solution)/shard_map/ppermute | solution.py:228
  3.4 7.0 %collective-permute-start.9 = (bf16[4,8,2,384]{3,2,1,0:T(2,128)(2,1)}, bf16[4,8,2,384]{3,2,1,0:T(2,128)(2,1)S(1)}, u32[]{:S(2)}, u32[]{:S(2)}) collective-permute-start(bf16[4,8,2,384]{3,2,1,0:T(2,128)(2,1)} %get-tuple-element.24), channel_id=1, source_target_pairs={{0,2},{1,3},{2,0},{3,1},{4,6},{5,7},{6,4},{7,5},{8,10},{9,11},{10,... | collective-permute-start | bytes 147464 | tf_op jit(solution)/shard_map/ppermute | solution.py:228
  6.1 5.5 %collective-permute-start.10 = (bf16[4,8,2,384]{3,2,1,0:T(2,128)(2,1)}, bf16[4,8,2,384]{3,2,1,0:T(2,128)(2,1)S(1)}, u32[]{:S(2)}, u32[]{:S(2)}) collective-permute-start(bf16[4,8,2,384]{3,2,1,0:T(2,128)(2,1)} %get-tuple-element.25), channel_id=1, source_target_pairs={{0,3},{1,2},{2,1},{3,0},{4,7},{5,6},{6,5},{7,4},{8,11},{9,10},{10,... | collective-permute-start | bytes 147464 | tf_op jit(solution)/shard_map/ppermute | solution.py:228
  6.2 18.1 %collective-permute-start.2 = (bf16[64,1536]{1,0:T(8,128)(2,1)}, bf16[64,1536]{1,0:T(8,128)(2,1)S(1)}, u32[]{:S(2)}, u32[]{:S(2)}) collective-permute-start(bf16[64,1536]{1,0:T(8,128)(2,1)} %refs_0_.1), channel_id=1, source_target_pairs={{0,1},{1,0},{2,3},{3,2},{4,5},{5,4},{6,7},{7,6},{8,9},{9,8},{10,11... | collective-permute-start | bytes 589832 | tf_op jit(solution)/shard_map/ppermute | solution.py:36
  6.5 16.0 %collective-permute-start = (f32[4,1536]{1,0:T(4,128)}, f32[4,1536]{1,0:T(4,128)S(1)}, u32[]{:S(2)}, u32[]{:S(2)}) collective-permute-start(f32[4,1536]{1,0:T(4,128)} %get-tuple-element.20), channel_id=1, source_target_pairs={{0,1},{1,0},{2,3},{3,2},{4,5},{5,4},{6,7},{7,6},{8,9},{9,8},{10,11... | collective-permute-start | bytes 73736 | tf_op jit(solution)/shard_map/ppermute | solution.py:36
  6.7 15.6 %collective-permute-start.15 = (bf16[96,1152]{1,0:T(8,128)(2,1)}, bf16[96,1152]{1,0:T(8,128)(2,1)S(1)}, u32[]{:S(2)}, u32[]{:S(2)}) collective-permute-start(bf16[96,1152]{1,0:T(8,128)(2,1)} %get-tuple-element.30), channel_id=1, source_target_pairs={{0,8},{1,11},{2,10},{3,9},{4,12},{5,15},{6,14},{7,13},{8,0},{9,3},... | collective-permute-start | bytes 663560 | tf_op jit(solution)/shard_map/ppermute | solution.py:36
  10.4 11.9 %collective-permute-start.14 = (bf16[96,1152]{1,0:T(8,128)(2,1)}, bf16[96,1152]{1,0:T(8,128)(2,1)S(1)}, u32[]{:S(2)}, u32[]{:S(2)}) collective-permute-start(bf16[96,1152]{1,0:T(8,128)(2,1)} %get-tuple-element.29), channel_id=1, source_target_pairs={{0,4},{1,7},{2,6},{3,5},{4,0},{5,3},{6,2},{7,1},{8,12},{9,15},{10,... | collective-permute-start | bytes 663560 | tf_op jit(solution)/shard_map/ppermute | solution.py:36
  12.9 11.0 %collective-permute-start.11 = (bf16[4,2,8,2,384]{4,3,2,1,0:T(2,128)(2,1)S(1)}, bf16[4,2,8,2,384]{4,3,2,1,0:T(2,128)(2,1)S(1)}, u32[]{:S(2)}, u32[]{:S(2)}) collective-permute-start(bf16[4,2,8,2,384]{4,3,2,1,0:T(2,128)(2,1)S(1)} %get-tuple-element.40), channel_id=1, source_target_pairs={{0,4},{1,5},{2,6},{3,7},{4,0},{5,1},{6,2},{7,3},{8,12},{9,13},{10,... | collective-permute-start | bytes 294920 | tf_op jit(solution)/shard_map/ppermute | solution.py:228
  22.4 23.5 %collective-permute-start.16 = (bf16[192,1152]{1,0:T(8,128)(2,1)S(1)}, bf16[192,1152]{1,0:T(8,128)(2,1)S(1)}, u32[]{:S(2)}, u32[]{:S(2)}) collective-permute-start(bf16[192,1152]{1,0:T(8,128)(2,1)S(1)} %constant_dynamic-update-slice_fusion.refs_2_.refs_3_), channel_id=1, source_target_pairs={{0,16},{1,17},{2,18},{3,19},{4,20},{5,21},{6,22},{7,23},{8,24},{9,... | collective-permute-start | bytes 1327112 | tf_op jit(solution)/shard_map/ppermute | solution.py:36
  22.4 14.7 %collective-permute-start.13 = (bf16[96,1152]{1,0:T(8,128)(2,1)}, bf16[96,1152]{1,0:T(8,128)(2,1)S(1)}, u32[]{:S(2)}, u32[]{:S(2)}) collective-permute-start(bf16[96,1152]{1,0:T(8,128)(2,1)} %get-tuple-element.28), channel_id=1, source_target_pairs={{0,2},{1,3},{2,0},{3,1},{4,6},{5,7},{6,4},{7,5},{8,10},{9,11},{10,... | collective-permute-start | bytes 663560 | tf_op jit(solution)/shard_map/ppermute | solution.py:36
  22.5 10.9 %collective-permute-start.1 = (bf16[64,1536]{1,0:T(8,128)(2,1)}, bf16[64,1536]{1,0:T(8,128)(2,1)S(1)}, u32[]{:S(2)}, u32[]{:S(2)}) collective-permute-start(bf16[64,1536]{1,0:T(8,128)(2,1)} %refs_0_.1), channel_id=1, source_target_pairs={{0,2},{1,3},{2,0},{3,1},{4,6},{5,7},{6,4},{7,5},{8,10},{9,11},{10,... | collective-permute-start | bytes 589832 | tf_op jit(solution)/shard_map/ppermute | solution.py:36
  24.0 13.2 %collective-permute-start.4 = (bf16[64,1536]{1,0:T(8,128)(2,1)}, bf16[64,1536]{1,0:T(8,128)(2,1)S(1)}, u32[]{:S(2)}, u32[]{:S(2)}) collective-permute-start(bf16[64,1536]{1,0:T(8,128)(2,1)} %refs_0_.1), channel_id=1, source_target_pairs={{0,4},{1,5},{2,6},{3,7},{4,0},{5,1},{6,2},{7,3},{8,12},{9,13},{10,... | collective-permute-start | bytes 589832 | tf_op jit(solution)/shard_map/ppermute | solution.py:36
  24.3 13.2 %collective-permute-start.17 = (bf16[96,1152]{1,0:T(8,128)(2,1)}, bf16[96,1152]{1,0:T(8,128)(2,1)S(1)}, u32[]{:S(2)}, u32[]{:S(2)}) collective-permute-start(bf16[96,1152]{1,0:T(8,128)(2,1)} %get-tuple-element.29), channel_id=1, source_target_pairs={{0,12},{1,15},{2,14},{3,13},{4,8},{5,11},{6,10},{7,9},{8,4},{9,7},... | collective-permute-start | bytes 663560 | tf_op jit(solution)/shard_map/ppermute | solution.py:36
  33.4 5.4 %collective-permute-start.19 = (bf16[96,1152]{1,0:T(8,128)(2,1)}, bf16[96,1152]{1,0:T(8,128)(2,1)S(1)}, u32[]{:S(2)}, u32[]{:S(2)}) collective-permute-start(bf16[96,1152]{1,0:T(8,128)(2,1)} %get-tuple-element.27.refs_0_.refs_1_), channel_id=1, source_target_pairs={{0,1},{1,0},{2,3},{3,2},{4,5},{5,4},{6,7},{7,6},{8,9},{9,8},{10,11... | collective-permute-start | bytes 663560 | tf_op jit(solution)/shard_map/ppermute | solution.py:36
  37.1 8.8 %collective-permute-start.3 = (bf16[64,1536]{1,0:T(8,128)(2,1)S(1)}, bf16[64,1536]{1,0:T(8,128)(2,1)S(1)}, u32[]{:S(2)}, u32[]{:S(2)}) collective-permute-start(bf16[64,1536]{1,0:T(8,128)(2,1)S(1)} %collective-permute-done.1.refs_1_), channel_id=1, source_target_pairs={{0,1},{1,0},{2,3},{3,2},{4,5},{5,4},{6,7},{7,6},{8,9},{9,8},{10,11... | collective-permute-start | bytes 589832 | tf_op jit(solution)/shard_map/ppermute | solution.py:36
  37.1 9.3 %collective-permute-start.5 = (bf16[64,1536]{1,0:T(8,128)(2,1)S(1)}, bf16[64,1536]{1,0:T(8,128)(2,1)S(1)}, u32[]{:S(2)}, u32[]{:S(2)}) collective-permute-start(bf16[64,1536]{1,0:T(8,128)(2,1)S(1)} %collective-permute-done.4.refs_4_), channel_id=1, source_target_pairs={{0,2},{1,3},{2,0},{3,1},{4,6},{5,7},{6,4},{7,5},{8,10},{9,11},{10,... | collective-permute-start | bytes 589832 | tf_op jit(solution)/shard_map/ppermute | solution.py:36
  37.5 4.4 %collective-permute-start.12 = (bf16[8,1,8,2,384]{4,3,2,1,0:T(2,128)(2,1)S(1)}, bf16[8,1,8,2,384]{4,3,2,1,0:T(2,128)(2,1)S(1)}, u32[]{:S(2)}, u32[]{:S(2)}) collective-permute-start(bf16[8,1,8,2,384]{4,3,2,1,0:T(2,128)(2,1)S(1)} %get-tuple-element.38), channel_id=1, source_target_pairs={{0,8},{1,9},{2,10},{3,11},{4,12},{5,13},{6,14},{7,15},{8,0},{9,1},... | collective-permute-start | bytes 294920 | tf_op jit(solution)/shard_map/ppermute | solution.py:228
  38.8 9.8 %collective-permute-start.18 = (bf16[96,1152]{1,0:T(8,128)(2,1)S(1)}, bf16[96,1152]{1,0:T(8,128)(2,1)S(1)}, u32[]{:S(2)}, u32[]{:S(2)}) collective-permute-start(bf16[96,1152]{1,0:T(8,128)(2,1)S(1)} %collective-permute-done.17.refs_4_.refs_0_), channel_id=1, source_target_pairs={{0,16},{1,17},{2,18},{3,19},{4,20},{5,21},{6,22},{7,23},{8,24},{9,... | collective-permute-start | bytes 663560 | tf_op jit(solution)/shard_map/ppermute | solution.py:36
  41.9 8.2 %collective-permute-start.21 = (bf16[192,1152]{1,0:T(8,128)(2,1)S(1)}, bf16[192,1152]{1,0:T(8,128)(2,1)S(1)}, u32[]{:S(2)}, u32[]{:S(2)}) collective-permute-start(bf16[192,1152]{1,0:T(8,128)(2,1)S(1)} %constant_dynamic-update-slice_fusion.refs_2_.refs_3_), channel_id=1, source_target_pairs={{0,1},{1,0},{2,3},{3,2},{4,5},{5,4},{6,7},{7,6},{8,9},{9,8},{10,11... | collective-permute-start | bytes 1327112 | tf_op jit(solution)/shard_map/ppermute | solution.py:36
  45.9 4.2 %collective-permute-start.22 = (bf16[192,1152]{1,0:T(8,128)(2,1)S(1)}, bf16[192,1152]{1,0:T(8,128)(2,1)S(1)}, u32[]{:S(2)}, u32[]{:S(2)}) collective-permute-start(bf16[192,1152]{1,0:T(8,128)(2,1)S(1)} %collective-permute-done.16.refs_3_.refs_4_), channel_id=1, source_target_pairs={{0,1},{1,0},{2,3},{3,2},{4,5},{5,4},{6,7},{7,6},{8,9},{9,8},{10,11... | collective-permute-start | bytes 1327112 | tf_op jit(solution)/shard_map/ppermute | solution.py:36
  45.9 2.3 %collective-permute-start.6 = (bf16[64,1536]{1,0:T(8,128)(2,1)S(1)}, bf16[64,1536]{1,0:T(8,128)(2,1)S(1)}, u32[]{:S(2)}, u32[]{:S(2)}) collective-permute-start(bf16[64,1536]{1,0:T(8,128)(2,1)S(1)} %collective-permute-done.4.refs_4_), channel_id=1, source_target_pairs={{0,1},{1,0},{2,3},{3,2},{4,5},{5,4},{6,7},{7,6},{8,9},{9,8},{10,11... | collective-permute-start | bytes 589832 | tf_op jit(solution)/shard_map/ppermute | solution.py:36
  46.4 2.3 %collective-permute-start.7 = (bf16[64,1536]{1,0:T(8,128)(2,1)S(1)}, bf16[64,1536]{1,0:T(8,128)(2,1)S(1)}, u32[]{:S(2)}, u32[]{:S(2)}) collective-permute-start(bf16[64,1536]{1,0:T(8,128)(2,1)S(1)} %collective-permute-done.5.refs_5_), channel_id=1, source_target_pairs={{0,1},{1,0},{2,3},{3,2},{4,5},{5,4},{6,7},{7,6},{8,9},{9,8},{10,11... | collective-permute-start | bytes 589832 | tf_op jit(solution)/shard_map/ppermute | solution.py:36
  48.2 3.1 %collective-permute-start.23 = (bf16[96,1152]{1,0:T(8,128)(2,1)S(1)}, bf16[96,1152]{1,0:T(8,128)(2,1)S(1)}, u32[]{:S(2)}, u32[]{:S(2)}) collective-permute-start(bf16[96,1152]{1,0:T(8,128)(2,1)S(1)} %collective-permute-done.17.refs_4_.refs_0_), channel_id=1, source_target_pairs={{0,1},{1,0},{2,3},{3,2},{4,5},{5,4},{6,7},{7,6},{8,9},{9,8},{10,11... | collective-permute-start | bytes 663560 | tf_op jit(solution)/shard_map/ppermute | solution.py:36
  48.6 1.5 %collective-permute-start.20 = (bf16[96,1152]{1,0:T(8,128)(2,1)S(1)}, bf16[96,1152]{1,0:T(8,128)(2,1)S(1)}, u32[]{:S(2)}, u32[]{:S(2)}) collective-permute-start(bf16[96,1152]{1,0:T(8,128)(2,1)S(1)} %collective-permute-done.13.refs_1_.refs_2_), channel_id=1, source_target_pairs={{0,1},{1,0},{2,3},{3,2},{4,5},{5,4},{6,7},{7,6},{8,9},{9,8},{10,11... | collective-permute-start | bytes 663560 | tf_op jit(solution)/shard_map/ppermute | solution.py:36
  48.8 2.6 %collective-permute-start.24 = (bf16[96,1152]{1,0:T(8,128)(2,1)S(1)}, bf16[96,1152]{1,0:T(8,128)(2,1)S(1)}, u32[]{:S(2)}, u32[]{:S(2)}) collective-permute-start(bf16[96,1152]{1,0:T(8,128)(2,1)S(1)} %collective-permute-done.18.refs_5_.refs_1_), channel_id=1, source_target_pairs={{0,1},{1,0},{2,3},{3,2},{4,5},{5,4},{6,7},{7,6},{8,9},{9,8},{10,11... | collective-permute-start | bytes 663560 | tf_op jit(solution)/shard_map/ppermute | solution.py:36
  52.9 6.2 %collective-permute-start.27 = (bf16[256,384]{1,0:T(8,128)(2,1)S(1)}, bf16[256,384]{1,0:T(8,128)(2,1)S(1)}, u32[]{:S(2)}, u32[]{:S(2)}) collective-permute-start(bf16[256,384]{1,0:T(8,128)(2,1)S(1)} %shard_map.103.first_part), channel_id=1, source_target_pairs={{0,2},{1,3},{2,0},{3,1},{4,6},{5,7},{6,4},{7,5},{8,10},{9,11},{10,... | collective-permute-start | bytes 589832 | tf_op jit(solution)/shard_map/ppermute | solution.py:36
  54.3 5.9 %collective-permute-start.26 = (bf16[256,384]{1,0:T(8,128)(2,1)S(1)}, bf16[256,384]{1,0:T(8,128)(2,1)S(1)}, u32[]{:S(2)}, u32[]{:S(2)}) collective-permute-start(bf16[256,384]{1,0:T(8,128)(2,1)S(1)} %shard_map.103.first_part), channel_id=1, source_target_pairs={{0,4},{1,5},{2,6},{3,7},{4,0},{5,1},{6,2},{7,3},{8,12},{9,13},{10,... | collective-permute-start | bytes 589832 | tf_op jit(solution)/shard_map/ppermute | solution.py:36
  54.3 9.9 %collective-permute-start.25 = (bf16[256,384]{1,0:T(8,128)(2,1)S(1)}, bf16[256,384]{1,0:T(8,128)(2,1)S(1)}, u32[]{:S(2)}, u32[]{:S(2)}) collective-permute-start(bf16[256,384]{1,0:T(8,128)(2,1)S(1)} %shard_map.103.first_part), channel_id=1, source_target_pairs={{0,6},{1,7},{2,4},{3,5},{4,2},{5,3},{6,0},{7,1},{8,14},{9,15},{10,... | collective-permute-start | bytes 589832 | tf_op jit(solution)/shard_map/ppermute | solution.py:36
  67.6 4.8 %collective-permute-start.28 = (bf16[128,384]{1,0:T(8,128)(2,1)S(1)}, bf16[128,384]{1,0:T(8,128)(2,1)S(1)}, u32[]{:S(2)}, u32[]{:S(2)}) collective-permute-start(bf16[128,384]{1,0:T(8,128)(2,1)S(1)} %get-tuple-element.33), channel_id=1, source_target_pairs={{0,2},{1,4},{2,0},{3,6},{4,1},{5,7},{6,3},{7,5},{8,10},{9,12},{10,... | collective-permute-start | bytes 294920 | tf_op jit(solution)/shard_map/ppermute | solution.py:36
  69.4 6.8 %collective-permute-start.29 = (bf16[128,384]{1,0:T(8,128)(2,1)S(1)}, bf16[128,384]{1,0:T(8,128)(2,1)S(1)}, u32[]{:S(2)}, u32[]{:S(2)}) collective-permute-start(bf16[128,384]{1,0:T(8,128)(2,1)S(1)} %get-tuple-element.34), channel_id=1, source_target_pairs={{1,6},{3,4},{4,3},{6,1},{9,14},{11,12},{12,11},{14,9},{17,22},{19,... | collective-permute-start | bytes 294920 | tf_op jit(solution)/shard_map/ppermute | solution.py:36
  72.4 3.8 %collective-permute-start.30 = (bf16[128,384]{1,0:T(8,128)(2,1)S(1)}, bf16[128,384]{1,0:T(8,128)(2,1)S(1)}, u32[]{:S(2)}, u32[]{:S(2)}) collective-permute-start(bf16[128,384]{1,0:T(8,128)(2,1)S(1)} %get-tuple-element.32.keep), channel_id=1, source_target_pairs={{0,1},{1,0},{2,3},{3,2},{4,5},{5,4},{6,7},{7,6},{8,9},{9,8},{10,11... | collective-permute-start | bytes 294920 | tf_op jit(solution)/shard_map/ppermute | solution.py:36
  72.5 3.7 %collective-permute-start.31 = (bf16[128,384]{1,0:T(8,128)(2,1)S(1)}, bf16[128,384]{1,0:T(8,128)(2,1)S(1)}, u32[]{:S(2)}, u32[]{:S(2)}) collective-permute-start(bf16[128,384]{1,0:T(8,128)(2,1)S(1)} %collective-permute-done.28.first), channel_id=1, source_target_pairs={{0,1},{1,0},{2,3},{3,2},{4,5},{5,4},{6,7},{7,6},{8,9},{9,8},{10,11... | collective-permute-start | bytes 294920 | tf_op jit(solution)/shard_map/ppermute | solution.py:36
  76.2 1.3 %collective-permute-start.32 = (bf16[128,384]{1,0:T(8,128)(2,1)S(1)}, bf16[128,384]{1,0:T(8,128)(2,1)S(1)}, u32[]{:S(2)}, u32[]{:S(2)}) collective-permute-start(bf16[128,384]{1,0:T(8,128)(2,1)S(1)} %collective-permute-done.29.second), channel_id=1, source_target_pairs={{0,1},{1,0},{2,3},{3,2},{4,5},{5,4},{6,7},{7,6},{8,9},{9,8},{10,11... | collective-permute-start | bytes 294920 | tf_op jit(solution)/shard_map/ppermute | solution.py:36

commit v11 on v9

--- a/solution.py
+++ b/solution.py
@@ -126,7 +126,7 @@
     extra[0:1, :] = gain[...].reshape(row)
     for number in range(STEPS):
         extra[1 + number : 2 + number, :] = jnp.full(row, scale_ref[number], jnp.float32)
-    live = lax.broadcasted_iota(jnp.int32, row, 1) % entries < count_ref[(plane // 2) * 2 + c]
+    live = lax.broadcasted_iota(jnp.int32, row, 1) % entries < count_ref[(plane // 2) * 2 + 1 - c]
     extra[1 + STEPS : 2 + STEPS, :] = jnp.where(live, 1.0, 0.0)
     gives.append(pltpu.make_async_copy(extra, extra_ref, scalar_sem.at[5]))
     gives[-1].start()
@@ -271,6 +271,7 @@
 
 
 BLOCK = 32
+ATTENTION_BLOCKS = 1
 
 
 def prepare_kernel(extra_ref, *refs):
@@ -315,7 +316,7 @@
     live = extra_ref[3:4, :mem_rows] > 0.5
     contract_last = (((1,), (1,)), ((), ()))
     frame_rows = projected.shape[0]
-    half = frame_rows // 2
+    half = frame_rows // ATTENTION_BLOCKS
     for head in range(head_count):
         span = slice(head * head_size, (head + 1) * head_size)
         keys = projected[:, width + head * head_size : width + (head + 1) * head_size]
@@ -547,6 +548,7 @@
     weights, extra, memory = pack(
         w_query, w_key, w_value, intersection, slot_of, counts, step_scale, norm_gain, mem_cache
     )
+    extra = moved(extra, lambda x, p, y, c: (x, p, y, 1 - c))
     pieces = all_pieces(*weights)
     tokens = all_tokens(latent)
     keys, values = all_memory(memory)

time: 79.3 us -> 77.9 us (0.982)
  Pallas kernels: 12.2 us -> 11 us
    ppermute x26 -> x27, waiting for transfers between devices: 24.8 us -> 27 us  [moved(): return lax.ppermute(array, AXES, pairs)]
    ppermute x5, waiting for transfers between devices: 3.75 us -> 2.2 us  [hop(): lax.ppermute(array, 'frame', [(i, i ^ bits) for i in range(lax.axis_size(...]
    pallas_call x6, Pallas kernels: 8.88 us -> 7.63 us  [kernel_call(): pl.pallas_call(kernel, out_shape=out_shape, in_specs=[free if number in a...]
    ppermute x26 -> x27, starting transfers between devices: 31.2 us -> 30.9 us  [moved(): return lax.ppermute(array, AXES, pairs)]
  transfers between devices with their start and end apart: 31 -> 32, of which waited for: 8 -> 9; matrix products, arithmetic and copies ran while one was open for 2% -> 2% of each run, Pallas kernels for 2% -> 3%
where the time goes in v11:
time: 77.9 us; the launch traced here: 77.7 us
  starting transfers between devices  35.3 us (45%)
  waiting for transfers between devices  29.2 us (37%)
  Pallas kernels  11 us (14%)
  other arithmetic  1.73 us (2%)
    ppermute x27, starting transfers between devices, moved(): return lax.ppermute(array, AXES, pairs)  30.9 us
    ppermute x27, waiting for transfers between devices, moved(): return lax.ppermute(array, AXES, pairs)  27 us
    pallas_call x6, Pallas kernels, kernel_call(): pl.pallas_call(kernel, out_shape=out_shape, in_specs=[free if number in a...  7.63 us
    ppermute x5, starting transfers between devices, hop(): lax.ppermute(array, 'frame', [(i, i ^ bits) for i in range(lax.axis_size(...  4.36 us
    pallas_call x1, Pallas kernels, pack(): pl.pallas_call(pack_kernel, out_shape=out_shape, in_specs=[held] * 9, out...  3.33 us
    ppermute x5, waiting for transfers between devices, hop(): lax.ppermute(array, 'frame', [(i, i ^ bits) for i in range(lax.axis_size(...  2.2 us
  transfers between devices with their start and end apart: 32, of which 9 were waited for; matrix products, arithmetic and copies ran while one was open for 2% of the time, Pallas kernels for 3%

profile of v11, /device:TPU:1, one launch (start us, length us, event | category | flops | bytes accessed | tf_op | source)
XLA Modules:
  0.0 77.7 jit_solution(3800338647869902184)
XLA Ops:
  0.0 3.3 %pack.1 = (bf16[96,1152]{1,0:T(8,128)(2,1)}, bf16[96,1152]{1,0:T(8,128)(2,1)}, bf16[96,1152]{1,0:T(8,128)(2,1)}, bf16[96,1152]{1,0:T(8,128)(2,1)}, f32[4,1536]{1...) custom-call(bf16[96,1536]{1,0:T(8,128)(2,1)} %w_query.1, ...), custom_call_target="tpu_custom_call" | custom-call | tf_op jit(solution)/shard_map/pack/pallas_call | solution.py:164
  3.4 0.1 collective-permute-start.8
  3.4 2.7 %collective-permute-start.9 = (bf16[4,8,2,384]{3,2,1,0:T(2,128)(2,1)}, bf16[4,8,2,384]{3,2,1,0:T(2,128)(2,1)S(1)}, u32[]{:S(2)}, u32[]{:S(2)}) collective-permute-start(bf16[4,8,2,384]{3,2,1,0:T(2,128)(2,1)} %get-tuple-element.26), channel_id=1, source_target_pairs={{0,2},{1,3},{2,0},{3,1},{4,6},{5,7},{6,4},{7,5},{8,10},{9,11},{10,... | collective-permute-start | bytes 147464 | tf_op jit(solution)/shard_map/ppermute | solution.py:228
  6.2 0.0 collective-permute-start.10
  6.2 0.4 collective-permute-start.2
  6.6 0.2 collective-permute-start
  6.7 3.7 %collective-permute-start.15 = (bf16[96,1152]{1,0:T(8,128)(2,1)}, bf16[96,1152]{1,0:T(8,128)(2,1)S(1)}, u32[]{:S(2)}, u32[]{:S(2)}) collective-permute-start(bf16[96,1152]{1,0:T(8,128)(2,1)} %get-tuple-element.32), channel_id=1, source_target_pairs={{0,8},{1,11},{2,10},{3,9},{4,12},{5,15},{6,14},{7,13},{8,0},{9,3},... | collective-permute-start | bytes 663560 | tf_op jit(solution)/shard_map/ppermute | solution.py:36
  10.4 1.2 %collective-permute-start.14 = (bf16[96,1152]{1,0:T(8,128)(2,1)}, bf16[96,1152]{1,0:T(8,128)(2,1)S(1)}, u32[]{:S(2)}, u32[]{:S(2)}) collective-permute-start(bf16[96,1152]{1,0:T(8,128)(2,1)} %get-tuple-element.31), channel_id=1, source_target_pairs={{0,4},{1,7},{2,6},{3,5},{4,0},{5,3},{6,2},{7,1},{8,12},{9,15},{10,... | collective-permute-start | bytes 663560 | tf_op jit(solution)/shard_map/ppermute | solution.py:36
  11.7 1.1 %pad_maximum_fusion.1 = bf16[4,4,8,2,384]{4,3,2,1,0:T(2,128)(2,1)S(1)} fusion(bf16[1,4,8,2,384]{4,3,2,1,0:T(2,128)(2,1)S(1)} %bitcast.11, bf16[1,4,8,2,384]{4,3,2,1,0:T(2,128)(2,1)S(1)} %bitcast.10, bf16[1,4,8,2,384]{4,3,2,1,0:T(2,128)(2,1)S(1)} %bitcast.9, bf16[1,4,8,2,384]{4,3,2,1,0:T(2,128)(2,1)} %bitcast.8), kind=kLoop, calls=%fused_computation.2 | loop fusion | flops 294912 | bytes 393216 | tf_op jit(solution)/shard_map/stack | solution.py:218
  12.8 0.1 fusion.1
  12.9 0.2 collective-permute-start.11
  13.2 9.1 %collective-permute-done.14 = bf16[96,1152]{1,0:T(8,128)(2,1)S(1)} collective-permute-done((bf16[96,1152]{1,0:T(8,128)(2,1)}, bf16[96,1152]{1,0:T(8,128)(2,1)S(1)}, u32[]{:S(2)}, u32[]{:S(2)}) %collective-permute-start.14) | collective-permute-done | bytes 221216 | tf_op jit(solution)/shard_map/ppermute | solution.py:36
  22.4 0.1 collective-permute-start.16
  22.4 0.1 collective-permute-start.13
  22.5 1.4 %collective-permute-start.1 = (bf16[64,1536]{1,0:T(8,128)(2,1)}, bf16[64,1536]{1,0:T(8,128)(2,1)S(1)}, u32[]{:S(2)}, u32[]{:S(2)}) collective-permute-start(bf16[64,1536]{1,0:T(8,128)(2,1)} %refs_0_.1), channel_id=1, source_target_pairs={{0,2},{1,3},{2,0},{3,1},{4,6},{5,7},{6,4},{7,5},{8,10},{9,11},{10,... | collective-permute-start | bytes 589832 | tf_op jit(solution)/shard_map/ppermute | solution.py:36
  24.0 0.3 collective-permute-start.4
  24.3 3.1 %collective-permute-start.17 = (bf16[96,1152]{1,0:T(8,128)(2,1)}, bf16[96,1152]{1,0:T(8,128)(2,1)S(1)}, u32[]{:S(2)}, u32[]{:S(2)}) collective-permute-start(bf16[96,1152]{1,0:T(8,128)(2,1)} %get-tuple-element.31), channel_id=1, source_target_pairs={{0,12},{1,15},{2,14},{3,13},{4,8},{5,11},{6,10},{7,9},{8,4},{9,7},... | collective-permute-start | bytes 663560 | tf_op jit(solution)/shard_map/ppermute | solution.py:36
  27.4 6.0 %collective-permute-done.1.refs_1_ = bf16[64,1536]{1,0:T(8,128)(2,1)S(1)} collective-permute-done((bf16[64,1536]{1,0:T(8,128)(2,1)}, bf16[64,1536]{1,0:T(8,128)(2,1)S(1)}, u32[]{:S(2)}, u32[]{:S(2)}) %collective-permute-start.1) | collective-permute-done | bytes 196640 | tf_op jit(solution)/shard_map/ppermute | solution.py:36
  33.4 3.7 %collective-permute-start.19 = (bf16[96,1152]{1,0:T(8,128)(2,1)}, bf16[96,1152]{1,0:T(8,128)(2,1)S(1)}, u32[]{:S(2)}, u32[]{:S(2)}) collective-permute-start(bf16[96,1152]{1,0:T(8,128)(2,1)} %get-tuple-element.29.refs_0_.refs_1_), channel_id=1, source_target_pairs={{0,1},{1,0},{2,3},{3,2},{4,5},{5,4},{6,7},{7,6},{8,9},{9,8},{10,11... | collective-permute-start | bytes 663560 | tf_op jit(solution)/shard_map/ppermute | solution.py:36
  37.2 0.1 collective-permute-start.5
  37.2 0.3 fusion
  37.5 1.3 %collective-permute-start.12 = (bf16[8,1,8,2,384]{4,3,2,1,0:T(2,128)(2,1)S(1)}, bf16[8,1,8,2,384]{4,3,2,1,0:T(2,128)(2,1)S(1)}, u32[]{:S(2)}, u32[]{:S(2)}) collective-permute-start(bf16[8,1,8,2,384]{4,3,2,1,0:T(2,128)(2,1)S(1)} %get-tuple-element.42), channel_id=1, source_target_pairs={{0,8},{1,9},{2,10},{3,11},{4,12},{5,13},{6,14},{7,15},{8,0},{9,1},... | collective-permute-start | bytes 294920 | tf_op jit(solution)/shard_map/ppermute | solution.py:228
  38.8 1.0 %collective-permute-start.18 = (bf16[96,1152]{1,0:T(8,128)(2,1)S(1)}, bf16[96,1152]{1,0:T(8,128)(2,1)S(1)}, u32[]{:S(2)}, u32[]{:S(2)}) collective-permute-start(bf16[96,1152]{1,0:T(8,128)(2,1)S(1)} %collective-permute-done.17.refs_4_.refs_0_), channel_id=1, source_target_pairs={{0,16},{1,17},{2,18},{3,19},{4,20},{5,21},{6,22},{7,23},{8,24},{9,... | collective-permute-start | bytes 663560 | tf_op jit(solution)/shard_map/ppermute | solution.py:36
  39.7 2.2 %collective-permute-done.12 = bf16[8,1,8,2,384]{4,3,2,1,0:T(2,128)(2,1)S(1)} collective-permute-done((bf16[8,1,8,2,384]{4,3,2,1,0:T(2,128)(2,1)S(1)}, bf16[8,1,8,2,384]{4,3,2,1,0:T(2,128)(2,1)S(1)}, u32[]{:S(2)}, u32[]{:S(2)}) %collective-permute-start.12) | collective-permute-done | bytes 98336 | tf_op jit(solution)/shard_map/ppermute | solution.py:228
  41.9 4.0 %collective-permute-start.21 = (bf16[192,1152]{1,0:T(8,128)(2,1)S(1)}, bf16[192,1152]{1,0:T(8,128)(2,1)S(1)}, u32[]{:S(2)}, u32[]{:S(2)}) collective-permute-start(bf16[192,1152]{1,0:T(8,128)(2,1)S(1)} %constant_dynamic-update-slice_fusion.refs_2_.refs_3_), channel_id=1, source_target_pairs={{0,1},{1,0},{2,3},{3,2},{4,5},{5,4},{6,7},{7,6},{8,9},{9,8},{10,11... | collective-permute-start | bytes 1327112 | tf_op jit(solution)/shard_map/ppermute | solution.py:36
  45.9 0.5 collective-permute-start.6
  46.4 0.1 collective-permute-start.7
  46.5 0.3 pad_maximum_fusion
  46.8 1.4 %collective-permute-done.6.refs_6_ = bf16[64,1536]{1,0:T(8,128)(2,1)S(1)} collective-permute-done((bf16[64,1536]{1,0:T(8,128)(2,1)S(1)}, bf16[64,1536]{1,0:T(8,128)(2,1)S(1)}, u32[]{:S(2)}, u32[]{:S(2)}) %collective-permute-start.6) | collective-permute-done | bytes 196640 | tf_op jit(solution)/shard_map/ppermute | solution.py:36
  48.2 0.4 collective-permute-start.23
  48.6 0.1 collective-permute-start.20
  48.8 0.4 collective-permute-start.24
  49.2 0.5 shard_map.100
  49.7 0.4 collective-permute-done.20.refs_7_.refs_6_
  50.1 1.2 %shard_map.102.part_ref = f32[256,1152]{1,0:T(8,128)S(1)} custom-call(bf16[256,1536]{1,0:T(8,128)(2,1)S(1)} %get-tuple-element.33.refs_0_.normed, bf16[96,1152]{1,0:T(8,128)(2,1)S(1)} %copy-done, bf16[96,1152]{1,0:T(8,128)(2,1)S(1)} %collective-permute-done.13.refs_1_.refs_2_, bf16[192,1152]{1,0:T(8,128)(2,1)S(1)} %constant_dynamic-update-slice_fusion.refs_2_.refs_3_, ...), custom_call_target="tpu_custom_call" | custom-call | flops 679477248 | bytes 3440640 | tf_op jit(solution)/shard_map/pallas_call | solution.py:414
  51.4 1.5 %shard_map.103.first_part = bf16[256,384]{1,0:T(8,128)(2,1)S(1)} custom-call(f32[4,1536]{1,0:T(4,128)S(1)} %get-tuple-element.23.extra_ref, bf16[128,384]{1,0:T(8,128)(2,1)S(1)} %get-tuple-element.46.key_ref, bf16[128,384]{1,0:T(8,128)(2,1)S(1)} %get-tuple-element.45.value_ref, bf16[256,1536]{1,0:T(8,128)(2,1)S(1)} %get-tuple-element.33.refs_0_.normed, ...), custom_call_target="tpu_custom_call" | custom-call | flops 377487360 | bytes 3072000 | tf_op jit(solution)/shard_map/pallas_call | solution.py:414
  52.9 1.4 %collective-permute-start.27 = (bf16[256,384]{1,0:T(8,128)(2,1)S(1)}, bf16[256,384]{1,0:T(8,128)(2,1)S(1)}, u32[]{:S(2)}, u32[]{:S(2)}) collective-permute-start(bf16[256,384]{1,0:T(8,128)(2,1)S(1)} %shard_map.103.first_part), channel_id=1, source_target_pairs={{0,2},{1,3},{2,0},{3,1},{4,6},{5,7},{6,4},{7,5},{8,10},{9,11},{10,... | collective-permute-start | bytes 589832 | tf_op jit(solution)/shard_map/ppermute | solution.py:36
  54.3 1.3 %collective-permute-start.25 = (bf16[256,384]{1,0:T(8,128)(2,1)S(1)}, bf16[256,384]{1,0:T(8,128)(2,1)S(1)}, u32[]{:S(2)}, u32[]{:S(2)}) collective-permute-start(bf16[256,384]{1,0:T(8,128)(2,1)S(1)} %shard_map.103.first_part), channel_id=1, source_target_pairs={{0,6},{1,7},{2,4},{3,5},{4,2},{5,3},{6,0},{7,1},{8,14},{9,15},{10,... | collective-permute-start | bytes 589832 | tf_op jit(solution)/shard_map/ppermute | solution.py:36
  55.6 0.3 shard_map.101.weights
  55.9 3.2 %collective-permute-done.27.fourth_part = bf16[256,384]{1,0:T(8,128)(2,1)S(1)} collective-permute-done((bf16[256,384]{1,0:T(8,128)(2,1)S(1)}, bf16[256,384]{1,0:T(8,128)(2,1)S(1)}, u32[]{:S(2)}, u32[]{:S(2)}) %collective-permute-start.27) | collective-permute-done | bytes 196640 | tf_op jit(solution)/shard_map/ppermute | solution.py:36
  59.1 1.1 %collective-permute-done.26.third_part = bf16[256,384]{1,0:T(8,128)(2,1)S(1)} collective-permute-done((bf16[256,384]{1,0:T(8,128)(2,1)S(1)}, bf16[256,384]{1,0:T(8,128)(2,1)S(1)}, u32[]{:S(2)}, u32[]{:S(2)}) %collective-permute-start.26) | collective-permute-done | bytes 196640 | tf_op jit(solution)/shard_map/ppermute | solution.py:36
  60.2 4.1 %collective-permute-done.25.second_part = bf16[256,384]{1,0:T(8,128)(2,1)S(1)} collective-permute-done((bf16[256,384]{1,0:T(8,128)(2,1)S(1)}, bf16[256,384]{1,0:T(8,128)(2,1)S(1)}, u32[]{:S(2)}, u32[]{:S(2)}) %collective-permute-start.25) | collective-permute-done | bytes 196640 | tf_op jit(solution)/shard_map/ppermute | solution.py:36
  64.2 3.4 %shard_map.104 = (bf16[64,384]{1,0:T(8,128)(2,1)S(1)}, bf16[64,384]{1,0:T(8,128)(2,1)S(1)}, bf16[64,384]{1,0:T(8,128)(2,1)S(1)}, bf16[64,384]{1,0:T(8,128)(2,1)S(1)}, bf16[64,384]{1,0:T(8,128)(2,1)S(1)}) custom-call(f32[4,1536]{1,0:T(4,128)S(1)} %get-tuple-element.23.extra_ref, bf16[128,384]{1,0:T(8,128)(2,1)S(1)} %get-tuple-element.46.key_ref, ...), custom_call_target="tpu_custom_call" | custom-call | flops 1056964608 | bytes 5332992 | tf_op jit(solution)/shard_map/pallas_call | solution.py:414
  67.6 1.8 %collective-permute-start.28 = (bf16[64,384]{1,0:T(8,128)(2,1)S(1)}, bf16[64,384]{1,0:T(8,128)(2,1)S(1)}, u32[]{:S(2)}, u32[]{:S(2)}) collective-permute-start(bf16[64,384]{1,0:T(8,128)(2,1)S(1)} %get-tuple-element.35), channel_id=1, source_target_pairs={{0,2},{1,4},{2,0},{3,6},{4,1},{5,7},{6,3},{7,5},{8,10},{9,12},{10,... | collective-permute-start | bytes 147464 | tf_op jit(solution)/shard_map/ppermute | solution.py:36
  69.4 1.3 %collective-permute-start.30 = (bf16[64,384]{1,0:T(8,128)(2,1)S(1)}, bf16[64,384]{1,0:T(8,128)(2,1)S(1)}, u32[]{:S(2)}, u32[]{:S(2)}) collective-permute-start(bf16[64,384]{1,0:T(8,128)(2,1)S(1)} %get-tuple-element.37), channel_id=1, source_target_pairs={{0,1},{1,7},{2,3},{3,5},{4,2},{5,4},{6,0},{7,6},{8,9},{9,15},{10,1... | collective-permute-start | bytes 147464 | tf_op jit(solution)/shard_map/ppermute | solution.py:36
  70.7 4.5 %collective-permute-start.31 = (bf16[64,384]{1,0:T(8,128)(2,1)S(1)}, bf16[64,384]{1,0:T(8,128)(2,1)S(1)}, u32[]{:S(2)}, u32[]{:S(2)}) collective-permute-start(bf16[64,384]{1,0:T(8,128)(2,1)S(1)} %get-tuple-element.38), channel_id=1, source_target_pairs={{1,6},{3,4},{4,3},{6,1},{9,14},{11,12},{12,11},{14,9},{17,22},{19,... | collective-permute-start | bytes 147464 | tf_op jit(solution)/shard_map/ppermute | solution.py:36
  75.2 1.7 %collective-permute-done.31.fourth = bf16[64,384]{1,0:T(8,128)(2,1)S(1)} collective-permute-done((bf16[64,384]{1,0:T(8,128)(2,1)S(1)}, bf16[64,384]{1,0:T(8,128)(2,1)S(1)}, u32[]{:S(2)}, u32[]{:S(2)}) %collective-permute-start.31) | collective-permute-done | bytes 49184 | tf_op jit(solution)/shard_map/ppermute | solution.py:36
  77.0 0.7 shard_map.105
  (34 shorter events, 0.2 us)
Async XLA Ops:
  0.0 49.2 %copy-start.1 = (bf16[64,1536]{1,0:T(8,128)(2,1)S(1)}, bf16[64,1536]{1,0:T(8,128)(2,1)}, u32[]{:S(2)}) copy-start(bf16[64,1536]{1,0:T(8,128)(2,1)} %refs_0_.1) | copy-start | bytes 589828
  3.3 46.8 %copy-start = (bf16[96,1152]{1,0:T(8,128)(2,1)S(1)}, bf16[96,1152]{1,0:T(8,128)(2,1)}, u32[]{:S(2)}) copy-start(bf16[96,1152]{1,0:T(8,128)(2,1)} %get-tuple-element.29.refs_0_.refs_1_) | copy-start | bytes 663556
  3.4 3.4 %collective-permute-start.8 = (bf16[4,8,2,384]{3,2,1,0:T(2,128)(2,1)}, bf16[4,8,2,384]{3,2,1,0:T(2,128)(2,1)S(1)}, u32[]{:S(2)}, u32[]{:S(2)}) collective-permute-start(bf16[4,8,2,384]{3,2,1,0:T(2,128)(2,1)} %get-tuple-element.25), channel_id=1, source_target_pairs={{0,1},{1,0},{2,3},{3,2},{4,5},{5,4},{6,7},{7,6},{8,9},{9,8},{10,11... | collective-permute-start | bytes 147464 | tf_op jit(solution)/shard_map/ppermute | solution.py:228
  3.4 7.0 %collective-permute-start.9 = (bf16[4,8,2,384]{3,2,1,0:T(2,128)(2,1)}, bf16[4,8,2,384]{3,2,1,0:T(2,128)(2,1)S(1)}, u32[]{:S(2)}, u32[]{:S(2)}) collective-permute-start(bf16[4,8,2,384]{3,2,1,0:T(2,128)(2,1)} %get-tuple-element.26), channel_id=1, source_target_pairs={{0,2},{1,3},{2,0},{3,1},{4,6},{5,7},{6,4},{7,5},{8,10},{9,11},{10,... | collective-permute-start | bytes 147464 | tf_op jit(solution)/shard_map/ppermute | solution.py:228
  6.2 5.5 %collective-permute-start.10 = (bf16[4,8,2,384]{3,2,1,0:T(2,128)(2,1)}, bf16[4,8,2,384]{3,2,1,0:T(2,128)(2,1)S(1)}, u32[]{:S(2)}, u32[]{:S(2)}) collective-permute-start(bf16[4,8,2,384]{3,2,1,0:T(2,128)(2,1)} %get-tuple-element.27), channel_id=1, source_target_pairs={{0,3},{1,2},{2,1},{3,0},{4,7},{5,6},{6,5},{7,4},{8,11},{9,10},{10,... | collective-permute-start | bytes 147464 | tf_op jit(solution)/shard_map/ppermute | solution.py:228
  6.2 18.1 %collective-permute-start.2 = (bf16[64,1536]{1,0:T(8,128)(2,1)}, bf16[64,1536]{1,0:T(8,128)(2,1)S(1)}, u32[]{:S(2)}, u32[]{:S(2)}) collective-permute-start(bf16[64,1536]{1,0:T(8,128)(2,1)} %refs_0_.1), channel_id=1, source_target_pairs={{0,1},{1,0},{2,3},{3,2},{4,5},{5,4},{6,7},{7,6},{8,9},{9,8},{10,11... | collective-permute-start | bytes 589832 | tf_op jit(solution)/shard_map/ppermute | solution.py:36
  6.6 16.0 %collective-permute-start = (f32[4,1536]{1,0:T(4,128)}, f32[4,1536]{1,0:T(4,128)S(1)}, u32[]{:S(2)}, u32[]{:S(2)}) collective-permute-start(f32[4,1536]{1,0:T(4,128)} %get-tuple-element.22), channel_id=1, source_target_pairs={{0,1},{1,0},{2,3},{3,2},{4,5},{5,4},{6,7},{7,6},{8,9},{9,8},{10,11... | collective-permute-start | bytes 73736 | tf_op jit(solution)/shard_map/ppermute | solution.py:36
  6.7 15.6 %collective-permute-start.15 = (bf16[96,1152]{1,0:T(8,128)(2,1)}, bf16[96,1152]{1,0:T(8,128)(2,1)S(1)}, u32[]{:S(2)}, u32[]{:S(2)}) collective-permute-start(bf16[96,1152]{1,0:T(8,128)(2,1)} %get-tuple-element.32), channel_id=1, source_target_pairs={{0,8},{1,11},{2,10},{3,9},{4,12},{5,15},{6,14},{7,13},{8,0},{9,3},... | collective-permute-start | bytes 663560 | tf_op jit(solution)/shard_map/ppermute | solution.py:36
  10.4 11.9 %collective-permute-start.14 = (bf16[96,1152]{1,0:T(8,128)(2,1)}, bf16[96,1152]{1,0:T(8,128)(2,1)S(1)}, u32[]{:S(2)}, u32[]{:S(2)}) collective-permute-start(bf16[96,1152]{1,0:T(8,128)(2,1)} %get-tuple-element.31), channel_id=1, source_target_pairs={{0,4},{1,7},{2,6},{3,5},{4,0},{5,3},{6,2},{7,1},{8,12},{9,15},{10,... | collective-permute-start | bytes 663560 | tf_op jit(solution)/shard_map/ppermute | solution.py:36
  12.9 11.0 %collective-permute-start.11 = (bf16[4,2,8,2,384]{4,3,2,1,0:T(2,128)(2,1)S(1)}, bf16[4,2,8,2,384]{4,3,2,1,0:T(2,128)(2,1)S(1)}, u32[]{:S(2)}, u32[]{:S(2)}) collective-permute-start(bf16[4,2,8,2,384]{4,3,2,1,0:T(2,128)(2,1)S(1)} %get-tuple-element.44), channel_id=1, source_target_pairs={{0,4},{1,5},{2,6},{3,7},{4,0},{5,1},{6,2},{7,3},{8,12},{9,13},{10,... | collective-permute-start | bytes 294920 | tf_op jit(solution)/shard_map/ppermute | solution.py:228
  22.4 23.5 %collective-permute-start.16 = (bf16[192,1152]{1,0:T(8,128)(2,1)S(1)}, bf16[192,1152]{1,0:T(8,128)(2,1)S(1)}, u32[]{:S(2)}, u32[]{:S(2)}) collective-permute-start(bf16[192,1152]{1,0:T(8,128)(2,1)S(1)} %constant_dynamic-update-slice_fusion.refs_2_.refs_3_), channel_id=1, source_target_pairs={{0,16},{1,17},{2,18},{3,19},{4,20},{5,21},{6,22},{7,23},{8,24},{9,... | collective-permute-start | bytes 1327112 | tf_op jit(solution)/shard_map/ppermute | solution.py:36
  22.4 14.7 %collective-permute-start.13 = (bf16[96,1152]{1,0:T(8,128)(2,1)}, bf16[96,1152]{1,0:T(8,128)(2,1)S(1)}, u32[]{:S(2)}, u32[]{:S(2)}) collective-permute-start(bf16[96,1152]{1,0:T(8,128)(2,1)} %get-tuple-element.30), channel_id=1, source_target_pairs={{0,2},{1,3},{2,0},{3,1},{4,6},{5,7},{6,4},{7,5},{8,10},{9,11},{10,... | collective-permute-start | bytes 663560 | tf_op jit(solution)/shard_map/ppermute | solution.py:36
  22.5 10.9 %collective-permute-start.1 = (bf16[64,1536]{1,0:T(8,128)(2,1)}, bf16[64,1536]{1,0:T(8,128)(2,1)S(1)}, u32[]{:S(2)}, u32[]{:S(2)}) collective-permute-start(bf16[64,1536]{1,0:T(8,128)(2,1)} %refs_0_.1), channel_id=1, source_target_pairs={{0,2},{1,3},{2,0},{3,1},{4,6},{5,7},{6,4},{7,5},{8,10},{9,11},{10,... | collective-permute-start | bytes 589832 | tf_op jit(solution)/shard_map/ppermute | solution.py:36
  24.0 13.2 %collective-permute-start.4 = (bf16[64,1536]{1,0:T(8,128)(2,1)}, bf16[64,1536]{1,0:T(8,128)(2,1)S(1)}, u32[]{:S(2)}, u32[]{:S(2)}) collective-permute-start(bf16[64,1536]{1,0:T(8,128)(2,1)} %refs_0_.1), channel_id=1, source_target_pairs={{0,4},{1,5},{2,6},{3,7},{4,0},{5,1},{6,2},{7,3},{8,12},{9,13},{10,... | collective-permute-start | bytes 589832 | tf_op jit(solution)/shard_map/ppermute | solution.py:36
  24.3 13.2 %collective-permute-start.17 = (bf16[96,1152]{1,0:T(8,128)(2,1)}, bf16[96,1152]{1,0:T(8,128)(2,1)S(1)}, u32[]{:S(2)}, u32[]{:S(2)}) collective-permute-start(bf16[96,1152]{1,0:T(8,128)(2,1)} %get-tuple-element.31), channel_id=1, source_target_pairs={{0,12},{1,15},{2,14},{3,13},{4,8},{5,11},{6,10},{7,9},{8,4},{9,7},... | collective-permute-start | bytes 663560 | tf_op jit(solution)/shard_map/ppermute | solution.py:36
  33.4 5.4 %collective-permute-start.19 = (bf16[96,1152]{1,0:T(8,128)(2,1)}, bf16[96,1152]{1,0:T(8,128)(2,1)S(1)}, u32[]{:S(2)}, u32[]{:S(2)}) collective-permute-start(bf16[96,1152]{1,0:T(8,128)(2,1)} %get-tuple-element.29.refs_0_.refs_1_), channel_id=1, source_target_pairs={{0,1},{1,0},{2,3},{3,2},{4,5},{5,4},{6,7},{7,6},{8,9},{9,8},{10,11... | collective-permute-start | bytes 663560 | tf_op jit(solution)/shard_map/ppermute | solution.py:36
  37.1 8.8 %collective-permute-start.3 = (bf16[64,1536]{1,0:T(8,128)(2,1)S(1)}, bf16[64,1536]{1,0:T(8,128)(2,1)S(1)}, u32[]{:S(2)}, u32[]{:S(2)}) collective-permute-start(bf16[64,1536]{1,0:T(8,128)(2,1)S(1)} %collective-permute-done.1.refs_1_), channel_id=1, source_target_pairs={{0,1},{1,0},{2,3},{3,2},{4,5},{5,4},{6,7},{7,6},{8,9},{9,8},{10,11... | collective-permute-start | bytes 589832 | tf_op jit(solution)/shard_map/ppermute | solution.py:36
  37.2 9.3 %collective-permute-start.5 = (bf16[64,1536]{1,0:T(8,128)(2,1)S(1)}, bf16[64,1536]{1,0:T(8,128)(2,1)S(1)}, u32[]{:S(2)}, u32[]{:S(2)}) collective-permute-start(bf16[64,1536]{1,0:T(8,128)(2,1)S(1)} %collective-permute-done.4.refs_4_), channel_id=1, source_target_pairs={{0,2},{1,3},{2,0},{3,1},{4,6},{5,7},{6,4},{7,5},{8,10},{9,11},{10,... | collective-permute-start | bytes 589832 | tf_op jit(solution)/shard_map/ppermute | solution.py:36
  37.5 4.4 %collective-permute-start.12 = (bf16[8,1,8,2,384]{4,3,2,1,0:T(2,128)(2,1)S(1)}, bf16[8,1,8,2,384]{4,3,2,1,0:T(2,128)(2,1)S(1)}, u32[]{:S(2)}, u32[]{:S(2)}) collective-permute-start(bf16[8,1,8,2,384]{4,3,2,1,0:T(2,128)(2,1)S(1)} %get-tuple-element.42), channel_id=1, source_target_pairs={{0,8},{1,9},{2,10},{3,11},{4,12},{5,13},{6,14},{7,15},{8,0},{9,1},... | collective-permute-start | bytes 294920 | tf_op jit(solution)/shard_map/ppermute | solution.py:228
  38.8 9.8 %collective-permute-start.18 = (bf16[96,1152]{1,0:T(8,128)(2,1)S(1)}, bf16[96,1152]{1,0:T(8,128)(2,1)S(1)}, u32[]{:S(2)}, u32[]{:S(2)}) collective-permute-start(bf16[96,1152]{1,0:T(8,128)(2,1)S(1)} %collective-permute-done.17.refs_4_.refs_0_), channel_id=1, source_target_pairs={{0,16},{1,17},{2,18},{3,19},{4,20},{5,21},{6,22},{7,23},{8,24},{9,... | collective-permute-start | bytes 663560 | tf_op jit(solution)/shard_map/ppermute | solution.py:36
  41.9 8.2 %collective-permute-start.21 = (bf16[192,1152]{1,0:T(8,128)(2,1)S(1)}, bf16[192,1152]{1,0:T(8,128)(2,1)S(1)}, u32[]{:S(2)}, u32[]{:S(2)}) collective-permute-start(bf16[192,1152]{1,0:T(8,128)(2,1)S(1)} %constant_dynamic-update-slice_fusion.refs_2_.refs_3_), channel_id=1, source_target_pairs={{0,1},{1,0},{2,3},{3,2},{4,5},{5,4},{6,7},{7,6},{8,9},{9,8},{10,11... | collective-permute-start | bytes 1327112 | tf_op jit(solution)/shard_map/ppermute | solution.py:36
  45.9 4.2 %collective-permute-start.22 = (bf16[192,1152]{1,0:T(8,128)(2,1)S(1)}, bf16[192,1152]{1,0:T(8,128)(2,1)S(1)}, u32[]{:S(2)}, u32[]{:S(2)}) collective-permute-start(bf16[192,1152]{1,0:T(8,128)(2,1)S(1)} %collective-permute-done.16.refs_3_.refs_4_), channel_id=1, source_target_pairs={{0,1},{1,0},{2,3},{3,2},{4,5},{5,4},{6,7},{7,6},{8,9},{9,8},{10,11... | collective-permute-start | bytes 1327112 | tf_op jit(solution)/shard_map/ppermute | solution.py:36
  45.9 2.3 %collective-permute-start.6 = (bf16[64,1536]{1,0:T(8,128)(2,1)S(1)}, bf16[64,1536]{1,0:T(8,128)(2,1)S(1)}, u32[]{:S(2)}, u32[]{:S(2)}) collective-permute-start(bf16[64,1536]{1,0:T(8,128)(2,1)S(1)} %collective-permute-done.4.refs_4_), channel_id=1, source_target_pairs={{0,1},{1,0},{2,3},{3,2},{4,5},{5,4},{6,7},{7,6},{8,9},{9,8},{10,11... | collective-permute-start | bytes 589832 | tf_op jit(solution)/shard_map/ppermute | solution.py:36
  46.4 2.3 %collective-permute-start.7 = (bf16[64,1536]{1,0:T(8,128)(2,1)S(1)}, bf16[64,1536]{1,0:T(8,128)(2,1)S(1)}, u32[]{:S(2)}, u32[]{:S(2)}) collective-permute-start(bf16[64,1536]{1,0:T(8,128)(2,1)S(1)} %collective-permute-done.5.refs_5_), channel_id=1, source_target_pairs={{0,1},{1,0},{2,3},{3,2},{4,5},{5,4},{6,7},{7,6},{8,9},{9,8},{10,11... | collective-permute-start | bytes 589832 | tf_op jit(solution)/shard_map/ppermute | solution.py:36
  48.2 3.1 %collective-permute-start.23 = (bf16[96,1152]{1,0:T(8,128)(2,1)S(1)}, bf16[96,1152]{1,0:T(8,128)(2,1)S(1)}, u32[]{:S(2)}, u32[]{:S(2)}) collective-permute-start(bf16[96,1152]{1,0:T(8,128)(2,1)S(1)} %collective-permute-done.17.refs_4_.refs_0_), channel_id=1, source_target_pairs={{0,1},{1,0},{2,3},{3,2},{4,5},{5,4},{6,7},{7,6},{8,9},{9,8},{10,11... | collective-permute-start | bytes 663560 | tf_op jit(solution)/shard_map/ppermute | solution.py:36
  48.6 1.5 %collective-permute-start.20 = (bf16[96,1152]{1,0:T(8,128)(2,1)S(1)}, bf16[96,1152]{1,0:T(8,128)(2,1)S(1)}, u32[]{:S(2)}, u32[]{:S(2)}) collective-permute-start(bf16[96,1152]{1,0:T(8,128)(2,1)S(1)} %collective-permute-done.13.refs_1_.refs_2_), channel_id=1, source_target_pairs={{0,1},{1,0},{2,3},{3,2},{4,5},{5,4},{6,7},{7,6},{8,9},{9,8},{10,11... | collective-permute-start | bytes 663560 | tf_op jit(solution)/shard_map/ppermute | solution.py:36
  48.8 2.6 %collective-permute-start.24 = (bf16[96,1152]{1,0:T(8,128)(2,1)S(1)}, bf16[96,1152]{1,0:T(8,128)(2,1)S(1)}, u32[]{:S(2)}, u32[]{:S(2)}) collective-permute-start(bf16[96,1152]{1,0:T(8,128)(2,1)S(1)} %collective-permute-done.18.refs_5_.refs_1_), channel_id=1, source_target_pairs={{0,1},{1,0},{2,3},{3,2},{4,5},{5,4},{6,7},{7,6},{8,9},{9,8},{10,11... | collective-permute-start | bytes 663560 | tf_op jit(solution)/shard_map/ppermute | solution.py:36
  52.9 6.2 %collective-permute-start.27 = (bf16[256,384]{1,0:T(8,128)(2,1)S(1)}, bf16[256,384]{1,0:T(8,128)(2,1)S(1)}, u32[]{:S(2)}, u32[]{:S(2)}) collective-permute-start(bf16[256,384]{1,0:T(8,128)(2,1)S(1)} %shard_map.103.first_part), channel_id=1, source_target_pairs={{0,2},{1,3},{2,0},{3,1},{4,6},{5,7},{6,4},{7,5},{8,10},{9,11},{10,... | collective-permute-start | bytes 589832 | tf_op jit(solution)/shard_map/ppermute | solution.py:36
  54.3 5.9 %collective-permute-start.26 = (bf16[256,384]{1,0:T(8,128)(2,1)S(1)}, bf16[256,384]{1,0:T(8,128)(2,1)S(1)}, u32[]{:S(2)}, u32[]{:S(2)}) collective-permute-start(bf16[256,384]{1,0:T(8,128)(2,1)S(1)} %shard_map.103.first_part), channel_id=1, source_target_pairs={{0,4},{1,5},{2,6},{3,7},{4,0},{5,1},{6,2},{7,3},{8,12},{9,13},{10,... | collective-permute-start | bytes 589832 | tf_op jit(solution)/shard_map/ppermute | solution.py:36
  54.3 9.9 %collective-permute-start.25 = (bf16[256,384]{1,0:T(8,128)(2,1)S(1)}, bf16[256,384]{1,0:T(8,128)(2,1)S(1)}, u32[]{:S(2)}, u32[]{:S(2)}) collective-permute-start(bf16[256,384]{1,0:T(8,128)(2,1)S(1)} %shard_map.103.first_part), channel_id=1, source_target_pairs={{0,6},{1,7},{2,4},{3,5},{4,2},{5,3},{6,0},{7,1},{8,14},{9,15},{10,... | collective-permute-start | bytes 589832 | tf_op jit(solution)/shard_map/ppermute | solution.py:36
  67.6 7.6 %collective-permute-start.28 = (bf16[64,384]{1,0:T(8,128)(2,1)S(1)}, bf16[64,384]{1,0:T(8,128)(2,1)S(1)}, u32[]{:S(2)}, u32[]{:S(2)}) collective-permute-start(bf16[64,384]{1,0:T(8,128)(2,1)S(1)} %get-tuple-element.35), channel_id=1, source_target_pairs={{0,2},{1,4},{2,0},{3,6},{4,1},{5,7},{6,3},{7,5},{8,10},{9,12},{10,... | collective-permute-start | bytes 147464 | tf_op jit(solution)/shard_map/ppermute | solution.py:36
  69.4 5.8 %collective-permute-start.29 = (bf16[64,384]{1,0:T(8,128)(2,1)S(1)}, bf16[64,384]{1,0:T(8,128)(2,1)S(1)}, u32[]{:S(2)}, u32[]{:S(2)}) collective-permute-start(bf16[64,384]{1,0:T(8,128)(2,1)S(1)} %get-tuple-element.36), channel_id=1, source_target_pairs={{0,3},{1,5},{2,1},{3,7},{4,0},{5,6},{6,2},{7,4},{8,11},{9,13},{10,... | collective-permute-start | bytes 147464 | tf_op jit(solution)/shard_map/ppermute | solution.py:36
  69.4 5.8 %collective-permute-start.30 = (bf16[64,384]{1,0:T(8,128)(2,1)S(1)}, bf16[64,384]{1,0:T(8,128)(2,1)S(1)}, u32[]{:S(2)}, u32[]{:S(2)}) collective-permute-start(bf16[64,384]{1,0:T(8,128)(2,1)S(1)} %get-tuple-element.37), channel_id=1, source_target_pairs={{0,1},{1,7},{2,3},{3,5},{4,2},{5,4},{6,0},{7,6},{8,9},{9,15},{10,1... | collective-permute-start | bytes 147464 | tf_op jit(solution)/shard_map/ppermute | solution.py:36
  70.7 6.3 %collective-permute-start.31 = (bf16[64,384]{1,0:T(8,128)(2,1)S(1)}, bf16[64,384]{1,0:T(8,128)(2,1)S(1)}, u32[]{:S(2)}, u32[]{:S(2)}) collective-permute-start(bf16[64,384]{1,0:T(8,128)(2,1)S(1)} %get-tuple-element.38), channel_id=1, source_target_pairs={{1,6},{3,4},{4,3},{6,1},{9,14},{11,12},{12,11},{14,9},{17,22},{19,... | collective-permute-start | bytes 147464 | tf_op jit(solution)/shard_map/ppermute | solution.py:36

commit v12 on v11

--- a/solution.py
+++ b/solution.py
@@ -63,48 +63,15 @@
     return pl.ds(pl.multiple_of(quarter * width, 128), width)
 
 
-def pack_kernel(
-    w_query, w_key, w_value, list_hbm, slot_hbm, count_hbm, scale_hbm, gain_hbm, mem_ref,
-    own_ref, beside_ref, even_ref, odd_ref, extra_ref, *refs,
+def pack_weights_kernel(
+    w_query, w_key, w_value, own_ref, beside_ref, even_ref, odd_ref, rows, row_sem, out_sem
 ):
-    near_count = SPATIAL
-    memory_refs = refs[:near_count]
-    (
-        list_ref, slot_ref, count_ref, scale_ref, gain, rows, stored, extra, row_sem, out_sem, scalar_sem, mem_sem, give_sem,
-    ) = refs[near_count:]
-    x, index, plane, y, c = here()
-    devices = lax.axis_size("frame")
-    frames, entries = list_ref.shape
+    x, _, plane, y, c = here()
     width = own_ref.shape[1] // 3
-    scalars = [
-        pltpu.make_async_copy(source, target, scalar_sem.at[number])
-        for number, (source, target) in enumerate(
-            (
-                (list_hbm, list_ref),
-                (slot_hbm, slot_ref),
-                (count_hbm, count_ref),
-                (scale_hbm, scale_ref),
-                (gain_hbm, gain),
-            )
-        )
-    ]
-    for copy in scalars[:2]:
-        copy.start()
     reads = []
     for number, weight in enumerate((w_query, w_key, w_value)):
         reads.append(pltpu.make_async_copy(weight, rows.at[number], row_sem.at[number]))
         reads[-1].start()
-    for copy in scalars[2:]:
-        copy.start()
-    for copy in scalars[:2]:
-        copy.wait()
-    picks = []
-    for frame in range(frames):
-        for entry in range(entries):
-            number = frame * entries + entry
-            row = slot_ref[list_ref[frame, entry]]
-            picks.append(pltpu.make_async_copy(mem_ref.at[row, 0], stored.at[number], mem_sem.at[number]))
-            picks[-1].start()
     across = joined_bits(joined_bits(x, y), c)
     low = plane % 2
     quarters = (low * 2 + across, (1 - low) * 2 + across, low * 2 + 1 - y, quarter_of(plane, y))
@@ -120,6 +87,53 @@
                 )
             )
             gives[-1].start()
+    for give in gives:
+        give.wait()
+
+
+def pack_weights(w_query, w_key, w_value):
+    shard_rows, features = w_query.shape
+    piece = jax.ShapeDtypeStruct((shard_rows, 3 * (features // SPATIAL)), w_query.dtype)
+    anywhere = pl.BlockSpec(memory_space=pl.ANY)
+    held = pl.BlockSpec(memory_space=pltpu.HBM)
+    return pl.pallas_call(
+        pack_weights_kernel,
+        out_shape=(piece,) * 4,
+        in_specs=[held] * 3,
+        out_specs=(anywhere,) * 4,
+        scratch_shapes=[
+            pltpu.VMEM((3, shard_rows, features), w_query.dtype),
+            pltpu.SemaphoreType.DMA((3,)),
+            pltpu.SemaphoreType.DMA((3, 4)),
+        ],
+        name="pack_weights",
+    )(w_query, w_key, w_value)
+
+
+def pack_memory_kernel(list_hbm, slot_hbm, count_hbm, scale_hbm, gain_hbm, mem_ref, extra_ref, *refs):
+    memory_refs = refs[:SPATIAL]
+    list_ref, slot_ref, count_ref, scale_ref, gain, stored, extra, scalar_sem, mem_sem, give_sem = refs[SPATIAL:]
+    _, index, plane, _, c = here()
+    devices = lax.axis_size("frame")
+    frames, entries = list_ref.shape
+    width = memory_refs[0].shape[-1]
+    sources = (list_hbm, slot_hbm, count_hbm, scale_hbm, gain_hbm)
+    targets = (list_ref, slot_ref, count_ref, scale_ref, gain)
+    scalars = [
+        pltpu.make_async_copy(source, target, scalar_sem.at[number])
+        for number, (source, target) in enumerate(zip(sources, targets))
+    ]
+    for copy in scalars:
+        copy.start()
+    for copy in scalars[:2]:
+        copy.wait()
+    picks = []
+    for frame in range(frames):
+        for entry in range(entries):
+            number = frame * entries + entry
+            row = slot_ref[list_ref[frame, entry]]
+            picks.append(pltpu.make_async_copy(mem_ref.at[row, 0], stored.at[number], mem_sem.at[number]))
+            picks[-1].start()
     for copy in scalars[2:]:
         copy.wait()
     row = (1, extra.shape[1])
@@ -128,16 +142,15 @@
         extra[1 + number : 2 + number, :] = jnp.full(row, scale_ref[number], jnp.float32)
     live = lax.broadcasted_iota(jnp.int32, row, 1) % entries < count_ref[(plane // 2) * 2 + 1 - c]
     extra[1 + STEPS : 2 + STEPS, :] = jnp.where(live, 1.0, 0.0)
-    gives.append(pltpu.make_async_copy(extra, extra_ref, scalar_sem.at[5]))
+    gives = [pltpu.make_async_copy(extra, extra_ref, scalar_sem.at[5])]
     gives[-1].start()
     for pick in picks:
         pick.wait()
-    bits = devices.bit_length() - 1
     for away in range(devices):
         to_plane, to_y, to_c = coords(flipped(index, away))
         to_frame = (to_plane // 2) * 2 + to_c
         place = 0
-        for bit in range(2, bits):
+        for bit in range(2, devices.bit_length() - 1):
             place = place * 2 + (away >> bit & 1)
         gives.append(
             pltpu.make_async_copy(
@@ -151,20 +164,19 @@
         give.wait()
 
 
-def pack(w_query, w_key, w_value, intersection, slot_of, counts, step_scale, norm_gain, mem_cache):
+def pack_memory(intersection, slot_of, counts, step_scale, norm_gain, mem_cache):
     devices = lax.axis_size("frame")
-    shard_rows, features = w_query.shape
+    features = mem_cache.shape[-1]
     frames, entries = intersection.shape
-    piece = jax.ShapeDtypeStruct((shard_rows, 3 * (features // SPATIAL)), w_query.dtype)
     small = jax.ShapeDtypeStruct((2 + STEPS, features), jnp.float32)
     memory = jax.ShapeDtypeStruct((devices // SPATIAL, entries, 2, features // SPATIAL), mem_cache.dtype)
-    out_shape = (piece,) * 4 + (small,) + (memory,) * SPATIAL
+    out_shape = (small,) + (memory,) * SPATIAL
     anywhere = pl.BlockSpec(memory_space=pl.ANY)
     held = pl.BlockSpec(memory_space=pltpu.HBM)
     outs = pl.pallas_call(
-        pack_kernel,
+        pack_memory_kernel,
         out_shape=out_shape,
-        in_specs=[held] * 9,
+        in_specs=[held] * 6,
         out_specs=(anywhere,) * len(out_shape),
         scratch_shapes=[
             pltpu.SMEM(intersection.shape, intersection.dtype),
@@ -172,18 +184,15 @@
             pltpu.SMEM(counts.shape, counts.dtype),
             pltpu.SMEM(step_scale.shape, step_scale.dtype),
             pltpu.VMEM(norm_gain.shape, norm_gain.dtype),
-            pltpu.VMEM((3, shard_rows, features), w_query.dtype),
             pltpu.VMEM((frames * entries, 2, features), mem_cache.dtype),
             pltpu.VMEM(small.shape, small.dtype),
-            pltpu.SemaphoreType.DMA((3,)),
-            pltpu.SemaphoreType.DMA((3, 4)),
             pltpu.SemaphoreType.DMA((6,)),
             pltpu.SemaphoreType.DMA((frames * entries,)),
             pltpu.SemaphoreType.DMA((devices,)),
         ],
-        name="pack",
-    )(w_query, w_key, w_value, intersection, slot_of, counts, step_scale, norm_gain, mem_cache)
-    return outs[:4], outs[4], outs[5:]
+        name="pack_memory",
+    )(intersection, slot_of, counts, step_scale, norm_gain, mem_cache)
+    return outs[0], outs[1:]
 
 
 def all_pieces(own, beside, even, odd):
@@ -545,9 +554,8 @@
     latent, norm_gain, w_query, w_key, w_value, mem_cache, intersection, counts, slot_of, step_scale
 ):
     late = late_plane(lax.axis_size("frame"))
-    weights, extra, memory = pack(
-        w_query, w_key, w_value, intersection, slot_of, counts, step_scale, norm_gain, mem_cache
-    )
+    weights = pack_weights(w_query, w_key, w_value)
+    extra, memory = pack_memory(intersection, slot_of, counts, step_scale, norm_gain, mem_cache)
     extra = moved(extra, lambda x, p, y, c: (x, p, y, 1 - c))
     pieces = all_pieces(*weights)
     tokens = all_tokens(latent)

time: 77.9 us -> 79.8 us (1.024)
  Pallas kernels: 11 us -> 12.8 us
    pallas_call x1 -> x2, Pallas kernels: 3.33 us -> 5.18 us  [the longest x1 3.15 us: pack_memory(): pl.pallas_call(pack_memory_kernel, out_shape=out_shape, in_specs=[held] *...]
    ppermute x27, waiting for transfers between devices: 27 us -> 25.9 us  [moved(): return lax.ppermute(array, AXES, pairs)]
    ppermute x5, waiting for transfers between devices: 2.2 us -> 3.22 us  [hop(): lax.ppermute(array, 'frame', [(i, i ^ bits) for i in range(lax.axis_size(...]
  transfers between devices with their start and end apart: 32 -> 32, of which waited for: 9 -> 9; matrix products, arithmetic and copies ran while one was open for 2% -> 2% of each run, Pallas kernels for 3% -> 5%
where the time goes in v12:
time: 79.8 us; the launch traced here: 79.6 us
  starting transfers between devices  35.5 us (44%)
  waiting for transfers between devices  29.1 us (36%)
  Pallas kernels  12.8 us (16%)
  other arithmetic  1.73 us (2%)
    ppermute x27, starting transfers between devices, moved(): return lax.ppermute(array, AXES, pairs)  31.4 us
    ppermute x27, waiting for transfers between devices, moved(): return lax.ppermute(array, AXES, pairs)  25.9 us
    pallas_call x6, Pallas kernels, kernel_call(): pl.pallas_call(kernel, out_shape=out_shape, in_specs=[free if number in a...  7.64 us
    ppermute x5, starting transfers between devices, hop(): lax.ppermute(array, 'frame', [(i, i ^ bits) for i in range(lax.axis_size(...  4.13 us
    ppermute x5, waiting for transfers between devices, hop(): lax.ppermute(array, 'frame', [(i, i ^ bits) for i in range(lax.axis_size(...  3.22 us
    pallas_call x1, Pallas kernels, pack_memory(): pl.pallas_call(pack_memory_kernel, out_shape=out_shape, in_specs=[held] *...  3.15 us
    pallas_call x1, Pallas kernels, pack_weights(): pl.pallas_call(pack_weights_kernel, out_shape=(piece,) * 4, in_specs=[hel...  2.03 us
  transfers between devices with their start and end apart: 32, of which 9 were waited for; matrix products, arithmetic and copies ran while one was open for 2% of the time, Pallas kernels for 5%

profile of v12, /device:TPU:1, one launch (start us, length us, event | category | flops | bytes accessed | tf_op | source)
XLA Modules:
  0.0 79.6 jit_solution(14658663240199613885)
XLA Ops:
  0.0 3.1 %pack_memory.1 = (f32[4,1536]{1,0:T(4,128)}, bf16[4,8,2,384]{3,2,1,0:T(2,128)(2,1)}, bf16[4,8,2,384]{3,2,1,0:T(2,128)(2,1)}, bf16[4,8,2,384]{3,2,1,0:T(2,128)(2,1)}, bf16[4,8,2,384]{3,2,1,0:T(2,128)(2,1)}) custom-call(s32[4,8]{1,0:T(4,128)} %list_hbm.1, s32[128]{0:T(128)} %slot_hbm.1, s32[4]{0:T(128)} %count_hbm.1, f32[2]{0:T(128)} %scale_hbm.1, ...), custom_call_target="tpu_custom_call" | custom-call | tf_op jit(solution)/shard_map/pack_memory/pallas_call | solution.py:176
  3.2 0.1 collective-permute-start.8
  3.2 2.7 %collective-permute-start.9 = (bf16[4,8,2,384]{3,2,1,0:T(2,128)(2,1)}, bf16[4,8,2,384]{3,2,1,0:T(2,128)(2,1)S(1)}, u32[]{:S(2)}, u32[]{:S(2)}) collective-permute-start(bf16[4,8,2,384]{3,2,1,0:T(2,128)(2,1)} %get-tuple-element.26), channel_id=1, source_target_pairs={{0,2},{1,3},{2,0},{3,1},{4,6},{5,7},{6,4},{7,5},{8,10},{9,11},{10,... | collective-permute-start | bytes 147464 | tf_op jit(solution)/shard_map/ppermute | solution.py:237
  6.0 0.4 collective-permute-start.2
  6.4 0.2 collective-permute-start
  6.5 2.0 %pack_weights.1 = (bf16[96,1152]{1,0:T(8,128)(2,1)}, bf16[96,1152]{1,0:T(8,128)(2,1)}, bf16[96,1152]{1,0:T(8,128)(2,1)}, bf16[96,1152]{1,0:T(8,128)(2,1)}) custom-call(bf16[96,1536]{1,0:T(8,128)(2,1)} %w_query.1, bf16[96,1536]{1,0:T(8,128)(2,1)} %w_key.1, bf16[96,1536]{1,0:T(8,128)(2,1)} %w_value.1), custom_call_target="tpu_custom_call" | custom-call | tf_op jit(solution)/shard_map/pack_weights/pallas_call | solution.py:99
  8.6 3.8 %collective-permute-start.15 = (bf16[96,1152]{1,0:T(8,128)(2,1)}, bf16[96,1152]{1,0:T(8,128)(2,1)S(1)}, u32[]{:S(2)}, u32[]{:S(2)}) collective-permute-start(bf16[96,1152]{1,0:T(8,128)(2,1)} %get-tuple-element.32), channel_id=1, source_target_pairs={{0,8},{1,11},{2,10},{3,9},{4,12},{5,15},{6,14},{7,13},{8,0},{9,3},... | collective-permute-start | bytes 663560 | tf_op jit(solution)/shard_map/ppermute | solution.py:36
  12.3 1.2 %collective-permute-start.14 = (bf16[96,1152]{1,0:T(8,128)(2,1)}, bf16[96,1152]{1,0:T(8,128)(2,1)S(1)}, u32[]{:S(2)}, u32[]{:S(2)}) collective-permute-start(bf16[96,1152]{1,0:T(8,128)(2,1)} %get-tuple-element.31), channel_id=1, source_target_pairs={{0,4},{1,7},{2,6},{3,5},{4,0},{5,3},{6,2},{7,1},{8,12},{9,15},{10,... | collective-permute-start | bytes 663560 | tf_op jit(solution)/shard_map/ppermute | solution.py:36
  13.6 1.1 %pad_maximum_fusion.1 = bf16[4,4,8,2,384]{4,3,2,1,0:T(2,128)(2,1)S(1)} fusion(bf16[1,4,8,2,384]{4,3,2,1,0:T(2,128)(2,1)S(1)} %bitcast.11, bf16[1,4,8,2,384]{4,3,2,1,0:T(2,128)(2,1)S(1)} %bitcast.10, bf16[1,4,8,2,384]{4,3,2,1,0:T(2,128)(2,1)S(1)} %bitcast.9, bf16[1,4,8,2,384]{4,3,2,1,0:T(2,128)(2,1)} %bitcast.8), kind=kLoop, calls=%fused_computation.2 | loop fusion | flops 294912 | bytes 393216 | tf_op jit(solution)/shard_map/stack | solution.py:227
  14.7 0.1 fusion.1
  14.9 0.2 collective-permute-start.11
  15.1 9.1 %collective-permute-done.14 = bf16[96,1152]{1,0:T(8,128)(2,1)S(1)} collective-permute-done((bf16[96,1152]{1,0:T(8,128)(2,1)}, bf16[96,1152]{1,0:T(8,128)(2,1)S(1)}, u32[]{:S(2)}, u32[]{:S(2)}) %collective-permute-start.14) | collective-permute-done | bytes 221216 | tf_op jit(solution)/shard_map/ppermute | solution.py:36
  24.3 0.1 collective-permute-start.16
  24.4 0.1 collective-permute-start.13
  24.5 1.4 %collective-permute-start.1 = (bf16[64,1536]{1,0:T(8,128)(2,1)}, bf16[64,1536]{1,0:T(8,128)(2,1)S(1)}, u32[]{:S(2)}, u32[]{:S(2)}) collective-permute-start(bf16[64,1536]{1,0:T(8,128)(2,1)} %refs_0_.1), channel_id=1, source_target_pairs={{0,2},{1,3},{2,0},{3,1},{4,6},{5,7},{6,4},{7,5},{8,10},{9,11},{10,... | collective-permute-start | bytes 589832 | tf_op jit(solution)/shard_map/ppermute | solution.py:36
  25.9 0.3 collective-permute-start.4
  26.2 3.1 %collective-permute-start.17 = (bf16[96,1152]{1,0:T(8,128)(2,1)}, bf16[96,1152]{1,0:T(8,128)(2,1)S(1)}, u32[]{:S(2)}, u32[]{:S(2)}) collective-permute-start(bf16[96,1152]{1,0:T(8,128)(2,1)} %get-tuple-element.31), channel_id=1, source_target_pairs={{0,12},{1,15},{2,14},{3,13},{4,8},{5,11},{6,10},{7,9},{8,4},{9,7},... | collective-permute-start | bytes 663560 | tf_op jit(solution)/shard_map/ppermute | solution.py:36
  29.4 4.8 %collective-permute-done.1.refs_1_ = bf16[64,1536]{1,0:T(8,128)(2,1)S(1)} collective-permute-done((bf16[64,1536]{1,0:T(8,128)(2,1)}, bf16[64,1536]{1,0:T(8,128)(2,1)S(1)}, u32[]{:S(2)}, u32[]{:S(2)}) %collective-permute-start.1) | collective-permute-done | bytes 196640 | tf_op jit(solution)/shard_map/ppermute | solution.py:36
  34.2 4.9 %collective-permute-start.19 = (bf16[96,1152]{1,0:T(8,128)(2,1)}, bf16[96,1152]{1,0:T(8,128)(2,1)S(1)}, u32[]{:S(2)}, u32[]{:S(2)}) collective-permute-start(bf16[96,1152]{1,0:T(8,128)(2,1)} %get-tuple-element.29.refs_0_.refs_1_), channel_id=1, source_target_pairs={{0,1},{1,0},{2,3},{3,2},{4,5},{5,4},{6,7},{7,6},{8,9},{9,8},{10,11... | collective-permute-start | bytes 663560 | tf_op jit(solution)/shard_map/ppermute | solution.py:36
  39.1 0.1 collective-permute-start.5
  39.2 0.3 fusion
  39.4 1.1 %collective-permute-start.12 = (bf16[8,1,8,2,384]{4,3,2,1,0:T(2,128)(2,1)S(1)}, bf16[8,1,8,2,384]{4,3,2,1,0:T(2,128)(2,1)S(1)}, u32[]{:S(2)}, u32[]{:S(2)}) collective-permute-start(bf16[8,1,8,2,384]{4,3,2,1,0:T(2,128)(2,1)S(1)} %get-tuple-element.42), channel_id=1, source_target_pairs={{0,8},{1,9},{2,10},{3,11},{4,12},{5,13},{6,14},{7,15},{8,0},{9,1},... | collective-permute-start | bytes 294920 | tf_op jit(solution)/shard_map/ppermute | solution.py:237
  40.5 0.2 collective-permute-start.18
  40.7 3.2 %collective-permute-done.12 = bf16[8,1,8,2,384]{4,3,2,1,0:T(2,128)(2,1)S(1)} collective-permute-done((bf16[8,1,8,2,384]{4,3,2,1,0:T(2,128)(2,1)S(1)}, bf16[8,1,8,2,384]{4,3,2,1,0:T(2,128)(2,1)S(1)}, u32[]{:S(2)}, u32[]{:S(2)}) %collective-permute-start.12) | collective-permute-done | bytes 98336 | tf_op jit(solution)/shard_map/ppermute | solution.py:237
  43.9 4.0 %collective-permute-start.21 = (bf16[192,1152]{1,0:T(8,128)(2,1)S(1)}, bf16[192,1152]{1,0:T(8,128)(2,1)S(1)}, u32[]{:S(2)}, u32[]{:S(2)}) collective-permute-start(bf16[192,1152]{1,0:T(8,128)(2,1)S(1)} %constant_dynamic-update-slice_fusion.refs_2_.refs_3_), channel_id=1, source_target_pairs={{0,1},{1,0},{2,3},{3,2},{4,5},{5,4},{6,7},{7,6},{8,9},{9,8},{10,11... | collective-permute-start | bytes 1327112 | tf_op jit(solution)/shard_map/ppermute | solution.py:36
  47.8 0.5 collective-permute-start.6
  48.4 0.1 collective-permute-start.7
  48.4 0.3 pad_maximum_fusion
  48.7 1.4 %collective-permute-done.6.refs_6_ = bf16[64,1536]{1,0:T(8,128)(2,1)S(1)} collective-permute-done((bf16[64,1536]{1,0:T(8,128)(2,1)S(1)}, bf16[64,1536]{1,0:T(8,128)(2,1)S(1)}, u32[]{:S(2)}, u32[]{:S(2)}) %collective-permute-start.6) | collective-permute-done | bytes 196640 | tf_op jit(solution)/shard_map/ppermute | solution.py:36
  50.2 0.4 collective-permute-start.23
  50.5 0.1 collective-permute-start.20
  50.7 0.4 collective-permute-start.24
  51.1 0.5 shard_map.100
  51.6 0.4 collective-permute-done.20.refs_7_.refs_6_
  52.0 1.2 %shard_map.102.part_ref = f32[256,1152]{1,0:T(8,128)S(1)} custom-call(bf16[256,1536]{1,0:T(8,128)(2,1)S(1)} %get-tuple-element.33.refs_0_.normed, bf16[96,1152]{1,0:T(8,128)(2,1)S(1)} %copy-done, bf16[96,1152]{1,0:T(8,128)(2,1)S(1)} %collective-permute-done.13.refs_1_.refs_2_, bf16[192,1152]{1,0:T(8,128)(2,1)S(1)} %constant_dynamic-update-slice_fusion.refs_2_.refs_3_, ...), custom_call_target="tpu_custom_call" | custom-call | flops 679477248 | bytes 3440640 | tf_op jit(solution)/shard_map/pallas_call | solution.py:423
  53.3 1.5 %shard_map.103.first_part = bf16[256,384]{1,0:T(8,128)(2,1)S(1)} custom-call(f32[4,1536]{1,0:T(4,128)S(1)} %get-tuple-element.23.extra_ref, bf16[128,384]{1,0:T(8,128)(2,1)S(1)} %get-tuple-element.46.key_ref, bf16[128,384]{1,0:T(8,128)(2,1)S(1)} %get-tuple-element.45.value_ref, bf16[256,1536]{1,0:T(8,128)(2,1)S(1)} %get-tuple-element.33.refs_0_.normed, ...), custom_call_target="tpu_custom_call" | custom-call | flops 377487360 | bytes 3072000 | tf_op jit(solution)/shard_map/pallas_call | solution.py:423
  54.8 1.4 %collective-permute-start.27 = (bf16[256,384]{1,0:T(8,128)(2,1)S(1)}, bf16[256,384]{1,0:T(8,128)(2,1)S(1)}, u32[]{:S(2)}, u32[]{:S(2)}) collective-permute-start(bf16[256,384]{1,0:T(8,128)(2,1)S(1)} %shard_map.103.first_part), channel_id=1, source_target_pairs={{0,2},{1,3},{2,0},{3,1},{4,6},{5,7},{6,4},{7,5},{8,10},{9,11},{10,... | collective-permute-start | bytes 589832 | tf_op jit(solution)/shard_map/ppermute | solution.py:36
  56.2 1.3 %collective-permute-start.25 = (bf16[256,384]{1,0:T(8,128)(2,1)S(1)}, bf16[256,384]{1,0:T(8,128)(2,1)S(1)}, u32[]{:S(2)}, u32[]{:S(2)}) collective-permute-start(bf16[256,384]{1,0:T(8,128)(2,1)S(1)} %shard_map.103.first_part), channel_id=1, source_target_pairs={{0,6},{1,7},{2,4},{3,5},{4,2},{5,3},{6,0},{7,1},{8,14},{9,15},{10,... | collective-permute-start | bytes 589832 | tf_op jit(solution)/shard_map/ppermute | solution.py:36
  57.5 0.3 shard_map.101.weights
  57.8 3.2 %collective-permute-done.27.fourth_part = bf16[256,384]{1,0:T(8,128)(2,1)S(1)} collective-permute-done((bf16[256,384]{1,0:T(8,128)(2,1)S(1)}, bf16[256,384]{1,0:T(8,128)(2,1)S(1)}, u32[]{:S(2)}, u32[]{:S(2)}) %collective-permute-start.27) | collective-permute-done | bytes 196640 | tf_op jit(solution)/shard_map/ppermute | solution.py:36
  61.0 1.0 %collective-permute-done.26.third_part = bf16[256,384]{1,0:T(8,128)(2,1)S(1)} collective-permute-done((bf16[256,384]{1,0:T(8,128)(2,1)S(1)}, bf16[256,384]{1,0:T(8,128)(2,1)S(1)}, u32[]{:S(2)}, u32[]{:S(2)}) %collective-permute-start.26) | collective-permute-done | bytes 196640 | tf_op jit(solution)/shard_map/ppermute | solution.py:36
  62.1 4.1 %collective-permute-done.25.second_part = bf16[256,384]{1,0:T(8,128)(2,1)S(1)} collective-permute-done((bf16[256,384]{1,0:T(8,128)(2,1)S(1)}, bf16[256,384]{1,0:T(8,128)(2,1)S(1)}, u32[]{:S(2)}, u32[]{:S(2)}) %collective-permute-start.25) | collective-permute-done | bytes 196640 | tf_op jit(solution)/shard_map/ppermute | solution.py:36
  66.2 3.4 %shard_map.104 = (bf16[64,384]{1,0:T(8,128)(2,1)S(1)}, bf16[64,384]{1,0:T(8,128)(2,1)S(1)}, bf16[64,384]{1,0:T(8,128)(2,1)S(1)}, bf16[64,384]{1,0:T(8,128)(2,1)S(1)}, bf16[64,384]{1,0:T(8,128)(2,1)S(1)}) custom-call(f32[4,1536]{1,0:T(4,128)S(1)} %get-tuple-element.23.extra_ref, bf16[128,384]{1,0:T(8,128)(2,1)S(1)} %get-tuple-element.46.key_ref, ...), custom_call_target="tpu_custom_call" | custom-call | flops 1056964608 | bytes 5332992 | tf_op jit(solution)/shard_map/pallas_call | solution.py:423
  69.6 1.8 %collective-permute-start.28 = (bf16[64,384]{1,0:T(8,128)(2,1)S(1)}, bf16[64,384]{1,0:T(8,128)(2,1)S(1)}, u32[]{:S(2)}, u32[]{:S(2)}) collective-permute-start(bf16[64,384]{1,0:T(8,128)(2,1)S(1)} %get-tuple-element.35), channel_id=1, source_target_pairs={{0,2},{1,4},{2,0},{3,6},{4,1},{5,7},{6,3},{7,5},{8,10},{9,12},{10,... | collective-permute-start | bytes 147464 | tf_op jit(solution)/shard_map/ppermute | solution.py:36
  71.3 1.3 %collective-permute-start.30 = (bf16[64,384]{1,0:T(8,128)(2,1)S(1)}, bf16[64,384]{1,0:T(8,128)(2,1)S(1)}, u32[]{:S(2)}, u32[]{:S(2)}) collective-permute-start(bf16[64,384]{1,0:T(8,128)(2,1)S(1)} %get-tuple-element.37), channel_id=1, source_target_pairs={{0,1},{1,7},{2,3},{3,5},{4,2},{5,4},{6,0},{7,6},{8,9},{9,15},{10,1... | collective-permute-start | bytes 147464 | tf_op jit(solution)/shard_map/ppermute | solution.py:36
  72.6 4.5 %collective-permute-start.31 = (bf16[64,384]{1,0:T(8,128)(2,1)S(1)}, bf16[64,384]{1,0:T(8,128)(2,1)S(1)}, u32[]{:S(2)}, u32[]{:S(2)}) collective-permute-start(bf16[64,384]{1,0:T(8,128)(2,1)S(1)} %get-tuple-element.38), channel_id=1, source_target_pairs={{1,6},{3,4},{4,3},{6,1},{9,14},{11,12},{12,11},{14,9},{17,22},{19,... | collective-permute-start | bytes 147464 | tf_op jit(solution)/shard_map/ppermute | solution.py:36
  77.2 1.7 %collective-permute-done.31.fourth = bf16[64,384]{1,0:T(8,128)(2,1)S(1)} collective-permute-done((bf16[64,384]{1,0:T(8,128)(2,1)S(1)}, bf16[64,384]{1,0:T(8,128)(2,1)S(1)}, u32[]{:S(2)}, u32[]{:S(2)}) %collective-permute-start.31) | collective-permute-done | bytes 49184 | tf_op jit(solution)/shard_map/ppermute | solution.py:36
  78.9 0.7 shard_map.105
  (35 shorter events, 0.2 us)
Async XLA Ops:
  0.0 51.1 %copy-start.1 = (bf16[64,1536]{1,0:T(8,128)(2,1)S(1)}, bf16[64,1536]{1,0:T(8,128)(2,1)}, u32[]{:S(2)}) copy-start(bf16[64,1536]{1,0:T(8,128)(2,1)} %refs_0_.1) | copy-start | bytes 589828
  3.2 5.4 %collective-permute-start.8 = (bf16[4,8,2,384]{3,2,1,0:T(2,128)(2,1)}, bf16[4,8,2,384]{3,2,1,0:T(2,128)(2,1)S(1)}, u32[]{:S(2)}, u32[]{:S(2)}) collective-permute-start(bf16[4,8,2,384]{3,2,1,0:T(2,128)(2,1)} %get-tuple-element.25), channel_id=1, source_target_pairs={{0,1},{1,0},{2,3},{3,2},{4,5},{5,4},{6,7},{7,6},{8,9},{9,8},{10,11... | collective-permute-start | bytes 147464 | tf_op jit(solution)/shard_map/ppermute | solution.py:237
  3.2 9.1 %collective-permute-start.9 = (bf16[4,8,2,384]{3,2,1,0:T(2,128)(2,1)}, bf16[4,8,2,384]{3,2,1,0:T(2,128)(2,1)S(1)}, u32[]{:S(2)}, u32[]{:S(2)}) collective-permute-start(bf16[4,8,2,384]{3,2,1,0:T(2,128)(2,1)} %get-tuple-element.26), channel_id=1, source_target_pairs={{0,2},{1,3},{2,0},{3,1},{4,6},{5,7},{6,4},{7,5},{8,10},{9,11},{10,... | collective-permute-start | bytes 147464 | tf_op jit(solution)/shard_map/ppermute | solution.py:237
  6.0 7.6 %collective-permute-start.10 = (bf16[4,8,2,384]{3,2,1,0:T(2,128)(2,1)}, bf16[4,8,2,384]{3,2,1,0:T(2,128)(2,1)S(1)}, u32[]{:S(2)}, u32[]{:S(2)}) collective-permute-start(bf16[4,8,2,384]{3,2,1,0:T(2,128)(2,1)} %get-tuple-element.27), channel_id=1, source_target_pairs={{0,3},{1,2},{2,1},{3,0},{4,7},{5,6},{6,5},{7,4},{8,11},{9,10},{10,... | collective-permute-start | bytes 147464 | tf_op jit(solution)/shard_map/ppermute | solution.py:237
  6.0 20.2 %collective-permute-start.2 = (bf16[64,1536]{1,0:T(8,128)(2,1)}, bf16[64,1536]{1,0:T(8,128)(2,1)S(1)}, u32[]{:S(2)}, u32[]{:S(2)}) collective-permute-start(bf16[64,1536]{1,0:T(8,128)(2,1)} %refs_0_.1), channel_id=1, source_target_pairs={{0,1},{1,0},{2,3},{3,2},{4,5},{5,4},{6,7},{7,6},{8,9},{9,8},{10,11... | collective-permute-start | bytes 589832 | tf_op jit(solution)/shard_map/ppermute | solution.py:36
  6.4 18.1 %collective-permute-start = (f32[4,1536]{1,0:T(4,128)}, f32[4,1536]{1,0:T(4,128)S(1)}, u32[]{:S(2)}, u32[]{:S(2)}) collective-permute-start(f32[4,1536]{1,0:T(4,128)} %get-tuple-element.22), channel_id=1, source_target_pairs={{0,1},{1,0},{2,3},{3,2},{4,5},{5,4},{6,7},{7,6},{8,9},{9,8},{10,11... | collective-permute-start | bytes 73736 | tf_op jit(solution)/shard_map/ppermute | solution.py:36
  8.6 43.5 %copy-start = (bf16[96,1152]{1,0:T(8,128)(2,1)S(1)}, bf16[96,1152]{1,0:T(8,128)(2,1)}, u32[]{:S(2)}) copy-start(bf16[96,1152]{1,0:T(8,128)(2,1)} %get-tuple-element.29.refs_0_.refs_1_) | copy-start | bytes 663556
  8.6 15.7 %collective-permute-start.15 = (bf16[96,1152]{1,0:T(8,128)(2,1)}, bf16[96,1152]{1,0:T(8,128)(2,1)S(1)}, u32[]{:S(2)}, u32[]{:S(2)}) collective-permute-start(bf16[96,1152]{1,0:T(8,128)(2,1)} %get-tuple-element.32), channel_id=1, source_target_pairs={{0,8},{1,11},{2,10},{3,9},{4,12},{5,15},{6,14},{7,13},{8,0},{9,3},... | collective-permute-start | bytes 663560 | tf_op jit(solution)/shard_map/ppermute | solution.py:36
  12.3 11.9 %collective-permute-start.14 = (bf16[96,1152]{1,0:T(8,128)(2,1)}, bf16[96,1152]{1,0:T(8,128)(2,1)S(1)}, u32[]{:S(2)}, u32[]{:S(2)}) collective-permute-start(bf16[96,1152]{1,0:T(8,128)(2,1)} %get-tuple-element.31), channel_id=1, source_target_pairs={{0,4},{1,7},{2,6},{3,5},{4,0},{5,3},{6,2},{7,1},{8,12},{9,15},{10,... | collective-permute-start | bytes 663560 | tf_op jit(solution)/shard_map/ppermute | solution.py:36
  14.9 11.0 %collective-permute-start.11 = (bf16[4,2,8,2,384]{4,3,2,1,0:T(2,128)(2,1)S(1)}, bf16[4,2,8,2,384]{4,3,2,1,0:T(2,128)(2,1)S(1)}, u32[]{:S(2)}, u32[]{:S(2)}) collective-permute-start(bf16[4,2,8,2,384]{4,3,2,1,0:T(2,128)(2,1)S(1)} %get-tuple-element.44), channel_id=1, source_target_pairs={{0,4},{1,5},{2,6},{3,7},{4,0},{5,1},{6,2},{7,3},{8,12},{9,13},{10,... | collective-permute-start | bytes 294920 | tf_op jit(solution)/shard_map/ppermute | solution.py:237
  24.3 23.5 %collective-permute-start.16 = (bf16[192,1152]{1,0:T(8,128)(2,1)S(1)}, bf16[192,1152]{1,0:T(8,128)(2,1)S(1)}, u32[]{:S(2)}, u32[]{:S(2)}) collective-permute-start(bf16[192,1152]{1,0:T(8,128)(2,1)S(1)} %constant_dynamic-update-slice_fusion.refs_2_.refs_3_), channel_id=1, source_target_pairs={{0,16},{1,17},{2,18},{3,19},{4,20},{5,21},{6,22},{7,23},{8,24},{9,... | collective-permute-start | bytes 1327112 | tf_op jit(solution)/shard_map/ppermute | solution.py:36
  24.4 14.7 %collective-permute-start.13 = (bf16[96,1152]{1,0:T(8,128)(2,1)}, bf16[96,1152]{1,0:T(8,128)(2,1)S(1)}, u32[]{:S(2)}, u32[]{:S(2)}) collective-permute-start(bf16[96,1152]{1,0:T(8,128)(2,1)} %get-tuple-element.30), channel_id=1, source_target_pairs={{0,2},{1,3},{2,0},{3,1},{4,6},{5,7},{6,4},{7,5},{8,10},{9,11},{10,... | collective-permute-start | bytes 663560 | tf_op jit(solution)/shard_map/ppermute | solution.py:36
  24.5 9.7 %collective-permute-start.1 = (bf16[64,1536]{1,0:T(8,128)(2,1)}, bf16[64,1536]{1,0:T(8,128)(2,1)S(1)}, u32[]{:S(2)}, u32[]{:S(2)}) collective-permute-start(bf16[64,1536]{1,0:T(8,128)(2,1)} %refs_0_.1), channel_id=1, source_target_pairs={{0,2},{1,3},{2,0},{3,1},{4,6},{5,7},{6,4},{7,5},{8,10},{9,11},{10,... | collective-permute-start | bytes 589832 | tf_op jit(solution)/shard_map/ppermute | solution.py:36
  25.9 13.2 %collective-permute-start.4 = (bf16[64,1536]{1,0:T(8,128)(2,1)}, bf16[64,1536]{1,0:T(8,128)(2,1)S(1)}, u32[]{:S(2)}, u32[]{:S(2)}) collective-permute-start(bf16[64,1536]{1,0:T(8,128)(2,1)} %refs_0_.1), channel_id=1, source_target_pairs={{0,4},{1,5},{2,6},{3,7},{4,0},{5,1},{6,2},{7,3},{8,12},{9,13},{10,... | collective-permute-start | bytes 589832 | tf_op jit(solution)/shard_map/ppermute | solution.py:36
  26.2 13.2 %collective-permute-start.17 = (bf16[96,1152]{1,0:T(8,128)(2,1)}, bf16[96,1152]{1,0:T(8,128)(2,1)S(1)}, u32[]{:S(2)}, u32[]{:S(2)}) collective-permute-start(bf16[96,1152]{1,0:T(8,128)(2,1)} %get-tuple-element.31), channel_id=1, source_target_pairs={{0,12},{1,15},{2,14},{3,13},{4,8},{5,11},{6,10},{7,9},{8,4},{9,7},... | collective-permute-start | bytes 663560 | tf_op jit(solution)/shard_map/ppermute | solution.py:36
  34.2 6.3 %collective-permute-start.19 = (bf16[96,1152]{1,0:T(8,128)(2,1)}, bf16[96,1152]{1,0:T(8,128)(2,1)S(1)}, u32[]{:S(2)}, u32[]{:S(2)}) collective-permute-start(bf16[96,1152]{1,0:T(8,128)(2,1)} %get-tuple-element.29.refs_0_.refs_1_), channel_id=1, source_target_pairs={{0,1},{1,0},{2,3},{3,2},{4,5},{5,4},{6,7},{7,6},{8,9},{9,8},{10,11... | collective-permute-start | bytes 663560 | tf_op jit(solution)/shard_map/ppermute | solution.py:36
  39.1 8.8 %collective-permute-start.3 = (bf16[64,1536]{1,0:T(8,128)(2,1)S(1)}, bf16[64,1536]{1,0:T(8,128)(2,1)S(1)}, u32[]{:S(2)}, u32[]{:S(2)}) collective-permute-start(bf16[64,1536]{1,0:T(8,128)(2,1)S(1)} %collective-permute-done.1.refs_1_), channel_id=1, source_target_pairs={{0,1},{1,0},{2,3},{3,2},{4,5},{5,4},{6,7},{7,6},{8,9},{9,8},{10,11... | collective-permute-start | bytes 589832 | tf_op jit(solution)/shard_map/ppermute | solution.py:36
  39.1 9.3 %collective-permute-start.5 = (bf16[64,1536]{1,0:T(8,128)(2,1)S(1)}, bf16[64,1536]{1,0:T(8,128)(2,1)S(1)}, u32[]{:S(2)}, u32[]{:S(2)}) collective-permute-start(bf16[64,1536]{1,0:T(8,128)(2,1)S(1)} %collective-permute-done.4.refs_4_), channel_id=1, source_target_pairs={{0,2},{1,3},{2,0},{3,1},{4,6},{5,7},{6,4},{7,5},{8,10},{9,11},{10,... | collective-permute-start | bytes 589832 | tf_op jit(solution)/shard_map/ppermute | solution.py:36
  39.4 4.4 %collective-permute-start.12 = (bf16[8,1,8,2,384]{4,3,2,1,0:T(2,128)(2,1)S(1)}, bf16[8,1,8,2,384]{4,3,2,1,0:T(2,128)(2,1)S(1)}, u32[]{:S(2)}, u32[]{:S(2)}) collective-permute-start(bf16[8,1,8,2,384]{4,3,2,1,0:T(2,128)(2,1)S(1)} %get-tuple-element.42), channel_id=1, source_target_pairs={{0,8},{1,9},{2,10},{3,11},{4,12},{5,13},{6,14},{7,15},{8,0},{9,1},... | collective-permute-start | bytes 294920 | tf_op jit(solution)/shard_map/ppermute | solution.py:237
  40.5 10.1 %collective-permute-start.18 = (bf16[96,1152]{1,0:T(8,128)(2,1)S(1)}, bf16[96,1152]{1,0:T(8,128)(2,1)S(1)}, u32[]{:S(2)}, u32[]{:S(2)}) collective-permute-start(bf16[96,1152]{1,0:T(8,128)(2,1)S(1)} %collective-permute-done.17.refs_4_.refs_0_), channel_id=1, source_target_pairs={{0,16},{1,17},{2,18},{3,19},{4,20},{5,21},{6,22},{7,23},{8,24},{9,... | collective-permute-start | bytes 663560 | tf_op jit(solution)/shard_map/ppermute | solution.py:36
  43.9 8.2 %collective-permute-start.21 = (bf16[192,1152]{1,0:T(8,128)(2,1)S(1)}, bf16[192,1152]{1,0:T(8,128)(2,1)S(1)}, u32[]{:S(2)}, u32[]{:S(2)}) collective-permute-start(bf16[192,1152]{1,0:T(8,128)(2,1)S(1)} %constant_dynamic-update-slice_fusion.refs_2_.refs_3_), channel_id=1, source_target_pairs={{0,1},{1,0},{2,3},{3,2},{4,5},{5,4},{6,7},{7,6},{8,9},{9,8},{10,11... | collective-permute-start | bytes 1327112 | tf_op jit(solution)/shard_map/ppermute | solution.py:36
  47.8 4.2 %collective-permute-start.22 = (bf16[192,1152]{1,0:T(8,128)(2,1)S(1)}, bf16[192,1152]{1,0:T(8,128)(2,1)S(1)}, u32[]{:S(2)}, u32[]{:S(2)}) collective-permute-start(bf16[192,1152]{1,0:T(8,128)(2,1)S(1)} %collective-permute-done.16.refs_3_.refs_4_), channel_id=1, source_target_pairs={{0,1},{1,0},{2,3},{3,2},{4,5},{5,4},{6,7},{7,6},{8,9},{9,8},{10,11... | collective-permute-start | bytes 1327112 | tf_op jit(solution)/shard_map/ppermute | solution.py:36
  47.8 2.3 %collective-permute-start.6 = (bf16[64,1536]{1,0:T(8,128)(2,1)S(1)}, bf16[64,1536]{1,0:T(8,128)(2,1)S(1)}, u32[]{:S(2)}, u32[]{:S(2)}) collective-permute-start(bf16[64,1536]{1,0:T(8,128)(2,1)S(1)} %collective-permute-done.4.refs_4_), channel_id=1, source_target_pairs={{0,1},{1,0},{2,3},{3,2},{4,5},{5,4},{6,7},{7,6},{8,9},{9,8},{10,11... | collective-permute-start | bytes 589832 | tf_op jit(solution)/shard_map/ppermute | solution.py:36
  48.4 2.3 %collective-permute-start.7 = (bf16[64,1536]{1,0:T(8,128)(2,1)S(1)}, bf16[64,1536]{1,0:T(8,128)(2,1)S(1)}, u32[]{:S(2)}, u32[]{:S(2)}) collective-permute-start(bf16[64,1536]{1,0:T(8,128)(2,1)S(1)} %collective-permute-done.5.refs_5_), channel_id=1, source_target_pairs={{0,1},{1,0},{2,3},{3,2},{4,5},{5,4},{6,7},{7,6},{8,9},{9,8},{10,11... | collective-permute-start | bytes 589832 | tf_op jit(solution)/shard_map/ppermute | solution.py:36
  50.2 3.1 %collective-permute-start.23 = (bf16[96,1152]{1,0:T(8,128)(2,1)S(1)}, bf16[96,1152]{1,0:T(8,128)(2,1)S(1)}, u32[]{:S(2)}, u32[]{:S(2)}) collective-permute-start(bf16[96,1152]{1,0:T(8,128)(2,1)S(1)} %collective-permute-done.17.refs_4_.refs_0_), channel_id=1, source_target_pairs={{0,1},{1,0},{2,3},{3,2},{4,5},{5,4},{6,7},{7,6},{8,9},{9,8},{10,11... | collective-permute-start | bytes 663560 | tf_op jit(solution)/shard_map/ppermute | solution.py:36
  50.5 1.5 %collective-permute-start.20 = (bf16[96,1152]{1,0:T(8,128)(2,1)S(1)}, bf16[96,1152]{1,0:T(8,128)(2,1)S(1)}, u32[]{:S(2)}, u32[]{:S(2)}) collective-permute-start(bf16[96,1152]{1,0:T(8,128)(2,1)S(1)} %collective-permute-done.13.refs_1_.refs_2_), channel_id=1, source_target_pairs={{0,1},{1,0},{2,3},{3,2},{4,5},{5,4},{6,7},{7,6},{8,9},{9,8},{10,11... | collective-permute-start | bytes 663560 | tf_op jit(solution)/shard_map/ppermute | solution.py:36
  50.7 2.6 %collective-permute-start.24 = (bf16[96,1152]{1,0:T(8,128)(2,1)S(1)}, bf16[96,1152]{1,0:T(8,128)(2,1)S(1)}, u32[]{:S(2)}, u32[]{:S(2)}) collective-permute-start(bf16[96,1152]{1,0:T(8,128)(2,1)S(1)} %collective-permute-done.18.refs_5_.refs_1_), channel_id=1, source_target_pairs={{0,1},{1,0},{2,3},{3,2},{4,5},{5,4},{6,7},{7,6},{8,9},{9,8},{10,11... | collective-permute-start | bytes 663560 | tf_op jit(solution)/shard_map/ppermute | solution.py:36
  54.8 6.2 %collective-permute-start.27 = (bf16[256,384]{1,0:T(8,128)(2,1)S(1)}, bf16[256,384]{1,0:T(8,128)(2,1)S(1)}, u32[]{:S(2)}, u32[]{:S(2)}) collective-permute-start(bf16[256,384]{1,0:T(8,128)(2,1)S(1)} %shard_map.103.first_part), channel_id=1, source_target_pairs={{0,2},{1,3},{2,0},{3,1},{4,6},{5,7},{6,4},{7,5},{8,10},{9,11},{10,... | collective-permute-start | bytes 589832 | tf_op jit(solution)/shard_map/ppermute | solution.py:36
  56.2 5.9 %collective-permute-start.26 = (bf16[256,384]{1,0:T(8,128)(2,1)S(1)}, bf16[256,384]{1,0:T(8,128)(2,1)S(1)}, u32[]{:S(2)}, u32[]{:S(2)}) collective-permute-start(bf16[256,384]{1,0:T(8,128)(2,1)S(1)} %shard_map.103.first_part), channel_id=1, source_target_pairs={{0,4},{1,5},{2,6},{3,7},{4,0},{5,1},{6,2},{7,3},{8,12},{9,13},{10,... | collective-permute-start | bytes 589832 | tf_op jit(solution)/shard_map/ppermute | solution.py:36
  56.2 9.9 %collective-permute-start.25 = (bf16[256,384]{1,0:T(8,128)(2,1)S(1)}, bf16[256,384]{1,0:T(8,128)(2,1)S(1)}, u32[]{:S(2)}, u32[]{:S(2)}) collective-permute-start(bf16[256,384]{1,0:T(8,128)(2,1)S(1)} %shard_map.103.first_part), channel_id=1, source_target_pairs={{0,6},{1,7},{2,4},{3,5},{4,2},{5,3},{6,0},{7,1},{8,14},{9,15},{10,... | collective-permute-start | bytes 589832 | tf_op jit(solution)/shard_map/ppermute | solution.py:36
  69.6 7.6 %collective-permute-start.28 = (bf16[64,384]{1,0:T(8,128)(2,1)S(1)}, bf16[64,384]{1,0:T(8,128)(2,1)S(1)}, u32[]{:S(2)}, u32[]{:S(2)}) collective-permute-start(bf16[64,384]{1,0:T(8,128)(2,1)S(1)} %get-tuple-element.35), channel_id=1, source_target_pairs={{0,2},{1,4},{2,0},{3,6},{4,1},{5,7},{6,3},{7,5},{8,10},{9,12},{10,... | collective-permute-start | bytes 147464 | tf_op jit(solution)/shard_map/ppermute | solution.py:36
  71.3 5.8 %collective-permute-start.29 = (bf16[64,384]{1,0:T(8,128)(2,1)S(1)}, bf16[64,384]{1,0:T(8,128)(2,1)S(1)}, u32[]{:S(2)}, u32[]{:S(2)}) collective-permute-start(bf16[64,384]{1,0:T(8,128)(2,1)S(1)} %get-tuple-element.36), channel_id=1, source_target_pairs={{0,3},{1,5},{2,1},{3,7},{4,0},{5,6},{6,2},{7,4},{8,11},{9,13},{10,... | collective-permute-start | bytes 147464 | tf_op jit(solution)/shard_map/ppermute | solution.py:36
  71.3 5.8 %collective-permute-start.30 = (bf16[64,384]{1,0:T(8,128)(2,1)S(1)}, bf16[64,384]{1,0:T(8,128)(2,1)S(1)}, u32[]{:S(2)}, u32[]{:S(2)}) collective-permute-start(bf16[64,384]{1,0:T(8,128)(2,1)S(1)} %get-tuple-element.37), channel_id=1, source_target_pairs={{0,1},{1,7},{2,3},{3,5},{4,2},{5,4},{6,0},{7,6},{8,9},{9,15},{10,1... | collective-permute-start | bytes 147464 | tf_op jit(solution)/shard_map/ppermute | solution.py:36
  72.6 6.3 %collective-permute-start.31 = (bf16[64,384]{1,0:T(8,128)(2,1)S(1)}, bf16[64,384]{1,0:T(8,128)(2,1)S(1)}, u32[]{:S(2)}, u32[]{:S(2)}) collective-permute-start(bf16[64,384]{1,0:T(8,128)(2,1)S(1)} %get-tuple-element.38), channel_id=1, source_target_pairs={{1,6},{3,4},{4,3},{6,1},{9,14},{11,12},{12,11},{14,9},{17,22},{19,... | collective-permute-start | bytes 147464 | tf_op jit(solution)/shard_map/ppermute | solution.py:36
